TPU v7x, 128 devices: a whole 4x4x4 slice. The times are simulated.
128 devices in a mesh: tile: 16 (over x, y), view: 8 (over z, core).
Axes of the slice: x: 4, y: 4, z: 4, core: 2. Of those that a mesh axis runs over, the one named last changes fastest.
Arguments:
- estimate: float32 [2, 224, 448, 128], P(None, 'view', 'tile'), may hold values from 0.25 to 4
- view_data: bfloat16 [8, 16, 3, 2, 58, 58, 128], P('view', 'tile'), may hold values from 0.25 to 4
- psf: float32 [6, 3, 31], replicated, may hold values from 0 to 0.5, as said below
- background: float32 [6], replicated, may hold values from 0.1 to 1
- slot_brick: int32 [8, 16, 3], P('view', 'tile'), may hold values from 0 to 15, as said below
- slot_view: int32 [8, 16, 3], P('view', 'tile'), may hold values from 0 to 5, as said below
- intersection: int32 [8, 16, 6], P('view', 'tile'), may hold values from 0 to 1, as said below
Outputs:
- updated: float32 [2, 224, 448, 128], P(None, 'view', 'tile')
Inputs may be any that keep to these rules, and one draw needn't show every extreme that they name: `slot_brick`: within a group, the jobs are exactly the pairs (brick, view) that intersection marks, each once; every brick has at least one view and one brick of each group has all 6; the jobs of a group fill its workers' 3 slots exactly. `slot_view`: the view of each job, consistent with intersection. `intersection`: each brick's row has between 1 and 6 ones. `psf`: all taps are positive.
All inputs are finite; a program needn't handle non-finite values.
Results may differ from a plain program's by a relative error of at most 0.0003.
Values may be sent and summed in bfloat16 or wider, within the bound.
No kernel may reach another device: no remote copies, remote signals or barrier semaphores. Data moves between devices by JAX's collectives and lax.ppermute only.
A program may use at most 128 MiB of HBM per device.

v0:
```python
import jax
import jax.numpy as jnp
from jax import lax
from jax.sharding import PartitionSpec as P


def extended(array, sides, width):
    for axis, dim in sides:
        count, length = (lax.axis_size(axis), array.shape[dim])
        up = [(i, (i + 1) % count) for i in range(count - 1)]
        down = [(j, i) for i, j in up]
        last = lax.slice_in_dim(array, length - width, length, axis=dim)
        leading = lax.slice_in_dim(array, 0, width, axis=dim)
        before = lax.ppermute(last, axis, up)
        after = lax.ppermute(leading, axis, down)
        array = jnp.concatenate([before, array, after], axis=dim)
    return array


def banded(kernel_taps, order, rim_width):
    offsets = jnp.arange(order)[None, :] - jnp.arange(order)[:, None] + rim_width
    matches = offsets[:, :, None] == jnp.arange(kernel_taps.shape[0])[None, None, :]
    return jnp.sum(jnp.where(matches, kernel_taps[None, None, :], 0.0), axis=2)


def forward_blur(block, kernels, rim_width):
    band_x = banded(kernels[0], block.shape[1], rim_width)
    band_y = banded(kernels[1], block.shape[2], rim_width)
    band_z = banded(kernels[2], block.shape[3], rim_width)
    result = jnp.einsum("cxyz,wz->cxyw", block, band_z, precision=lax.Precision.HIGHEST)
    result = jnp.einsum("cxyz,vy->cxvz", result, band_y, precision=lax.Precision.HIGHEST)
    return jnp.einsum("cxyz,ux->cuyz", result, band_x, precision=lax.Precision.HIGHEST)


def backward_blur(ratio, kernels, rim_width, brick_x, brick_y):
    band_x = banded(kernels[0], ratio.shape[1], rim_width)[:, rim_width : rim_width + brick_x]
    band_y = banded(kernels[1], ratio.shape[2], rim_width)[:, rim_width : rim_width + brick_y]
    band_z = banded(kernels[2], ratio.shape[3], rim_width)
    result = jnp.einsum("cxyz,xu->cuyz", ratio, band_x, precision=lax.Precision.HIGHEST)
    result = jnp.einsum("cxyz,yv->cxvz", result, band_y, precision=lax.Precision.HIGHEST)
    return jnp.einsum("cxyz,zw->cxyw", result, band_z, precision=lax.Precision.HIGHEST)


def correction(block, measured, psf, background, view_index, rim_width, brick_x, brick_y):
    kernels = lax.dynamic_index_in_dim(psf, view_index, 0, keepdims=False)
    backdrop = lax.dynamic_index_in_dim(background, view_index, 0, keepdims=False)
    predicted = forward_blur(block, kernels, rim_width) + backdrop
    ratio = measured.astype(jnp.float32) / predicted
    return backward_blur(ratio, kernels, rim_width, brick_x, brick_y)


def on_device(estimate, view_data, psf, background, slot_brick, slot_view, intersection):
    rim_width = psf.shape[2] // 2
    channels, brick_x, brick_y, depth_cells = estimate.shape
    est_wire = estimate.astype(jnp.bfloat16)
    padded = extended(est_wire, (("tile", 2), ("view", 1)), rim_width)
    gathered = lax.all_gather(padded[None], "tile", axis=0, tiled=True)
    owners = lax.axis_size("tile")
    contrib = jnp.zeros((owners, channels, brick_x, brick_y, depth_cells), jnp.float32)
    for slot_index in range(slot_brick.shape[2]):
        brick_index = slot_brick[0, 0, slot_index]
        view_index = slot_view[0, 0, slot_index]
        block = lax.dynamic_index_in_dim(gathered, brick_index, 0, keepdims=False).astype(
            jnp.float32
        )
        factor = correction(
            block,
            view_data[0, 0, slot_index],
            psf,
            background,
            view_index,
            rim_width,
            brick_x,
            brick_y,
        )
        owner_marks = (jnp.arange(owners) == brick_index).astype(jnp.float32)
        contrib = contrib + owner_marks[:, None, None, None, None] * factor[None]
    summed = lax.psum_scatter(contrib, "tile", scatter_dimension=0, tiled=True)[0]
    views_seen = jnp.sum(intersection[0, 0]).astype(jnp.float32)
    return estimate * summed / views_seen


def solution(mesh):
    placed = (
        P(None, "view", "tile", None),
        P("view", "tile", None, None, None, None, None),
        P(),
        P(),
        P("view", "tile", None),
        P("view", "tile", None),
        P("view", "tile", None),
    )
    return jax.shard_map(
        on_device,
        mesh=mesh,
        in_specs=placed,
        out_specs=P(None, "view", "tile", None),
        check_vma=False,
    )
```

profile of v0, /device:TPU:32, one launch (start us, length us, event | category | flops | bytes accessed | tf_op | source)
XLA Modules:
  0.0 481.1 jit_solution(7533203977830049392)
XLA Ops:
  7.9 3.5 collective-permute-start
  12.7 3.5 collective-permute-done
  16.2 4.1 collective-permute-done.1
  22.8 3.6 collective-permute-start.3
  26.4 4.6 collective-permute-done.2
  53.1 6.5 %fusion.59 = (bf16[1,1,1,2,58,58,128]{6,3,5,4,2,1,0:T(2,128)(2,1)S(1)}, bf16[1,1,1,2,58,58,128]{6,3,5,4,2,1,0:T(2,128)(2,1)S(1)}, bf16[1,1,1,2,58,58,128]{6,3,5,4,2,1,0:T(2,128)(2,1)}) fusion(bf16[1,1,3,2,58,58,128]{6,3,5,4,2,1,0:T(2,128)(2,1)} %param.8), kind=kLoop, calls=%fused_computation.101 | loop fusion | bytes 10334208 | tf_op jit(solution)/shard_map/slice | solution.py:68
  59.6 160.5 %all-gather.3.cloned.1.call-done = bf16[32,58,58,128]{3,2,1,0:T(8,128)(2,1)} async-done(((bf16[2,58,58,128]{3,2,1,0:T(8,128)(2,1)}), bf16[32,58,58,128]{3,2,1,0:T(8,128)(2,1)}) %all-gather.3.cloned.1.call-update) | async-done | bytes 27557904 | tf_op jit(solution)/shard_map/all_gather | solution.py:57
  220.1 3.2 fusion.9
  223.4 3.6 convolution_bitcast_fusion
  227.1 5.5 %fusion = f32[58,2,58,128]{3,0,2,1:T(8,128)S(1)} fusion(f32[2,58,58,128]{3,2,1,0:T(8,128)S(1)} %convolution_bitcast_fusion, f32[58,58]{1,0:T(8,128)S(1)} %copy-done.8), kind=kOutput, calls=%fused_computation.4 | convolution fusion | flops 599384064 | bytes 6902928 | tf_op jit(solution)/shard_map/cxyz,ux->cuyz/dot_general | solution.py:32
  232.6 3.6 fusion.27
  236.2 2.0 fusion.36
  239.7 3.2 fusion.13
  243.0 3.7 convolution_bitcast_fusion.2
  246.7 5.9 %fusion.4 = f32[58,2,58,128]{3,0,2,1:T(8,128)S(1)} fusion(f32[2,58,58,128]{3,2,1,0:T(8,128)S(1)} %convolution_bitcast_fusion.2, f32[58,58]{1,0:T(8,128)S(1)} %copy-done.7), kind=kOutput, calls=%fused_computation.8 | convolution fusion | flops 599384064 | bytes 6902928 | tf_op jit(solution)/shard_map/cxyz,ux->cuyz/dot_general | solution.py:32
  252.6 3.4 fusion.29
  258.1 3.2 fusion.11
  261.3 3.8 convolution_bitcast_fusion.1
  265.2 5.5 %fusion.2 = f32[58,2,58,128]{3,0,2,1:T(8,128)S(1)} fusion(f32[2,58,58,128]{3,2,1,0:T(8,128)S(1)} %convolution_bitcast_fusion.1, f32[58,58]{1,0:T(8,128)S(1)} %copy-done.6), kind=kOutput, calls=%fused_computation.6 | convolution fusion | flops 599384064 | bytes 6902928 | tf_op jit(solution)/shard_map/cxyz,ux->cuyz/dot_general | solution.py:32
  270.7 3.4 fusion.28
  274.1 2.0 fusion.33
  279.4 10.7 %multiply_add_fusion = f32[16,2,28,28,128]{4,1,3,2,0:T(2,128)} fusion(f32[2,28,28,128]{3,0,2,1:T(2,128)S(1)} %copy.33, f32[2,28,28,128]{3,0,2,1:T(2,128)S(1)} %copy.27, f32[2,28,28,128]{3,0,2,1:T(2,128)S(1)} %copy.21, f32[16]{0:T(128)S(1)} %get-tuple-element.45, f32[16]{0:T(128)S(1)} %get-tuple-element.46, f32[16]{0:T(128)S(1)} %copy-done.13), kind=kLoop, calls=%fused_computation | loop fusion | flops 16056320 | bytes 15253696 | tf_op jit(solution)/shard_map/add | solution.py:77
  292.7 178.3 %all-reduce.3.cloned.1.call-done = f32[16,2,28,28,128]{4,1,3,2,0:T(2,128)} async-done(((f32[16,2,28,28,128]{4,1,3,2,0:T(2,128)}), f32[16,2,28,28,128]{4,1,3,2,0:T(2,128)}) %all-reduce.3.cloned.1.call-update) | async-done | bytes 12845072
  470.9 3.1 fusion.40
  (65 shorter events, 24.8 us)
Async XLA Ops:
  6.5 213.6 %all-gather.3.cloned.1.call-start = ((), (), s32[]{:S(2)}) async-start(), calls=%async_computation | async-start | bytes 32309248 | tf_op jit(solution)/shard_map/all_gather | solution.py:57
  7.9 8.3 %collective-permute-start = (bf16[2,28,15,128]{3,2,1,0:T(8,128)(2,1)S(1)}, bf16[2,28,15,128]{3,2,1,0:T(8,128)(2,1)S(1)}, u32[]{:S(2)}, u32[]{:S(2)}) collective-permute-start(bf16[2,28,15,128]{3,2,1,0:T(8,128)(2,1)S(1)} %get-tuple-element.19), channel_id=1, source_target_pairs={{0,8},{8,16},{16,24},{24,32},{32,40},{40,48},{48,56},{56,64},{64,7... | collective-permute-start | bytes 645128 | tf_op jit(solution)/shard_map/ppermute | solution.py:14
  11.4 9.0 %collective-permute-start.1 = (bf16[2,28,15,128]{3,2,1,0:T(8,128)(2,1)S(1)}, bf16[2,28,15,128]{3,2,1,0:T(8,128)(2,1)S(1)}, u32[]{:S(2)}, u32[]{:S(2)}) collective-permute-start(bf16[2,28,15,128]{3,2,1,0:T(8,128)(2,1)S(1)} %get-tuple-element.20), channel_id=1, source_target_pairs={{8,0},{16,8},{24,16},{32,24},{40,32},{48,40},{56,48},{64,56},{72,6... | collective-permute-start | bytes 645128 | tf_op jit(solution)/shard_map/ppermute | solution.py:15
  20.7 13.9 %copy-start.9 = (s32[1,1,3]{2,1,0:T(1,128)S(1)}, s32[1,1,3]{2,1,0:T(1,128)}, u32[]{:S(2)}) copy-start(s32[1,1,3]{2,1,0:T(1,128)} %param.11) | copy-start | bytes 40
  20.7 18.2 %copy-start.10 = (s32[1,1,3]{2,1,0:T(1,128)S(1)}, s32[1,1,3]{2,1,0:T(1,128)}, u32[]{:S(2)}) copy-start(s32[1,1,3]{2,1,0:T(1,128)} %param.12) | copy-start | bytes 40
  20.7 26.0 %copy-start.11 = (f32[6]{0:T(128)S(1)}, f32[6]{0:T(128)}, u32[]{:S(2)}) copy-start(f32[6]{0:T(128)} %param.10) | copy-start | bytes 76
  20.7 29.0 %copy-start.12 = (f32[6,3,31]{2,1,0:T(4,128)S(1)}, f32[6,3,31]{2,1,0:T(4,128)}, u32[]{:S(2)}) copy-start(f32[6,3,31]{2,1,0:T(4,128)} %param.9) | copy-start | bytes 6700
  20.8 10.1 %collective-permute-start.2 = (bf16[2,15,58,128]{3,2,1,0:T(8,128)(2,1)S(1)}, bf16[2,15,58,128]{3,2,1,0:T(8,128)(2,1)S(1)}, u32[]{:S(2)}, u32[]{:S(2)}) collective-permute-start(bf16[2,15,58,128]{3,2,1,0:T(8,128)(2,1)S(1)} %get-tuple-element.17), channel_id=1, source_target_pairs={{0,1},{1,2},{2,3},{3,4},{4,5},{5,6},{6,7},{8,9},{9,10},{10,11},{11... | collective-permute-start | bytes 1336328 | tf_op jit(solution)/shard_map/ppermute | solution.py:14
  22.8 10.0 %collective-permute-start.3 = (bf16[2,15,58,128]{3,2,1,0:T(8,128)(2,1)S(1)}, bf16[2,15,58,128]{3,2,1,0:T(8,128)(2,1)S(1)}, u32[]{:S(2)}, u32[]{:S(2)}) collective-permute-start(bf16[2,15,58,128]{3,2,1,0:T(8,128)(2,1)S(1)} %get-tuple-element.18), channel_id=1, source_target_pairs={{1,0},{2,1},{3,2},{4,3},{5,4},{6,5},{7,6},{9,8},{10,9},{11,10},{12... | collective-permute-start | bytes 1336328 | tf_op jit(solution)/shard_map/ppermute | solution.py:15
  34.5 436.4 %all-reduce.3.cloned.1.call-start = ((), (), s32[]{:S(2)}) async-start(), calls=%async_computation.1 | async-start | bytes 25690112
  220.1 3.2 copy-start.5
  223.4 3.7 copy-start.8
  227.1 5.5 %copy-start.1 = (bf16[1,1,1,2,58,58,128]{6,3,5,4,2,1,0:T(2,128)(2,1)S(1)}, bf16[1,1,1,2,58,58,128]{6,3,5,4,2,1,0:T(2,128)(2,1)}, u32[]{:S(2)}) copy-start(bf16[1,1,1,2,58,58,128]{6,3,5,4,2,1,0:T(2,128)(2,1)} %get-tuple-element.16) | copy-start | bytes 5167108
  232.5 5.7 %copy-start.3 = (f32[128,128]{1,0:T(8,128)S(1)}, f32[128,128]{1,0:T(8,128)}, u32[]{:S(2)}) copy-start(f32[128,128]{1,0:T(8,128)} %get-tuple-element.6) | copy-start | bytes 196612
  239.1 3.9 copy-start.4
  243.0 3.7 copy-start.7
  252.6 5.5 %copy-start.2 = (f32[128,128]{1,0:T(8,128)S(1)}, f32[128,128]{1,0:T(8,128)}, u32[]{:S(2)}) copy-start(f32[128,128]{1,0:T(8,128)} %get-tuple-element.7) | copy-start | bytes 196612
  261.3 3.9 copy-start.6
  276.1 3.3 copy-start.13
  290.1 0.7 copy-start.14
  290.1 1.9 copy-start.15
  290.1 180.8 %copy-start = (f32[2,28,28,128]{3,0,2,1:T(2,128)S(1)}, f32[2,28,28,128]{3,0,2,1:T(2,128)}, u32[]{:S(2)}) copy-start(f32[2,28,28,128]{3,0,2,1:T(2,128)} %param.7) | copy-start | bytes 2408452
Sparse Core Ops, SparseCore 0:
  34.6 185.4 all-gather.2
  290.3 180.6 all-reduce.2
where the time goes:
time: 487 us; the launch traced here: 481 us
  waiting for transfers between devices  353 us (72%)
  matrix products  57.1 us (12%)
  between operations  25.6 us (5%)
  other arithmetic  22.1 us (5%)
  local copies, waits for them, and re-layouts  13 us (3%)
  starting transfers between devices  10.4 us (2%)
    unnamed x3, waiting for transfers between devices  178 us
    all_gather x1, waiting for transfers between devices, on_device(): gathered = lax.all_gather(padded[None], 'tile', axis=0, tiled=True)  161 us
    dot_general x3, matrix products, forward_blur(): jnp.einsum('cxyz,ux->cuyz', result, band_x, precision=lax.Precision.HIGHEST)  16.8 us
    dot_general x3, matrix products, forward_blur(): jnp.einsum('cxyz,vy->cxvz', result, band_y, precision=lax.Precision.HIGHEST)  11.1 us
    add x1, other arithmetic, on_device(): contrib = contrib + owner_marks[:, None, None, None, None] * factor[None]  10.7 us
    dot_general x3, matrix products, backward_blur(): jnp.einsum('cxyz,xu->cuyz', ratio, band_x, precision=lax.Precision.HIGHEST)  10.5 us
  transfers between devices with their start and end apart: 6, of which 6 were waited for; matrix products, arithmetic and copies ran while one was open for 3% of the time, Pallas kernels for 0%

commit v1 on v0

v1 whole, which is shorter than its diff:
```python
import functools

import jax
import jax.numpy as jnp
from jax import lax
from jax.experimental import pallas as pl
from jax.experimental.pallas import tpu as pltpu
from jax.sharding import PartitionSpec as P

F32, BF16, I32 = jnp.float32, jnp.bfloat16, jnp.int32
HALO = 15
SIDE = 28
WIN = SIDE + 2 * HALO
PADW = 64
PADS = 32
RIM = 16
RING = 4


def torus_step(array, dx, dy):
    pairs = [
        (x * RING + y, ((x + dx) % RING) * RING + (y + dy) % RING)
        for x in range(RING)
        for y in range(RING)
    ]
    return lax.ppermute(array, "tile", pairs)


def ring_gather(arrays, axes):
    step = lambda a, axis, d: torus_step(a, d if axis == 0 else 0, d if axis == 1 else 0)
    near = [(step(a, ax, 1), step(a, ax, -1)) for a, ax in zip(arrays, axes)]
    far = []
    for (lower, upper), ax in zip(near, axes):
        half = lower.shape[0] // 2
        far.append((step(lower[:half], ax, 1), step(upper[half:], ax, -1)))
    return [
        jnp.concatenate([a, lo, up, f0, f1], axis=0)
        for a, (lo, up), (f0, f1) in zip(arrays, near, far)
    ]


def place_of(brick, me, x_first):
    def rank(delta):
        delta = delta % RING
        return jnp.where(delta == 3, 1, jnp.where(delta == 1, 2, jnp.where(delta == 2, 3, 0)))

    in_x = rank(brick // RING - me // RING)
    in_y = rank(brick % RING - me % RING)
    return (in_y * RING + in_x if x_first else in_x * RING + in_y).astype(I32)


def window_table(bricks, me, x_first):
    count = RING * RING
    before = jnp.maximum(bricks - 1, 0)
    after = jnp.minimum(bricks + 1, count - 1)
    return jnp.stack(
        [
            place_of(before, me, x_first),
            place_of(bricks, me, x_first),
            place_of(after, me, x_first),
            (bricks > 0).astype(I32),
            (bricks < count - 1).astype(I32),
        ]
    )


def margin_kernel(table, prev_ref, own_ref, next_ref, out_ref):
    side, slot = pl.program_id(0), pl.program_id(1)
    item = side * pl.num_programs(1) + slot
    has_prev, has_next = table[3, item] > 0, table[4, item] > 0

    def move(first):
        zero = jnp.zeros((HALO, RIM, 128), F32)
        rows = slice(first, first + RIM)
        prev = prev_ref[SIDE - HALO : SIDE, rows, :].astype(F32)
        out_ref[0, 0, 0:HALO] = jnp.where(has_prev, prev, zero).astype(BF16)
        out_ref[0, 0, HALO : HALO + SIDE] = own_ref[:, rows, :]
        after = next_ref[0:HALO, rows, :].astype(F32)
        out_ref[0, 0, HALO + SIDE : WIN] = jnp.where(has_next, after, zero).astype(BF16)

    pl.when(side == 0)(functools.partial(move, SIDE - RIM))
    pl.when(side == 1)(functools.partial(move, 0))


def brick_spec(which, item_of):
    return pl.BlockSpec(
        (SIDE, PADS, 128), lambda *args: (args[-1][which, item_of(*args[:-1])], 0, 0)
    )


def margins(gathered, table):
    slots = table.shape[1] // 2
    specs = [brick_spec(i, lambda side, slot: side * slots + slot) for i in range(3)]
    return pl.pallas_call(
        margin_kernel,
        grid_spec=pltpu.PrefetchScalarGridSpec(
            num_scalar_prefetch=1,
            grid=(2, slots),
            in_specs=specs,
            out_specs=pl.BlockSpec(
                (1, 1, WIN, RIM, 128), lambda side, slot, table: (side, slot, 0, 0, 0)
            ),
        ),
        out_shape=jax.ShapeDtypeStruct((2, slots, WIN, RIM, 128), BF16),
        name="margins",
    )(table, gathered, gathered, gathered)


def split(value):
    high = value.astype(BF16)
    low = (value - high.astype(F32)).astype(BF16)
    return high, low


def stacked(first, second):
    (h0, l0), (h1, l1) = split(first), split(second)
    high = jnp.concatenate([h0, h1], axis=1)
    low = jnp.concatenate([l0, l1], axis=1)
    return jnp.concatenate([high, low, high], axis=0)


def dot(a, b):
    return jnp.dot(a, b, preferred_element_type=F32)


def job_kernel(
    table, prev_ref, own_ref, next_ref, top_ref, bottom_ref, data_ref, back_ref,
    mz_ref, mx_ref, my_ref, myt_ref, mxt_ref, mzt_ref, out_ref,
    block, blurred_x, back_y, back_x,
):
    slot = pl.program_id(0)
    has_prev, has_next = table[3, slot] > 0, table[4, slot] > 0
    mid = slice(RIM, RIM + PADS)

    @pl.when(slot == 0)
    def _():
        block[WIN:] = jnp.zeros_like(block[WIN:])
        blurred_x[WIN * PADW :] = jnp.zeros_like(blurred_x[WIN * PADW :])
        back_y[WIN * PADS :] = jnp.zeros_like(back_y[WIN * PADS :])
        back_x[SIDE * PADS :] = jnp.zeros_like(back_x[SIDE * PADS :])

    zero = jnp.zeros((HALO, PADS, 128), F32)
    block[0:WIN, 0:RIM, :] = top_ref[0]
    block[0:WIN, RIM + PADS :, :] = bottom_ref[0]
    prev = prev_ref[SIDE - HALO : SIDE].astype(F32)
    block[0:HALO, mid, :] = jnp.where(has_prev, prev, zero).astype(BF16)
    block[HALO : HALO + SIDE, mid, :] = own_ref[...]
    after = next_ref[0:HALO].astype(F32)
    block[HALO + SIDE : WIN, mid, :] = jnp.where(has_next, after, zero).astype(BF16)

    mz, mx, my = mz_ref[0], mx_ref[0], my_ref[0]
    myt, mxt, mzt = myt_ref[0], mxt_ref[0], mzt_ref[0]
    backdrop = back_ref[slot]

    def along_zx(i, carry):
        rows = block[pl.ds(2 * i, 2)].reshape(2 * PADW, 128)
        in_z = dot(jnp.concatenate([rows, rows], axis=1), mz)
        in_x = dot(mx, stacked(in_z[:PADW], in_z[PADW:]))
        start = pl.multiple_of(2 * i * PADW, 2 * PADW)
        blurred_x[pl.ds(start, PADW), :] = in_x[:, :128]
        blurred_x[pl.ds(start + PADW, PADW), :] = in_x[:, 128:]
        return carry

    lax.fori_loop(0, WIN // 2, along_zx, 0, unroll=UNROLL)

    valid = lax.broadcasted_iota(I32, (PADW, 256), 0) < WIN

    def along_y(i, carry):
        u = 2 * i
        lines = [blurred_x[pl.ds(u + j, PADW, stride=PADW), :] for j in range(2)]
        predicted = dot(my, stacked(*lines)) + backdrop
        seen = jnp.concatenate([data_ref[0, 0, u], data_ref[0, 0, u + 1]], axis=1)
        ratio = jnp.where(valid, seen.astype(F32) / predicted, 0.0)
        in_y = dot(myt, stacked(ratio[:, :128], ratio[:, 128:]))
        start = pl.multiple_of(u * PADS, 2 * PADS)
        back_y[pl.ds(start, PADS), :] = in_y[:, :128]
        back_y[pl.ds(start + PADS, PADS), :] = in_y[:, 128:]
        return carry

    lax.fori_loop(0, WIN // 2, along_y, 0, unroll=UNROLL)

    def along_x(i, carry):
        y = 2 * i
        lines = [back_y[pl.ds(y + j, PADW, stride=PADS), :] for j in range(2)]
        in_x = dot(mxt, stacked(*lines))
        start = pl.multiple_of(y * PADS, 2 * PADS)
        back_x[pl.ds(start, PADS), :] = in_x[:, :128]
        back_x[pl.ds(start + PADS, PADS), :] = in_x[:, 128:]
        return carry

    lax.fori_loop(0, SIDE // 2, along_x, 0, unroll=UNROLL)

    group = 4
    for i in range(SIDE // group):
        lines = [back_x[pl.ds(group * i + j, PADS, stride=PADS), :] for j in range(group)]
        high, low = split(jnp.concatenate(lines, axis=0))
        factor = dot(jnp.concatenate([high, low, high], axis=1), mzt)
        for j in range(group):
            x = group * i + j
            first = (x % 2) * SIDE
            out_ref[x // 2, 0, first : first + SIDE, :] = factor[j * PADS : j * PADS + SIDE]
    for k in range(SIDE // 2, 16):
        out_ref[k, 0] = jnp.zeros_like(out_ref[k, 0])


UNROLL = 4


def run_jobs(channel, gathered, table, top, bottom, view_data, backdrops, mats):
    slots = table.shape[1]
    per_slot = lambda shape: pl.BlockSpec(
        (1,) + shape, lambda slot, table: (slot,) + (0,) * len(shape)
    )
    specs = [brick_spec(i, lambda slot: slot) for i in range(3)]
    specs += [per_slot((WIN, RIM, 128))] * 2
    specs += [
        pl.BlockSpec((1, 1, WIN, PADW, 128), lambda slot, table: (slot, channel, 0, 0, 0)),
        pl.BlockSpec(memory_space=pltpu.SMEM),
    ]
    specs += [per_slot(m.shape[1:]) for m in mats]
    return pl.pallas_call(
        job_kernel,
        grid_spec=pltpu.PrefetchScalarGridSpec(
            num_scalar_prefetch=1,
            grid=(slots,),
            in_specs=specs,
            out_specs=pl.BlockSpec((16, 1, 2 * SIDE, 128), lambda slot, table: (0, slot, 0, 0)),
            scratch_shapes=[
                pltpu.VMEM((PADW, PADW, 128), BF16),
                pltpu.VMEM((PADW * PADW, 128), F32),
                pltpu.VMEM((PADW * PADS, 128), F32),
                pltpu.VMEM((PADS * PADS, 128), F32),
            ],
        ),
        out_shape=jax.ShapeDtypeStruct((16, slots, 2 * SIDE, 128), F32),
        compiler_params=pltpu.CompilerParams(vmem_limit_bytes=40 << 20),
        name="jobs",
    )(table, gathered, gathered, gathered, top, bottom, view_data, backdrops, *mats)


def bands(taps, positions_out, positions_in):
    offsets = positions_in[None, :] - positions_out[:, None] + HALO
    sel = offsets[None, :, :, None] == jnp.arange(taps.shape[1])[None, None, None, :]
    return jnp.sum(jnp.where(sel, taps[:, None, None, :], 0.0), axis=3)


def high_low(matrix):
    high = lax.reduce_precision(matrix, 8, 7)
    return high.astype(BF16), (matrix - high).astype(BF16)


def job_matrices(taps):
    none = -1000
    far = 1000
    line = jnp.arange(128)
    row = jnp.arange(PADW)
    win_in = jnp.where(row < WIN, row, none)
    win_out = jnp.where(row < WIN, row, far)
    short = jnp.arange(PADS)
    inner_out = jnp.where(short < SIDE, short + HALO, far)
    x_in = jnp.where(row < RIM + SIDE, row - 1, row - 1 - (PADS - SIDE))
    x_in = jnp.where((row >= RIM + SIDE) & (row < RIM + PADS), none, x_in)
    x_in = jnp.where((x_in < 0) | (x_in >= WIN), none, x_in)
    forward = lambda t, out, inp: bands(t, out, inp)
    backward = lambda t, out, inp: jnp.swapaxes(bands(t, inp, out), 1, 2)
    three = lambda pair: jnp.concatenate([pair[0], pair[0], pair[1]], axis=2)
    mz = high_low(jnp.swapaxes(forward(taps[:, 2], line, line), 1, 2))
    mzt = high_low(jnp.swapaxes(backward(taps[:, 2], line, line), 1, 2))
    win_in_far = jnp.where(row < WIN, row, far)
    inner_none = jnp.where(short < SIDE, short + HALO, none)
    return (
        jnp.concatenate(mz, axis=1),
        three(high_low(forward(taps[:, 0], win_out, x_in))),
        three(high_low(forward(taps[:, 1], win_out, win_in))),
        three(high_low(backward(taps[:, 1], inner_none, win_in_far))),
        three(high_low(backward(taps[:, 0], inner_none, win_in_far))),
        jnp.concatenate([mzt[0], mzt[0], mzt[1]], axis=1),
    )


def add_kernel(owners, parts_ref, out_ref):
    out_ref[...] = jnp.zeros_like(out_ref)
    slots = parts_ref.shape[1]
    for w in range(parts_ref.shape[0]):
        for s in range(slots):
            b = owners[w * slots + s]
            out_ref[b] += parts_ref[w, s]


def add_up(owners, parts):
    return pl.pallas_call(
        add_kernel,
        in_specs=[pl.BlockSpec(memory_space=pltpu.SMEM), pl.BlockSpec(memory_space=pltpu.VMEM)],
        out_specs=pl.BlockSpec(memory_space=pltpu.VMEM),
        out_shape=jax.ShapeDtypeStruct((16,) + parts.shape[2:], F32),
        name="add_up",
    )(owners, parts)


def update_kernel(count, est_ref, *refs):
    out_ref = refs[-1]
    seen = count[0].astype(F32)
    for c, total in enumerate(refs[:-1]):
        for k in range(SIDE // 2):
            for j in range(2):
                rows = total[k, j * SIDE : (j + 1) * SIDE, :]
                out_ref[c, 2 * k + j] = est_ref[c, 2 * k + j] * rows / seen


def update(count, estimate, totals):
    vmem = pl.BlockSpec(memory_space=pltpu.VMEM)
    return pl.pallas_call(
        update_kernel,
        in_specs=[pl.BlockSpec(memory_space=pltpu.SMEM)] + [vmem] * (1 + len(totals)),
        out_specs=vmem,
        out_shape=jax.ShapeDtypeStruct(estimate.shape, F32),
        compiler_params=pltpu.CompilerParams(vmem_limit_bytes=24 << 20),
        name="update",
    )(count, estimate, *totals)


def pick(table, rows):
    return jnp.stack([lax.dynamic_index_in_dim(table, r, 0, keepdims=False) for r in rows])


def on_device(estimate, view_data, psf, background, slot_brick, slot_view, intersection):
    me = lax.axis_index("tile").astype(I32)
    groups = lax.axis_size("view")
    upward = [(i, i + 1) for i in range(groups - 1)]
    downward = [(j, i) for i, j in upward]
    bricks, views = slot_brick[0, 0], slot_view[0, 0]

    wire = estimate.astype(BF16).transpose(0, 2, 1, 3)
    wire = jnp.pad(wire, ((0, 0), (0, 0), (0, PADS - SIDE), (0, 0)))
    above = lax.ppermute(bricks, "view", downward)
    below = lax.ppermute(bricks, "view", upward)
    gathered = ring_gather([wire[0], wire[1]], (0, 1))
    gathered = ring_gather(gathered, (1, 0))

    taps = pick(psf, views)
    backdrops = pick(background, views)
    mats = job_matrices(taps)
    owners = lax.all_gather(bricks, "tile", axis=0, tiled=True)
    count = jnp.sum(intersection[0, 0]).reshape(1)

    totals = []
    for channel in range(2):
        x_first = channel == 0
        wanted = window_table(jnp.concatenate([above, below]), me, x_first)
        edge = margins(gathered[channel], wanted)
        top = lax.ppermute(edge[0], "view", upward)
        bottom = lax.ppermute(edge[1], "view", downward)
        factors = run_jobs(
            channel,
            gathered[channel],
            window_table(bricks, me, x_first),
            top,
            bottom,
            view_data[0, 0],
            backdrops,
            mats,
        )
        parts = lax.all_to_all(factors, "tile", 0, 0, tiled=True)
        summed = add_up(owners, parts)
        totals.append(lax.all_to_all(summed, "tile", 0, 0, tiled=True))
    return update(count, estimate, totals)


def solution(mesh):
    placed = (
        P(None, "view", "tile", None),
        P("view", "tile", None, None, None, None, None),
        P(),
        P(),
        P("view", "tile", None),
        P("view", "tile", None),
        P("view", "tile", None),
    )
    return jax.shard_map(
        on_device,
        mesh=mesh,
        in_specs=placed,
        out_specs=P(None, "view", "tile", None),
        check_vma=False,
    )
```

time: 487 us -> 289 us (0.59)
  waiting for transfers between devices: 353 us -> 51.9 us
  Pallas kernels: 0 us -> 91.2 us
  matrix products: 57.1 us -> 0 us
  starting transfers between devices: 10.4 us -> 60.2 us
  local copies, waits for them, and re-layouts: 13 us -> 44.5 us
  blocking collectives: 0 us -> 25.7 us
  between operations: 25.6 us -> 6.71 us
  other arithmetic: 22.1 us -> 7.46 us
    unnamed x3 -> x0, waiting for transfers between devices: 178 us -> none
    all_gather x1 -> x0, waiting for transfers between devices: 161 us -> none  [on_device(): gathered = lax.all_gather(padded[None], 'tile', axis=0, tiled=True)]
    pallas_call x0 -> x7, Pallas kernels: none -> 91.2 us  [the longest x2 73.8 us: run_jobs(): pl.pallas_call(job_kernel, grid_spec=pltpu.PrefetchScalarGridSpec(num_sca...]
    dot_general x18 -> x0, matrix products: 57.1 us -> none  [the longest x3 16.8 us: forward_blur(): jnp.einsum('cxyz,ux->cuyz', result, band_x, precision=lax.Precision.HIGHEST)]
    ppermute x4 -> x22, starting transfers between devices: 10.3 us -> 38.6 us  [the longest x16 23 us: torus_step(): return lax.ppermute(array, 'tile', pairs)]
    unnamed x34 -> x42, local copies, waits for them, and re-layouts: 2.52 us -> 28.3 us
    all_gather x0 -> x1, blocking collectives: none -> 25.7 us  [on_device(): owners = lax.all_gather(bricks, 'tile', axis=0, tiled=True)]
    all_to_all x0 -> x4, starting transfers between devices: none -> 21.6 us  [the longest x2 11.6 us: on_device(): parts = lax.all_to_all(factors, 'tile', 0, 0, tiled=True)]
  transfers between devices with their start and end apart: 6 -> 26, of which waited for: 6 -> 10; matrix products, arithmetic and copies ran while one was open for 3% -> 14% of each run, Pallas kernels for 0% -> 31%
where the time goes in v1:
time: 289 us; the launch traced here: 288 us
  Pallas kernels  91.2 us (32%)
  starting transfers between devices  60.2 us (21%)
  waiting for transfers between devices  51.9 us (18%)
  local copies, waits for them, and re-layouts  44.5 us (15%)
  blocking collectives  25.7 us (9%)
  other arithmetic  7.46 us (3%)
  between operations  6.71 us (2%)
    pallas_call x2, Pallas kernels, run_jobs(): pl.pallas_call(job_kernel, grid_spec=pltpu.PrefetchScalarGridSpec(num_sca...  73.8 us
    unnamed x42, local copies, waits for them, and re-layouts  28.3 us
    ppermute x16, waiting for transfers between devices, torus_step(): return lax.ppermute(array, 'tile', pairs)  27 us
    all_gather x1, blocking collectives, on_device(): owners = lax.all_gather(bricks, 'tile', axis=0, tiled=True)  25.7 us
    ppermute x16, starting transfers between devices, torus_step(): return lax.ppermute(array, 'tile', pairs)  23 us
    all_to_all x2, waiting for transfers between devices, on_device(): totals.append(lax.all_to_all(summed, 'tile', 0, 0, tiled=True))  16.3 us
    pallas_call x2, Pallas kernels, margins(): pl.pallas_call(margin_kernel, grid_spec=pltpu.PrefetchScalarGridSpec(num_...  12.1 us
    all_to_all x2, starting transfers between devices, on_device(): parts = lax.all_to_all(factors, 'tile', 0, 0, tiled=True)  11.6 us
  transfers between devices with their start and end apart: 26, of which 10 were waited for; matrix products, arithmetic and copies ran while one was open for 14% of the time, Pallas kernels for 31%

profile of v1, /device:TPU:32, one launch (start us, length us, event | category | flops | bytes accessed | tf_op | source)
XLA Modules:
  0.0 287.7 jit_solution(16798930011576149610)
XLA Ops:
  26.2 5.1 %collective-permute-done.14 = bf16[14,32,128]{2,1,0:T(8,128)(2,1)S(1)} collective-permute-done((bf16[14,32,128]{2,1,0:T(8,128)(2,1)S(1)}, bf16[14,32,128]{2,1,0:T(8,128)(2,1)S(1)}, u32[]{:S(2)}, u32[]{:S(2)}) %collective-permute-start.14) | collective-permute-done | bytes 114720 | tf_op jit(solution)/shard_map/ppermute | solution.py:26
  32.6 3.9 %collective-permute-done.15 = bf16[14,32,128]{2,1,0:T(8,128)(2,1)S(1)} collective-permute-done((bf16[14,32,128]{2,1,0:T(8,128)(2,1)S(1)}, bf16[14,32,128]{2,1,0:T(8,128)(2,1)S(1)}, u32[]{:S(2)}, u32[]{:S(2)}) %collective-permute-start.15) | collective-permute-done | bytes 114720 | tf_op jit(solution)/shard_map/ppermute | solution.py:26
  37.6 3.0 %collective-permute-start.17 = (bf16[112,32,128]{2,1,0:T(8,128)(2,1)}, bf16[112,32,128]{2,1,0:T(8,128)(2,1)S(1)}, u32[]{:S(2)}, u32[]{:S(2)}) collective-permute-start(bf16[112,32,128]{2,1,0:T(8,128)(2,1)} %get-tuple-element.48), channel_id=1, source_target_pairs={{0,96},{8,104},{16,112},{24,120},{32,0},{40,8},{48,16},{56,24},{64... | collective-permute-start | bytes 2752520 | tf_op jit(solution)/shard_map/ppermute | solution.py:26
  41.5 3.3 %collective-permute-start.3 = (bf16[14,32,128]{2,1,0:T(8,128)(2,1)S(1)}, bf16[14,32,128]{2,1,0:T(8,128)(2,1)S(1)}, u32[]{:S(2)}, u32[]{:S(2)}) collective-permute-start(bf16[14,32,128]{2,1,0:T(8,128)(2,1)S(1)} %slice.75), channel_id=1, source_target_pairs={{0,96},{8,104},{16,112},{24,120},{32,0},{40,8},{48,16},{56,24},{64... | collective-permute-start | bytes 344072 | tf_op jit(solution)/shard_map/ppermute | solution.py:26
  46.5 14.9 %collective-permute-done.16 = bf16[112,32,128]{2,1,0:T(8,128)(2,1)S(1)} collective-permute-done((bf16[112,32,128]{2,1,0:T(8,128)(2,1)}, bf16[112,32,128]{2,1,0:T(8,128)(2,1)S(1)}, u32[]{:S(2)}, u32[]{:S(2)}) %collective-permute-start.16) | collective-permute-done | bytes 917536 | tf_op jit(solution)/shard_map/ppermute | solution.py:26
  66.3 3.2 %collective-permute-start.5 = (bf16[112,32,128]{2,1,0:T(8,128)(2,1)}, bf16[112,32,128]{2,1,0:T(8,128)(2,1)S(1)}, u32[]{:S(2)}, u32[]{:S(2)}) collective-permute-start(bf16[112,32,128]{2,1,0:T(8,128)(2,1)} %get-tuple-element.52), channel_id=1, source_target_pairs={{0,24},{8,0},{16,8},{24,16},{32,56},{40,32},{48,40},{56,48},{64,88... | collective-permute-start | bytes 2752520 | tf_op jit(solution)/shard_map/ppermute | solution.py:26
  75.0 6.0 %margins.3 = bf16[2,3,58,16,128]{4,3,2,1,0:T(8,128)(2,1)} custom-call(s32[5,6]{1,0:T(8,128)} %stack.17.table, bf16[448,32,128]{2,1,0:T(8,128)(2,1)} %constant_dynamic-update-slice_fusion.19.prev_ref.own_ref.next_ref, bf16[448,32,128]{2,1,0:T(8,128)(2,1)} %constant_dynamic-update-slice_fusion.19.prev_ref.own_ref.next_ref, ...), custom_call_target="tpu_custom_call" | custom-call | tf_op jit(solution)/shard_map/margins/pallas_call | solution.py:94
  81.1 2.7 slice_bitcast_fusion
  85.6 3.8 %collective-permute-start.21 = (bf16[3,58,16,128]{3,2,1,0:T(8,128)(2,1)}, bf16[3,58,16,128]{3,2,1,0:T(8,128)(2,1)S(1)}, u32[]{:S(2)}, u32[]{:S(2)}) collective-permute-start(bf16[3,58,16,128]{3,2,1,0:T(8,128)(2,1)} %get-tuple-element.26), channel_id=1, source_target_pairs={{1,0},{2,1},{3,2},{4,3},{5,4},{6,5},{7,6},{9,8},{10,9},{11,10},{12... | collective-permute-start | bytes 2138120 | tf_op jit(solution)/shard_map/ppermute | solution.py:352
  91.3 6.5 %copy.38 = bf16[1,1,3,2,58,58,128]{6,5,4,3,2,1,0:T(8,128)(2,1)} copy(bf16[1,1,3,2,58,58,128]{6,3,5,4,2,1,0:T(2,128)(2,1)} %param.8) | data formatting | bytes 10334208 | tf_op args[1]
  100.5 3.2 %collective-permute-start.7 = (bf16[56,32,128]{2,1,0:T(8,128)(2,1)}, bf16[56,32,128]{2,1,0:T(8,128)(2,1)}, u32[]{:S(2)}, u32[]{:S(2)}) collective-permute-start(bf16[56,32,128]{2,1,0:T(8,128)(2,1)} %slice.77), channel_id=1, source_target_pairs={{0,24},{8,0},{16,8},{24,16},{32,56},{40,32},{48,40},{56,48},{64,88... | collective-permute-start | bytes 1376264 | tf_op jit(solution)/shard_map/ppermute | solution.py:26
  109.2 37.2 %jobs.3 = f32[16,3,56,128]{3,2,1,0:T(8,128)} custom-call(s32[5,3]{1,0:T(8,128)S(1)} %stack.16.table, bf16[448,32,128]{2,1,0:T(8,128)(2,1)} %constant_dynamic-update-slice_fusion.19.prev_ref.own_ref.next_ref, bf16[448,32,128]{2,1,0:T(8,128)(2,1)} %constant_dynamic-update-slice_fusion.19.prev_ref.own_ref.next_ref, ...), custom_call_target="tpu_custom_call" | custom-call | tf_op jit(solution)/shard_map/jobs/pallas_call | solution.py:221
  146.4 4.4 %all-to-all-start.2 = ((f32[16,3,56,128]{3,2,1,0:T(8,128)}), f32[16,3,56,128]{3,2,1,0:T(8,128)}, u32[]{:S(2)}, u32[]{:S(2)}) async-start(f32[16,3,56,128]{3,2,1,0:T(8,128)} %jobs.3), calls=%async_computation.2 | async-start | bytes 2752512 | tf_op jit(solution)/shard_map/all_to_all | solution.py:363
  155.4 6.0 %margins.2 = bf16[2,3,58,16,128]{4,3,2,1,0:T(8,128)(2,1)} custom-call(s32[5,6]{1,0:T(8,128)} %stack.13.table, bf16[448,32,128]{2,1,0:T(8,128)(2,1)} %constant_dynamic-update-slice_fusion.5.prev_ref.own_ref.next_ref, bf16[448,32,128]{2,1,0:T(8,128)(2,1)} %constant_dynamic-update-slice_fusion.5.prev_ref.own_ref.next_ref, ...), custom_call_target="tpu_custom_call" | custom-call | tf_op jit(solution)/shard_map/margins/pallas_call | solution.py:94
  165.8 3.6 %collective-permute-start.11 = (bf16[3,58,16,128]{3,2,1,0:T(8,128)(2,1)S(1)}, bf16[3,58,16,128]{3,2,1,0:T(8,128)(2,1)S(1)}, u32[]{:S(2)}, u32[]{:S(2)}) collective-permute-start(bf16[3,58,16,128]{3,2,1,0:T(8,128)(2,1)S(1)} %get-tuple-element.28), channel_id=1, source_target_pairs={{1,0},{2,1},{3,2},{4,3},{5,4},{6,5},{7,6},{9,8},{10,9},{11,10},{12... | collective-permute-start | bytes 2138120 | tf_op jit(solution)/shard_map/ppermute | solution.py:352
  169.5 7.1 %collective-permute-done.10.top_ref = bf16[3,58,16,128]{3,2,1,0:T(8,128)(2,1)S(1)} collective-permute-done((bf16[3,58,16,128]{3,2,1,0:T(8,128)(2,1)}, bf16[3,58,16,128]{3,2,1,0:T(8,128)(2,1)S(1)}, u32[]{:S(2)}, u32[]{:S(2)}) %collective-permute-start.10) | collective-permute-done | bytes 712736 | tf_op jit(solution)/shard_map/ppermute | solution.py:351
  180.2 2.6 copy-done.2
  182.8 36.5 %jobs.2 = f32[16,3,56,128]{3,2,1,0:T(8,128)} custom-call(s32[5,3]{1,0:T(8,128)S(1)} %stack.12.table, bf16[448,32,128]{2,1,0:T(8,128)(2,1)S(1)} %copy-done, bf16[448,32,128]{2,1,0:T(8,128)(2,1)S(1)} %copy-done, bf16[448,32,128]{2,1,0:T(8,128)(2,1)S(1)} %copy-done, bf16[3,58,16,128]{3,2,1,0:T(8,128)(2,1)S(1)} %collective-permute-done.10.top_ref, ...), custom_call_target="tpu_custom_call" | custom-call | tf_op jit(solution)/shard_map/jobs/pallas_call | solution.py:221
  219.3 7.2 %all-to-all-start = ((f32[16,3,56,128]{3,2,1,0:T(8,128)}), f32[16,3,56,128]{3,2,1,0:T(8,128)S(1)}, u32[]{:S(2)}, u32[]{:S(2)}) async-start(f32[16,3,56,128]{3,2,1,0:T(8,128)} %jobs.2), calls=%async_computation | async-start | bytes 2752512 | tf_op jit(solution)/shard_map/all_to_all | solution.py:363
  227.9 25.7 %all-reduce.1.owners = s32[48]{0:T(128)} all-reduce(s32[48]{0:T(128)S(1)} %bitcast_dynamic-update-slice_fusion), channel_id=2, replica_groups=mesh['tile'=16,'view'=8] {'tile'}, use_global_device_ids=true, to_apply=%add.1 | all-reduce | flops 48 | bytes 384 | tf_op jit(solution)/shard_map/all_gather | solution.py:343
  256.0 6.5 %all-to-all-start.3 = ((f32[16,56,128]{2,1,0:T(8,128)}), f32[16,56,128]{2,1,0:T(8,128)S(1)}, u32[]{:S(2)}, u32[]{:S(2)}) async-start(f32[16,56,128]{2,1,0:T(8,128)} %add_up.3), calls=%async_computation.3 | async-start | bytes 917504 | tf_op jit(solution)/shard_map/all_to_all | solution.py:365
  264.9 7.4 %all-to-all-done.3.refs_1_ = f32[16,56,128]{2,1,0:T(8,128)S(1)} async-done(((f32[16,56,128]{2,1,0:T(8,128)}), f32[16,56,128]{2,1,0:T(8,128)S(1)}, u32[]{:S(2)}, u32[]{:S(2)}) %all-to-all-start.3) | async-done | bytes 458784 | tf_op jit(solution)/shard_map/all_to_all | solution.py:365
  272.3 3.6 %all-to-all-start.1 = ((f32[16,56,128]{2,1,0:T(8,128)}), f32[16,56,128]{2,1,0:T(8,128)S(1)}, u32[]{:S(2)}, u32[]{:S(2)}) async-start(f32[16,56,128]{2,1,0:T(8,128)} %add_up.2), calls=%async_computation.1 | async-start | bytes 917504 | tf_op jit(solution)/shard_map/all_to_all | solution.py:365
  276.6 8.9 %all-to-all-done.1.refs_0_ = f32[16,56,128]{2,1,0:T(8,128)S(1)} async-done(((f32[16,56,128]{2,1,0:T(8,128)}), f32[16,56,128]{2,1,0:T(8,128)S(1)}, u32[]{:S(2)}, u32[]{:S(2)}) %all-to-all-start.1) | async-done | bytes 458784 | tf_op jit(solution)/shard_map/all_to_all | solution.py:365
  (142 shorter events, 68.6 us)
Async XLA Ops:
  1.6 20.6 %collective-permute-start.12 = (bf16[28,32,128]{2,1,0:T(8,128)(2,1)S(1)}, bf16[28,32,128]{2,1,0:T(8,128)(2,1)S(1)}, u32[]{:S(2)}, u32[]{:S(2)}) collective-permute-start(bf16[28,32,128]{2,1,0:T(8,128)(2,1)S(1)} %get-tuple-element.34), channel_id=1, source_target_pairs={{0,8},{8,16},{16,24},{24,0},{32,40},{40,48},{48,56},{56,32},{64,72... | collective-permute-start | bytes 688136 | tf_op jit(solution)/shard_map/ppermute | solution.py:26
  3.3 20.8 %collective-permute-start.13 = (bf16[28,32,128]{2,1,0:T(8,128)(2,1)S(1)}, bf16[28,32,128]{2,1,0:T(8,128)(2,1)S(1)}, u32[]{:S(2)}, u32[]{:S(2)}) collective-permute-start(bf16[28,32,128]{2,1,0:T(8,128)(2,1)S(1)} %get-tuple-element.34), channel_id=1, source_target_pairs={{0,24},{8,0},{16,8},{24,16},{32,56},{40,32},{48,40},{56,48},{64,88... | collective-permute-start | bytes 688136 | tf_op jit(solution)/shard_map/ppermute | solution.py:26
  4.9 32.7 %collective-permute-start.8 = (s32[3]{0:T(128)}, s32[3]{0:T(128)S(1)}, u32[]{:S(2)}, u32[]{:S(2)}) collective-permute-start(s32[3]{0:T(128)} %bitcast.99), channel_id=1, source_target_pairs={{1,0},{2,1},{3,2},{4,3},{5,4},{6,5},{7,6},{9,8},{10,9},{11,10},{12... | collective-permute-start | bytes 44 | tf_op jit(solution)/shard_map/ppermute | solution.py:335
  6.9 33.8 %collective-permute-start.9 = (s32[3]{0:T(128)}, s32[3]{0:T(128)S(1)}, u32[]{:S(2)}, u32[]{:S(2)}) collective-permute-start(s32[3]{0:T(128)} %bitcast.100), channel_id=1, source_target_pairs={{0,1},{1,2},{2,3},{3,4},{4,5},{5,6},{6,7},{8,9},{9,10},{10,11},{11... | collective-permute-start | bytes 44 | tf_op jit(solution)/shard_map/ppermute | solution.py:336
  9.3 32.1 %collective-permute-start = (bf16[28,32,128]{2,1,0:T(8,128)(2,1)S(1)}, bf16[28,32,128]{2,1,0:T(8,128)(2,1)S(1)}, u32[]{:S(2)}, u32[]{:S(2)}) collective-permute-start(bf16[28,32,128]{2,1,0:T(8,128)(2,1)S(1)} %get-tuple-element.35), channel_id=1, source_target_pairs={{0,32},{8,40},{16,48},{24,56},{32,64},{40,72},{48,80},{56,88},{64,... | collective-permute-start | bytes 688136 | tf_op jit(solution)/shard_map/ppermute | solution.py:26
  22.2 19.3 %collective-permute-start.1 = (bf16[28,32,128]{2,1,0:T(8,128)(2,1)S(1)}, bf16[28,32,128]{2,1,0:T(8,128)(2,1)S(1)}, u32[]{:S(2)}, u32[]{:S(2)}) collective-permute-start(bf16[28,32,128]{2,1,0:T(8,128)(2,1)S(1)} %get-tuple-element.35), channel_id=1, source_target_pairs={{0,96},{8,104},{16,112},{24,120},{32,0},{40,8},{48,16},{56,24},{64... | collective-permute-start | bytes 688136 | tf_op jit(solution)/shard_map/ppermute | solution.py:26
  37.2 24.2 %collective-permute-start.16 = (bf16[112,32,128]{2,1,0:T(8,128)(2,1)}, bf16[112,32,128]{2,1,0:T(8,128)(2,1)S(1)}, u32[]{:S(2)}, u32[]{:S(2)}) collective-permute-start(bf16[112,32,128]{2,1,0:T(8,128)(2,1)} %get-tuple-element.48), channel_id=1, source_target_pairs={{0,32},{8,40},{16,48},{24,56},{32,64},{40,72},{48,80},{56,88},{64,... | collective-permute-start | bytes 2752520 | tf_op jit(solution)/shard_map/ppermute | solution.py:26
  37.6 25.9 %collective-permute-start.17 = (bf16[112,32,128]{2,1,0:T(8,128)(2,1)}, bf16[112,32,128]{2,1,0:T(8,128)(2,1)S(1)}, u32[]{:S(2)}, u32[]{:S(2)}) collective-permute-start(bf16[112,32,128]{2,1,0:T(8,128)(2,1)} %get-tuple-element.48), channel_id=1, source_target_pairs={{0,96},{8,104},{16,112},{24,120},{32,0},{40,8},{48,16},{56,24},{64... | collective-permute-start | bytes 2752520 | tf_op jit(solution)/shard_map/ppermute | solution.py:26
  41.4 21.4 %collective-permute-start.2 = (bf16[14,32,128]{2,1,0:T(8,128)(2,1)S(1)}, bf16[14,32,128]{2,1,0:T(8,128)(2,1)S(1)}, u32[]{:S(2)}, u32[]{:S(2)}) collective-permute-start(bf16[14,32,128]{2,1,0:T(8,128)(2,1)S(1)} %slice.74), channel_id=1, source_target_pairs={{0,32},{8,40},{16,48},{24,56},{32,64},{40,72},{48,80},{56,88},{64,... | collective-permute-start | bytes 344072 | tf_op jit(solution)/shard_map/ppermute | solution.py:26
  41.5 24.1 %collective-permute-start.3 = (bf16[14,32,128]{2,1,0:T(8,128)(2,1)S(1)}, bf16[14,32,128]{2,1,0:T(8,128)(2,1)S(1)}, u32[]{:S(2)}, u32[]{:S(2)}) collective-permute-start(bf16[14,32,128]{2,1,0:T(8,128)(2,1)S(1)} %slice.75), channel_id=1, source_target_pairs={{0,96},{8,104},{16,112},{24,120},{32,0},{40,8},{48,16},{56,24},{64... | collective-permute-start | bytes 344072 | tf_op jit(solution)/shard_map/ppermute | solution.py:26
  61.4 11.0 %collective-permute-start.18 = (bf16[56,32,128]{2,1,0:T(8,128)(2,1)S(1)}, bf16[56,32,128]{2,1,0:T(8,128)(2,1)S(1)}, u32[]{:S(2)}, u32[]{:S(2)}) collective-permute-start(bf16[56,32,128]{2,1,0:T(8,128)(2,1)S(1)} %slice.82), channel_id=1, source_target_pairs={{0,32},{8,40},{16,48},{24,56},{32,64},{40,72},{48,80},{56,88},{64,... | collective-permute-start | bytes 1376264 | tf_op jit(solution)/shard_map/ppermute | solution.py:26
  63.5 10.7 %collective-permute-start.19 = (bf16[56,32,128]{2,1,0:T(8,128)(2,1)S(1)}, bf16[56,32,128]{2,1,0:T(8,128)(2,1)S(1)}, u32[]{:S(2)}, u32[]{:S(2)}) collective-permute-start(bf16[56,32,128]{2,1,0:T(8,128)(2,1)S(1)} %slice.83), channel_id=1, source_target_pairs={{0,96},{8,104},{16,112},{24,120},{32,0},{40,8},{48,16},{56,24},{64... | collective-permute-start | bytes 1376264 | tf_op jit(solution)/shard_map/ppermute | solution.py:26
  66.3 31.6 %collective-permute-start.4 = (bf16[112,32,128]{2,1,0:T(8,128)(2,1)}, bf16[112,32,128]{2,1,0:T(8,128)(2,1)}, u32[]{:S(2)}, u32[]{:S(2)}) collective-permute-start(bf16[112,32,128]{2,1,0:T(8,128)(2,1)} %get-tuple-element.52), channel_id=1, source_target_pairs={{0,8},{8,16},{16,24},{24,0},{32,40},{40,48},{48,56},{56,32},{64,72... | collective-permute-start | bytes 2752520 | tf_op jit(solution)/shard_map/ppermute | solution.py:26
  66.3 33.4 %collective-permute-start.5 = (bf16[112,32,128]{2,1,0:T(8,128)(2,1)}, bf16[112,32,128]{2,1,0:T(8,128)(2,1)S(1)}, u32[]{:S(2)}, u32[]{:S(2)}) collective-permute-start(bf16[112,32,128]{2,1,0:T(8,128)(2,1)} %get-tuple-element.52), channel_id=1, source_target_pairs={{0,24},{8,0},{16,8},{24,16},{32,56},{40,32},{48,40},{56,48},{64,88... | collective-permute-start | bytes 2752520 | tf_op jit(solution)/shard_map/ppermute | solution.py:26
  83.7 22.8 %collective-permute-start.20 = (bf16[3,58,16,128]{3,2,1,0:T(8,128)(2,1)}, bf16[3,58,16,128]{3,2,1,0:T(8,128)(2,1)S(1)}, u32[]{:S(2)}, u32[]{:S(2)}) collective-permute-start(bf16[3,58,16,128]{3,2,1,0:T(8,128)(2,1)} %get-tuple-element.27), channel_id=1, source_target_pairs={{0,1},{1,2},{2,3},{3,4},{4,5},{5,6},{6,7},{8,9},{9,10},{10,11},{11... | collective-permute-start | bytes 2138120 | tf_op jit(solution)/shard_map/ppermute | solution.py:351
  85.6 20.9 %collective-permute-start.21 = (bf16[3,58,16,128]{3,2,1,0:T(8,128)(2,1)}, bf16[3,58,16,128]{3,2,1,0:T(8,128)(2,1)S(1)}, u32[]{:S(2)}, u32[]{:S(2)}) collective-permute-start(bf16[3,58,16,128]{3,2,1,0:T(8,128)(2,1)} %get-tuple-element.26), channel_id=1, source_target_pairs={{1,0},{2,1},{3,2},{4,3},{5,4},{6,5},{7,6},{9,8},{10,9},{11,10},{12... | collective-permute-start | bytes 2138120 | tf_op jit(solution)/shard_map/ppermute | solution.py:352
  99.7 52.1 %collective-permute-start.6 = (bf16[56,32,128]{2,1,0:T(8,128)(2,1)}, bf16[56,32,128]{2,1,0:T(8,128)(2,1)}, u32[]{:S(2)}, u32[]{:S(2)}) collective-permute-start(bf16[56,32,128]{2,1,0:T(8,128)(2,1)} %slice.76), channel_id=1, source_target_pairs={{0,8},{8,16},{16,24},{24,0},{32,40},{40,48},{48,56},{56,32},{64,72... | collective-permute-start | bytes 1376264 | tf_op jit(solution)/shard_map/ppermute | solution.py:26
  100.5 53.1 %collective-permute-start.7 = (bf16[56,32,128]{2,1,0:T(8,128)(2,1)}, bf16[56,32,128]{2,1,0:T(8,128)(2,1)}, u32[]{:S(2)}, u32[]{:S(2)}) collective-permute-start(bf16[56,32,128]{2,1,0:T(8,128)(2,1)} %slice.77), channel_id=1, source_target_pairs={{0,24},{8,0},{16,8},{24,16},{32,56},{40,32},{48,40},{56,48},{64,88... | collective-permute-start | bytes 1376264 | tf_op jit(solution)/shard_map/ppermute | solution.py:26
  146.4 73.0 %all-to-all-start.2 = ((f32[16,3,56,128]{3,2,1,0:T(8,128)}), f32[16,3,56,128]{3,2,1,0:T(8,128)}, u32[]{:S(2)}, u32[]{:S(2)}) async-start(f32[16,3,56,128]{3,2,1,0:T(8,128)} %jobs.3), calls=%async_computation.2 | async-start | bytes 2752512 | tf_op jit(solution)/shard_map/all_to_all | solution.py:363
  163.9 12.7 %collective-permute-start.10 = (bf16[3,58,16,128]{3,2,1,0:T(8,128)(2,1)}, bf16[3,58,16,128]{3,2,1,0:T(8,128)(2,1)S(1)}, u32[]{:S(2)}, u32[]{:S(2)}) collective-permute-start(bf16[3,58,16,128]{3,2,1,0:T(8,128)(2,1)} %get-tuple-element.29), channel_id=1, source_target_pairs={{0,1},{1,2},{2,3},{3,4},{4,5},{5,6},{6,7},{8,9},{9,10},{10,11},{11... | collective-permute-start | bytes 2138120 | tf_op jit(solution)/shard_map/ppermute | solution.py:351
  165.8 12.3 %collective-permute-start.11 = (bf16[3,58,16,128]{3,2,1,0:T(8,128)(2,1)S(1)}, bf16[3,58,16,128]{3,2,1,0:T(8,128)(2,1)S(1)}, u32[]{:S(2)}, u32[]{:S(2)}) collective-permute-start(bf16[3,58,16,128]{3,2,1,0:T(8,128)(2,1)S(1)} %get-tuple-element.28), channel_id=1, source_target_pairs={{1,0},{2,1},{3,2},{4,3},{5,4},{6,5},{7,6},{9,8},{10,9},{11,10},{12... | collective-permute-start | bytes 2138120 | tf_op jit(solution)/shard_map/ppermute | solution.py:352
  219.3 36.7 %all-to-all-start = ((f32[16,3,56,128]{3,2,1,0:T(8,128)}), f32[16,3,56,128]{3,2,1,0:T(8,128)S(1)}, u32[]{:S(2)}, u32[]{:S(2)}) async-start(f32[16,3,56,128]{3,2,1,0:T(8,128)} %jobs.2), calls=%async_computation | async-start | bytes 2752512 | tf_op jit(solution)/shard_map/all_to_all | solution.py:363
  256.0 16.2 %all-to-all-start.3 = ((f32[16,56,128]{2,1,0:T(8,128)}), f32[16,56,128]{2,1,0:T(8,128)S(1)}, u32[]{:S(2)}, u32[]{:S(2)}) async-start(f32[16,56,128]{2,1,0:T(8,128)} %add_up.3), calls=%async_computation.3 | async-start | bytes 917504 | tf_op jit(solution)/shard_map/all_to_all | solution.py:365
  272.3 13.3 %all-to-all-start.1 = ((f32[16,56,128]{2,1,0:T(8,128)}), f32[16,56,128]{2,1,0:T(8,128)S(1)}, u32[]{:S(2)}, u32[]{:S(2)}) async-start(f32[16,56,128]{2,1,0:T(8,128)} %add_up.2), calls=%async_computation.1 | async-start | bytes 917504 | tf_op jit(solution)/shard_map/all_to_all | solution.py:365
  (13 other events, 255.1 us)

commit v2 on v1

v2 whole, which is shorter than its diff:
```python
import functools

import jax
import jax.numpy as jnp
from jax import lax
from jax.experimental import pallas as pl
from jax.experimental.pallas import tpu as pltpu
from jax.sharding import PartitionSpec as P

F32, BF16, I32 = jnp.float32, jnp.bfloat16, jnp.int32
HALO = 15
SIDE = 28
WIN = SIDE + 2 * HALO
PADW = 64
PADS = 32
RIM = 16
RING = 4


def far_memory(*arrays):
    return [pltpu.with_memory_space_constraint(a, pltpu.HBM) for a in arrays]


def torus_step(array, dx, dy):
    pairs = [
        (x * RING + y, ((x + dx) % RING) * RING + (y + dy) % RING)
        for x in range(RING)
        for y in range(RING)
    ]
    return lax.ppermute(array, "tile", pairs)


def ring_gather(arrays, axes):
    step = lambda a, axis, d: torus_step(a, d if axis == 0 else 0, d if axis == 1 else 0)
    near = [(step(a, ax, 1), step(a, ax, -1)) for a, ax in zip(arrays, axes)]
    far = []
    for (lower, upper), ax in zip(near, axes):
        half = lower.shape[0] // 2
        far.append((step(lower[:half], ax, 1), step(upper[half:], ax, -1)))
    return [[a, *n, *f] for a, n, f in zip(arrays, near, far)]


def place_of(brick, me, x_first):
    def rank(delta):
        delta = delta % RING
        return jnp.where(delta == 3, 1, jnp.where(delta == 1, 2, jnp.where(delta == 2, 3, 0)))

    in_x = rank(brick // RING - me // RING)
    in_y = rank(brick % RING - me % RING)
    return (in_y * RING + in_x if x_first else in_x * RING + in_y).astype(I32)


def window_table(bricks, me, x_first):
    count = RING * RING
    near = [jnp.maximum(bricks - 1, 0), bricks, jnp.minimum(bricks + 1, count - 1)]
    return jnp.stack([place_of(b, me, x_first) for b in near])


WINDOWS = ((SIDE - HALO, HALO, 0), (0, SIDE, HALO), (0, HALO, HALO + SIDE))


def copy_window(parts, which, place, rows, target, sem):
    first, count, _ = WINDOWS[which]
    base = 0
    for part in parts:
        held = part.shape[0] // SIDE

        @pl.when((place >= base) & (place < base + held))
        def _(part=part, base=base):
            source = part.at[pl.ds((place - base) * SIDE + first, count), rows]
            pltpu.make_async_copy(source, target, sem).start()

        base += held


def wait_window(parts, which, rows, target, sem):
    count = WINDOWS[which][1]
    pltpu.make_async_copy(parts[0].at[pl.ds(0, count), rows], target, sem).wait()


def margin_kernel(*refs):
    tables, refs = refs[:2], refs[2:]
    sems, refs = refs[-1], refs[:-1]
    gathered, outs = (refs[:PARTS], refs[PARTS : 2 * PARTS]), refs[2 * PARTS :]
    slots = outs[0].shape[0]
    everything = []
    for channel, (table, parts) in enumerate(zip(tables, gathered)):
        for side in range(2):
            rows = pl.ds(RIM, RIM) if side == 0 else pl.ds(0, RIM)
            for slot in range(slots):
                item = side * slots + slot
                for which, (_, count, to) in enumerate(WINDOWS):
                    target = outs[2 * channel + side].at[slot, pl.ds(to, count)]
                    sem = sems.at[channel, item, which]
                    copy_window(parts, which, table[which, item], rows, target, sem)
                    everything.append((parts, which, rows, target, sem))
    for item in everything:
        wait_window(*item)


PARTS = 5


def margins(gathered, tables):
    slots = tables[0].shape[1] // 2
    hbm, smem = pl.BlockSpec(memory_space=pltpu.HBM), pl.BlockSpec(memory_space=pltpu.SMEM)
    return pl.pallas_call(
        margin_kernel,
        in_specs=[smem] * 2 + [hbm] * (2 * PARTS),
        out_specs=[hbm] * 4,
        out_shape=[pltpu.HBM((slots, WIN, RIM, 128), BF16)] * 4,
        scratch_shapes=[pltpu.SemaphoreType.DMA((2, 2 * slots, 3))],
        compiler_params=pltpu.CompilerParams(vmem_limit_bytes=1 << 20),
        name="margins",
    )(*tables, *far_memory(*gathered[0], *gathered[1]))


def split(value):
    high = value.astype(BF16)
    low = (value - high.astype(F32)).astype(BF16)
    return high, low


def pair(first, second):
    (h0, l0), (h1, l1) = split(first), split(second)
    return jnp.concatenate([h0, h1], axis=1), jnp.concatenate([l0, l1], axis=1)


def three_term(matrix, high, low):
    return dot(matrix, jnp.concatenate([high, low, high], axis=0))


def dot(a, b):
    return jnp.dot(a, b, preferred_element_type=F32)


def job_kernel(channel, table, backdrops, *refs):
    parts, refs = refs[:PARTS], refs[PARTS:]
    top_ref, bottom_ref, data_ref, mz_ref, mx_ref, my_ref, myt_ref, mxt_ref, mzt_ref, out_ref = refs[:10]
    blocks, seen_data, z_high, z_low, blurred_x, back_y, back_x, sems = refs[10:]
    slot, slots = pl.program_id(0), pl.num_programs(0)
    mid = pl.ds(RIM, PADS)

    def others(which_slot, buffer):
        span = pl.ds(0, WIN)
        return (
            (top_ref.at[which_slot], blocks.at[buffer, span, pl.ds(0, RIM)], sems.at[buffer, 3]),
            (bottom_ref.at[which_slot], blocks.at[buffer, span, pl.ds(RIM + PADS, RIM)], sems.at[buffer, 4]),
            (data_ref.at[which_slot, channel], seen_data.at[buffer], sems.at[buffer, 5]),
        )

    def fetch(which_slot, buffer):
        for which, (_, count, to) in enumerate(WINDOWS):
            target = blocks.at[buffer, pl.ds(to, count), mid]
            place = table[which, which_slot]
            copy_window(parts, which, place, pl.ds(0, PADS), target, sems.at[buffer, which])
        for source, target, sem in others(which_slot, buffer):
            pltpu.make_async_copy(source, target, sem).start()

    buffer = lax.rem(slot, 2)

    @pl.when(slot == 0)
    def _():
        fetch(0, 0)
        blurred_x[WIN * PW :] = jnp.zeros_like(blurred_x[WIN * PW :])
        back_y[WIN * PS :] = jnp.zeros_like(back_y[WIN * PS :])
        back_x[SIDE * PS :] = jnp.zeros_like(back_x[SIDE * PS :])

    @pl.when(slot + 1 < slots)
    def _():
        fetch(slot + 1, 1 - buffer)

    for which, (_, count, to) in enumerate(WINDOWS):
        target = blocks.at[buffer, pl.ds(to, count), mid]
        wait_window(parts, which, pl.ds(0, PADS), target, sems.at[buffer, which])
    for source, target, sem in others(slot, buffer):
        pltpu.make_async_copy(source, target, sem).wait()

    mz, mx, my = mz_ref[0], mx_ref[0], my_ref[0]
    myt, mxt, mzt = myt_ref[0], mxt_ref[0], mzt_ref[0]
    backdrop = backdrops[table[3, slot]]

    def along_z(i, carry):
        start = i * CHUNK
        rows = blocks[buffer, pl.ds(start, CHUNK)].reshape(CHUNK * PADW, 128)
        in_z = dot(jnp.concatenate([rows, rows], axis=1), mz)
        high, low = split(in_z)
        z_high[pl.ds(start, CHUNK)] = high.reshape(CHUNK, PADW, 128)
        z_low[pl.ds(start, CHUNK)] = low.reshape(CHUNK, PADW, 128)
        return carry

    lax.fori_loop(0, -(-WIN // CHUNK), along_z, 0, unroll=UZ)

    def along_x_first(i, carry):
        y = 2 * i
        high = jnp.concatenate([z_high[y], z_high[y + 1]], axis=1)
        low = jnp.concatenate([z_low[y], z_low[y + 1]], axis=1)
        in_x = three_term(mx, high, low)
        start = pl.multiple_of(y * PW, 16)
        blurred_x[pl.ds(start, PADW), :] = in_x[:, :128]
        blurred_x[pl.ds(start + PW, PADW), :] = in_x[:, 128:]
        return carry

    lax.fori_loop(0, WIN // 2, along_x_first, 0, unroll=UNROLL)

    def along_y(i, carry):
        u = 2 * i
        lines = [blurred_x[pl.ds(u + j, PADW, stride=PW), :] for j in range(2)]
        predicted = three_term(my, *pair(*lines)) + backdrop
        seen = jnp.concatenate([seen_data[buffer, u], seen_data[buffer, u + 1]], axis=1)
        ratio = seen.astype(F32) / predicted
        in_y = three_term(myt, *pair(ratio[:, :128], ratio[:, 128:]))
        start = pl.multiple_of(u * PS, 16)
        back_y[pl.ds(start, PADS), :] = in_y[:, :128]
        back_y[pl.ds(start + PS, PADS), :] = in_y[:, 128:]
        return carry

    lax.fori_loop(0, WIN // 2, along_y, 0, unroll=UNROLL)

    def along_x(i, carry):
        y = 2 * i
        lines = [back_y[pl.ds(y + j, PADW, stride=PS), :] for j in range(2)]
        in_x = three_term(mxt, *pair(*lines))
        start = pl.multiple_of(y * PS, 16)
        back_x[pl.ds(start, PADS), :] = in_x[:, :128]
        back_x[pl.ds(start + PS, PADS), :] = in_x[:, 128:]
        return carry

    lax.fori_loop(0, SIDE // 2, along_x, 0, unroll=UNROLL)

    group = 4
    for i in range(SIDE // group):
        lines = [back_x[pl.ds(group * i + j, PADS, stride=PS), :] for j in range(group)]
        high, low = split(jnp.concatenate(lines, axis=0))
        factor = dot(jnp.concatenate([high, low, high], axis=1), mzt)
        for j in range(group):
            x = group * i + j
            first = (x % 2) * SIDE
            out_ref[x // 2, 0, first : first + SIDE, :] = factor[j * PADS : j * PADS + SIDE]
    for k in range(SIDE // 2, 16):
        out_ref[k, 0] = jnp.zeros_like(out_ref[k, 0])


UNROLL = 29
CHUNK = 29
PEXTRA = 8
SEXTRA = 8
PW = PADW + PEXTRA
PS = PADS + SEXTRA
UZ = 1


def run_jobs(channel, parts, table, top, bottom, view_data, backdrops, mats):
    slots = table.shape[1]
    hbm = pl.BlockSpec(memory_space=pltpu.HBM)
    smem = pl.BlockSpec(memory_space=pltpu.SMEM)
    specs = [smem, smem] + [hbm] * (len(parts) + 3)
    specs += [pl.BlockSpec((1,) + m.shape[1:], lambda slot: (slot, 0, 0)) for m in mats]
    return pl.pallas_call(
        functools.partial(job_kernel, channel),
        grid=(slots,),
        in_specs=specs,
        out_specs=pl.BlockSpec((16, 1, 2 * SIDE, 128), lambda slot: (0, slot, 0, 0)),
        scratch_shapes=[
            pltpu.VMEM((2, WIN, PADW, 128), BF16),
            pltpu.VMEM((2, WIN, PADW, 128), BF16),
            pltpu.VMEM((WIN, PADW, 128), BF16),
            pltpu.VMEM((WIN, PADW, 128), BF16),
            pltpu.VMEM((PADW * PW, 128), F32),
            pltpu.VMEM((PADW * PS, 128), F32),
            pltpu.VMEM((PADS * PS, 128), F32),
            pltpu.SemaphoreType.DMA((2, 6)),
        ],
        out_shape=pltpu.HBM((16, slots, 2 * SIDE, 128), F32),
        compiler_params=pltpu.CompilerParams(vmem_limit_bytes=18 << 20),
        cost_estimate=pl.CostEstimate(
            flops=slots * 2 * 128 * (WIN * PADW * (256 + 192 + 192 + 96) + 2 * SIDE * PADS * 192),
            transcendentals=slots * WIN * PADW * 128,
            bytes_accessed=slots * (2 * WIN * PADW * 128 * 2 + 16 * 2 * SIDE * 128 * 4),
        ),
        name="jobs",
    )(table, backdrops, *far_memory(*parts, top, bottom, view_data, *mats))


def bands(taps, positions_out, positions_in):
    offsets = positions_in[None, :] - positions_out[:, None] + HALO
    sel = offsets[None, :, :, None] == jnp.arange(taps.shape[1])[None, None, None, :]
    return jnp.sum(jnp.where(sel, taps[:, None, None, :], 0.0), axis=3)


def high_low(matrix):
    high = lax.reduce_precision(matrix, 8, 7)
    return high.astype(BF16), (matrix - high).astype(BF16)


def job_matrices(taps, bricks):
    none = -1000
    far = 1000
    line = jnp.arange(128)
    row = jnp.arange(PADW)
    win_in = jnp.where(row < WIN, row, none)
    win_out = jnp.where(row < WIN, row, far)
    short = jnp.arange(PADS)
    inner_out = jnp.where(short < SIDE, short + HALO, far)
    x_in = jnp.where(row < RIM + 16, row - 1, row - 5)
    x_in = jnp.where((row >= RIM + 16) & (row < RIM + 20), none, x_in)
    x_in = jnp.where((x_in < 0) | (x_in >= WIN), none, x_in)
    inside = (row >= HALO)[None, :] | (bricks > 0)[:, None]
    inside &= (row < HALO + SIDE)[None, :] | (bricks < RING * RING - 1)[:, None]
    forward = lambda t, out, inp: bands(t, out, inp)
    backward = lambda t, out, inp: jnp.swapaxes(bands(t, inp, out), 1, 2)
    three = lambda pair: jnp.concatenate([pair[0], pair[0], pair[1]], axis=2)
    mz = high_low(jnp.swapaxes(forward(taps[:, 2], line, line), 1, 2))
    mzt = high_low(jnp.swapaxes(backward(taps[:, 2], line, line), 1, 2))
    win_in_far = jnp.where(row < WIN, row, far)
    inner_none = jnp.where(short < SIDE, short + HALO, none)
    return (
        jnp.concatenate(mz, axis=1),
        three(high_low(forward(taps[:, 0], win_out, x_in))),
        three(high_low(jnp.where(inside[:, None, :], forward(taps[:, 1], win_out, win_in), 0.0))),
        three(high_low(backward(taps[:, 1], inner_none, win_in_far))),
        three(high_low(backward(taps[:, 0], inner_none, win_in_far))),
        jnp.concatenate([mzt[0], mzt[0], mzt[1]], axis=1),
    )


def add_kernel(owners, parts_ref, out_ref):
    out_ref[...] = jnp.zeros_like(out_ref)
    slots = parts_ref.shape[1]
    for w in range(parts_ref.shape[0]):
        for s in range(slots):
            b = owners[w * slots + s]
            out_ref[b] += parts_ref[w, s]


def add_up(owners, parts):
    return pl.pallas_call(
        add_kernel,
        in_specs=[pl.BlockSpec(memory_space=pltpu.SMEM), pl.BlockSpec(memory_space=pltpu.VMEM)],
        out_specs=pl.BlockSpec(memory_space=pltpu.VMEM),
        out_shape=pltpu.HBM((16,) + parts.shape[2:], F32),
        compiler_params=pltpu.CompilerParams(vmem_limit_bytes=8 << 20),
        name="add_up",
    )(owners, parts)


def update_kernel(count, est_ref, *refs):
    out_ref = refs[-1]
    seen = count[0].astype(F32)
    for c, total in enumerate(refs[:-1]):
        for k in range(SIDE // 2):
            for j in range(2):
                rows = total[k, j * SIDE : (j + 1) * SIDE, :]
                out_ref[c, 2 * k + j] = est_ref[c, 2 * k + j] * rows / seen


def update(count, estimate, totals):
    vmem = pl.BlockSpec(memory_space=pltpu.VMEM)
    return pl.pallas_call(
        update_kernel,
        in_specs=[pl.BlockSpec(memory_space=pltpu.SMEM)] + [vmem] * (1 + len(totals)),
        out_specs=vmem,
        out_shape=jax.ShapeDtypeStruct(estimate.shape, F32),
        compiler_params=pltpu.CompilerParams(vmem_limit_bytes=12 << 20),
        name="update",
    )(count, estimate, *totals)


def on_device(estimate, view_data, psf, background, slot_brick, slot_view, intersection):
    me = lax.axis_index("tile").astype(I32)
    groups, workers = lax.axis_size("view"), lax.axis_size("tile")
    upward = [(i, i + 1) for i in range(groups - 1)]
    downward = [(j, i) for i, j in upward]
    bricks, views = slot_brick[0, 0], slot_view[0, 0]
    slots = bricks.shape[0]

    wire = estimate.astype(BF16).transpose(0, 2, 1, 3)
    wire = jnp.concatenate([wire[:, :, :RIM], wire[:, :, SIDE - RIM :]], axis=2)
    rings = ring_gather([wire[0], wire[1]], (0, 1))
    above = lax.ppermute(bricks, "view", downward)
    below = lax.ppermute(bricks, "view", upward)
    spread = jnp.broadcast_to(jnp.pad(bricks, (0, 128 - slots))[None, None], (workers, 8, 128))
    owners = lax.all_to_all(spread, "tile", 0, 0, tiled=True)[:, 0, :slots].reshape(-1)

    taps = jnp.stack([lax.dynamic_index_in_dim(psf, v, 0, keepdims=False) for v in views])
    mats = job_matrices(taps, bricks)
    data = jnp.pad(view_data[0, 0], ((0, 0),) * 3 + ((0, PADW - WIN), (0, 0)))
    count = jnp.sum(intersection[0, 0]).reshape(1)
    tables = []
    for x_first in (True, False):
        wanted = window_table(jnp.concatenate([above, below]), me, x_first)
        mine = jnp.concatenate([window_table(bricks, me, x_first), views[None]])
        tables.append((wanted, mine))

    rings = [jnp.concatenate(parts, axis=0) for parts in rings]
    rings, mats, data, tables, owners, count = lax.optimization_barrier(
        (rings, mats, data, tables, owners, count)
    )
    gathered = ring_gather(rings, (1, 0))

    rims = margins(gathered, [wanted for wanted, _ in tables])
    edges = [
        (lax.ppermute(rims[2 * c], "view", upward), lax.ppermute(rims[2 * c + 1], "view", downward))
        for c in range(2)
    ]
    edges = lax.optimization_barrier(edges)
    totals = []
    for channel in range(2):
        factors = run_jobs(
            channel, gathered[channel], tables[channel][1], *edges[channel], data, background, mats
        )
        parts = lax.all_to_all(factors, "tile", 0, 0, tiled=True)
        summed = add_up(owners, parts)
        totals.append(lax.all_to_all(summed, "tile", 0, 0, tiled=True))
    return update(count, estimate, totals)


def solution(mesh):
    placed = (
        P(None, "view", "tile", None),
        P("view", "tile", None, None, None, None, None),
        P(),
        P(),
        P("view", "tile", None),
        P("view", "tile", None),
        P("view", "tile", None),
    )
    return jax.shard_map(
        on_device,
        mesh=mesh,
        in_specs=placed,
        out_specs=P(None, "view", "tile", None),
        check_vma=False,
    )
```

time: 289 us -> 317 us (1.097)
  Pallas kernels: 91.2 us -> 131 us
  blocking collectives: 25.7 us -> 0 us
  waiting for transfers between devices: 51.9 us -> 75.6 us
  local copies, waits for them, and re-layouts: 44.5 us -> 22 us
  other arithmetic: 7.46 us -> 14.2 us
  starting transfers between devices: 60.2 us -> 66.4 us
    pallas_call x4 -> x3, Pallas kernels: 85.8 us -> 127 us  [the longest x1 88.4 us: margins(): pl.pallas_call(margin_kernel, in_specs=[smem] * 2 + [hbm] * (2 * PARTS),...]
    all_gather x1 -> x0, blocking collectives: 25.7 us -> none  [on_device(): owners = lax.all_gather(bricks, 'tile', axis=0, tiled=True)]
    all_to_all x2, waiting for transfers between devices: 0.01 us -> 23.6 us  [on_device(): parts = lax.all_to_all(factors, 'tile', 0, 0, tiled=True)]
    unnamed x42 -> x66, local copies, waits for them, and re-layouts: 28.3 us -> 10.4 us
    pad x0 -> x2, local copies, waits for them, and re-layouts: none -> 7.39 us  [the longest x1 7.38 us: on_device(): data = jnp.pad(view_data[0, 0], ((0, 0),) * 3 + ((0, PADW - WIN), (0, 0)))]
    ppermute x16, starting transfers between devices: 23 us -> 28.7 us  [torus_step(): return lax.ppermute(array, 'tile', pairs)]
    all_to_all x0 -> x1, starting transfers between devices: none -> 5.58 us  [on_device(): lax.all_to_all(spread, 'tile', 0, 0, tiled=True)[:, 0, :slots].reshape(-1)]
    squeeze x3 -> x0, local copies, waits for them, and re-layouts: 5.16 us -> none  [the longest x2 5.1 us: on_device(): bottom = lax.ppermute(edge[1], 'view', downward)]
  transfers between devices with their start and end apart: 26 -> 27, of which waited for: 10 -> 12; matrix products, arithmetic and copies ran while one was open for 14% -> 10% of each run, Pallas kernels for 31% -> 7%
where the time goes in v2:
time: 317 us; the launch traced here: 315 us
  Pallas kernels  131 us (41%)
  waiting for transfers between devices  75.6 us (24%)
  starting transfers between devices  66.4 us (21%)
  local copies, waits for them, and re-layouts  22 us (7%)
  other arithmetic  14.2 us (4%)
  between operations  6.48 us (2%)
    pallas_call x1, Pallas kernels, margins(): pl.pallas_call(margin_kernel, in_specs=[smem] * 2 + [hbm] * (2 * PARTS),...  88.4 us
    pallas_call x2, Pallas kernels, run_jobs(): pl.pallas_call(functools.partial(job_kernel, channel), grid=(slots,), in_...  38.3 us
    ppermute x16, starting transfers between devices, torus_step(): return lax.ppermute(array, 'tile', pairs)  28.7 us
    ppermute x16, waiting for transfers between devices, torus_step(): return lax.ppermute(array, 'tile', pairs)  24.4 us
    all_to_all x2, waiting for transfers between devices, on_device(): parts = lax.all_to_all(factors, 'tile', 0, 0, tiled=True)  23.6 us
    all_to_all x2, waiting for transfers between devices, on_device(): totals.append(lax.all_to_all(summed, 'tile', 0, 0, tiled=True))  16.6 us
    unnamed x66, local copies, waits for them, and re-layouts  10.4 us
    all_to_all x2, starting transfers between devices, on_device(): parts = lax.all_to_all(factors, 'tile', 0, 0, tiled=True)  9.23 us
  transfers between devices with their start and end apart: 27, of which 12 were waited for; matrix products, arithmetic and copies ran while one was open for 10% of the time, Pallas kernels for 7%

profile of v2, /device:TPU:32, one launch (start us, length us, event | category | flops | bytes accessed | tf_op | source)
XLA Modules:
  0.0 315.5 jit_solution(596898673464966516)
XLA Ops:
  12.3 5.6 %all-to-all-start = ((s32[16,8,128]{2,1,0:T(8,128)}), s32[16,8,128]{2,1,0:T(8,128)}, u32[]{:S(2)}, u32[]{:S(2)}) async-start(s32[16,8,128]{2,1,0:T(8,128)} %broadcast_in_dim.285), calls=%async_computation | async-start | bytes 131072 | tf_op jit(solution)/shard_map/all_to_all | solution.py:383
  30.0 6.5 %copy.44 = bf16[1,1,3,2,58,58,128]{6,5,4,3,2,1,0:T(8,128)(2,1)} copy(bf16[1,1,3,2,58,58,128]{6,3,5,4,2,1,0:T(2,128)(2,1)} %param.8) | data formatting | bytes 10334208 | tf_op args[1]
  42.3 7.4 %pad.8.refs_7_ = bf16[3,2,58,64,128]{4,3,2,1,0:T(8,128)(2,1)} pad(bf16[3,2,58,58,128]{4,3,2,1,0:T(8,128)(2,1)} %bitcast.79, bf16[]{:T(256)} %constant.344.clone.1), padding=0_0x0_0x0_0x0_6x0_0 | pad | bytes 10868738 | tf_op jit(solution)/shard_map/jit(_pad)/pad | solution.py:387
  49.7 3.1 collective-permute-start.1
  58.2 3.6 %collective-permute-start.3 = (bf16[14,32,128]{2,1,0:T(8,128)(2,1)S(1)}, bf16[14,32,128]{2,1,0:T(8,128)(2,1)S(1)}, u32[]{:S(2)}, u32[]{:S(2)}) collective-permute-start(bf16[14,32,128]{2,1,0:T(8,128)(2,1)S(1)} %slice.75), channel_id=1, source_target_pairs={{0,96},{8,104},{16,112},{24,120},{32,0},{40,8},{48,16},{56,24},{64... | collective-permute-start | bytes 344072 | tf_op jit(solution)/shard_map/ppermute | solution.py:30
  67.5 3.6 %collective-permute-start.15 = (bf16[112,32,128]{2,1,0:T(8,128)(2,1)S(1)}, bf16[112,32,128]{2,1,0:T(8,128)(2,1)S(1)}, u32[]{:S(2)}, u32[]{:S(2)}) collective-permute-start(bf16[112,32,128]{2,1,0:T(8,128)(2,1)S(1)} %constant_dynamic-update-slice_fusion.5.refs_7_.refs_0_), channel_id=1, source_target_pairs={{0,96},{8,104},{16,112},{24,120},{32,0},{40,8},{48,16},{56,24},{64... | collective-permute-start | bytes 2752520 | tf_op jit(solution)/shard_map/ppermute | solution.py:30
  71.2 15.1 %collective-permute-done.10.refs_3_.refs_1_ = bf16[112,32,128]{2,1,0:T(8,128)(2,1)S(1)} collective-permute-done((bf16[112,32,128]{2,1,0:T(8,128)(2,1)S(1)}, bf16[112,32,128]{2,1,0:T(8,128)(2,1)S(1)}, u32[]{:S(2)}, u32[]{:S(2)}) %collective-permute-start.10) | collective-permute-done | bytes 917536 | tf_op jit(solution)/shard_map/ppermute | solution.py:30
  86.6 3.1 collective-permute-start.13
  89.9 3.4 %collective-permute-start.17 = (bf16[56,32,128]{2,1,0:T(8,128)(2,1)S(1)}, bf16[56,32,128]{2,1,0:T(8,128)(2,1)S(1)}, u32[]{:S(2)}, u32[]{:S(2)}) collective-permute-start(bf16[56,32,128]{2,1,0:T(8,128)(2,1)S(1)} %slice.82), channel_id=1, source_target_pairs={{0,96},{8,104},{16,112},{24,120},{32,0},{40,8},{48,16},{56,24},{64... | collective-permute-start | bytes 1376264 | tf_op jit(solution)/shard_map/ppermute | solution.py:30
  93.3 4.2 %collective-permute-done.12.refs_5_.refs_3_ = bf16[56,32,128]{2,1,0:T(8,128)(2,1)S(1)} collective-permute-done((bf16[56,32,128]{2,1,0:T(8,128)(2,1)S(1)}, bf16[56,32,128]{2,1,0:T(8,128)(2,1)S(1)}, u32[]{:S(2)}, u32[]{:S(2)}) %collective-permute-start.12) | collective-permute-done | bytes 458784 | tf_op jit(solution)/shard_map/ppermute | solution.py:30
  102.1 88.4 %margins.1 = (bf16[3,58,16,128]{3,2,1,0:T(8,128)(2,1)}, bf16[3,58,16,128]{3,2,1,0:T(8,128)(2,1)}, bf16[3,58,16,128]{3,2,1,0:T(8,128)(2,1)}, bf16[3,58,16,128]{3,2,1,0:T(8,128)(2,1)}) custom-call(s32[3,6]{1,0:T(4,128)S(1)} %pad_add_fusion.2.refs_0_, s32[3,6]{1,0:T(4,128)S(1)} %pad_add_fusion.3.refs_1_, bf16[112,32,128]{2,1,0:T(8,128)(2,1)} %copy-done.5, ...), custom_call_target="tpu_custom_call" | custom-call | tf_op jit(solution)/shard_map/margins/pallas_call | solution.py:107
  192.4 3.6 %collective-permute-start.19 = (bf16[3,58,16,128]{3,2,1,0:T(8,128)(2,1)}, bf16[3,58,16,128]{3,2,1,0:T(8,128)(2,1)S(1)}, u32[]{:S(2)}, u32[]{:S(2)}) collective-permute-start(bf16[3,58,16,128]{3,2,1,0:T(8,128)(2,1)} %get-tuple-element.36), channel_id=1, source_target_pairs={{1,0},{2,1},{3,2},{4,3},{5,4},{6,5},{7,6},{9,8},{10,9},{11,10},{12... | collective-permute-start | bytes 2138120 | tf_op jit(solution)/shard_map/ppermute | solution.py:403
  198.0 3.6 %collective-permute-start.21 = (bf16[3,58,16,128]{3,2,1,0:T(8,128)(2,1)}, bf16[3,58,16,128]{3,2,1,0:T(8,128)(2,1)S(1)}, u32[]{:S(2)}, u32[]{:S(2)}) collective-permute-start(bf16[3,58,16,128]{3,2,1,0:T(8,128)(2,1)} %get-tuple-element.38), channel_id=1, source_target_pairs={{1,0},{2,1},{3,2},{4,3},{5,4},{6,5},{7,6},{9,8},{10,9},{11,10},{12... | collective-permute-start | bytes 2138120 | tf_op jit(solution)/shard_map/ppermute | solution.py:403
  205.1 5.8 %collective-permute-done.20.refs_5_ = bf16[3,58,16,128]{3,2,1,0:T(8,128)(2,1)S(1)} collective-permute-done((bf16[3,58,16,128]{3,2,1,0:T(8,128)(2,1)}, bf16[3,58,16,128]{3,2,1,0:T(8,128)(2,1)S(1)}, u32[]{:S(2)}, u32[]{:S(2)}) %collective-permute-start.20) | collective-permute-done | bytes 712736 | tf_op jit(solution)/shard_map/ppermute | solution.py:403
  213.6 19.1 %jobs.3 = f32[16,3,56,128]{3,2,1,0:T(8,128)} custom-call(s32[4,3]{1,0:T(4,128)S(1)} %get-tuple-element.48.table, f32[6]{0:T(128)S(1)} %copy-done, bf16[112,32,128]{2,1,0:T(8,128)(2,1)} %copy-done.6, bf16[112,32,128]{2,1,0:T(8,128)(2,1)} %copy-done.3, bf16[112,32,128]{2,1,0:T(8,128)(2,1)} %copy-done.4, bf16[56,32,128]{2,1,0:T(8,128)(2,1)} %copy-done.9, ...), custom_call_target="tpu_custom_call" | custom-call | flops 2362441728 | bytes 7077888 | tf_op jit(solution)/shard_map/jobs/pallas_call | solution.py:259
  232.8 4.4 %all-to-all-start.3 = ((f32[16,3,56,128]{3,2,1,0:T(8,128)}), f32[16,3,56,128]{3,2,1,0:T(8,128)S(1)}, u32[]{:S(2)}, u32[]{:S(2)}) async-start(f32[16,3,56,128]{3,2,1,0:T(8,128)} %jobs.3), calls=%async_computation.3 | async-start | bytes 2752512 | tf_op jit(solution)/shard_map/all_to_all | solution.py:412
  237.2 19.2 %jobs.2 = f32[16,3,56,128]{3,2,1,0:T(8,128)} custom-call(s32[4,3]{1,0:T(4,128)S(1)} %get-tuple-element.30.table, f32[6]{0:T(128)S(1)} %copy-done, bf16[112,32,128]{2,1,0:T(8,128)(2,1)} %copy-done.5, bf16[112,32,128]{2,1,0:T(8,128)(2,1)} %copy-done.1, bf16[112,32,128]{2,1,0:T(8,128)(2,1)} %copy-done.2, bf16[56,32,128]{2,1,0:T(8,128)(2,1)} %copy-done.7, ...), custom_call_target="tpu_custom_call" | custom-call | flops 2362441728 | bytes 7077888 | tf_op jit(solution)/shard_map/jobs/pallas_call | solution.py:259
  256.4 3.6 %all-to-all-done.3.parts_ref = f32[16,3,56,128]{3,2,1,0:T(8,128)S(1)} async-done(((f32[16,3,56,128]{3,2,1,0:T(8,128)}), f32[16,3,56,128]{3,2,1,0:T(8,128)S(1)}, u32[]{:S(2)}, u32[]{:S(2)}) %all-to-all-start.3) | async-done | bytes 1376288 | tf_op jit(solution)/shard_map/all_to_all | solution.py:412
  260.0 4.8 %all-to-all-start.1 = ((f32[16,3,56,128]{3,2,1,0:T(8,128)}), f32[16,3,56,128]{3,2,1,0:T(8,128)S(1)}, u32[]{:S(2)}, u32[]{:S(2)}) async-start(f32[16,3,56,128]{3,2,1,0:T(8,128)} %jobs.2), calls=%async_computation.1 | async-start | bytes 2752512 | tf_op jit(solution)/shard_map/all_to_all | solution.py:412
  266.4 20.0 %all-to-all-done.1.parts_ref = f32[16,3,56,128]{3,2,1,0:T(8,128)S(1)} async-done(((f32[16,3,56,128]{3,2,1,0:T(8,128)}), f32[16,3,56,128]{3,2,1,0:T(8,128)S(1)}, u32[]{:S(2)}, u32[]{:S(2)}) %all-to-all-start.1) | async-done | bytes 1376288 | tf_op jit(solution)/shard_map/all_to_all | solution.py:412
  286.4 3.7 %all-to-all-start.4 = ((f32[16,56,128]{2,1,0:T(8,128)}), f32[16,56,128]{2,1,0:T(8,128)S(1)}, u32[]{:S(2)}, u32[]{:S(2)}) async-start(f32[16,56,128]{2,1,0:T(8,128)} %add_up.3), calls=%async_computation.4 | async-start | bytes 917504 | tf_op jit(solution)/shard_map/all_to_all | solution.py:414
  291.8 8.1 %all-to-all-done.4.refs_1_ = f32[16,56,128]{2,1,0:T(8,128)S(1)} async-done(((f32[16,56,128]{2,1,0:T(8,128)}), f32[16,56,128]{2,1,0:T(8,128)S(1)}, u32[]{:S(2)}, u32[]{:S(2)}) %all-to-all-start.4) | async-done | bytes 458784 | tf_op jit(solution)/shard_map/all_to_all | solution.py:414
  299.9 3.6 %all-to-all-start.2 = ((f32[16,56,128]{2,1,0:T(8,128)}), f32[16,56,128]{2,1,0:T(8,128)S(1)}, u32[]{:S(2)}, u32[]{:S(2)}) async-start(f32[16,56,128]{2,1,0:T(8,128)} %add_up.2), calls=%async_computation.2 | async-start | bytes 917504 | tf_op jit(solution)/shard_map/all_to_all | solution.py:414
  304.7 8.4 %all-to-all-done.2.refs_0_ = f32[16,56,128]{2,1,0:T(8,128)S(1)} async-done(((f32[16,56,128]{2,1,0:T(8,128)}), f32[16,56,128]{2,1,0:T(8,128)S(1)}, u32[]{:S(2)}, u32[]{:S(2)}) %all-to-all-start.2) | async-done | bytes 458784 | tf_op jit(solution)/shard_map/all_to_all | solution.py:414
  (166 shorter events, 57.0 us)
Async XLA Ops:
  0.0 49.7 %collective-permute-start.8 = (s32[3]{0:T(128)}, s32[3]{0:T(128)}, u32[]{:S(2)}, u32[]{:S(2)}) collective-permute-start(s32[3]{0:T(128)} %bitcast.83), channel_id=1, source_target_pairs={{1,0},{2,1},{3,2},{4,3},{5,4},{6,5},{7,6},{9,8},{10,9},{11,10},{12... | collective-permute-start | bytes 44 | tf_op jit(solution)/shard_map/ppermute | solution.py:380
  2.1 50.8 %collective-permute-start.9 = (s32[3]{0:T(128)}, s32[3]{0:T(128)}, u32[]{:S(2)}, u32[]{:S(2)}) collective-permute-start(s32[3]{0:T(128)} %bitcast.84), channel_id=1, source_target_pairs={{0,1},{1,2},{2,3},{3,4},{4,5},{5,6},{6,7},{8,9},{9,10},{10,11},{11... | collective-permute-start | bytes 44 | tf_op jit(solution)/shard_map/ppermute | solution.py:381
  6.9 47.7 %collective-permute-start.4 = (bf16[28,32,128]{2,1,0:T(8,128)(2,1)}, bf16[28,32,128]{2,1,0:T(8,128)(2,1)S(1)}, u32[]{:S(2)}, u32[]{:S(2)}) collective-permute-start(bf16[28,32,128]{2,1,0:T(8,128)(2,1)} %get-tuple-element.73), channel_id=1, source_target_pairs={{0,8},{8,16},{16,24},{24,0},{32,40},{40,48},{48,56},{56,32},{64,72... | collective-permute-start | bytes 688136 | tf_op jit(solution)/shard_map/ppermute | solution.py:30
  8.5 47.7 %collective-permute-start.5 = (bf16[28,32,128]{2,1,0:T(8,128)(2,1)}, bf16[28,32,128]{2,1,0:T(8,128)(2,1)S(1)}, u32[]{:S(2)}, u32[]{:S(2)}) collective-permute-start(bf16[28,32,128]{2,1,0:T(8,128)(2,1)} %get-tuple-element.73), channel_id=1, source_target_pairs={{0,24},{8,0},{16,8},{24,16},{32,56},{40,32},{48,40},{56,48},{64,88... | collective-permute-start | bytes 688136 | tf_op jit(solution)/shard_map/ppermute | solution.py:30
  10.2 47.9 %collective-permute-start = (bf16[28,32,128]{2,1,0:T(8,128)(2,1)S(1)}, bf16[28,32,128]{2,1,0:T(8,128)(2,1)S(1)}, u32[]{:S(2)}, u32[]{:S(2)}) collective-permute-start(bf16[28,32,128]{2,1,0:T(8,128)(2,1)S(1)} %get-tuple-element.77), channel_id=1, source_target_pairs={{0,32},{8,40},{16,48},{24,56},{32,64},{40,72},{48,80},{56,88},{64,... | collective-permute-start | bytes 688136 | tf_op jit(solution)/shard_map/ppermute | solution.py:30
  12.3 41.4 %all-to-all-start = ((s32[16,8,128]{2,1,0:T(8,128)}), s32[16,8,128]{2,1,0:T(8,128)}, u32[]{:S(2)}, u32[]{:S(2)}) async-start(s32[16,8,128]{2,1,0:T(8,128)} %broadcast_in_dim.285), calls=%async_computation | async-start | bytes 131072 | tf_op jit(solution)/shard_map/all_to_all | solution.py:383
  49.7 8.4 %collective-permute-start.1 = (bf16[28,32,128]{2,1,0:T(8,128)(2,1)S(1)}, bf16[28,32,128]{2,1,0:T(8,128)(2,1)S(1)}, u32[]{:S(2)}, u32[]{:S(2)}) collective-permute-start(bf16[28,32,128]{2,1,0:T(8,128)(2,1)S(1)} %get-tuple-element.77), channel_id=1, source_target_pairs={{0,96},{8,104},{16,112},{24,120},{32,0},{40,8},{48,16},{56,24},{64... | collective-permute-start | bytes 688136 | tf_op jit(solution)/shard_map/ppermute | solution.py:30
  54.7 7.3 %collective-permute-start.6 = (bf16[14,32,128]{2,1,0:T(8,128)(2,1)S(1)}, bf16[14,32,128]{2,1,0:T(8,128)(2,1)S(1)}, u32[]{:S(2)}, u32[]{:S(2)}) collective-permute-start(bf16[14,32,128]{2,1,0:T(8,128)(2,1)S(1)} %slice.76), channel_id=1, source_target_pairs={{0,8},{8,16},{16,24},{24,0},{32,40},{40,48},{48,56},{56,32},{64,72... | collective-permute-start | bytes 344072 | tf_op jit(solution)/shard_map/ppermute | solution.py:30
  64.2 22.0 %collective-permute-start.10 = (bf16[112,32,128]{2,1,0:T(8,128)(2,1)S(1)}, bf16[112,32,128]{2,1,0:T(8,128)(2,1)S(1)}, u32[]{:S(2)}, u32[]{:S(2)}) collective-permute-start(bf16[112,32,128]{2,1,0:T(8,128)(2,1)S(1)} %constant_dynamic-update-slice_fusion.refs_2_.refs_0_), channel_id=1, source_target_pairs={{0,8},{8,16},{16,24},{24,0},{32,40},{40,48},{48,56},{56,32},{64,72... | collective-permute-start | bytes 2752520 | tf_op jit(solution)/shard_map/ppermute | solution.py:30
  65.7 20.8 %collective-permute-start.11 = (bf16[112,32,128]{2,1,0:T(8,128)(2,1)S(1)}, bf16[112,32,128]{2,1,0:T(8,128)(2,1)S(1)}, u32[]{:S(2)}, u32[]{:S(2)}) collective-permute-start(bf16[112,32,128]{2,1,0:T(8,128)(2,1)S(1)} %constant_dynamic-update-slice_fusion.refs_2_.refs_0_), channel_id=1, source_target_pairs={{0,24},{8,0},{16,8},{24,16},{32,56},{40,32},{48,40},{56,48},{64,88... | collective-permute-start | bytes 2752520 | tf_op jit(solution)/shard_map/ppermute | solution.py:30
  67.5 22.1 %collective-permute-start.14 = (bf16[112,32,128]{2,1,0:T(8,128)(2,1)S(1)}, bf16[112,32,128]{2,1,0:T(8,128)(2,1)S(1)}, u32[]{:S(2)}, u32[]{:S(2)}) collective-permute-start(bf16[112,32,128]{2,1,0:T(8,128)(2,1)S(1)} %constant_dynamic-update-slice_fusion.5.refs_7_.refs_0_), channel_id=1, source_target_pairs={{0,32},{8,40},{16,48},{24,56},{32,64},{40,72},{48,80},{56,88},{64,... | collective-permute-start | bytes 2752520 | tf_op jit(solution)/shard_map/ppermute | solution.py:30
  67.5 22.3 %collective-permute-start.15 = (bf16[112,32,128]{2,1,0:T(8,128)(2,1)S(1)}, bf16[112,32,128]{2,1,0:T(8,128)(2,1)S(1)}, u32[]{:S(2)}, u32[]{:S(2)}) collective-permute-start(bf16[112,32,128]{2,1,0:T(8,128)(2,1)S(1)} %constant_dynamic-update-slice_fusion.5.refs_7_.refs_0_), channel_id=1, source_target_pairs={{0,96},{8,104},{16,112},{24,120},{32,0},{40,8},{48,16},{56,24},{64... | collective-permute-start | bytes 2752520 | tf_op jit(solution)/shard_map/ppermute | solution.py:30
  86.3 11.2 %collective-permute-start.12 = (bf16[56,32,128]{2,1,0:T(8,128)(2,1)S(1)}, bf16[56,32,128]{2,1,0:T(8,128)(2,1)S(1)}, u32[]{:S(2)}, u32[]{:S(2)}) collective-permute-start(bf16[56,32,128]{2,1,0:T(8,128)(2,1)S(1)} %slice.79), channel_id=1, source_target_pairs={{0,8},{8,16},{16,24},{24,0},{32,40},{40,48},{48,56},{56,32},{64,72... | collective-permute-start | bytes 1376264 | tf_op jit(solution)/shard_map/ppermute | solution.py:30
  86.6 10.9 %collective-permute-start.13 = (bf16[56,32,128]{2,1,0:T(8,128)(2,1)S(1)}, bf16[56,32,128]{2,1,0:T(8,128)(2,1)S(1)}, u32[]{:S(2)}, u32[]{:S(2)}) collective-permute-start(bf16[56,32,128]{2,1,0:T(8,128)(2,1)S(1)} %slice.80), channel_id=1, source_target_pairs={{0,24},{8,0},{16,8},{24,16},{32,56},{40,32},{48,40},{56,48},{64,88... | collective-permute-start | bytes 1376264 | tf_op jit(solution)/shard_map/ppermute | solution.py:30
  89.7 10.8 %collective-permute-start.16 = (bf16[56,32,128]{2,1,0:T(8,128)(2,1)S(1)}, bf16[56,32,128]{2,1,0:T(8,128)(2,1)S(1)}, u32[]{:S(2)}, u32[]{:S(2)}) collective-permute-start(bf16[56,32,128]{2,1,0:T(8,128)(2,1)S(1)} %slice.81), channel_id=1, source_target_pairs={{0,32},{8,40},{16,48},{24,56},{32,64},{40,72},{48,80},{56,88},{64,... | collective-permute-start | bytes 1376264 | tf_op jit(solution)/shard_map/ppermute | solution.py:30
  89.9 10.6 %collective-permute-start.17 = (bf16[56,32,128]{2,1,0:T(8,128)(2,1)S(1)}, bf16[56,32,128]{2,1,0:T(8,128)(2,1)S(1)}, u32[]{:S(2)}, u32[]{:S(2)}) collective-permute-start(bf16[56,32,128]{2,1,0:T(8,128)(2,1)S(1)} %slice.82), channel_id=1, source_target_pairs={{0,96},{8,104},{16,112},{24,120},{32,0},{40,8},{48,16},{56,24},{64... | collective-permute-start | bytes 1376264 | tf_op jit(solution)/shard_map/ppermute | solution.py:30
  190.5 12.7 %collective-permute-start.18 = (bf16[3,58,16,128]{3,2,1,0:T(8,128)(2,1)}, bf16[3,58,16,128]{3,2,1,0:T(8,128)(2,1)S(1)}, u32[]{:S(2)}, u32[]{:S(2)}) collective-permute-start(bf16[3,58,16,128]{3,2,1,0:T(8,128)(2,1)} %get-tuple-element.35), channel_id=1, source_target_pairs={{0,1},{1,2},{2,3},{3,4},{4,5},{5,6},{6,7},{8,9},{9,10},{10,11},{11... | collective-permute-start | bytes 2138120 | tf_op jit(solution)/shard_map/ppermute | solution.py:403
  192.4 12.7 %collective-permute-start.19 = (bf16[3,58,16,128]{3,2,1,0:T(8,128)(2,1)}, bf16[3,58,16,128]{3,2,1,0:T(8,128)(2,1)S(1)}, u32[]{:S(2)}, u32[]{:S(2)}) collective-permute-start(bf16[3,58,16,128]{3,2,1,0:T(8,128)(2,1)} %get-tuple-element.36), channel_id=1, source_target_pairs={{1,0},{2,1},{3,2},{4,3},{5,4},{6,5},{7,6},{9,8},{10,9},{11,10},{12... | collective-permute-start | bytes 2138120 | tf_op jit(solution)/shard_map/ppermute | solution.py:403
  196.1 14.8 %collective-permute-start.20 = (bf16[3,58,16,128]{3,2,1,0:T(8,128)(2,1)}, bf16[3,58,16,128]{3,2,1,0:T(8,128)(2,1)S(1)}, u32[]{:S(2)}, u32[]{:S(2)}) collective-permute-start(bf16[3,58,16,128]{3,2,1,0:T(8,128)(2,1)} %get-tuple-element.37), channel_id=1, source_target_pairs={{0,1},{1,2},{2,3},{3,4},{4,5},{5,6},{6,7},{8,9},{9,10},{10,11},{11... | collective-permute-start | bytes 2138120 | tf_op jit(solution)/shard_map/ppermute | solution.py:403
  198.0 14.7 %collective-permute-start.21 = (bf16[3,58,16,128]{3,2,1,0:T(8,128)(2,1)}, bf16[3,58,16,128]{3,2,1,0:T(8,128)(2,1)S(1)}, u32[]{:S(2)}, u32[]{:S(2)}) collective-permute-start(bf16[3,58,16,128]{3,2,1,0:T(8,128)(2,1)} %get-tuple-element.38), channel_id=1, source_target_pairs={{1,0},{2,1},{3,2},{4,3},{5,4},{6,5},{7,6},{9,8},{10,9},{11,10},{12... | collective-permute-start | bytes 2138120 | tf_op jit(solution)/shard_map/ppermute | solution.py:403
  232.8 27.2 %all-to-all-start.3 = ((f32[16,3,56,128]{3,2,1,0:T(8,128)}), f32[16,3,56,128]{3,2,1,0:T(8,128)S(1)}, u32[]{:S(2)}, u32[]{:S(2)}) async-start(f32[16,3,56,128]{3,2,1,0:T(8,128)} %jobs.3), calls=%async_computation.3 | async-start | bytes 2752512 | tf_op jit(solution)/shard_map/all_to_all | solution.py:412
  260.0 26.5 %all-to-all-start.1 = ((f32[16,3,56,128]{3,2,1,0:T(8,128)}), f32[16,3,56,128]{3,2,1,0:T(8,128)S(1)}, u32[]{:S(2)}, u32[]{:S(2)}) async-start(f32[16,3,56,128]{3,2,1,0:T(8,128)} %jobs.2), calls=%async_computation.1 | async-start | bytes 2752512 | tf_op jit(solution)/shard_map/all_to_all | solution.py:412
  286.4 13.5 %all-to-all-start.4 = ((f32[16,56,128]{2,1,0:T(8,128)}), f32[16,56,128]{2,1,0:T(8,128)S(1)}, u32[]{:S(2)}, u32[]{:S(2)}) async-start(f32[16,56,128]{2,1,0:T(8,128)} %add_up.3), calls=%async_computation.4 | async-start | bytes 917504 | tf_op jit(solution)/shard_map/all_to_all | solution.py:414
  299.9 13.3 %all-to-all-start.2 = ((f32[16,56,128]{2,1,0:T(8,128)}), f32[16,56,128]{2,1,0:T(8,128)S(1)}, u32[]{:S(2)}, u32[]{:S(2)}) async-start(f32[16,56,128]{2,1,0:T(8,128)} %add_up.2), calls=%async_computation.2 | async-start | bytes 917504 | tf_op jit(solution)/shard_map/all_to_all | solution.py:414
  (31 other events, 468.4 us)

commit v3 on v2

--- a/solution.py
+++ b/solution.py
@@ -30,14 +30,24 @@
     return lax.ppermute(array, "tile", pairs)
 
 
-def ring_gather(arrays, axes):
-    step = lambda a, axis, d: torus_step(a, d if axis == 0 else 0, d if axis == 1 else 0)
-    near = [(step(a, ax, 1), step(a, ax, -1)) for a, ax in zip(arrays, axes)]
-    far = []
-    for (lower, upper), ax in zip(near, axes):
+def along(axis, step):
+    return (step, 0) if axis == 0 else (0, step)
+
+
+def ring_near(arrays, axes):
+    return [
+        [a, torus_step(a, *along(ax, 1)), torus_step(a, *along(ax, -1))]
+        for a, ax in zip(arrays, axes)
+    ]
+
+
+def ring_far(near, axes):
+    result = []
+    for (own, lower, upper), ax in zip(near, axes):
         half = lower.shape[0] // 2
-        far.append((step(lower[:half], ax, 1), step(upper[half:], ax, -1)))
-    return [[a, *n, *f] for a, n, f in zip(arrays, near, far)]
+        far = [torus_step(lower[:half], *along(ax, 1)), torus_step(upper[half:], *along(ax, -1))]
+        result.append([own, lower, upper, *far])
+    return result
 
 
 def place_of(brick, me, x_first):
@@ -80,22 +90,33 @@
 
 def margin_kernel(*refs):
     tables, refs = refs[:2], refs[2:]
-    sems, refs = refs[-1], refs[:-1]
+    refs, (stage, sems) = refs[:-2], refs[-2:]
     gathered, outs = (refs[:PARTS], refs[PARTS : 2 * PARTS]), refs[2 * PARTS :]
     slots = outs[0].shape[0]
-    everything = []
+    copies = []
     for channel, (table, parts) in enumerate(zip(tables, gathered)):
         for side in range(2):
             rows = pl.ds(RIM, RIM) if side == 0 else pl.ds(0, RIM)
             for slot in range(slots):
                 item = side * slots + slot
+                waits = []
                 for which, (_, count, to) in enumerate(WINDOWS):
-                    target = outs[2 * channel + side].at[slot, pl.ds(to, count)]
+                    target = stage.at[channel, item, pl.ds(to, count)]
                     sem = sems.at[channel, item, which]
                     copy_window(parts, which, table[which, item], rows, target, sem)
-                    everything.append((parts, which, rows, target, sem))
-    for item in everything:
-        wait_window(*item)
+                    waits.append((parts, which, rows, target, sem))
+                out = pltpu.make_async_copy(
+                    stage.at[channel, item],
+                    outs[2 * channel + side].at[slot],
+                    sems.at[channel, item, 3],
+                )
+                copies.append((waits, out))
+    for waits, out in copies:
+        for item in waits:
+            wait_window(*item)
+        out.start()
+    for _, out in copies:
+        out.wait()
 
 
 PARTS = 5
@@ -109,8 +130,11 @@
         in_specs=[smem] * 2 + [hbm] * (2 * PARTS),
         out_specs=[hbm] * 4,
         out_shape=[pltpu.HBM((slots, WIN, RIM, 128), BF16)] * 4,
-        scratch_shapes=[pltpu.SemaphoreType.DMA((2, 2 * slots, 3))],
-        compiler_params=pltpu.CompilerParams(vmem_limit_bytes=1 << 20),
+        scratch_shapes=[
+            pltpu.VMEM((2, 2 * slots, WIN, RIM, 128), BF16),
+            pltpu.SemaphoreType.DMA((2, 2 * slots, 4)),
+        ],
+        compiler_params=pltpu.CompilerParams(vmem_limit_bytes=4 << 20),
         name="margins",
     )(*tables, *far_memory(*gathered[0], *gathered[1]))
 
@@ -203,12 +227,14 @@
 
     lax.fori_loop(0, WIN // 2, along_x_first, 0, unroll=UNROLL)
 
+    past = jnp.zeros((PADW - WIN, 256), F32)
+
     def along_y(i, carry):
         u = 2 * i
         lines = [blurred_x[pl.ds(u + j, PADW, stride=PW), :] for j in range(2)]
         predicted = three_term(my, *pair(*lines)) + backdrop
         seen = jnp.concatenate([seen_data[buffer, u], seen_data[buffer, u + 1]], axis=1)
-        ratio = seen.astype(F32) / predicted
+        ratio = jnp.concatenate([seen.astype(F32) / predicted[:WIN], past], axis=0)
         in_y = three_term(myt, *pair(ratio[:, :128], ratio[:, 128:]))
         start = pl.multiple_of(u * PS, 16)
         back_y[pl.ds(start, PADS), :] = in_y[:, :128]
@@ -263,7 +289,7 @@
         out_specs=pl.BlockSpec((16, 1, 2 * SIDE, 128), lambda slot: (0, slot, 0, 0)),
         scratch_shapes=[
             pltpu.VMEM((2, WIN, PADW, 128), BF16),
-            pltpu.VMEM((2, WIN, PADW, 128), BF16),
+            pltpu.VMEM((2, WIN, WIN, 128), BF16),
             pltpu.VMEM((WIN, PADW, 128), BF16),
             pltpu.VMEM((WIN, PADW, 128), BF16),
             pltpu.VMEM((PADW * PW, 128), F32),
@@ -324,46 +350,47 @@
     )
 
 
-def add_kernel(owners, parts_ref, out_ref):
+def add_kernel(owners, *refs):
+    out_ref = refs[-1]
     out_ref[...] = jnp.zeros_like(out_ref)
-    slots = parts_ref.shape[1]
-    for w in range(parts_ref.shape[0]):
-        for s in range(slots):
-            b = owners[w * slots + s]
-            out_ref[b] += parts_ref[w, s]
+    workers, slots = refs[0].shape[:2]
+    for channel, parts_ref in enumerate(refs[:-1]):
+        for w in range(workers):
+            for s in range(slots):
+                out_ref[owners[w * slots + s], channel] += parts_ref[w, s]
 
 
 def add_up(owners, parts):
+    vmem, smem = pl.BlockSpec(memory_space=pltpu.VMEM), pl.BlockSpec(memory_space=pltpu.SMEM)
     return pl.pallas_call(
         add_kernel,
-        in_specs=[pl.BlockSpec(memory_space=pltpu.SMEM), pl.BlockSpec(memory_space=pltpu.VMEM)],
-        out_specs=pl.BlockSpec(memory_space=pltpu.VMEM),
-        out_shape=pltpu.HBM((16,) + parts.shape[2:], F32),
+        in_specs=[smem] + [vmem] * len(parts),
+        out_specs=vmem,
+        out_shape=pltpu.HBM((16, len(parts)) + parts[0].shape[2:], F32),
         compiler_params=pltpu.CompilerParams(vmem_limit_bytes=8 << 20),
         name="add_up",
-    )(owners, parts)
-
-
-def update_kernel(count, est_ref, *refs):
-    out_ref = refs[-1]
+    )(owners, *parts)
+
+
+def update_kernel(count, est_ref, total, out_ref):
     seen = count[0].astype(F32)
-    for c, total in enumerate(refs[:-1]):
+    for c in range(out_ref.shape[0]):
         for k in range(SIDE // 2):
             for j in range(2):
-                rows = total[k, j * SIDE : (j + 1) * SIDE, :]
+                rows = total[k, c, j * SIDE : (j + 1) * SIDE, :]
                 out_ref[c, 2 * k + j] = est_ref[c, 2 * k + j] * rows / seen
 
 
-def update(count, estimate, totals):
-    vmem = pl.BlockSpec(memory_space=pltpu.VMEM)
+def update(count, estimate, total):
+    vmem, smem = pl.BlockSpec(memory_space=pltpu.VMEM), pl.BlockSpec(memory_space=pltpu.SMEM)
     return pl.pallas_call(
         update_kernel,
-        in_specs=[pl.BlockSpec(memory_space=pltpu.SMEM)] + [vmem] * (1 + len(totals)),
+        in_specs=[smem, vmem, vmem],
         out_specs=vmem,
         out_shape=jax.ShapeDtypeStruct(estimate.shape, F32),
         compiler_params=pltpu.CompilerParams(vmem_limit_bytes=12 << 20),
         name="update",
-    )(count, estimate, *totals)
+    )(count, estimate, total)
 
 
 def on_device(estimate, view_data, psf, background, slot_brick, slot_view, intersection):
@@ -375,28 +402,30 @@
     slots = bricks.shape[0]
 
     wire = estimate.astype(BF16).transpose(0, 2, 1, 3)
-    wire = jnp.concatenate([wire[:, :, :RIM], wire[:, :, SIDE - RIM :]], axis=2)
-    rings = ring_gather([wire[0], wire[1]], (0, 1))
+    note = jnp.pad(bricks.astype(BF16)[None, None], ((0, 0), (0, SIDE - 1), (0, 128 - slots)))
+    note = jnp.broadcast_to(note, (wire.shape[0],) + note.shape[1:])
+    wire = jnp.concatenate([wire[:, :, :RIM], note[:, :, None], wire[:, :, SIDE - RIM + 1 :]], axis=2)
+    near = ring_near([wire[0], wire[1]], (0, 1))
+    near, bricks = lax.optimization_barrier((near, bricks))
     above = lax.ppermute(bricks, "view", downward)
     below = lax.ppermute(bricks, "view", upward)
-    spread = jnp.broadcast_to(jnp.pad(bricks, (0, 128 - slots))[None, None], (workers, 8, 128))
-    owners = lax.all_to_all(spread, "tile", 0, 0, tiled=True)[:, 0, :slots].reshape(-1)
+    rings = [jnp.concatenate(parts, axis=0) for parts in ring_far(near, (0, 1))]
+    rings, view_data, psf, views, bricks = lax.optimization_barrier(
+        (rings, view_data, psf, views, bricks)
+    )
+    near = ring_near(rings, (1, 0))
 
     taps = jnp.stack([lax.dynamic_index_in_dim(psf, v, 0, keepdims=False) for v in views])
     mats = job_matrices(taps, bricks)
-    data = jnp.pad(view_data[0, 0], ((0, 0),) * 3 + ((0, PADW - WIN), (0, 0)))
+    data = view_data[0, 0]
     count = jnp.sum(intersection[0, 0]).reshape(1)
     tables = []
     for x_first in (True, False):
         wanted = window_table(jnp.concatenate([above, below]), me, x_first)
         mine = jnp.concatenate([window_table(bricks, me, x_first), views[None]])
         tables.append((wanted, mine))
-
-    rings = [jnp.concatenate(parts, axis=0) for parts in rings]
-    rings, mats, data, tables, owners, count = lax.optimization_barrier(
-        (rings, mats, data, tables, owners, count)
-    )
-    gathered = ring_gather(rings, (1, 0))
+    near, mats, data, tables, count = lax.optimization_barrier((near, mats, data, tables, count))
+    gathered = ring_far(near, (1, 0))
 
     rims = margins(gathered, [wanted for wanted, _ in tables])
     edges = [
@@ -404,15 +433,20 @@
         for c in range(2)
     ]
     edges = lax.optimization_barrier(edges)
-    totals = []
+    notes = jnp.concatenate([p[::SIDE, RIM, :slots] for p in gathered[0]], axis=0)
+    places = place_of(jnp.arange(workers), me, True)
+    match = places[:, None] == jnp.arange(workers)[None, :]
+    owners = jnp.sum(jnp.where(match[:, :, None], notes.astype(F32)[None], 0.0), axis=1)
+    owners = owners.astype(I32).reshape(-1)
+
+    parts = []
     for channel in range(2):
         factors = run_jobs(
             channel, gathered[channel], tables[channel][1], *edges[channel], data, background, mats
         )
-        parts = lax.all_to_all(factors, "tile", 0, 0, tiled=True)
-        summed = add_up(owners, parts)
-        totals.append(lax.all_to_all(summed, "tile", 0, 0, tiled=True))
-    return update(count, estimate, totals)
+        parts.append(lax.all_to_all(factors, "tile", 0, 0, tiled=True))
+    total = lax.all_to_all(add_up(owners, parts), "tile", 0, 0, tiled=True)
+    return update(count, estimate, total)
 
 
 def solution(mesh):

time: 317 us -> 212 us (0.67)
  Pallas kernels: 131 us -> 44.8 us
  waiting for transfers between devices: 75.6 us -> 57.7 us
  starting transfers between devices: 66.4 us -> 55 us
  other arithmetic: 14.2 us -> 23.3 us
    pallas_call x1, Pallas kernels: 88.4 us -> 3.61 us  [margins(): pl.pallas_call(margin_kernel, in_specs=[smem] * 2 + [hbm] * (2 * PARTS),...]
    ppermute x16, waiting for transfers between devices: 24.4 us -> 11.2 us  [torus_step(): return lax.ppermute(array, 'tile', pairs)]
    all_to_all x5 -> x3, starting transfers between devices: 22.1 us -> 13.1 us  [the longest x2 9.37 us: on_device(): parts.append(lax.all_to_all(factors, 'tile', 0, 0, tiled=True))]
    pad x2 -> x0, local copies, waits for them, and re-layouts: 7.39 us -> none  [the longest x1 7.38 us: on_device(): data = jnp.pad(view_data[0, 0], ((0, 0),) * 3 + ((0, PADW - WIN), (0, 0)))]
    optimization_barrier x0 -> x1, local copies, waits for them, and re-layouts: none -> 6.46 us  [on_device(): lax.optimization_barrier((rings, view_data, psf, views, bricks))]
    all_to_all x5 -> x3, waiting for transfers between devices: 40.2 us -> 35.4 us  [the longest x2 21.1 us: on_device(): parts.append(lax.all_to_all(factors, 'tile', 0, 0, tiled=True))]
    slice x10 -> x15, local copies, waits for them, and re-layouts: 1.12 us -> 4.74 us  [the longest x5 3.47 us: on_device(): p[::SIDE, RIM, :slots]]
    unnamed x66 -> x49, local copies, waits for them, and re-layouts: 10.4 us -> 7.04 us
  transfers between devices with their start and end apart: 27 -> 25, of which waited for: 12 -> 12; matrix products, arithmetic and copies ran while one was open for 10% -> 18% of each run, Pallas kernels for 7% -> 9%
where the time goes in v3:
time: 212 us; the launch traced here: 210 us
  waiting for transfers between devices  57.7 us (27%)
  starting transfers between devices  55 us (26%)
  Pallas kernels  44.8 us (21%)
  other arithmetic  23.3 us (11%)
  local copies, waits for them, and re-layouts  22.8 us (11%)
  between operations  6.58 us (3%)
    pallas_call x2, Pallas kernels, run_jobs(): pl.pallas_call(functools.partial(job_kernel, channel), grid=(slots,), in_...  38.3 us
    ppermute x16, starting transfers between devices, torus_step(): return lax.ppermute(array, 'tile', pairs)  26.5 us
    all_to_all x2, waiting for transfers between devices, on_device(): parts.append(lax.all_to_all(factors, 'tile', 0, 0, tiled=True))  21.1 us
    all_to_all x1, waiting for transfers between devices, on_device(): total = lax.all_to_all(add_up(owners, parts), 'tile', 0, 0, tiled=True)  14.3 us
    ppermute x16, waiting for transfers between devices, torus_step(): return lax.ppermute(array, 'tile', pairs)  11.2 us
    all_to_all x2, starting transfers between devices, on_device(): parts.append(lax.all_to_all(factors, 'tile', 0, 0, tiled=True))  9.37 us
    ppermute x2, waiting for transfers between devices, on_device(): lax.ppermute(rims[2 * c], 'view', upward)  7.35 us
    ppermute x2, starting transfers between devices, on_device(): lax.ppermute(rims[2 * c + 1], 'view', downward)  7.28 us
  transfers between devices with their start and end apart: 25, of which 12 were waited for; matrix products, arithmetic and copies ran while one was open for 18% of the time, Pallas kernels for 9%

profile of v3, /device:TPU:32, one launch (start us, length us, event | category | flops | bytes accessed | tf_op | source)
XLA Modules:
  0.0 210.2 jit_solution(6014448522254774803)
XLA Ops:
  15.2 2.4 %collective-permute-start.13 = (s32[3]{0:T(128)S(1)}, s32[3]{0:T(128)S(1)}, u32[]{:S(2)}, u32[]{:S(2)}) collective-permute-start(s32[3]{0:T(128)S(1)} %bitcast.73), channel_id=1, source_target_pairs={{0,1},{1,2},{2,3},{3,4},{4,5},{5,6},{6,7},{8,9},{9,10},{10,11},{11... | collective-permute-start | bytes 44 | tf_op jit(solution)/shard_map/ppermute | solution.py:411
  24.9 3.0 %collective-permute-start.5 = (bf16[14,32,128]{2,1,0:T(8,128)(2,1)S(1)}, bf16[14,32,128]{2,1,0:T(8,128)(2,1)S(1)}, u32[]{:S(2)}, u32[]{:S(2)}) collective-permute-start(bf16[14,32,128]{2,1,0:T(8,128)(2,1)S(1)} %slice.68), channel_id=1, source_target_pairs={{0,96},{8,104},{16,112},{24,120},{32,0},{40,8},{48,16},{56,24},{64... | collective-permute-start | bytes 344072 | tf_op jit(solution)/shard_map/ppermute | solution.py:30
  38.7 2.8 %collective-permute-start.11 = (bf16[112,32,128]{2,1,0:T(8,128)(2,1)}, bf16[112,32,128]{2,1,0:T(8,128)(2,1)}, u32[]{:S(2)}, u32[]{:S(2)}) collective-permute-start(bf16[112,32,128]{2,1,0:T(8,128)(2,1)} %constant_dynamic-update-slice_fusion.5.refs_7_.refs_0_), channel_id=1, source_target_pairs={{0,96},{8,104},{16,112},{24,120},{32,0},{40,8},{48,16},{56,24},{64... | collective-permute-start | bytes 2752520 | tf_op jit(solution)/shard_map/ppermute | solution.py:30
  41.8 2.9 %collective-permute-start.9 = (bf16[112,32,128]{2,1,0:T(8,128)(2,1)}, bf16[112,32,128]{2,1,0:T(8,128)(2,1)S(1)}, u32[]{:S(2)}, u32[]{:S(2)}) collective-permute-start(bf16[112,32,128]{2,1,0:T(8,128)(2,1)} %constant_dynamic-update-slice_fusion.refs_2_.refs_0_), channel_id=1, source_target_pairs={{0,24},{8,0},{16,8},{24,16},{32,56},{40,32},{48,40},{56,48},{64,88... | collective-permute-start | bytes 2752520 | tf_op jit(solution)/shard_map/ppermute | solution.py:30
  49.3 2.0 select_reduce_fusion.1
  52.4 6.5 %copy.67 = bf16[1,1,3,2,58,58,128]{6,5,4,3,2,1,0:T(8,128)(2,1)} copy(bf16[1,1,3,2,58,58,128]{6,3,5,4,2,1,0:T(2,128)(2,1)} %param.8) | data formatting | bytes 10334208 | tf_op jit(solution)/shard_map/optimization_barrier | solution.py:413
  70.5 3.3 %collective-permute-start.15 = (bf16[56,32,128]{2,1,0:T(8,128)(2,1)S(1)}, bf16[56,32,128]{2,1,0:T(8,128)(2,1)S(1)}, u32[]{:S(2)}, u32[]{:S(2)}) collective-permute-start(bf16[56,32,128]{2,1,0:T(8,128)(2,1)S(1)} %slice.79), channel_id=1, source_target_pairs={{0,24},{8,0},{16,8},{24,16},{32,56},{40,32},{48,40},{56,48},{64,88... | collective-permute-start | bytes 1376264 | tf_op jit(solution)/shard_map/ppermute | solution.py:30
  74.9 3.5 %collective-permute-start.17 = (bf16[56,32,128]{2,1,0:T(8,128)(2,1)S(1)}, bf16[56,32,128]{2,1,0:T(8,128)(2,1)S(1)}, u32[]{:S(2)}, u32[]{:S(2)}) collective-permute-start(bf16[56,32,128]{2,1,0:T(8,128)(2,1)S(1)} %slice.82), channel_id=1, source_target_pairs={{0,96},{8,104},{16,112},{24,120},{32,0},{40,8},{48,16},{56,24},{64... | collective-permute-start | bytes 1376264 | tf_op jit(solution)/shard_map/ppermute | solution.py:30
  78.4 4.6 %collective-permute-done.14.refs_5_.refs_3_ = bf16[56,32,128]{2,1,0:T(8,128)(2,1)S(1)} collective-permute-done((bf16[56,32,128]{2,1,0:T(8,128)(2,1)S(1)}, bf16[56,32,128]{2,1,0:T(8,128)(2,1)S(1)}, u32[]{:S(2)}, u32[]{:S(2)}) %collective-permute-start.14) | collective-permute-done | bytes 458784 | tf_op jit(solution)/shard_map/ppermute | solution.py:30
  83.0 2.9 %collective-permute-done.16.refs_10_.refs_3_ = bf16[56,32,128]{2,1,0:T(8,128)(2,1)S(1)} collective-permute-done((bf16[56,32,128]{2,1,0:T(8,128)(2,1)S(1)}, bf16[56,32,128]{2,1,0:T(8,128)(2,1)S(1)}, u32[]{:S(2)}, u32[]{:S(2)}) %collective-permute-start.16) | collective-permute-done | bytes 458784 | tf_op jit(solution)/shard_map/ppermute | solution.py:30
  87.5 3.6 %margins.1 = (bf16[3,58,16,128]{3,2,1,0:T(8,128)(2,1)}, bf16[3,58,16,128]{3,2,1,0:T(8,128)(2,1)}, bf16[3,58,16,128]{3,2,1,0:T(8,128)(2,1)}, bf16[3,58,16,128]{3,2,1,0:T(8,128)(2,1)}) custom-call(s32[3,6]{1,0:T(4,128)S(1)} %pad_add_fusion.2.refs_0_, s32[3,6]{1,0:T(4,128)S(1)} %pad_add_fusion.3.refs_1_, ...), custom_call_target="tpu_custom_call" | custom-call | tf_op jit(solution)/shard_map/margins/pallas_call | solution.py:128
  91.1 1.9 collective-permute-start.18
  93.1 3.6 %collective-permute-start.19 = (bf16[3,58,16,128]{3,2,1,0:T(8,128)(2,1)}, bf16[3,58,16,128]{3,2,1,0:T(8,128)(2,1)S(1)}, u32[]{:S(2)}, u32[]{:S(2)}) collective-permute-start(bf16[3,58,16,128]{3,2,1,0:T(8,128)(2,1)} %get-tuple-element.68), channel_id=1, source_target_pairs={{1,0},{2,1},{3,2},{4,3},{5,4},{6,5},{7,6},{9,8},{10,9},{11,10},{12... | collective-permute-start | bytes 2138120 | tf_op jit(solution)/shard_map/ppermute | solution.py:432
  98.6 3.6 %collective-permute-start.21 = (bf16[3,58,16,128]{3,2,1,0:T(8,128)(2,1)}, bf16[3,58,16,128]{3,2,1,0:T(8,128)(2,1)S(1)}, u32[]{:S(2)}, u32[]{:S(2)}) collective-permute-start(bf16[3,58,16,128]{3,2,1,0:T(8,128)(2,1)} %get-tuple-element.70), channel_id=1, source_target_pairs={{1,0},{2,1},{3,2},{4,3},{5,4},{6,5},{7,6},{9,8},{10,9},{11,10},{12... | collective-permute-start | bytes 2138120 | tf_op jit(solution)/shard_map/ppermute | solution.py:432
  105.7 5.8 %collective-permute-done.20.refs_5_ = bf16[3,58,16,128]{3,2,1,0:T(8,128)(2,1)S(1)} collective-permute-done((bf16[3,58,16,128]{3,2,1,0:T(8,128)(2,1)}, bf16[3,58,16,128]{3,2,1,0:T(8,128)(2,1)S(1)}, u32[]{:S(2)}, u32[]{:S(2)}) %collective-permute-start.20) | collective-permute-done | bytes 712736 | tf_op jit(solution)/shard_map/ppermute | solution.py:432
  114.2 19.1 %jobs.3 = f32[16,3,56,128]{3,2,1,0:T(8,128)} custom-call(s32[4,3]{1,0:T(4,128)S(1)} %get-tuple-element.80.table, f32[6]{0:T(128)S(1)} %copy-done, bf16[112,32,128]{2,1,0:T(8,128)(2,1)} %constant_dynamic-update-slice_fusion.5.refs_7_.refs_0_, bf16[112,32,128]{2,1,0:T(8,128)(2,1)} %copy-done.3, bf16[112,32,128]{2,1,0:T(8,128)(2,1)} %collective-permute-done.11.refs_9_.refs_2_, ...), custom_call_target="tpu_custom_call" | custom-call | flops 2362441728 | bytes 7077888 | tf_op jit(solution)/shard_map/jobs/pallas_call | solution.py:285
  133.4 4.9 %all-to-all-start.1 = ((f32[16,3,56,128]{3,2,1,0:T(8,128)}), f32[16,3,56,128]{3,2,1,0:T(8,128)S(1)}, u32[]{:S(2)}, u32[]{:S(2)}) async-start(f32[16,3,56,128]{3,2,1,0:T(8,128)} %jobs.3), calls=%async_computation.1 | async-start | bytes 2752512 | tf_op jit(solution)/shard_map/all_to_all | solution.py:447
  138.3 19.2 %jobs.2 = f32[16,3,56,128]{3,2,1,0:T(8,128)} custom-call(s32[4,3]{1,0:T(4,128)S(1)} %get-tuple-element.61.table, f32[6]{0:T(128)S(1)} %copy-done, bf16[112,32,128]{2,1,0:T(8,128)(2,1)} %constant_dynamic-update-slice_fusion.refs_2_.refs_0_, bf16[112,32,128]{2,1,0:T(8,128)(2,1)} %copy-done.1, bf16[112,32,128]{2,1,0:T(8,128)(2,1)} %copy-done.2, ...), custom_call_target="tpu_custom_call" | custom-call | flops 2362441728 | bytes 7077888 | tf_op jit(solution)/shard_map/jobs/pallas_call | solution.py:285
  157.5 3.4 %all-to-all-done.1.refs_1_ = f32[16,3,56,128]{3,2,1,0:T(8,128)S(1)} async-done(((f32[16,3,56,128]{3,2,1,0:T(8,128)}), f32[16,3,56,128]{3,2,1,0:T(8,128)S(1)}, u32[]{:S(2)}, u32[]{:S(2)}) %all-to-all-start.1) | async-done | bytes 1376288 | tf_op jit(solution)/shard_map/all_to_all | solution.py:447
  160.9 4.5 %all-to-all-start = ((f32[16,3,56,128]{3,2,1,0:T(8,128)}), f32[16,3,56,128]{3,2,1,0:T(8,128)S(1)}, u32[]{:S(2)}, u32[]{:S(2)}) async-start(f32[16,3,56,128]{3,2,1,0:T(8,128)} %jobs.2), calls=%async_computation | async-start | bytes 2752512 | tf_op jit(solution)/shard_map/all_to_all | solution.py:447
  169.9 17.6 %all-to-all-done.refs_0_ = f32[16,3,56,128]{3,2,1,0:T(8,128)S(1)} async-done(((f32[16,3,56,128]{3,2,1,0:T(8,128)}), f32[16,3,56,128]{3,2,1,0:T(8,128)S(1)}, u32[]{:S(2)}, u32[]{:S(2)}) %all-to-all-start) | async-done | bytes 1376288 | tf_op jit(solution)/shard_map/all_to_all | solution.py:447
  187.6 2.1 %add_up.1 = f32[16,2,56,128]{3,2,1,0:T(8,128)} custom-call(s32[48]{0:T(128)S(1)} %convert_element_type.75.owners, f32[16,3,56,128]{3,2,1,0:T(8,128)S(1)} %all-to-all-done.refs_0_, f32[16,3,56,128]{3,2,1,0:T(8,128)S(1)} %all-to-all-done.1.refs_1_), custom_call_target="tpu_custom_call" | custom-call | tf_op jit(solution)/shard_map/add_up/pallas_call | solution.py:365
  189.7 3.8 %all-to-all-start.2 = ((f32[16,2,56,128]{3,2,1,0:T(8,128)}), f32[16,2,56,128]{3,2,1,0:T(8,128)S(1)}, u32[]{:S(2)}, u32[]{:S(2)}) async-start(f32[16,2,56,128]{3,2,1,0:T(8,128)} %add_up.1), calls=%async_computation.2 | async-start | bytes 1835008 | tf_op jit(solution)/shard_map/all_to_all | solution.py:448
  193.6 14.3 %all-to-all-done.2.total = f32[16,2,56,128]{3,2,1,0:T(8,128)S(1)} async-done(((f32[16,2,56,128]{3,2,1,0:T(8,128)}), f32[16,2,56,128]{3,2,1,0:T(8,128)S(1)}, u32[]{:S(2)}, u32[]{:S(2)}) %all-to-all-start.2) | async-done | bytes 917536 | tf_op jit(solution)/shard_map/all_to_all | solution.py:448
  (164 shorter events, 62.3 us)
Async XLA Ops:
  1.9 10.0 %collective-permute-start = (bf16[28,32,128]{2,1,0:T(8,128)(2,1)S(1)}, bf16[28,32,128]{2,1,0:T(8,128)(2,1)S(1)}, u32[]{:S(2)}, u32[]{:S(2)}) collective-permute-start(bf16[28,32,128]{2,1,0:T(8,128)(2,1)S(1)} %get-tuple-element.44), channel_id=1, source_target_pairs={{0,32},{8,40},{16,48},{24,56},{32,64},{40,72},{48,80},{56,88},{64,... | collective-permute-start | bytes 688136 | tf_op jit(solution)/shard_map/ppermute | solution.py:30
  3.4 8.4 %collective-permute-start.1 = (bf16[28,32,128]{2,1,0:T(8,128)(2,1)S(1)}, bf16[28,32,128]{2,1,0:T(8,128)(2,1)S(1)}, u32[]{:S(2)}, u32[]{:S(2)}) collective-permute-start(bf16[28,32,128]{2,1,0:T(8,128)(2,1)S(1)} %get-tuple-element.44), channel_id=1, source_target_pairs={{0,96},{8,104},{16,112},{24,120},{32,0},{40,8},{48,16},{56,24},{64... | collective-permute-start | bytes 688136 | tf_op jit(solution)/shard_map/ppermute | solution.py:30
  5.2 8.1 %collective-permute-start.2 = (bf16[28,32,128]{2,1,0:T(8,128)(2,1)S(1)}, bf16[28,32,128]{2,1,0:T(8,128)(2,1)S(1)}, u32[]{:S(2)}, u32[]{:S(2)}) collective-permute-start(bf16[28,32,128]{2,1,0:T(8,128)(2,1)S(1)} %get-tuple-element.47), channel_id=1, source_target_pairs={{0,8},{8,16},{16,24},{24,0},{32,40},{40,48},{48,56},{56,32},{64,72... | collective-permute-start | bytes 688136 | tf_op jit(solution)/shard_map/ppermute | solution.py:30
  13.3 11.7 %collective-permute-start.12 = (s32[3]{0:T(128)S(1)}, s32[3]{0:T(128)S(1)}, u32[]{:S(2)}, u32[]{:S(2)}) collective-permute-start(s32[3]{0:T(128)S(1)} %bitcast.72), channel_id=1, source_target_pairs={{1,0},{2,1},{3,2},{4,3},{5,4},{6,5},{7,6},{9,8},{10,9},{11,10},{12... | collective-permute-start | bytes 44 | tf_op jit(solution)/shard_map/ppermute | solution.py:410
  15.2 12.7 %collective-permute-start.13 = (s32[3]{0:T(128)S(1)}, s32[3]{0:T(128)S(1)}, u32[]{:S(2)}, u32[]{:S(2)}) collective-permute-start(s32[3]{0:T(128)S(1)} %bitcast.73), channel_id=1, source_target_pairs={{0,1},{1,2},{2,3},{3,4},{4,5},{5,6},{6,7},{8,9},{9,10},{10,11},{11... | collective-permute-start | bytes 44 | tf_op jit(solution)/shard_map/ppermute | solution.py:411
  20.5 7.6 %collective-permute-start.6 = (bf16[14,32,128]{2,1,0:T(8,128)(2,1)S(1)}, bf16[14,32,128]{2,1,0:T(8,128)(2,1)S(1)}, u32[]{:S(2)}, u32[]{:S(2)}) collective-permute-start(bf16[14,32,128]{2,1,0:T(8,128)(2,1)S(1)} %slice.69), channel_id=1, source_target_pairs={{0,8},{8,16},{16,24},{24,0},{32,40},{40,48},{48,56},{56,32},{64,72... | collective-permute-start | bytes 344072 | tf_op jit(solution)/shard_map/ppermute | solution.py:30
  22.1 6.7 %collective-permute-start.7 = (bf16[14,32,128]{2,1,0:T(8,128)(2,1)S(1)}, bf16[14,32,128]{2,1,0:T(8,128)(2,1)S(1)}, u32[]{:S(2)}, u32[]{:S(2)}) collective-permute-start(bf16[14,32,128]{2,1,0:T(8,128)(2,1)S(1)} %slice.70), channel_id=1, source_target_pairs={{0,24},{8,0},{16,8},{24,16},{32,56},{40,32},{48,40},{56,48},{64,88... | collective-permute-start | bytes 344072 | tf_op jit(solution)/shard_map/ppermute | solution.py:30
  23.8 7.2 %collective-permute-start.4 = (bf16[14,32,128]{2,1,0:T(8,128)(2,1)S(1)}, bf16[14,32,128]{2,1,0:T(8,128)(2,1)S(1)}, u32[]{:S(2)}, u32[]{:S(2)}) collective-permute-start(bf16[14,32,128]{2,1,0:T(8,128)(2,1)S(1)} %slice.67), channel_id=1, source_target_pairs={{0,32},{8,40},{16,48},{24,56},{32,64},{40,72},{48,80},{56,88},{64,... | collective-permute-start | bytes 344072 | tf_op jit(solution)/shard_map/ppermute | solution.py:30
  24.9 6.8 %collective-permute-start.5 = (bf16[14,32,128]{2,1,0:T(8,128)(2,1)S(1)}, bf16[14,32,128]{2,1,0:T(8,128)(2,1)S(1)}, u32[]{:S(2)}, u32[]{:S(2)}) collective-permute-start(bf16[14,32,128]{2,1,0:T(8,128)(2,1)S(1)} %slice.68), channel_id=1, source_target_pairs={{0,96},{8,104},{16,112},{24,120},{32,0},{40,8},{48,16},{56,24},{64... | collective-permute-start | bytes 344072 | tf_op jit(solution)/shard_map/ppermute | solution.py:30
  38.2 32.0 %collective-permute-start.10 = (bf16[112,32,128]{2,1,0:T(8,128)(2,1)}, bf16[112,32,128]{2,1,0:T(8,128)(2,1)S(1)}, u32[]{:S(2)}, u32[]{:S(2)}) collective-permute-start(bf16[112,32,128]{2,1,0:T(8,128)(2,1)} %constant_dynamic-update-slice_fusion.5.refs_7_.refs_0_), channel_id=1, source_target_pairs={{0,32},{8,40},{16,48},{24,56},{32,64},{40,72},{48,80},{56,88},{64,... | collective-permute-start | bytes 2752520 | tf_op jit(solution)/shard_map/ppermute | solution.py:30
  38.7 31.6 %collective-permute-start.11 = (bf16[112,32,128]{2,1,0:T(8,128)(2,1)}, bf16[112,32,128]{2,1,0:T(8,128)(2,1)}, u32[]{:S(2)}, u32[]{:S(2)}) collective-permute-start(bf16[112,32,128]{2,1,0:T(8,128)(2,1)} %constant_dynamic-update-slice_fusion.5.refs_7_.refs_0_), channel_id=1, source_target_pairs={{0,96},{8,104},{16,112},{24,120},{32,0},{40,8},{48,16},{56,24},{64... | collective-permute-start | bytes 2752520 | tf_op jit(solution)/shard_map/ppermute | solution.py:30
  41.5 28.8 %collective-permute-start.8 = (bf16[112,32,128]{2,1,0:T(8,128)(2,1)}, bf16[112,32,128]{2,1,0:T(8,128)(2,1)S(1)}, u32[]{:S(2)}, u32[]{:S(2)}) collective-permute-start(bf16[112,32,128]{2,1,0:T(8,128)(2,1)} %constant_dynamic-update-slice_fusion.refs_2_.refs_0_), channel_id=1, source_target_pairs={{0,8},{8,16},{16,24},{24,0},{32,40},{40,48},{48,56},{56,32},{64,72... | collective-permute-start | bytes 2752520 | tf_op jit(solution)/shard_map/ppermute | solution.py:30
  41.8 28.5 %collective-permute-start.9 = (bf16[112,32,128]{2,1,0:T(8,128)(2,1)}, bf16[112,32,128]{2,1,0:T(8,128)(2,1)S(1)}, u32[]{:S(2)}, u32[]{:S(2)}) collective-permute-start(bf16[112,32,128]{2,1,0:T(8,128)(2,1)} %constant_dynamic-update-slice_fusion.refs_2_.refs_0_), channel_id=1, source_target_pairs={{0,24},{8,0},{16,8},{24,16},{32,56},{40,32},{48,40},{56,48},{64,88... | collective-permute-start | bytes 2752520 | tf_op jit(solution)/shard_map/ppermute | solution.py:30
  70.3 12.7 %collective-permute-start.14 = (bf16[56,32,128]{2,1,0:T(8,128)(2,1)S(1)}, bf16[56,32,128]{2,1,0:T(8,128)(2,1)S(1)}, u32[]{:S(2)}, u32[]{:S(2)}) collective-permute-start(bf16[56,32,128]{2,1,0:T(8,128)(2,1)S(1)} %slice.77), channel_id=1, source_target_pairs={{0,8},{8,16},{16,24},{24,0},{32,40},{40,48},{48,56},{56,32},{64,72... | collective-permute-start | bytes 1376264 | tf_op jit(solution)/shard_map/ppermute | solution.py:30
  70.5 12.6 %collective-permute-start.15 = (bf16[56,32,128]{2,1,0:T(8,128)(2,1)S(1)}, bf16[56,32,128]{2,1,0:T(8,128)(2,1)S(1)}, u32[]{:S(2)}, u32[]{:S(2)}) collective-permute-start(bf16[56,32,128]{2,1,0:T(8,128)(2,1)S(1)} %slice.79), channel_id=1, source_target_pairs={{0,24},{8,0},{16,8},{24,16},{32,56},{40,32},{48,40},{56,48},{64,88... | collective-permute-start | bytes 1376264 | tf_op jit(solution)/shard_map/ppermute | solution.py:30
  73.8 12.1 %collective-permute-start.16 = (bf16[56,32,128]{2,1,0:T(8,128)(2,1)S(1)}, bf16[56,32,128]{2,1,0:T(8,128)(2,1)S(1)}, u32[]{:S(2)}, u32[]{:S(2)}) collective-permute-start(bf16[56,32,128]{2,1,0:T(8,128)(2,1)S(1)} %slice.81), channel_id=1, source_target_pairs={{0,32},{8,40},{16,48},{24,56},{32,64},{40,72},{48,80},{56,88},{64,... | collective-permute-start | bytes 1376264 | tf_op jit(solution)/shard_map/ppermute | solution.py:30
  74.9 11.6 %collective-permute-start.17 = (bf16[56,32,128]{2,1,0:T(8,128)(2,1)S(1)}, bf16[56,32,128]{2,1,0:T(8,128)(2,1)S(1)}, u32[]{:S(2)}, u32[]{:S(2)}) collective-permute-start(bf16[56,32,128]{2,1,0:T(8,128)(2,1)S(1)} %slice.82), channel_id=1, source_target_pairs={{0,96},{8,104},{16,112},{24,120},{32,0},{40,8},{48,16},{56,24},{64... | collective-permute-start | bytes 1376264 | tf_op jit(solution)/shard_map/ppermute | solution.py:30
  91.1 12.7 %collective-permute-start.18 = (bf16[3,58,16,128]{3,2,1,0:T(8,128)(2,1)}, bf16[3,58,16,128]{3,2,1,0:T(8,128)(2,1)S(1)}, u32[]{:S(2)}, u32[]{:S(2)}) collective-permute-start(bf16[3,58,16,128]{3,2,1,0:T(8,128)(2,1)} %get-tuple-element.67), channel_id=1, source_target_pairs={{0,1},{1,2},{2,3},{3,4},{4,5},{5,6},{6,7},{8,9},{9,10},{10,11},{11... | collective-permute-start | bytes 2138120 | tf_op jit(solution)/shard_map/ppermute | solution.py:432
  93.1 12.7 %collective-permute-start.19 = (bf16[3,58,16,128]{3,2,1,0:T(8,128)(2,1)}, bf16[3,58,16,128]{3,2,1,0:T(8,128)(2,1)S(1)}, u32[]{:S(2)}, u32[]{:S(2)}) collective-permute-start(bf16[3,58,16,128]{3,2,1,0:T(8,128)(2,1)} %get-tuple-element.68), channel_id=1, source_target_pairs={{1,0},{2,1},{3,2},{4,3},{5,4},{6,5},{7,6},{9,8},{10,9},{11,10},{12... | collective-permute-start | bytes 2138120 | tf_op jit(solution)/shard_map/ppermute | solution.py:432
  96.7 14.8 %collective-permute-start.20 = (bf16[3,58,16,128]{3,2,1,0:T(8,128)(2,1)}, bf16[3,58,16,128]{3,2,1,0:T(8,128)(2,1)S(1)}, u32[]{:S(2)}, u32[]{:S(2)}) collective-permute-start(bf16[3,58,16,128]{3,2,1,0:T(8,128)(2,1)} %get-tuple-element.69), channel_id=1, source_target_pairs={{0,1},{1,2},{2,3},{3,4},{4,5},{5,6},{6,7},{8,9},{9,10},{10,11},{11... | collective-permute-start | bytes 2138120 | tf_op jit(solution)/shard_map/ppermute | solution.py:432
  98.6 14.7 %collective-permute-start.21 = (bf16[3,58,16,128]{3,2,1,0:T(8,128)(2,1)}, bf16[3,58,16,128]{3,2,1,0:T(8,128)(2,1)S(1)}, u32[]{:S(2)}, u32[]{:S(2)}) collective-permute-start(bf16[3,58,16,128]{3,2,1,0:T(8,128)(2,1)} %get-tuple-element.70), channel_id=1, source_target_pairs={{1,0},{2,1},{3,2},{4,3},{5,4},{6,5},{7,6},{9,8},{10,9},{11,10},{12... | collective-permute-start | bytes 2138120 | tf_op jit(solution)/shard_map/ppermute | solution.py:432
  133.4 27.6 %all-to-all-start.1 = ((f32[16,3,56,128]{3,2,1,0:T(8,128)}), f32[16,3,56,128]{3,2,1,0:T(8,128)S(1)}, u32[]{:S(2)}, u32[]{:S(2)}) async-start(f32[16,3,56,128]{3,2,1,0:T(8,128)} %jobs.3), calls=%async_computation.1 | async-start | bytes 2752512 | tf_op jit(solution)/shard_map/all_to_all | solution.py:447
  160.9 26.6 %all-to-all-start = ((f32[16,3,56,128]{3,2,1,0:T(8,128)}), f32[16,3,56,128]{3,2,1,0:T(8,128)S(1)}, u32[]{:S(2)}, u32[]{:S(2)}) async-start(f32[16,3,56,128]{3,2,1,0:T(8,128)} %jobs.2), calls=%async_computation | async-start | bytes 2752512 | tf_op jit(solution)/shard_map/all_to_all | solution.py:447
  189.7 18.3 %all-to-all-start.2 = ((f32[16,2,56,128]{3,2,1,0:T(8,128)}), f32[16,2,56,128]{3,2,1,0:T(8,128)S(1)}, u32[]{:S(2)}, u32[]{:S(2)}) async-start(f32[16,2,56,128]{3,2,1,0:T(8,128)} %add_up.1), calls=%async_computation.2 | async-start | bytes 1835008 | tf_op jit(solution)/shard_map/all_to_all | solution.py:448
  (20 other events, 249.1 us)

commit v4 on v3

--- a/solution.py
+++ b/solution.py
@@ -7,7 +7,7 @@
 from jax.experimental.pallas import tpu as pltpu
 from jax.sharding import PartitionSpec as P
 
-F32, BF16, I32 = jnp.float32, jnp.bfloat16, jnp.int32
+F32, BF16, I32, I16 = jnp.float32, jnp.bfloat16, jnp.int32, jnp.int16
 HALO = 15
 SIDE = 28
 WIN = SIDE + 2 * HALO
@@ -21,6 +21,10 @@
     return [pltpu.with_memory_space_constraint(a, pltpu.HBM) for a in arrays]
 
 
+def gathered_memory(parts):
+    return [parts[0]] + far_memory(*parts[1:])
+
+
 def torus_step(array, dx, dy):
     pairs = [
         (x * RING + y, ((x + dx) % RING) * RING + (y + dy) % RING)
@@ -50,20 +54,19 @@
     return result
 
 
+def rank(delta):
+    delta = lax.rem(delta + RING, RING)
+    return jnp.where(delta == 3, 1, jnp.where(delta == 1, 2, jnp.where(delta == 2, 3, 0)))
+
+
 def place_of(brick, me, x_first):
-    def rank(delta):
-        delta = delta % RING
-        return jnp.where(delta == 3, 1, jnp.where(delta == 1, 2, jnp.where(delta == 2, 3, 0)))
-
-    in_x = rank(brick // RING - me // RING)
-    in_y = rank(brick % RING - me % RING)
-    return (in_y * RING + in_x if x_first else in_x * RING + in_y).astype(I32)
-
-
-def window_table(bricks, me, x_first):
-    count = RING * RING
-    near = [jnp.maximum(bricks - 1, 0), bricks, jnp.minimum(bricks + 1, count - 1)]
-    return jnp.stack([place_of(b, me, x_first) for b in near])
+    in_x = rank(lax.div(brick, RING) - lax.div(me, RING))
+    in_y = rank(lax.rem(brick, RING) - lax.rem(me, RING))
+    return in_y * RING + in_x if x_first else in_x * RING + in_y
+
+
+def window_place(which, brick, me, x_first):
+    return place_of(jnp.clip(brick + which - 1, 0, RING * RING - 1), me, x_first)
 
 
 WINDOWS = ((SIDE - HALO, HALO, 0), (0, SIDE, HALO), (0, HALO, HALO + SIDE))
@@ -89,12 +92,13 @@
 
 
 def margin_kernel(*refs):
-    tables, refs = refs[:2], refs[2:]
+    me, *asked = refs[:3]
+    refs = refs[3:]
     refs, (stage, sems) = refs[:-2], refs[-2:]
     gathered, outs = (refs[:PARTS], refs[PARTS : 2 * PARTS]), refs[2 * PARTS :]
     slots = outs[0].shape[0]
     copies = []
-    for channel, (table, parts) in enumerate(zip(tables, gathered)):
+    for channel, parts in enumerate(gathered):
         for side in range(2):
             rows = pl.ds(RIM, RIM) if side == 0 else pl.ds(0, RIM)
             for slot in range(slots):
@@ -103,7 +107,8 @@
                 for which, (_, count, to) in enumerate(WINDOWS):
                     target = stage.at[channel, item, pl.ds(to, count)]
                     sem = sems.at[channel, item, which]
-                    copy_window(parts, which, table[which, item], rows, target, sem)
+                    place = window_place(which, asked[side][slot], me[0], channel == 0)
+                    copy_window(parts, which, place, rows, target, sem)
                     waits.append((parts, which, rows, target, sem))
                 out = pltpu.make_async_copy(
                     stage.at[channel, item],
@@ -122,12 +127,12 @@
 PARTS = 5
 
 
-def margins(gathered, tables):
-    slots = tables[0].shape[1] // 2
+def margins(gathered, me, above, below):
+    slots = above.shape[0]
     hbm, smem = pl.BlockSpec(memory_space=pltpu.HBM), pl.BlockSpec(memory_space=pltpu.SMEM)
     return pl.pallas_call(
         margin_kernel,
-        in_specs=[smem] * 2 + [hbm] * (2 * PARTS),
+        in_specs=[smem] * 3 + [hbm] * (2 * PARTS),
         out_specs=[hbm] * 4,
         out_shape=[pltpu.HBM((slots, WIN, RIM, 128), BF16)] * 4,
         scratch_shapes=[
@@ -136,7 +141,7 @@
         ],
         compiler_params=pltpu.CompilerParams(vmem_limit_bytes=4 << 20),
         name="margins",
-    )(*tables, *far_memory(*gathered[0], *gathered[1]))
+    )(me, above, below, *gathered_memory(gathered[0]), *gathered_memory(gathered[1]))
 
 
 def split(value):
@@ -154,11 +159,23 @@
     return dot(matrix, jnp.concatenate([high, low, high], axis=0))
 
 
+STEPS = 2048.0
+
+
+def encode(value, level):
+    code = (jnp.log2(jnp.maximum(value, 1e-37)) - level) * STEPS
+    return jnp.round(jnp.clip(code, -32767.0, 32767.0)).astype(I32)
+
+
+def decode(code, level):
+    return jnp.exp2(code.astype(I32).astype(F32) * (1.0 / STEPS) + level)
+
+
 def dot(a, b):
     return jnp.dot(a, b, preferred_element_type=F32)
 
 
-def job_kernel(channel, table, backdrops, *refs):
+def job_kernel(channel, me, bricks, views, backdrops, logs, *refs):
     parts, refs = refs[:PARTS], refs[PARTS:]
     top_ref, bottom_ref, data_ref, mz_ref, mx_ref, my_ref, myt_ref, mxt_ref, mzt_ref, out_ref = refs[:10]
     blocks, seen_data, z_high, z_low, blurred_x, back_y, back_x, sems = refs[10:]
@@ -176,7 +193,7 @@
     def fetch(which_slot, buffer):
         for which, (_, count, to) in enumerate(WINDOWS):
             target = blocks.at[buffer, pl.ds(to, count), mid]
-            place = table[which, which_slot]
+            place = window_place(which, bricks[which_slot], me[0], channel == 0)
             copy_window(parts, which, place, pl.ds(0, PADS), target, sems.at[buffer, which])
         for source, target, sem in others(which_slot, buffer):
             pltpu.make_async_copy(source, target, sem).start()
@@ -202,7 +219,8 @@
 
     mz, mx, my = mz_ref[0], mx_ref[0], my_ref[0]
     myt, mxt, mzt = myt_ref[0], mxt_ref[0], mzt_ref[0]
-    backdrop = backdrops[table[3, slot]]
+    backdrop = backdrops[views[slot]]
+    level = logs[views[slot]]
 
     def along_z(i, carry):
         start = i * CHUNK
@@ -258,11 +276,10 @@
     for i in range(SIDE // group):
         lines = [back_x[pl.ds(group * i + j, PADS, stride=PS), :] for j in range(group)]
         high, low = split(jnp.concatenate(lines, axis=0))
-        factor = dot(jnp.concatenate([high, low, high], axis=1), mzt)
-        for j in range(group):
-            x = group * i + j
-            first = (x % 2) * SIDE
-            out_ref[x // 2, 0, first : first + SIDE, :] = factor[j * PADS : j * PADS + SIDE]
+        factor = encode(dot(jnp.concatenate([high, low, high], axis=1), mzt), level)
+        for j in range(0, group, 2):
+            rows = [factor[k * PADS : k * PADS + SIDE] for k in (j, j + 1)]
+            out_ref[(group * i + j) // 2, 0] = jnp.concatenate(rows, axis=0).astype(I16)
     for k in range(SIDE // 2, 16):
         out_ref[k, 0] = jnp.zeros_like(out_ref[k, 0])
 
@@ -276,11 +293,11 @@
 UZ = 1
 
 
-def run_jobs(channel, parts, table, top, bottom, view_data, backdrops, mats):
-    slots = table.shape[1]
+def run_jobs(channel, parts, scalars, top, bottom, view_data, mats):
+    slots = mats[0].shape[0]
     hbm = pl.BlockSpec(memory_space=pltpu.HBM)
     smem = pl.BlockSpec(memory_space=pltpu.SMEM)
-    specs = [smem, smem] + [hbm] * (len(parts) + 3)
+    specs = [smem] * len(scalars) + [hbm] * (len(parts) + 3)
     specs += [pl.BlockSpec((1,) + m.shape[1:], lambda slot: (slot, 0, 0)) for m in mats]
     return pl.pallas_call(
         functools.partial(job_kernel, channel),
@@ -297,7 +314,7 @@
             pltpu.VMEM((PADS * PS, 128), F32),
             pltpu.SemaphoreType.DMA((2, 6)),
         ],
-        out_shape=pltpu.HBM((16, slots, 2 * SIDE, 128), F32),
+        out_shape=pltpu.HBM((16, slots, 2 * SIDE, 128), I16),
         compiler_params=pltpu.CompilerParams(vmem_limit_bytes=18 << 20),
         cost_estimate=pl.CostEstimate(
             flops=slots * 2 * 128 * (WIN * PADW * (256 + 192 + 192 + 96) + 2 * SIDE * PADS * 192),
@@ -305,7 +322,7 @@
             bytes_accessed=slots * (2 * WIN * PADW * 128 * 2 + 16 * 2 * SIDE * 128 * 4),
         ),
         name="jobs",
-    )(table, backdrops, *far_memory(*parts, top, bottom, view_data, *mats))
+    )(*scalars, *gathered_memory(parts), *far_memory(top, bottom, view_data, *mats))
 
 
 def bands(taps, positions_out, positions_in):
@@ -350,51 +367,68 @@
     )
 
 
-def add_kernel(owners, *refs):
-    out_ref = refs[-1]
-    out_ref[...] = jnp.zeros_like(out_ref)
+MORE = 2.6
+
+
+def add_kernel(owners, views, logs, *refs):
+    total, level = refs[-2:]
+    out_ref = refs[-3]
     workers, slots = refs[0].shape[:2]
-    for channel, parts_ref in enumerate(refs[:-1]):
-        for w in range(workers):
-            for s in range(slots):
-                out_ref[owners[w * slots + s], channel] += parts_ref[w, s]
-
-
-def add_up(owners, parts):
+    jobs = range(workers * slots)
+    for b in range(workers):
+        level[b] = -200.0
+    for i in jobs:
+        level[owners[i]] = jnp.maximum(level[owners[i]], logs[views[i]] + MORE)
+    for channel, parts_ref in enumerate(refs[:-3]):
+        total[...] = jnp.zeros_like(total)
+        for i in jobs:
+            total[owners[i]] += decode(parts_ref[i // slots, i % slots], logs[views[i]])
+        for b in range(workers):
+            out_ref[b, channel] = encode(total[b], level[b]).astype(I16)
+
+
+def add_up(owners, views, logs, parts):
     vmem, smem = pl.BlockSpec(memory_space=pltpu.VMEM), pl.BlockSpec(memory_space=pltpu.SMEM)
+    workers, rows = parts[0].shape[0], parts[0].shape[2:]
     return pl.pallas_call(
         add_kernel,
-        in_specs=[smem] + [vmem] * len(parts),
+        in_specs=[smem] * 3 + [vmem] * len(parts),
         out_specs=vmem,
-        out_shape=pltpu.HBM((16, len(parts)) + parts[0].shape[2:], F32),
+        out_shape=pltpu.HBM((workers, len(parts)) + rows, I16),
+        scratch_shapes=[pltpu.VMEM((workers,) + rows, F32), pltpu.SMEM((workers,), F32)],
         compiler_params=pltpu.CompilerParams(vmem_limit_bytes=8 << 20),
         name="add_up",
-    )(owners, *parts)
-
-
-def update_kernel(count, est_ref, total, out_ref):
-    seen = count[0].astype(F32)
+    )(owners, views, logs, *parts)
+
+
+def update_kernel(met, logs, est_ref, total, out_ref):
+    seen, level = jnp.int32(0), jnp.float32(-200.0)
+    for v in range(met.shape[0]):
+        seen += met[v]
+        level = jnp.where(met[v] > 0, jnp.maximum(level, logs[v] + MORE), level)
+    seen = seen.astype(F32)
     for c in range(out_ref.shape[0]):
         for k in range(SIDE // 2):
+            rows = decode(total[k, c], level)
             for j in range(2):
-                rows = total[k, c, j * SIDE : (j + 1) * SIDE, :]
-                out_ref[c, 2 * k + j] = est_ref[c, 2 * k + j] * rows / seen
-
-
-def update(count, estimate, total):
+                part = rows[j * SIDE : (j + 1) * SIDE]
+                out_ref[c, 2 * k + j] = est_ref[c, 2 * k + j] * part / seen
+
+
+def update(met, logs, estimate, total):
     vmem, smem = pl.BlockSpec(memory_space=pltpu.VMEM), pl.BlockSpec(memory_space=pltpu.SMEM)
     return pl.pallas_call(
         update_kernel,
-        in_specs=[smem, vmem, vmem],
+        in_specs=[smem, smem, vmem, vmem],
         out_specs=vmem,
         out_shape=jax.ShapeDtypeStruct(estimate.shape, F32),
         compiler_params=pltpu.CompilerParams(vmem_limit_bytes=12 << 20),
         name="update",
-    )(count, estimate, total)
+    )(met, logs, estimate, total)
 
 
 def on_device(estimate, view_data, psf, background, slot_brick, slot_view, intersection):
-    me = lax.axis_index("tile").astype(I32)
+    me = lax.axis_index("tile").astype(I32).reshape(1)
     groups, workers = lax.axis_size("view"), lax.axis_size("tile")
     upward = [(i, i + 1) for i in range(groups - 1)]
     downward = [(j, i) for i, j in upward]
@@ -402,51 +436,49 @@
     slots = bricks.shape[0]
 
     wire = estimate.astype(BF16).transpose(0, 2, 1, 3)
-    note = jnp.pad(bricks.astype(BF16)[None, None], ((0, 0), (0, SIDE - 1), (0, 128 - slots)))
+    jobs = jnp.concatenate([bricks, views])
+    note = jnp.pad(jobs.astype(BF16)[None, None], ((0, 0), (0, SIDE - 1), (0, 128 - 2 * slots)))
     note = jnp.broadcast_to(note, (wire.shape[0],) + note.shape[1:])
     wire = jnp.concatenate([wire[:, :, :RIM], note[:, :, None], wire[:, :, SIDE - RIM + 1 :]], axis=2)
     near = ring_near([wire[0], wire[1]], (0, 1))
-    near, bricks = lax.optimization_barrier((near, bricks))
-    above = lax.ppermute(bricks, "view", downward)
-    below = lax.ppermute(bricks, "view", upward)
     rings = [jnp.concatenate(parts, axis=0) for parts in ring_far(near, (0, 1))]
     rings, view_data, psf, views, bricks = lax.optimization_barrier(
         (rings, view_data, psf, views, bricks)
     )
     near = ring_near(rings, (1, 0))
-
-    taps = jnp.stack([lax.dynamic_index_in_dim(psf, v, 0, keepdims=False) for v in views])
+    above = lax.ppermute(bricks, "view", downward)
+    below = lax.ppermute(bricks, "view", upward)
+
+    chosen = views[:, None] == jnp.arange(psf.shape[0])[None, :]
+    taps = jnp.sum(jnp.where(chosen[:, :, None, None], psf[None], 0.0), axis=1)
     mats = job_matrices(taps, bricks)
     data = view_data[0, 0]
-    count = jnp.sum(intersection[0, 0]).reshape(1)
-    tables = []
-    for x_first in (True, False):
-        wanted = window_table(jnp.concatenate([above, below]), me, x_first)
-        mine = jnp.concatenate([window_table(bricks, me, x_first), views[None]])
-        tables.append((wanted, mine))
-    near, mats, data, tables, count = lax.optimization_barrier((near, mats, data, tables, count))
+    logs = jnp.log2(jnp.maximum(4.0 / background * jnp.prod(jnp.sum(psf, axis=2), axis=1), 1e-30)) - 15.9
+    near, mats, data, above, below, logs = lax.optimization_barrier(
+        (near, mats, data, above, below, logs)
+    )
     gathered = ring_far(near, (1, 0))
 
-    rims = margins(gathered, [wanted for wanted, _ in tables])
+    rims = margins(gathered, me, above, below)
     edges = [
         (lax.ppermute(rims[2 * c], "view", upward), lax.ppermute(rims[2 * c + 1], "view", downward))
         for c in range(2)
     ]
     edges = lax.optimization_barrier(edges)
-    notes = jnp.concatenate([p[::SIDE, RIM, :slots] for p in gathered[0]], axis=0)
-    places = place_of(jnp.arange(workers), me, True)
+    notes = jnp.concatenate([p[::SIDE, RIM, : 2 * slots] for p in gathered[0]], axis=0)
+    places = place_of(jnp.arange(workers, dtype=I32), me[0], True)
     match = places[:, None] == jnp.arange(workers)[None, :]
-    owners = jnp.sum(jnp.where(match[:, :, None], notes.astype(F32)[None], 0.0), axis=1)
-    owners = owners.astype(I32).reshape(-1)
+    notes = jnp.sum(jnp.where(match[:, :, None], notes.astype(F32)[None], 0.0), axis=1)
+    notes = notes.astype(I32)
+    owners, seen_by = notes[:, :slots].reshape(-1), notes[:, slots:].reshape(-1)
 
     parts = []
+    scalars = (me, bricks, views, background, logs)
     for channel in range(2):
-        factors = run_jobs(
-            channel, gathered[channel], tables[channel][1], *edges[channel], data, background, mats
-        )
+        factors = run_jobs(channel, gathered[channel], scalars, *edges[channel], data, mats)
         parts.append(lax.all_to_all(factors, "tile", 0, 0, tiled=True))
-    total = lax.all_to_all(add_up(owners, parts), "tile", 0, 0, tiled=True)
-    return update(count, estimate, total)
+    total = lax.all_to_all(add_up(owners, seen_by, logs, parts), "tile", 0, 0, tiled=True)
+    return update(intersection[0, 0], logs, estimate, total)
 
 
 def solution(mesh):

time: 212 us -> 186 us (0.88)
  other arithmetic: 23.3 us -> 10.9 us
  waiting for transfers between devices: 57.7 us -> 50.2 us
  between operations: 6.58 us -> 0.56 us
  starting transfers between devices: 55 us -> 58.3 us
  local copies, waits for them, and re-layouts: 22.8 us -> 19.7 us
    all_to_all x2, waiting for transfers between devices: 21.1 us -> 10.8 us  [on_device(): parts.append(lax.all_to_all(factors, 'tile', 0, 0, tiled=True))]
    unnamed x49 -> x34, local copies, waits for them, and re-layouts: 7.04 us -> 1.23 us
    all_to_all x2, starting transfers between devices: 9.37 us -> 13.4 us  [on_device(): parts.append(lax.all_to_all(factors, 'tile', 0, 0, tiled=True))]
    all_to_all x1, waiting for transfers between devices: 14.3 us -> 11 us  [on_device(): lax.all_to_all(add_up(owners, seen_by, logs, parts), 'tile', 0, 0, tiled=...]
    ppermute x16, waiting for transfers between devices: 11.2 us -> 14.3 us  [torus_step(): return lax.ppermute(array, 'tile', pairs)]
    ppermute x1, waiting for transfers between devices: 0.01 us -> 2.93 us  [on_device(): below = lax.ppermute(bricks, 'view', upward)]
    convert_element_type x6, other arithmetic: 2.87 us -> 0.14 us  [high_low(): return (high.astype(BF16), (matrix - high).astype(BF16))]
    slice x4, local copies, waits for them, and re-layouts: 0.08 us -> 2.72 us  [ring_far(): lower[:half]]
  transfers between devices with their start and end apart: 25 -> 25, of which waited for: 12 -> 15; matrix products, arithmetic and copies ran while one was open for 18% -> 13% of each run, Pallas kernels for 9% -> 10%
where the time goes in v4:
time: 186 us; the launch traced here: 185 us
  starting transfers between devices  58.3 us (31%)
  waiting for transfers between devices  50.2 us (27%)
  Pallas kernels  45.5 us (24%)
  local copies, waits for them, and re-layouts  19.7 us (11%)
  other arithmetic  10.9 us (6%)
    pallas_call x2, Pallas kernels, run_jobs(): pl.pallas_call(functools.partial(job_kernel, channel), grid=(slots,), in_...  38.5 us
    ppermute x16, starting transfers between devices, torus_step(): return lax.ppermute(array, 'tile', pairs)  26.3 us
    ppermute x16, waiting for transfers between devices, torus_step(): return lax.ppermute(array, 'tile', pairs)  14.3 us
    all_to_all x2, starting transfers between devices, on_device(): parts.append(lax.all_to_all(factors, 'tile', 0, 0, tiled=True))  13.4 us
    all_to_all x1, waiting for transfers between devices, on_device(): lax.all_to_all(add_up(owners, seen_by, logs, parts), 'tile', 0, 0, tiled=...  11 us
    all_to_all x2, waiting for transfers between devices, on_device(): parts.append(lax.all_to_all(factors, 'tile', 0, 0, tiled=True))  10.8 us
    ppermute x2, waiting for transfers between devices, on_device(): lax.ppermute(rims[2 * c], 'view', upward)  7.35 us
    ppermute x2, starting transfers between devices, on_device(): lax.ppermute(rims[2 * c + 1], 'view', downward)  7 us
  transfers between devices with their start and end apart: 25, of which 15 were waited for; matrix products, arithmetic and copies ran while one was open for 13% of the time, Pallas kernels for 10%

profile of v4, /device:TPU:32, one launch (start us, length us, event | category | flops | bytes accessed | tf_op | source)
XLA Modules:
  0.0 185.1 jit_solution(9060311483779913429)
XLA Ops:
  12.3 3.0 %collective-permute-start.7 = (bf16[14,32,128]{2,1,0:T(8,128)(2,1)S(1)}, bf16[14,32,128]{2,1,0:T(8,128)(2,1)S(1)}, u32[]{:S(2)}, u32[]{:S(2)}) collective-permute-start(bf16[14,32,128]{2,1,0:T(8,128)(2,1)S(1)} %slice.98), channel_id=1, source_target_pairs={{0,24},{8,0},{16,8},{24,16},{32,56},{40,32},{48,40},{56,48},{64,88... | collective-permute-start | bytes 344072 | tf_op jit(solution)/shard_map/ppermute | solution.py:34
  19.0 2.5 %collective-permute-done.2 = bf16[14,32,128]{2,1,0:T(8,128)(2,1)S(1)} collective-permute-done((bf16[14,32,128]{2,1,0:T(8,128)(2,1)S(1)}, bf16[14,32,128]{2,1,0:T(8,128)(2,1)S(1)}, u32[]{:S(2)}, u32[]{:S(2)}) %collective-permute-start.2) | collective-permute-done | bytes 114720 | tf_op jit(solution)/shard_map/ppermute | solution.py:34
  21.8 1.9 %collective-permute-start.12 = (s32[3]{0:T(128)S(1)}, s32[3]{0:T(128)S(1)}, u32[]{:S(2)}, u32[]{:S(2)}) collective-permute-start(s32[3]{0:T(128)S(1)} %bitcast.45), channel_id=1, source_target_pairs={{1,0},{2,1},{3,2},{4,3},{5,4},{6,5},{7,6},{9,8},{10,9},{11,10},{12... | collective-permute-start | bytes 44 | tf_op jit(solution)/shard_map/ppermute | solution.py:449
  27.1 3.2 %collective-permute-start.9 = (bf16[112,32,128]{2,1,0:T(8,128)(2,1)S(1)}, bf16[112,32,128]{2,1,0:T(8,128)(2,1)}, u32[]{:S(2)}, u32[]{:S(2)}) collective-permute-start(bf16[112,32,128]{2,1,0:T(8,128)(2,1)S(1)} %constant_dynamic-update-slice_fusion.refs_3_.refs_0_), channel_id=1, source_target_pairs={{0,24},{8,0},{16,8},{24,16},{32,56},{40,32},{48,40},{56,48},{64,88... | collective-permute-start | bytes 2752520 | tf_op jit(solution)/shard_map/ppermute | solution.py:34
  32.8 6.5 %copy.67 = bf16[1,1,3,2,58,58,128]{6,5,4,3,2,1,0:T(8,128)(2,1)} copy(bf16[1,1,3,2,58,58,128]{6,3,5,4,2,1,0:T(2,128)(2,1)} %param.8) | data formatting | bytes 10334208 | tf_op jit(solution)/shard_map/optimization_barrier | solution.py:445
  44.0 1.9 %collective-permute-start.13 = (s32[3]{0:T(128)S(1)}, s32[3]{0:T(128)S(1)}, u32[]{:S(2)}, u32[]{:S(2)}) collective-permute-start(s32[3]{0:T(128)S(1)} %bitcast.46), channel_id=1, source_target_pairs={{0,1},{1,2},{2,3},{3,4},{4,5},{5,6},{6,7},{8,9},{9,10},{10,11},{11... | collective-permute-start | bytes 44 | tf_op jit(solution)/shard_map/ppermute | solution.py:450
  45.9 2.9 %collective-permute-done.13.refs_2_ = s32[3]{0:T(128)S(1)} collective-permute-done((s32[3]{0:T(128)S(1)}, s32[3]{0:T(128)S(1)}, u32[]{:S(2)}, u32[]{:S(2)}) %collective-permute-start.13) | collective-permute-done | bytes 44 | tf_op jit(solution)/shard_map/ppermute | solution.py:450
  53.2 3.2 %collective-permute-start.15 = (bf16[56,32,128]{2,1,0:T(8,128)(2,1)}, bf16[56,32,128]{2,1,0:T(8,128)(2,1)}, u32[]{:S(2)}, u32[]{:S(2)}) collective-permute-start(bf16[56,32,128]{2,1,0:T(8,128)(2,1)} %slice.85), channel_id=1, source_target_pairs={{0,24},{8,0},{16,8},{24,16},{32,56},{40,32},{48,40},{56,48},{64,88... | collective-permute-start | bytes 1376264 | tf_op jit(solution)/shard_map/ppermute | solution.py:34
  60.3 3.0 %collective-permute-start.17 = (bf16[56,32,128]{2,1,0:T(8,128)(2,1)}, bf16[56,32,128]{2,1,0:T(8,128)(2,1)}, u32[]{:S(2)}, u32[]{:S(2)}) collective-permute-start(bf16[56,32,128]{2,1,0:T(8,128)(2,1)} %slice.90), channel_id=1, source_target_pairs={{0,96},{8,104},{16,112},{24,120},{32,0},{40,8},{48,16},{56,24},{64... | collective-permute-start | bytes 1376264 | tf_op jit(solution)/shard_map/ppermute | solution.py:34
  65.6 5.3 %collective-permute-done.16.refs_11_.refs_3_ = bf16[56,32,128]{2,1,0:T(8,128)(2,1)} collective-permute-done((bf16[56,32,128]{2,1,0:T(8,128)(2,1)}, bf16[56,32,128]{2,1,0:T(8,128)(2,1)}, u32[]{:S(2)}, u32[]{:S(2)}) %collective-permute-start.16) | collective-permute-done | bytes 458784 | tf_op jit(solution)/shard_map/ppermute | solution.py:34
  72.0 4.0 %margins.1 = (bf16[3,58,16,128]{3,2,1,0:T(8,128)(2,1)}, bf16[3,58,16,128]{3,2,1,0:T(8,128)(2,1)}, bf16[3,58,16,128]{3,2,1,0:T(8,128)(2,1)}, bf16[3,58,16,128]{3,2,1,0:T(8,128)(2,1)}) custom-call(s32[1]{0:T(128)} %bitcast.16.refs_0_.me, s32[3]{0:T(128)S(1)} %collective-permute-done.12.refs_1_, s32[3]{0:T(128)S(1)} %collective-permute-done.13.refs_2_, ...), custom_call_target="tpu_custom_call" | custom-call | tf_op jit(solution)/shard_map/margins/pallas_call | solution.py:133
  76.0 1.9 %collective-permute-start.18 = (bf16[3,58,16,128]{3,2,1,0:T(8,128)(2,1)}, bf16[3,58,16,128]{3,2,1,0:T(8,128)(2,1)S(1)}, u32[]{:S(2)}, u32[]{:S(2)}) collective-permute-start(bf16[3,58,16,128]{3,2,1,0:T(8,128)(2,1)} %get-tuple-element.50), channel_id=1, source_target_pairs={{0,1},{1,2},{2,3},{3,4},{4,5},{5,6},{6,7},{8,9},{9,10},{10,11},{11... | collective-permute-start | bytes 2138120 | tf_op jit(solution)/shard_map/ppermute | solution.py:464
  77.9 3.6 %collective-permute-start.19 = (bf16[3,58,16,128]{3,2,1,0:T(8,128)(2,1)}, bf16[3,58,16,128]{3,2,1,0:T(8,128)(2,1)S(1)}, u32[]{:S(2)}, u32[]{:S(2)}) collective-permute-start(bf16[3,58,16,128]{3,2,1,0:T(8,128)(2,1)} %get-tuple-element.51), channel_id=1, source_target_pairs={{1,0},{2,1},{3,2},{4,3},{5,4},{6,5},{7,6},{9,8},{10,9},{11,10},{12... | collective-permute-start | bytes 2138120 | tf_op jit(solution)/shard_map/ppermute | solution.py:464
  81.5 2.2 %collective-permute-start.20 = (bf16[3,58,16,128]{3,2,1,0:T(8,128)(2,1)}, bf16[3,58,16,128]{3,2,1,0:T(8,128)(2,1)S(1)}, u32[]{:S(2)}, u32[]{:S(2)}) collective-permute-start(bf16[3,58,16,128]{3,2,1,0:T(8,128)(2,1)} %get-tuple-element.52), channel_id=1, source_target_pairs={{0,1},{1,2},{2,3},{3,4},{4,5},{5,6},{6,7},{8,9},{9,10},{10,11},{11... | collective-permute-start | bytes 2138120 | tf_op jit(solution)/shard_map/ppermute | solution.py:464
  83.7 3.4 %collective-permute-start.21 = (bf16[3,58,16,128]{3,2,1,0:T(8,128)(2,1)}, bf16[3,58,16,128]{3,2,1,0:T(8,128)(2,1)S(1)}, u32[]{:S(2)}, u32[]{:S(2)}) collective-permute-start(bf16[3,58,16,128]{3,2,1,0:T(8,128)(2,1)} %get-tuple-element.53), channel_id=1, source_target_pairs={{1,0},{2,1},{3,2},{4,3},{5,4},{6,5},{7,6},{9,8},{10,9},{11,10},{12... | collective-permute-start | bytes 2138120 | tf_op jit(solution)/shard_map/ppermute | solution.py:464
  90.6 5.8 %collective-permute-done.20.refs_5_ = bf16[3,58,16,128]{3,2,1,0:T(8,128)(2,1)S(1)} collective-permute-done((bf16[3,58,16,128]{3,2,1,0:T(8,128)(2,1)}, bf16[3,58,16,128]{3,2,1,0:T(8,128)(2,1)S(1)}, u32[]{:S(2)}, u32[]{:S(2)}) %collective-permute-start.20) | collective-permute-done | bytes 712736 | tf_op jit(solution)/shard_map/ppermute | solution.py:464
  99.0 19.2 %jobs.3 = s16[16,3,56,128]{3,2,1,0:T(8,128)(2,1)} custom-call(s32[1]{0:T(128)} %bitcast.16.refs_0_.me, s32[3]{0:T(128)S(1)} %bitcast.47, s32[3]{0:T(128)S(1)} %bitcast.42, f32[6]{0:T(128)S(1)} %copy-done, f32[6]{0:T(128)S(1)} %multiply_add_fusion.logs, bf16[112,32,128]{2,1,0:T(8,128)(2,1)S(1)} %constant_dynamic-update-slice_fusion.5.refs_8_.refs_0_, ...), custom_call_target="tpu_custom_call" | custom-call | flops 2362441728 | bytes 7077888 | tf_op jit(solution)/shard_map/jobs/pallas_call | solution.py:302
  118.3 6.1 %all-to-all-start.1 = ((s16[16,3,56,128]{3,2,1,0:T(8,128)(2,1)}), s16[16,3,56,128]{3,2,1,0:T(8,128)(2,1)S(1)}, u32[]{:S(2)}, u32[]{:S(2)}) async-start(s16[16,3,56,128]{3,2,1,0:T(8,128)(2,1)} %jobs.3), calls=%async_computation.1 | async-start | bytes 1376256 | tf_op jit(solution)/shard_map/all_to_all | solution.py:479
  124.4 19.3 %jobs.2 = s16[16,3,56,128]{3,2,1,0:T(8,128)(2,1)} custom-call(s32[1]{0:T(128)} %bitcast.16.refs_0_.me, s32[3]{0:T(128)S(1)} %bitcast.48, s32[3]{0:T(128)S(1)} %bitcast.43, f32[6]{0:T(128)S(1)} %copy-done, f32[6]{0:T(128)S(1)} %multiply_add_fusion.logs, bf16[112,32,128]{2,1,0:T(8,128)(2,1)S(1)} %constant_dynamic-update-slice_fusion.refs_3_.refs_0_, ...), custom_call_target="tpu_custom_call" | custom-call | flops 2362441728 | bytes 7077888 | tf_op jit(solution)/shard_map/jobs/pallas_call | solution.py:302
  143.7 7.3 %all-to-all-start = ((s16[16,3,56,128]{3,2,1,0:T(8,128)(2,1)}), s16[16,3,56,128]{3,2,1,0:T(8,128)(2,1)S(1)}, u32[]{:S(2)}, u32[]{:S(2)}) async-start(s16[16,3,56,128]{3,2,1,0:T(8,128)(2,1)} %jobs.2), calls=%async_computation | async-start | bytes 1376256 | tf_op jit(solution)/shard_map/all_to_all | solution.py:479
  155.0 10.8 %all-to-all-done.refs_0_ = s16[16,3,56,128]{3,2,1,0:T(8,128)(2,1)S(1)} async-done(((s16[16,3,56,128]{3,2,1,0:T(8,128)(2,1)}), s16[16,3,56,128]{3,2,1,0:T(8,128)(2,1)S(1)}, u32[]{:S(2)}, u32[]{:S(2)}) %all-to-all-start) | async-done | bytes 688160 | tf_op jit(solution)/shard_map/all_to_all | solution.py:479
  165.8 2.3 %add_up.1 = s16[16,2,56,128]{3,2,1,0:T(8,128)(2,1)} custom-call(s32[48]{0:T(128)S(1)} %reshape.391.owners, s32[48]{0:T(128)S(1)} %reshape.392.views, f32[6]{0:T(128)S(1)} %multiply_add_fusion.logs, s16[16,3,56,128]{3,2,1,0:T(8,128)(2,1)S(1)} %all-to-all-done.refs_0_, s16[16,3,56,128]{3,2,1,0:T(8,128)(2,1)S(1)} %all-to-all-done.1.refs_1_), custom_call_target="tpu_custom_call" | custom-call | tf_op jit(solution)/shard_map/add_up/pallas_call | solution.py:393
  168.1 3.6 %all-to-all-start.2 = ((s16[16,2,56,128]{3,2,1,0:T(8,128)(2,1)}), s16[16,2,56,128]{3,2,1,0:T(8,128)(2,1)S(1)}, u32[]{:S(2)}, u32[]{:S(2)}) async-start(s16[16,2,56,128]{3,2,1,0:T(8,128)(2,1)} %add_up.1), calls=%async_computation.2 | async-start | bytes 917504 | tf_op jit(solution)/shard_map/all_to_all | solution.py:480
  171.8 11.0 %all-to-all-done.2.total = s16[16,2,56,128]{3,2,1,0:T(8,128)(2,1)S(1)} async-done(((s16[16,2,56,128]{3,2,1,0:T(8,128)(2,1)}), s16[16,2,56,128]{3,2,1,0:T(8,128)(2,1)S(1)}, u32[]{:S(2)}, u32[]{:S(2)}) %all-to-all-start.2) | async-done | bytes 458784 | tf_op jit(solution)/shard_map/all_to_all | solution.py:480
  (145 shorter events, 50.6 us)
Async XLA Ops:
  3.2 8.7 %collective-permute-start.4 = (bf16[28,32,128]{2,1,0:T(8,128)(2,1)S(1)}, bf16[28,32,128]{2,1,0:T(8,128)(2,1)S(1)}, u32[]{:S(2)}, u32[]{:S(2)}) collective-permute-start(bf16[28,32,128]{2,1,0:T(8,128)(2,1)S(1)} %get-tuple-element.67), channel_id=1, source_target_pairs={{0,8},{8,16},{16,24},{24,0},{32,40},{40,48},{48,56},{56,32},{64,72... | collective-permute-start | bytes 688136 | tf_op jit(solution)/shard_map/ppermute | solution.py:34
  4.9 7.4 %collective-permute-start.5 = (bf16[28,32,128]{2,1,0:T(8,128)(2,1)S(1)}, bf16[28,32,128]{2,1,0:T(8,128)(2,1)S(1)}, u32[]{:S(2)}, u32[]{:S(2)}) collective-permute-start(bf16[28,32,128]{2,1,0:T(8,128)(2,1)S(1)} %get-tuple-element.67), channel_id=1, source_target_pairs={{0,24},{8,0},{16,8},{24,16},{32,56},{40,32},{48,40},{56,48},{64,88... | collective-permute-start | bytes 688136 | tf_op jit(solution)/shard_map/ppermute | solution.py:34
  6.5 8.8 %collective-permute-start = (bf16[28,32,128]{2,1,0:T(8,128)(2,1)S(1)}, bf16[28,32,128]{2,1,0:T(8,128)(2,1)S(1)}, u32[]{:S(2)}, u32[]{:S(2)}) collective-permute-start(bf16[28,32,128]{2,1,0:T(8,128)(2,1)S(1)} %get-tuple-element.68), channel_id=1, source_target_pairs={{0,32},{8,40},{16,48},{24,56},{32,64},{40,72},{48,80},{56,88},{64,... | collective-permute-start | bytes 688136 | tf_op jit(solution)/shard_map/ppermute | solution.py:34
  8.0 8.9 %collective-permute-start.1 = (bf16[28,32,128]{2,1,0:T(8,128)(2,1)S(1)}, bf16[28,32,128]{2,1,0:T(8,128)(2,1)S(1)}, u32[]{:S(2)}, u32[]{:S(2)}) collective-permute-start(bf16[28,32,128]{2,1,0:T(8,128)(2,1)S(1)} %get-tuple-element.68), channel_id=1, source_target_pairs={{0,96},{8,104},{16,112},{24,120},{32,0},{40,8},{48,16},{56,24},{64... | collective-permute-start | bytes 688136 | tf_op jit(solution)/shard_map/ppermute | solution.py:34
  11.9 7.0 %collective-permute-start.6 = (bf16[14,32,128]{2,1,0:T(8,128)(2,1)S(1)}, bf16[14,32,128]{2,1,0:T(8,128)(2,1)S(1)}, u32[]{:S(2)}, u32[]{:S(2)}) collective-permute-start(bf16[14,32,128]{2,1,0:T(8,128)(2,1)S(1)} %slice.97), channel_id=1, source_target_pairs={{0,8},{8,16},{16,24},{24,0},{32,40},{40,48},{48,56},{56,32},{64,72... | collective-permute-start | bytes 344072 | tf_op jit(solution)/shard_map/ppermute | solution.py:34
  12.3 6.6 %collective-permute-start.7 = (bf16[14,32,128]{2,1,0:T(8,128)(2,1)S(1)}, bf16[14,32,128]{2,1,0:T(8,128)(2,1)S(1)}, u32[]{:S(2)}, u32[]{:S(2)}) collective-permute-start(bf16[14,32,128]{2,1,0:T(8,128)(2,1)S(1)} %slice.98), channel_id=1, source_target_pairs={{0,24},{8,0},{16,8},{24,16},{32,56},{40,32},{48,40},{56,48},{64,88... | collective-permute-start | bytes 344072 | tf_op jit(solution)/shard_map/ppermute | solution.py:34
  15.3 6.1 %collective-permute-start.2 = (bf16[14,32,128]{2,1,0:T(8,128)(2,1)S(1)}, bf16[14,32,128]{2,1,0:T(8,128)(2,1)S(1)}, u32[]{:S(2)}, u32[]{:S(2)}) collective-permute-start(bf16[14,32,128]{2,1,0:T(8,128)(2,1)S(1)} %slice.94), channel_id=1, source_target_pairs={{0,32},{8,40},{16,48},{24,56},{32,64},{40,72},{48,80},{56,88},{64,... | collective-permute-start | bytes 344072 | tf_op jit(solution)/shard_map/ppermute | solution.py:34
  16.9 4.9 %collective-permute-start.3 = (bf16[14,32,128]{2,1,0:T(8,128)(2,1)S(1)}, bf16[14,32,128]{2,1,0:T(8,128)(2,1)S(1)}, u32[]{:S(2)}, u32[]{:S(2)}) collective-permute-start(bf16[14,32,128]{2,1,0:T(8,128)(2,1)S(1)} %slice.95), channel_id=1, source_target_pairs={{0,96},{8,104},{16,112},{24,120},{32,0},{40,8},{48,16},{56,24},{64... | collective-permute-start | bytes 344072 | tf_op jit(solution)/shard_map/ppermute | solution.py:34
  21.8 22.1 %collective-permute-start.12 = (s32[3]{0:T(128)S(1)}, s32[3]{0:T(128)S(1)}, u32[]{:S(2)}, u32[]{:S(2)}) collective-permute-start(s32[3]{0:T(128)S(1)} %bitcast.45), channel_id=1, source_target_pairs={{1,0},{2,1},{3,2},{4,3},{5,4},{6,5},{7,6},{9,8},{10,9},{11,10},{12... | collective-permute-start | bytes 44 | tf_op jit(solution)/shard_map/ppermute | solution.py:449
  23.7 25.1 %collective-permute-start.10 = (bf16[112,32,128]{2,1,0:T(8,128)(2,1)S(1)}, bf16[112,32,128]{2,1,0:T(8,128)(2,1)}, u32[]{:S(2)}, u32[]{:S(2)}) collective-permute-start(bf16[112,32,128]{2,1,0:T(8,128)(2,1)S(1)} %constant_dynamic-update-slice_fusion.5.refs_8_.refs_0_), channel_id=1, source_target_pairs={{0,32},{8,40},{16,48},{24,56},{32,64},{40,72},{48,80},{56,88},{64,... | collective-permute-start | bytes 2752520 | tf_op jit(solution)/shard_map/ppermute | solution.py:34
  25.3 23.5 %collective-permute-start.11 = (bf16[112,32,128]{2,1,0:T(8,128)(2,1)S(1)}, bf16[112,32,128]{2,1,0:T(8,128)(2,1)}, u32[]{:S(2)}, u32[]{:S(2)}) collective-permute-start(bf16[112,32,128]{2,1,0:T(8,128)(2,1)S(1)} %constant_dynamic-update-slice_fusion.5.refs_8_.refs_0_), channel_id=1, source_target_pairs={{0,96},{8,104},{16,112},{24,120},{32,0},{40,8},{48,16},{56,24},{64... | collective-permute-start | bytes 2752520 | tf_op jit(solution)/shard_map/ppermute | solution.py:34
  27.1 23.5 %collective-permute-start.8 = (bf16[112,32,128]{2,1,0:T(8,128)(2,1)S(1)}, bf16[112,32,128]{2,1,0:T(8,128)(2,1)S(1)}, u32[]{:S(2)}, u32[]{:S(2)}) collective-permute-start(bf16[112,32,128]{2,1,0:T(8,128)(2,1)S(1)} %constant_dynamic-update-slice_fusion.refs_3_.refs_0_), channel_id=1, source_target_pairs={{0,8},{8,16},{16,24},{24,0},{32,40},{40,48},{48,56},{56,32},{64,72... | collective-permute-start | bytes 2752520 | tf_op jit(solution)/shard_map/ppermute | solution.py:34
  27.1 23.5 %collective-permute-start.9 = (bf16[112,32,128]{2,1,0:T(8,128)(2,1)S(1)}, bf16[112,32,128]{2,1,0:T(8,128)(2,1)}, u32[]{:S(2)}, u32[]{:S(2)}) collective-permute-start(bf16[112,32,128]{2,1,0:T(8,128)(2,1)S(1)} %constant_dynamic-update-slice_fusion.refs_3_.refs_0_), channel_id=1, source_target_pairs={{0,24},{8,0},{16,8},{24,16},{32,56},{40,32},{48,40},{56,48},{64,88... | collective-permute-start | bytes 2752520 | tf_op jit(solution)/shard_map/ppermute | solution.py:34
  51.4 13.0 %collective-permute-start.14 = (bf16[56,32,128]{2,1,0:T(8,128)(2,1)}, bf16[56,32,128]{2,1,0:T(8,128)(2,1)S(1)}, u32[]{:S(2)}, u32[]{:S(2)}) collective-permute-start(bf16[56,32,128]{2,1,0:T(8,128)(2,1)} %slice.83), channel_id=1, source_target_pairs={{0,8},{8,16},{16,24},{24,0},{32,40},{40,48},{48,56},{56,32},{64,72... | collective-permute-start | bytes 1376264 | tf_op jit(solution)/shard_map/ppermute | solution.py:34
  53.2 12.4 %collective-permute-start.15 = (bf16[56,32,128]{2,1,0:T(8,128)(2,1)}, bf16[56,32,128]{2,1,0:T(8,128)(2,1)}, u32[]{:S(2)}, u32[]{:S(2)}) collective-permute-start(bf16[56,32,128]{2,1,0:T(8,128)(2,1)} %slice.85), channel_id=1, source_target_pairs={{0,24},{8,0},{16,8},{24,16},{32,56},{40,32},{48,40},{56,48},{64,88... | collective-permute-start | bytes 1376264 | tf_op jit(solution)/shard_map/ppermute | solution.py:34
  58.3 12.6 %collective-permute-start.16 = (bf16[56,32,128]{2,1,0:T(8,128)(2,1)}, bf16[56,32,128]{2,1,0:T(8,128)(2,1)}, u32[]{:S(2)}, u32[]{:S(2)}) collective-permute-start(bf16[56,32,128]{2,1,0:T(8,128)(2,1)} %slice.89), channel_id=1, source_target_pairs={{0,32},{8,40},{16,48},{24,56},{32,64},{40,72},{48,80},{56,88},{64,... | collective-permute-start | bytes 1376264 | tf_op jit(solution)/shard_map/ppermute | solution.py:34
  60.3 11.6 %collective-permute-start.17 = (bf16[56,32,128]{2,1,0:T(8,128)(2,1)}, bf16[56,32,128]{2,1,0:T(8,128)(2,1)}, u32[]{:S(2)}, u32[]{:S(2)}) collective-permute-start(bf16[56,32,128]{2,1,0:T(8,128)(2,1)} %slice.90), channel_id=1, source_target_pairs={{0,96},{8,104},{16,112},{24,120},{32,0},{40,8},{48,16},{56,24},{64... | collective-permute-start | bytes 1376264 | tf_op jit(solution)/shard_map/ppermute | solution.py:34
  76.0 12.7 %collective-permute-start.18 = (bf16[3,58,16,128]{3,2,1,0:T(8,128)(2,1)}, bf16[3,58,16,128]{3,2,1,0:T(8,128)(2,1)S(1)}, u32[]{:S(2)}, u32[]{:S(2)}) collective-permute-start(bf16[3,58,16,128]{3,2,1,0:T(8,128)(2,1)} %get-tuple-element.50), channel_id=1, source_target_pairs={{0,1},{1,2},{2,3},{3,4},{4,5},{5,6},{6,7},{8,9},{9,10},{10,11},{11... | collective-permute-start | bytes 2138120 | tf_op jit(solution)/shard_map/ppermute | solution.py:464
  77.9 12.7 %collective-permute-start.19 = (bf16[3,58,16,128]{3,2,1,0:T(8,128)(2,1)}, bf16[3,58,16,128]{3,2,1,0:T(8,128)(2,1)S(1)}, u32[]{:S(2)}, u32[]{:S(2)}) collective-permute-start(bf16[3,58,16,128]{3,2,1,0:T(8,128)(2,1)} %get-tuple-element.51), channel_id=1, source_target_pairs={{1,0},{2,1},{3,2},{4,3},{5,4},{6,5},{7,6},{9,8},{10,9},{11,10},{12... | collective-permute-start | bytes 2138120 | tf_op jit(solution)/shard_map/ppermute | solution.py:464
  81.5 14.8 %collective-permute-start.20 = (bf16[3,58,16,128]{3,2,1,0:T(8,128)(2,1)}, bf16[3,58,16,128]{3,2,1,0:T(8,128)(2,1)S(1)}, u32[]{:S(2)}, u32[]{:S(2)}) collective-permute-start(bf16[3,58,16,128]{3,2,1,0:T(8,128)(2,1)} %get-tuple-element.52), channel_id=1, source_target_pairs={{0,1},{1,2},{2,3},{3,4},{4,5},{5,6},{6,7},{8,9},{9,10},{10,11},{11... | collective-permute-start | bytes 2138120 | tf_op jit(solution)/shard_map/ppermute | solution.py:464
  83.7 14.4 %collective-permute-start.21 = (bf16[3,58,16,128]{3,2,1,0:T(8,128)(2,1)}, bf16[3,58,16,128]{3,2,1,0:T(8,128)(2,1)S(1)}, u32[]{:S(2)}, u32[]{:S(2)}) collective-permute-start(bf16[3,58,16,128]{3,2,1,0:T(8,128)(2,1)} %get-tuple-element.53), channel_id=1, source_target_pairs={{1,0},{2,1},{3,2},{4,3},{5,4},{6,5},{7,6},{9,8},{10,9},{11,10},{12... | collective-permute-start | bytes 2138120 | tf_op jit(solution)/shard_map/ppermute | solution.py:464
  118.3 25.4 %all-to-all-start.1 = ((s16[16,3,56,128]{3,2,1,0:T(8,128)(2,1)}), s16[16,3,56,128]{3,2,1,0:T(8,128)(2,1)S(1)}, u32[]{:S(2)}, u32[]{:S(2)}) async-start(s16[16,3,56,128]{3,2,1,0:T(8,128)(2,1)} %jobs.3), calls=%async_computation.1 | async-start | bytes 1376256 | tf_op jit(solution)/shard_map/all_to_all | solution.py:479
  143.7 22.1 %all-to-all-start = ((s16[16,3,56,128]{3,2,1,0:T(8,128)(2,1)}), s16[16,3,56,128]{3,2,1,0:T(8,128)(2,1)S(1)}, u32[]{:S(2)}, u32[]{:S(2)}) async-start(s16[16,3,56,128]{3,2,1,0:T(8,128)(2,1)} %jobs.2), calls=%async_computation | async-start | bytes 1376256 | tf_op jit(solution)/shard_map/all_to_all | solution.py:479
  168.1 14.7 %all-to-all-start.2 = ((s16[16,2,56,128]{3,2,1,0:T(8,128)(2,1)}), s16[16,2,56,128]{3,2,1,0:T(8,128)(2,1)S(1)}, u32[]{:S(2)}, u32[]{:S(2)}) async-start(s16[16,2,56,128]{3,2,1,0:T(8,128)(2,1)} %add_up.1), calls=%async_computation.2 | async-start | bytes 917504 | tf_op jit(solution)/shard_map/all_to_all | solution.py:480
  (13 other events, 245.0 us)

commit v5 on v4

--- a/solution.py
+++ b/solution.py
@@ -22,7 +22,7 @@
 
 
 def gathered_memory(parts):
-    return [parts[0]] + far_memory(*parts[1:])
+    return [*parts[:2], *far_memory(*parts[2:])]
 
 
 def torus_step(array, dx, dy):
@@ -38,20 +38,33 @@
     return (step, 0) if axis == 0 else (0, step)
 
 
-def ring_near(arrays, axes):
-    return [
-        [a, torus_step(a, *along(ax, 1)), torus_step(a, *along(ax, -1))]
-        for a, ax in zip(arrays, axes)
-    ]
-
-
-def ring_far(near, axes):
-    result = []
-    for (own, lower, upper), ax in zip(near, axes):
-        half = lower.shape[0] // 2
-        far = [torus_step(lower[:half], *along(ax, 1)), torus_step(upper[half:], *along(ax, -1))]
-        result.append([own, lower, upper, *far])
-    return result
+def first_ring(arrays, axes):
+    near = [
+        (torus_step(a, *along(ax, 1)), torus_step(a, *along(ax, -1))) for a, ax in zip(arrays, axes)
+    ]
+    return near, [
+        (
+            torus_step(lower[: lower.shape[0] // 2], *along(ax, 1)),
+            torus_step(upper[upper.shape[0] // 2 :], *along(ax, -1)),
+        )
+        for (lower, upper), ax in zip(near, axes)
+    ]
+
+
+def second_ring(halves, axes):
+    ahead = [
+        (torus_step(a, *along(ax, 1)), torus_step(b, *along(ax, -1)))
+        for (a, b), ax in zip(halves, axes)
+    ]
+    behind = [
+        (torus_step(b, *along(ax, 1)), torus_step(a, *along(ax, -1)))
+        for (a, b), ax in zip(halves, axes)
+    ]
+    far = [
+        (torus_step(la, *along(ax, 1)), torus_step(ub, *along(ax, -1)))
+        for (la, ub), ax in zip(ahead, axes)
+    ]
+    return ahead, behind, far
 
 
 def rank(delta):
@@ -124,7 +137,7 @@
         out.wait()
 
 
-PARTS = 5
+PARTS = 8
 
 
 def margins(gathered, me, above, below):
@@ -317,7 +330,7 @@
         out_shape=pltpu.HBM((16, slots, 2 * SIDE, 128), I16),
         compiler_params=pltpu.CompilerParams(vmem_limit_bytes=18 << 20),
         cost_estimate=pl.CostEstimate(
-            flops=slots * 2 * 128 * (WIN * PADW * (256 + 192 + 192 + 96) + 2 * SIDE * PADS * 192),
+            flops=slots * 20 * 128 * (WIN * PADW * (256 + 192 + 192 + 96) + 2 * SIDE * PADS * 192),
             transcendentals=slots * WIN * PADW * 128,
             bytes_accessed=slots * (2 * WIN * PADW * 128 * 2 + 16 * 2 * SIDE * 128 * 4),
         ),
@@ -440,31 +453,34 @@
     note = jnp.pad(jobs.astype(BF16)[None, None], ((0, 0), (0, SIDE - 1), (0, 128 - 2 * slots)))
     note = jnp.broadcast_to(note, (wire.shape[0],) + note.shape[1:])
     wire = jnp.concatenate([wire[:, :, :RIM], note[:, :, None], wire[:, :, SIDE - RIM + 1 :]], axis=2)
-    near = ring_near([wire[0], wire[1]], (0, 1))
-    rings = [jnp.concatenate(parts, axis=0) for parts in ring_far(near, (0, 1))]
-    rings, view_data, psf, views, bricks = lax.optimization_barrier(
-        (rings, view_data, psf, views, bricks)
-    )
-    near = ring_near(rings, (1, 0))
+    near, far = first_ring([wire[0], wire[1]], (0, 1))
     above = lax.ppermute(bricks, "view", downward)
     below = lax.ppermute(bricks, "view", upward)
+    near, above, below = lax.optimization_barrier((near, above, below))
+    halves = [
+        (jnp.concatenate([wire[c], near[c][0]], axis=0), jnp.concatenate([near[c][1], *far[c]], axis=0))
+        for c in range(2)
+    ]
+    halves, view_data, psf, views, bricks = lax.optimization_barrier(
+        (halves, view_data, psf, views, bricks)
+    )
+    ahead, behind, far = second_ring(halves, (1, 0))
 
     chosen = views[:, None] == jnp.arange(psf.shape[0])[None, :]
     taps = jnp.sum(jnp.where(chosen[:, :, None, None], psf[None], 0.0), axis=1)
     mats = job_matrices(taps, bricks)
     data = view_data[0, 0]
     logs = jnp.log2(jnp.maximum(4.0 / background * jnp.prod(jnp.sum(psf, axis=2), axis=1), 1e-30)) - 15.9
-    near, mats, data, above, below, logs = lax.optimization_barrier(
-        (near, mats, data, above, below, logs)
-    )
-    gathered = ring_far(near, (1, 0))
+    behind, mats, data, logs = lax.optimization_barrier((behind, mats, data, logs))
+    gathered = [
+        [*halves[c], ahead[c][0], behind[c][0], behind[c][1], ahead[c][1], *far[c]] for c in range(2)
+    ]
 
     rims = margins(gathered, me, above, below)
     edges = [
         (lax.ppermute(rims[2 * c], "view", upward), lax.ppermute(rims[2 * c + 1], "view", downward))
         for c in range(2)
     ]
-    edges = lax.optimization_barrier(edges)
     notes = jnp.concatenate([p[::SIDE, RIM, : 2 * slots] for p in gathered[0]], axis=0)
     places = place_of(jnp.arange(workers, dtype=I32), me[0], True)
     match = places[:, None] == jnp.arange(workers)[None, :]

time: 186 us -> 187 us (level)
  waiting for transfers between devices: 50.2 us -> 41.7 us
  starting transfers between devices: 58.3 us -> 65.7 us
  other arithmetic: 10.9 us -> 17.5 us
  local copies, waits for them, and re-layouts: 19.7 us -> 14.9 us
    slice x8 -> x4, local copies, waits for them, and re-layouts: 6.38 us -> 0.03 us  [the longest x2 0.02 us: first_ring(): lower[:lower.shape[0] // 2]]
    ppermute x16 -> x20, starting transfers between devices: 26.3 us -> 32.4 us  [torus_step(): return lax.ppermute(array, 'tile', pairs)]
    ppermute x2, waiting for transfers between devices: 7.35 us -> 1.57 us  [on_device(): lax.ppermute(rims[2 * c], 'view', upward)]
    ppermute x16 -> x20, waiting for transfers between devices: 14.3 us -> 17 us  [torus_step(): return lax.ppermute(array, 'tile', pairs)]
    convert_element_type x6, other arithmetic: 0.14 us -> 2.6 us  [high_low(): return (high.astype(BF16), (matrix - high).astype(BF16))]
    all_to_all x2, waiting for transfers between devices: 10.8 us -> 8.83 us  [on_device(): parts.append(lax.all_to_all(factors, 'tile', 0, 0, tiled=True))]
    slice x5 -> x8, local copies, waits for them, and re-layouts: 2.76 us -> 4.07 us  [on_device(): p[::SIDE, RIM, :2 * slots]]
  transfers between devices with their start and end apart: 25 -> 29, of which waited for: 15 -> 10; matrix products, arithmetic and copies ran while one was open for 13% -> 14% of each run, Pallas kernels for 10% -> 21%
where the time goes in v5:
time: 187 us; the launch traced here: 186 us
  starting transfers between devices  65.7 us (35%)
  Pallas kernels  45.8 us (24%)
  waiting for transfers between devices  41.7 us (22%)
  other arithmetic  17.5 us (9%)
  local copies, waits for them, and re-layouts  14.9 us (8%)
    pallas_call x2, Pallas kernels, run_jobs(): pl.pallas_call(functools.partial(job_kernel, channel), grid=(slots,), in_...  38.5 us
    ppermute x20, starting transfers between devices, torus_step(): return lax.ppermute(array, 'tile', pairs)  32.4 us
    ppermute x20, waiting for transfers between devices, torus_step(): return lax.ppermute(array, 'tile', pairs)  17 us
    all_to_all x2, starting transfers between devices, on_device(): parts.append(lax.all_to_all(factors, 'tile', 0, 0, tiled=True))  12.9 us
    all_to_all x1, waiting for transfers between devices, on_device(): lax.all_to_all(add_up(owners, seen_by, logs, parts), 'tile', 0, 0, tiled=...  11.3 us
    all_to_all x2, waiting for transfers between devices, on_device(): parts.append(lax.all_to_all(factors, 'tile', 0, 0, tiled=True))  8.83 us
    ppermute x2, starting transfers between devices, on_device(): lax.ppermute(rims[2 * c + 1], 'view', downward)  7.25 us
    optimization_barrier x2, local copies, waits for them, and re-layouts, on_device(): lax.optimization_barrier((halves, view_data, psf, views, bricks))  6.5 us
  transfers between devices with their start and end apart: 29, of which 10 were waited for; matrix products, arithmetic and copies ran while one was open for 14% of the time, Pallas kernels for 21%

profile of v5, /device:TPU:32, one launch (start us, length us, event | category | flops | bytes accessed | tf_op | source)
XLA Modules:
  0.0 186.1 jit_solution(10793419620744771568)
XLA Ops:
  13.1 3.7 %collective-permute-start.5 = (s32[3]{0:T(128)S(1)}, s32[3]{0:T(128)S(1)}, u32[]{:S(2)}, u32[]{:S(2)}) collective-permute-start(s32[3]{0:T(128)S(1)} %bitcast.47), channel_id=1, source_target_pairs={{0,1},{1,2},{2,3},{3,4},{4,5},{5,6},{6,7},{8,9},{9,10},{10,11},{11... | collective-permute-start | bytes 44 | tf_op jit(solution)/shard_map/ppermute | solution.py:458
  18.5 2.9 %collective-permute-start.9 = (bf16[14,32,128]{2,1,0:T(8,128)(2,1)S(1)}, bf16[14,32,128]{2,1,0:T(8,128)(2,1)S(1)}, u32[]{:S(2)}, u32[]{:S(2)}) collective-permute-start(bf16[14,32,128]{2,1,0:T(8,128)(2,1)S(1)} %slice.96), channel_id=1, source_target_pairs={{0,24},{8,0},{16,8},{24,16},{32,56},{40,32},{48,40},{56,48},{64,88... | collective-permute-start | bytes 344072 | tf_op jit(solution)/shard_map/ppermute | solution.py:34
  21.8 3.0 %collective-permute-start.7 = (bf16[14,32,128]{2,1,0:T(8,128)(2,1)S(1)}, bf16[14,32,128]{2,1,0:T(8,128)(2,1)S(1)}, u32[]{:S(2)}, u32[]{:S(2)}) collective-permute-start(bf16[14,32,128]{2,1,0:T(8,128)(2,1)S(1)} %slice.94), channel_id=1, source_target_pairs={{0,96},{8,104},{16,112},{24,120},{32,0},{40,8},{48,16},{56,24},{64... | collective-permute-start | bytes 344072 | tf_op jit(solution)/shard_map/ppermute | solution.py:34
  25.0 2.5 %collective-permute-done.6 = bf16[14,32,128]{2,1,0:T(8,128)(2,1)S(1)} collective-permute-done((bf16[14,32,128]{2,1,0:T(8,128)(2,1)S(1)}, bf16[14,32,128]{2,1,0:T(8,128)(2,1)S(1)}, u32[]{:S(2)}, u32[]{:S(2)}) %collective-permute-start.6) | collective-permute-done | bytes 114720 | tf_op jit(solution)/shard_map/ppermute | solution.py:34
  29.7 3.2 %collective-permute-start.15 = (bf16[56,32,128]{2,1,0:T(8,128)(2,1)S(1)}, bf16[56,32,128]{2,1,0:T(8,128)(2,1)}, u32[]{:S(2)}, u32[]{:S(2)}) collective-permute-start(bf16[56,32,128]{2,1,0:T(8,128)(2,1)S(1)} %pad_maximum_fusion.2.refs_4_.refs_1_), channel_id=1, source_target_pairs={{0,24},{8,0},{16,8},{24,16},{32,56},{40,32},{48,40},{56,48},{64,88... | collective-permute-start | bytes 1376264 | tf_op jit(solution)/shard_map/ppermute | solution.py:34
  43.1 6.5 %copy.73 = bf16[1,1,3,2,58,58,128]{6,5,4,3,2,1,0:T(8,128)(2,1)} copy(bf16[1,1,3,2,58,58,128]{6,3,5,4,2,1,0:T(2,128)(2,1)} %param.8) | data formatting | bytes 10334208 | tf_op jit(solution)/shard_map/optimization_barrier | solution.py:464
  51.4 2.7 %collective-permute-start.19 = (bf16[56,32,128]{2,1,0:T(8,128)(2,1)S(1)}, bf16[56,32,128]{2,1,0:T(8,128)(2,1)}, u32[]{:S(2)}, u32[]{:S(2)}) collective-permute-start(bf16[56,32,128]{2,1,0:T(8,128)(2,1)S(1)} %pad_maximum_fusion.4.refs_12_.refs_1_), channel_id=1, source_target_pairs={{0,96},{8,104},{16,112},{24,120},{32,0},{40,8},{48,16},{56,24},{64... | collective-permute-start | bytes 1376264 | tf_op jit(solution)/shard_map/ppermute | solution.py:34
  54.3 3.3 %collective-permute-start.13 = (bf16[56,32,128]{2,1,0:T(8,128)(2,1)S(1)}, bf16[56,32,128]{2,1,0:T(8,128)(2,1)}, u32[]{:S(2)}, u32[]{:S(2)}) collective-permute-start(bf16[56,32,128]{2,1,0:T(8,128)(2,1)S(1)} %get-tuple-element.42.refs_11_.refs_0_), channel_id=1, source_target_pairs={{0,96},{8,104},{16,112},{24,120},{32,0},{40,8},{48,16},{56,24},{64... | collective-permute-start | bytes 1376264 | tf_op jit(solution)/shard_map/ppermute | solution.py:34
  57.7 3.2 %collective-permute-start.17 = (bf16[56,32,128]{2,1,0:T(8,128)(2,1)}, bf16[56,32,128]{2,1,0:T(8,128)(2,1)}, u32[]{:S(2)}, u32[]{:S(2)}) collective-permute-start(bf16[56,32,128]{2,1,0:T(8,128)(2,1)} %collective-permute-done.15.refs_8_.refs_5_), channel_id=1, source_target_pairs={{0,24},{8,0},{16,8},{24,16},{32,56},{40,32},{48,40},{56,48},{64,88... | collective-permute-start | bytes 1376264 | tf_op jit(solution)/shard_map/ppermute | solution.py:34
  60.9 3.8 %collective-permute-done.18.refs_13_.refs_2_ = bf16[56,32,128]{2,1,0:T(8,128)(2,1)} collective-permute-done((bf16[56,32,128]{2,1,0:T(8,128)(2,1)S(1)}, bf16[56,32,128]{2,1,0:T(8,128)(2,1)}, u32[]{:S(2)}, u32[]{:S(2)}) %collective-permute-start.18) | collective-permute-done | bytes 458784 | tf_op jit(solution)/shard_map/ppermute | solution.py:34
  65.2 3.8 %collective-permute-start.21 = (bf16[56,32,128]{2,1,0:T(8,128)(2,1)}, bf16[56,32,128]{2,1,0:T(8,128)(2,1)}, u32[]{:S(2)}, u32[]{:S(2)}) collective-permute-start(bf16[56,32,128]{2,1,0:T(8,128)(2,1)} %collective-permute-done.19.refs_16_.refs_5_), channel_id=1, source_target_pairs={{0,96},{8,104},{16,112},{24,120},{32,0},{40,8},{48,16},{56,24},{64... | collective-permute-start | bytes 1376264 | tf_op jit(solution)/shard_map/ppermute | solution.py:34
  70.6 4.4 %collective-permute-done.13.refs_15_.refs_4_ = bf16[56,32,128]{2,1,0:T(8,128)(2,1)} collective-permute-done((bf16[56,32,128]{2,1,0:T(8,128)(2,1)S(1)}, bf16[56,32,128]{2,1,0:T(8,128)(2,1)}, u32[]{:S(2)}, u32[]{:S(2)}) %collective-permute-start.13) | collective-permute-done | bytes 458784 | tf_op jit(solution)/shard_map/ppermute | solution.py:34
  75.0 5.7 %collective-permute-done.21.refs_18_.refs_7_ = bf16[56,32,128]{2,1,0:T(8,128)(2,1)} collective-permute-done((bf16[56,32,128]{2,1,0:T(8,128)(2,1)}, bf16[56,32,128]{2,1,0:T(8,128)(2,1)}, u32[]{:S(2)}, u32[]{:S(2)}) %collective-permute-start.21) | collective-permute-done | bytes 458784 | tf_op jit(solution)/shard_map/ppermute | solution.py:34
  80.7 4.2 %margins.1 = (bf16[3,58,16,128]{3,2,1,0:T(8,128)(2,1)}, bf16[3,58,16,128]{3,2,1,0:T(8,128)(2,1)}, bf16[3,58,16,128]{3,2,1,0:T(8,128)(2,1)}, bf16[3,58,16,128]{3,2,1,0:T(8,128)(2,1)}) custom-call(s32[1]{0:T(128)} %bitcast.19.refs_0_.me, s32[3]{0:T(128)S(1)} %collective-permute-done.4.refs_1_, s32[3]{0:T(128)S(1)} %collective-permute-done.5.refs_2_, ...), custom_call_target="tpu_custom_call" | custom-call | tf_op jit(solution)/shard_map/margins/pallas_call | solution.py:146
  86.9 3.6 %collective-permute-start.25 = (bf16[3,58,16,128]{3,2,1,0:T(8,128)(2,1)}, bf16[3,58,16,128]{3,2,1,0:T(8,128)(2,1)S(1)}, u32[]{:S(2)}, u32[]{:S(2)}) collective-permute-start(bf16[3,58,16,128]{3,2,1,0:T(8,128)(2,1)} %get-tuple-element.64), channel_id=1, source_target_pairs={{1,0},{2,1},{3,2},{4,3},{5,4},{6,5},{7,6},{9,8},{10,9},{11,10},{12... | collective-permute-start | bytes 2138120 | tf_op jit(solution)/shard_map/ppermute | solution.py:481
  92.5 3.6 %collective-permute-start.23 = (bf16[3,58,16,128]{3,2,1,0:T(8,128)(2,1)}, bf16[3,58,16,128]{3,2,1,0:T(8,128)(2,1)}, u32[]{:S(2)}, u32[]{:S(2)}) collective-permute-start(bf16[3,58,16,128]{3,2,1,0:T(8,128)(2,1)} %get-tuple-element.55), channel_id=1, source_target_pairs={{1,0},{2,1},{3,2},{4,3},{5,4},{6,5},{7,6},{9,8},{10,9},{11,10},{12... | collective-permute-start | bytes 2138120 | tf_op jit(solution)/shard_map/ppermute | solution.py:481
  100.4 19.3 %jobs.3 = s16[16,3,56,128]{3,2,1,0:T(8,128)(2,1)} custom-call(s32[1]{0:T(128)} %bitcast.19.refs_0_.me, s32[3]{0:T(128)S(1)} %bitcast.49, s32[3]{0:T(128)S(1)} %bitcast.44, f32[6]{0:T(128)S(1)} %copy-done.1, f32[6]{0:T(128)S(1)} %multiply_add_fusion.logs, bf16[56,32,128]{2,1,0:T(8,128)(2,1)S(1)} %get-tuple-element.42.refs_11_.refs_0_, ...), custom_call_target="tpu_custom_call" | custom-call | flops 23624417280 | bytes 7077888 | tf_op jit(solution)/shard_map/jobs/pallas_call | solution.py:315
  119.7 5.5 %all-to-all-start.1 = ((s16[16,3,56,128]{3,2,1,0:T(8,128)(2,1)}), s16[16,3,56,128]{3,2,1,0:T(8,128)(2,1)S(1)}, u32[]{:S(2)}, u32[]{:S(2)}) async-start(s16[16,3,56,128]{3,2,1,0:T(8,128)(2,1)} %jobs.3), calls=%async_computation.1 | async-start | bytes 1376256 | tf_op jit(solution)/shard_map/all_to_all | solution.py:495
  125.3 19.3 %jobs.2 = s16[16,3,56,128]{3,2,1,0:T(8,128)(2,1)} custom-call(s32[1]{0:T(128)} %bitcast.19.refs_0_.me, s32[3]{0:T(128)S(1)} %bitcast.50, s32[3]{0:T(128)S(1)} %bitcast.45, f32[6]{0:T(128)S(1)} %copy-done.1, f32[6]{0:T(128)S(1)} %multiply_add_fusion.logs, bf16[56,32,128]{2,1,0:T(8,128)(2,1)S(1)} %get-tuple-element.40.refs_3_.refs_0_, ...), custom_call_target="tpu_custom_call" | custom-call | flops 23624417280 | bytes 7077888 | tf_op jit(solution)/shard_map/jobs/pallas_call | solution.py:315
  144.6 7.4 %all-to-all-start = ((s16[16,3,56,128]{3,2,1,0:T(8,128)(2,1)}), s16[16,3,56,128]{3,2,1,0:T(8,128)(2,1)S(1)}, u32[]{:S(2)}, u32[]{:S(2)}) async-start(s16[16,3,56,128]{3,2,1,0:T(8,128)(2,1)} %jobs.2), calls=%async_computation | async-start | bytes 1376256 | tf_op jit(solution)/shard_map/all_to_all | solution.py:495
  157.6 8.8 %all-to-all-done.refs_0_ = s16[16,3,56,128]{3,2,1,0:T(8,128)(2,1)S(1)} async-done(((s16[16,3,56,128]{3,2,1,0:T(8,128)(2,1)}), s16[16,3,56,128]{3,2,1,0:T(8,128)(2,1)S(1)}, u32[]{:S(2)}, u32[]{:S(2)}) %all-to-all-start) | async-done | bytes 688160 | tf_op jit(solution)/shard_map/all_to_all | solution.py:495
  166.5 2.3 %add_up.1 = s16[16,2,56,128]{3,2,1,0:T(8,128)(2,1)} custom-call(s32[48]{0:T(128)S(1)} %reshape.415.owners, s32[48]{0:T(128)S(1)} %reshape.416.views, f32[6]{0:T(128)S(1)} %multiply_add_fusion.logs, s16[16,3,56,128]{3,2,1,0:T(8,128)(2,1)S(1)} %all-to-all-done.refs_0_, s16[16,3,56,128]{3,2,1,0:T(8,128)(2,1)S(1)} %all-to-all-done.1.refs_1_), custom_call_target="tpu_custom_call" | custom-call | tf_op jit(solution)/shard_map/add_up/pallas_call | solution.py:406
  168.7 3.6 %all-to-all-start.2 = ((s16[16,2,56,128]{3,2,1,0:T(8,128)(2,1)}), s16[16,2,56,128]{3,2,1,0:T(8,128)(2,1)S(1)}, u32[]{:S(2)}, u32[]{:S(2)}) async-start(s16[16,2,56,128]{3,2,1,0:T(8,128)(2,1)} %add_up.1), calls=%async_computation.2 | async-start | bytes 917504 | tf_op jit(solution)/shard_map/all_to_all | solution.py:496
  172.5 11.3 %all-to-all-done.2.total = s16[16,2,56,128]{3,2,1,0:T(8,128)(2,1)S(1)} async-done(((s16[16,2,56,128]{3,2,1,0:T(8,128)(2,1)}), s16[16,2,56,128]{3,2,1,0:T(8,128)(2,1)S(1)}, u32[]{:S(2)}, u32[]{:S(2)}) %all-to-all-start.2) | async-done | bytes 458784 | tf_op jit(solution)/shard_map/all_to_all | solution.py:496
  (152 shorter events, 47.8 us)
Async XLA Ops:
  3.2 14.7 %collective-permute-start = (bf16[28,32,128]{2,1,0:T(8,128)(2,1)S(1)}, bf16[28,32,128]{2,1,0:T(8,128)(2,1)S(1)}, u32[]{:S(2)}, u32[]{:S(2)}) collective-permute-start(bf16[28,32,128]{2,1,0:T(8,128)(2,1)S(1)} %get-tuple-element.68), channel_id=1, source_target_pairs={{0,32},{8,40},{16,48},{24,56},{32,64},{40,72},{48,80},{56,88},{64,... | collective-permute-start | bytes 688136 | tf_op jit(solution)/shard_map/ppermute | solution.py:34
  4.8 13.2 %collective-permute-start.1 = (bf16[28,32,128]{2,1,0:T(8,128)(2,1)S(1)}, bf16[28,32,128]{2,1,0:T(8,128)(2,1)S(1)}, u32[]{:S(2)}, u32[]{:S(2)}) collective-permute-start(bf16[28,32,128]{2,1,0:T(8,128)(2,1)S(1)} %get-tuple-element.68), channel_id=1, source_target_pairs={{0,96},{8,104},{16,112},{24,120},{32,0},{40,8},{48,16},{56,24},{64... | collective-permute-start | bytes 688136 | tf_op jit(solution)/shard_map/ppermute | solution.py:34
  6.5 11.4 %collective-permute-start.2 = (bf16[28,32,128]{2,1,0:T(8,128)(2,1)S(1)}, bf16[28,32,128]{2,1,0:T(8,128)(2,1)S(1)}, u32[]{:S(2)}, u32[]{:S(2)}) collective-permute-start(bf16[28,32,128]{2,1,0:T(8,128)(2,1)S(1)} %get-tuple-element.67), channel_id=1, source_target_pairs={{0,8},{8,16},{16,24},{24,0},{32,40},{40,48},{48,56},{56,32},{64,72... | collective-permute-start | bytes 688136 | tf_op jit(solution)/shard_map/ppermute | solution.py:34
  8.1 9.9 %collective-permute-start.3 = (bf16[28,32,128]{2,1,0:T(8,128)(2,1)S(1)}, bf16[28,32,128]{2,1,0:T(8,128)(2,1)S(1)}, u32[]{:S(2)}, u32[]{:S(2)}) collective-permute-start(bf16[28,32,128]{2,1,0:T(8,128)(2,1)S(1)} %get-tuple-element.67), channel_id=1, source_target_pairs={{0,24},{8,0},{16,8},{24,16},{32,56},{40,32},{48,40},{56,48},{64,88... | collective-permute-start | bytes 688136 | tf_op jit(solution)/shard_map/ppermute | solution.py:34
  18.0 6.9 %collective-permute-start.8 = (bf16[14,32,128]{2,1,0:T(8,128)(2,1)S(1)}, bf16[14,32,128]{2,1,0:T(8,128)(2,1)S(1)}, u32[]{:S(2)}, u32[]{:S(2)}) collective-permute-start(bf16[14,32,128]{2,1,0:T(8,128)(2,1)S(1)} %slice.95), channel_id=1, source_target_pairs={{0,8},{8,16},{16,24},{24,0},{32,40},{40,48},{48,56},{56,32},{64,72... | collective-permute-start | bytes 344072 | tf_op jit(solution)/shard_map/ppermute | solution.py:34
  27.6 26.6 %collective-permute-start.11 = (bf16[56,32,128]{2,1,0:T(8,128)(2,1)S(1)}, bf16[56,32,128]{2,1,0:T(8,128)(2,1)}, u32[]{:S(2)}, u32[]{:S(2)}) collective-permute-start(bf16[56,32,128]{2,1,0:T(8,128)(2,1)S(1)} %get-tuple-element.40.refs_3_.refs_0_), channel_id=1, source_target_pairs={{0,24},{8,0},{16,8},{24,16},{32,56},{40,32},{48,40},{56,48},{64,88... | collective-permute-start | bytes 1376264 | tf_op jit(solution)/shard_map/ppermute | solution.py:34
  28.3 29.3 %collective-permute-start.14 = (bf16[56,32,128]{2,1,0:T(8,128)(2,1)S(1)}, bf16[56,32,128]{2,1,0:T(8,128)(2,1)S(1)}, u32[]{:S(2)}, u32[]{:S(2)}) collective-permute-start(bf16[56,32,128]{2,1,0:T(8,128)(2,1)S(1)} %get-tuple-element.40.refs_3_.refs_0_), channel_id=1, source_target_pairs={{0,8},{8,16},{16,24},{24,0},{32,40},{40,48},{48,56},{56,32},{64,72... | collective-permute-start | bytes 1376264 | tf_op jit(solution)/shard_map/ppermute | solution.py:34
  29.7 21.8 %collective-permute-start.10 = (bf16[56,32,128]{2,1,0:T(8,128)(2,1)S(1)}, bf16[56,32,128]{2,1,0:T(8,128)(2,1)}, u32[]{:S(2)}, u32[]{:S(2)}) collective-permute-start(bf16[56,32,128]{2,1,0:T(8,128)(2,1)S(1)} %pad_maximum_fusion.2.refs_4_.refs_1_), channel_id=1, source_target_pairs={{0,8},{8,16},{16,24},{24,0},{32,40},{40,48},{48,56},{56,32},{64,72... | collective-permute-start | bytes 1376264 | tf_op jit(solution)/shard_map/ppermute | solution.py:34
  29.7 28.0 %collective-permute-start.15 = (bf16[56,32,128]{2,1,0:T(8,128)(2,1)S(1)}, bf16[56,32,128]{2,1,0:T(8,128)(2,1)}, u32[]{:S(2)}, u32[]{:S(2)}) collective-permute-start(bf16[56,32,128]{2,1,0:T(8,128)(2,1)S(1)} %pad_maximum_fusion.2.refs_4_.refs_1_), channel_id=1, source_target_pairs={{0,24},{8,0},{16,8},{24,16},{32,56},{40,32},{48,40},{56,48},{64,88... | collective-permute-start | bytes 1376264 | tf_op jit(solution)/shard_map/ppermute | solution.py:34
  37.3 17.0 %collective-permute-start.12 = (bf16[56,32,128]{2,1,0:T(8,128)(2,1)S(1)}, bf16[56,32,128]{2,1,0:T(8,128)(2,1)S(1)}, u32[]{:S(2)}, u32[]{:S(2)}) collective-permute-start(bf16[56,32,128]{2,1,0:T(8,128)(2,1)S(1)} %pad_maximum_fusion.4.refs_12_.refs_1_), channel_id=1, source_target_pairs={{0,32},{8,40},{16,48},{24,56},{32,64},{40,72},{48,80},{56,88},{64,... | collective-permute-start | bytes 1376264 | tf_op jit(solution)/shard_map/ppermute | solution.py:34
  51.4 13.7 %collective-permute-start.19 = (bf16[56,32,128]{2,1,0:T(8,128)(2,1)S(1)}, bf16[56,32,128]{2,1,0:T(8,128)(2,1)}, u32[]{:S(2)}, u32[]{:S(2)}) collective-permute-start(bf16[56,32,128]{2,1,0:T(8,128)(2,1)S(1)} %pad_maximum_fusion.4.refs_12_.refs_1_), channel_id=1, source_target_pairs={{0,96},{8,104},{16,112},{24,120},{32,0},{40,8},{48,16},{56,24},{64... | collective-permute-start | bytes 1376264 | tf_op jit(solution)/shard_map/ppermute | solution.py:34
  54.2 10.5 %collective-permute-start.18 = (bf16[56,32,128]{2,1,0:T(8,128)(2,1)S(1)}, bf16[56,32,128]{2,1,0:T(8,128)(2,1)}, u32[]{:S(2)}, u32[]{:S(2)}) collective-permute-start(bf16[56,32,128]{2,1,0:T(8,128)(2,1)S(1)} %get-tuple-element.42.refs_11_.refs_0_), channel_id=1, source_target_pairs={{0,32},{8,40},{16,48},{24,56},{32,64},{40,72},{48,80},{56,88},{64,... | collective-permute-start | bytes 1376264 | tf_op jit(solution)/shard_map/ppermute | solution.py:34
  54.3 20.7 %collective-permute-start.13 = (bf16[56,32,128]{2,1,0:T(8,128)(2,1)S(1)}, bf16[56,32,128]{2,1,0:T(8,128)(2,1)}, u32[]{:S(2)}, u32[]{:S(2)}) collective-permute-start(bf16[56,32,128]{2,1,0:T(8,128)(2,1)S(1)} %get-tuple-element.42.refs_11_.refs_0_), channel_id=1, source_target_pairs={{0,96},{8,104},{16,112},{24,120},{32,0},{40,8},{48,16},{56,24},{64... | collective-permute-start | bytes 1376264 | tf_op jit(solution)/shard_map/ppermute | solution.py:34
  57.6 17.4 %collective-permute-start.16 = (bf16[56,32,128]{2,1,0:T(8,128)(2,1)S(1)}, bf16[56,32,128]{2,1,0:T(8,128)(2,1)S(1)}, u32[]{:S(2)}, u32[]{:S(2)}) collective-permute-start(bf16[56,32,128]{2,1,0:T(8,128)(2,1)S(1)} %collective-permute-done.14.refs_5_.refs_2_), channel_id=1, source_target_pairs={{0,8},{8,16},{16,24},{24,0},{32,40},{40,48},{48,56},{56,32},{64,72... | collective-permute-start | bytes 1376264 | tf_op jit(solution)/shard_map/ppermute | solution.py:34
  57.7 17.3 %collective-permute-start.17 = (bf16[56,32,128]{2,1,0:T(8,128)(2,1)}, bf16[56,32,128]{2,1,0:T(8,128)(2,1)}, u32[]{:S(2)}, u32[]{:S(2)}) collective-permute-start(bf16[56,32,128]{2,1,0:T(8,128)(2,1)} %collective-permute-done.15.refs_8_.refs_5_), channel_id=1, source_target_pairs={{0,24},{8,0},{16,8},{24,16},{32,56},{40,32},{48,40},{56,48},{64,88... | collective-permute-start | bytes 1376264 | tf_op jit(solution)/shard_map/ppermute | solution.py:34
  64.7 10.3 %collective-permute-start.20 = (bf16[56,32,128]{2,1,0:T(8,128)(2,1)}, bf16[56,32,128]{2,1,0:T(8,128)(2,1)}, u32[]{:S(2)}, u32[]{:S(2)}) collective-permute-start(bf16[56,32,128]{2,1,0:T(8,128)(2,1)} %collective-permute-done.18.refs_13_.refs_2_), channel_id=1, source_target_pairs={{0,32},{8,40},{16,48},{24,56},{32,64},{40,72},{48,80},{56,88},{64,... | collective-permute-start | bytes 1376264 | tf_op jit(solution)/shard_map/ppermute | solution.py:34
  65.2 15.6 %collective-permute-start.21 = (bf16[56,32,128]{2,1,0:T(8,128)(2,1)}, bf16[56,32,128]{2,1,0:T(8,128)(2,1)}, u32[]{:S(2)}, u32[]{:S(2)}) collective-permute-start(bf16[56,32,128]{2,1,0:T(8,128)(2,1)} %collective-permute-done.19.refs_16_.refs_5_), channel_id=1, source_target_pairs={{0,96},{8,104},{16,112},{24,120},{32,0},{40,8},{48,16},{56,24},{64... | collective-permute-start | bytes 1376264 | tf_op jit(solution)/shard_map/ppermute | solution.py:34
  85.0 12.7 %collective-permute-start.24 = (bf16[3,58,16,128]{3,2,1,0:T(8,128)(2,1)}, bf16[3,58,16,128]{3,2,1,0:T(8,128)(2,1)S(1)}, u32[]{:S(2)}, u32[]{:S(2)}) collective-permute-start(bf16[3,58,16,128]{3,2,1,0:T(8,128)(2,1)} %get-tuple-element.63), channel_id=1, source_target_pairs={{0,1},{1,2},{2,3},{3,4},{4,5},{5,6},{6,7},{8,9},{9,10},{10,11},{11... | collective-permute-start | bytes 2138120 | tf_op jit(solution)/shard_map/ppermute | solution.py:481
  86.9 12.7 %collective-permute-start.25 = (bf16[3,58,16,128]{3,2,1,0:T(8,128)(2,1)}, bf16[3,58,16,128]{3,2,1,0:T(8,128)(2,1)S(1)}, u32[]{:S(2)}, u32[]{:S(2)}) collective-permute-start(bf16[3,58,16,128]{3,2,1,0:T(8,128)(2,1)} %get-tuple-element.64), channel_id=1, source_target_pairs={{1,0},{2,1},{3,2},{4,3},{5,4},{6,5},{7,6},{9,8},{10,9},{11,10},{12... | collective-permute-start | bytes 2138120 | tf_op jit(solution)/shard_map/ppermute | solution.py:481
  90.5 34.8 %collective-permute-start.22 = (bf16[3,58,16,128]{3,2,1,0:T(8,128)(2,1)}, bf16[3,58,16,128]{3,2,1,0:T(8,128)(2,1)}, u32[]{:S(2)}, u32[]{:S(2)}) collective-permute-start(bf16[3,58,16,128]{3,2,1,0:T(8,128)(2,1)} %get-tuple-element.54), channel_id=1, source_target_pairs={{0,1},{1,2},{2,3},{3,4},{4,5},{5,6},{6,7},{8,9},{9,10},{10,11},{11... | collective-permute-start | bytes 2138120 | tf_op jit(solution)/shard_map/ppermute | solution.py:481
  92.5 32.8 %collective-permute-start.23 = (bf16[3,58,16,128]{3,2,1,0:T(8,128)(2,1)}, bf16[3,58,16,128]{3,2,1,0:T(8,128)(2,1)}, u32[]{:S(2)}, u32[]{:S(2)}) collective-permute-start(bf16[3,58,16,128]{3,2,1,0:T(8,128)(2,1)} %get-tuple-element.55), channel_id=1, source_target_pairs={{1,0},{2,1},{3,2},{4,3},{5,4},{6,5},{7,6},{9,8},{10,9},{11,10},{12... | collective-permute-start | bytes 2138120 | tf_op jit(solution)/shard_map/ppermute | solution.py:481
  119.7 24.9 %all-to-all-start.1 = ((s16[16,3,56,128]{3,2,1,0:T(8,128)(2,1)}), s16[16,3,56,128]{3,2,1,0:T(8,128)(2,1)S(1)}, u32[]{:S(2)}, u32[]{:S(2)}) async-start(s16[16,3,56,128]{3,2,1,0:T(8,128)(2,1)} %jobs.3), calls=%async_computation.1 | async-start | bytes 1376256 | tf_op jit(solution)/shard_map/all_to_all | solution.py:495
  144.6 21.8 %all-to-all-start = ((s16[16,3,56,128]{3,2,1,0:T(8,128)(2,1)}), s16[16,3,56,128]{3,2,1,0:T(8,128)(2,1)S(1)}, u32[]{:S(2)}, u32[]{:S(2)}) async-start(s16[16,3,56,128]{3,2,1,0:T(8,128)(2,1)} %jobs.2), calls=%async_computation | async-start | bytes 1376256 | tf_op jit(solution)/shard_map/all_to_all | solution.py:495
  168.7 15.1 %all-to-all-start.2 = ((s16[16,2,56,128]{3,2,1,0:T(8,128)(2,1)}), s16[16,2,56,128]{3,2,1,0:T(8,128)(2,1)S(1)}, u32[]{:S(2)}, u32[]{:S(2)}) async-start(s16[16,2,56,128]{3,2,1,0:T(8,128)(2,1)} %add_up.1), calls=%async_computation.2 | async-start | bytes 917504 | tf_op jit(solution)/shard_map/all_to_all | solution.py:496
  (18 other events, 238.8 us)

commit v6 on v4

--- a/solution.py
+++ b/solution.py
@@ -42,6 +42,49 @@
     return [
         [a, torus_step(a, *along(ax, 1)), torus_step(a, *along(ax, -1))]
         for a, ax in zip(arrays, axes)
+    ]
+
+
+def halves_kernel(*refs):
+    stage, sems, refs = refs[-2], refs[-1], refs[:-2]
+    count = len(refs) // 2
+    ins, outs = [], []
+    for i in range(count):
+        half = refs[i].shape[0] // 2
+        source = refs[i].at[pl.ds(0 if i % 2 == 0 else half, half)]
+        ins.append(pltpu.make_async_copy(source, stage.at[i], sems.at[i, 0]))
+        outs.append(pltpu.make_async_copy(stage.at[i], refs[count + i], sems.at[i, 1]))
+        ins[i].start()
+    for i in range(count):
+        ins[i].wait()
+        outs[i].start()
+    for i in range(count):
+        outs[i].wait()
+
+
+def take_halves(near):
+    arrays = [a for _, lower, upper in near for a in (lower, upper)]
+    anywhere = pl.BlockSpec(memory_space=pl.ANY)
+    shape = arrays[0].shape
+    taken = pl.pallas_call(
+        halves_kernel,
+        in_specs=[anywhere] * len(arrays),
+        out_specs=[anywhere] * len(arrays),
+        out_shape=[pltpu.HBM((shape[0] // 2,) + shape[1:], BF16)] * len(arrays),
+        scratch_shapes=[
+            pltpu.VMEM((len(arrays), shape[0] // 2) + shape[1:], BF16),
+            pltpu.SemaphoreType.DMA((len(arrays), 2)),
+        ],
+        compiler_params=pltpu.CompilerParams(vmem_limit_bytes=4 << 20),
+        name="halves",
+    )(*arrays)
+    return [(taken[2 * i], taken[2 * i + 1]) for i in range(len(near))]
+
+
+def ring_pass_on(near, axes):
+    return [
+        [*n, torus_step(low, *along(ax, 1)), torus_step(high, *along(ax, -1))]
+        for n, (low, high), ax in zip(near, take_halves(near), axes)
     ]
 
 
@@ -317,7 +360,7 @@
         out_shape=pltpu.HBM((16, slots, 2 * SIDE, 128), I16),
         compiler_params=pltpu.CompilerParams(vmem_limit_bytes=18 << 20),
         cost_estimate=pl.CostEstimate(
-            flops=slots * 2 * 128 * (WIN * PADW * (256 + 192 + 192 + 96) + 2 * SIDE * PADS * 192),
+            flops=slots * 20 * 128 * (WIN * PADW * (256 + 192 + 192 + 96) + 2 * SIDE * PADS * 192),
             transcendentals=slots * WIN * PADW * 128,
             bytes_accessed=slots * (2 * WIN * PADW * 128 * 2 + 16 * 2 * SIDE * 128 * 4),
         ),
@@ -441,30 +484,28 @@
     note = jnp.broadcast_to(note, (wire.shape[0],) + note.shape[1:])
     wire = jnp.concatenate([wire[:, :, :RIM], note[:, :, None], wire[:, :, SIDE - RIM + 1 :]], axis=2)
     near = ring_near([wire[0], wire[1]], (0, 1))
+    above = lax.ppermute(bricks, "view", downward)
+    below = lax.ppermute(bricks, "view", upward)
+    near, above, below = lax.optimization_barrier((near, above, below))
     rings = [jnp.concatenate(parts, axis=0) for parts in ring_far(near, (0, 1))]
     rings, view_data, psf, views, bricks = lax.optimization_barrier(
         (rings, view_data, psf, views, bricks)
     )
     near = ring_near(rings, (1, 0))
-    above = lax.ppermute(bricks, "view", downward)
-    below = lax.ppermute(bricks, "view", upward)
 
     chosen = views[:, None] == jnp.arange(psf.shape[0])[None, :]
     taps = jnp.sum(jnp.where(chosen[:, :, None, None], psf[None], 0.0), axis=1)
     mats = job_matrices(taps, bricks)
     data = view_data[0, 0]
     logs = jnp.log2(jnp.maximum(4.0 / background * jnp.prod(jnp.sum(psf, axis=2), axis=1), 1e-30)) - 15.9
-    near, mats, data, above, below, logs = lax.optimization_barrier(
-        (near, mats, data, above, below, logs)
-    )
-    gathered = ring_far(near, (1, 0))
+    near, mats, data, logs = lax.optimization_barrier((near, mats, data, logs))
+    gathered = ring_pass_on(near, (1, 0))
 
     rims = margins(gathered, me, above, below)
     edges = [
         (lax.ppermute(rims[2 * c], "view", upward), lax.ppermute(rims[2 * c + 1], "view", downward))
         for c in range(2)
     ]
-    edges = lax.optimization_barrier(edges)
     notes = jnp.concatenate([p[::SIDE, RIM, : 2 * slots] for p in gathered[0]], axis=0)
     places = place_of(jnp.arange(workers, dtype=I32), me[0], True)
     match = places[:, None] == jnp.arange(workers)[None, :]

time: 186 us -> 178 us (0.957)
  waiting for transfers between devices: 50.2 us -> 40.4 us
  Pallas kernels: 45.5 us -> 48.3 us
    ppermute x2, waiting for transfers between devices: 7.35 us -> 1.58 us  [on_device(): lax.ppermute(rims[2 * c], 'view', upward)]
    unnamed x34 -> x39, local copies, waits for them, and re-layouts: 1.23 us -> 6.86 us
    slice x4 -> x2, local copies, waits for them, and re-layouts: 3.67 us -> 0.02 us  [ring_far(): upper[half:]]
    pallas_call x0 -> x1, Pallas kernels: none -> 3 us  [take_halves(): pl.pallas_call(halves_kernel, in_specs=[anywhere] * len(arrays), out_spec...]
    slice x4 -> x2, local copies, waits for them, and re-layouts: 2.72 us -> 0.02 us  [ring_far(): lower[:half]]
    optimization_barrier x2, local copies, waits for them, and re-layouts: 6.48 us -> 4.01 us  [on_device(): lax.optimization_barrier((rings, view_data, psf, views, bricks))]
    ppermute x1, starting transfers between devices: 1.92 us -> 3.85 us  [on_device(): below = lax.ppermute(bricks, 'view', upward)]
  transfers between devices with their start and end apart: 25 -> 25, of which waited for: 15 -> 11; matrix products, arithmetic and copies ran while one was open for 13% -> 11% of each run, Pallas kernels for 10% -> 22%
where the time goes in v6:
time: 178 us; the launch traced here: 177 us
  starting transfers between devices  58.6 us (33%)
  Pallas kernels  48.3 us (27%)
  waiting for transfers between devices  40.4 us (23%)
  local copies, waits for them, and re-layouts  18.5 us (10%)
  other arithmetic  10.9 us (6%)
    pallas_call x2, Pallas kernels, run_jobs(): pl.pallas_call(functools.partial(job_kernel, channel), grid=(slots,), in_...  38.6 us
    ppermute x16, starting transfers between devices, torus_step(): return lax.ppermute(array, 'tile', pairs)  26.2 us
    ppermute x16, waiting for transfers between devices, torus_step(): return lax.ppermute(array, 'tile', pairs)  14.2 us
    all_to_all x2, starting transfers between devices, on_device(): parts.append(lax.all_to_all(factors, 'tile', 0, 0, tiled=True))  12 us
    all_to_all x1, waiting for transfers between devices, on_device(): lax.all_to_all(add_up(owners, seen_by, logs, parts), 'tile', 0, 0, tiled=...  11.2 us
    all_to_all x2, waiting for transfers between devices, on_device(): parts.append(lax.all_to_all(factors, 'tile', 0, 0, tiled=True))  9.98 us
    ppermute x2, starting transfers between devices, on_device(): lax.ppermute(rims[2 * c + 1], 'view', downward)  7.24 us
    unnamed x39, local copies, waits for them, and re-layouts  6.86 us
  transfers between devices with their start and end apart: 25, of which 11 were waited for; matrix products, arithmetic and copies ran while one was open for 11% of the time, Pallas kernels for 22%

profile of v6, /device:TPU:32, one launch (start us, length us, event | category | flops | bytes accessed | tf_op | source)
XLA Modules:
  0.0 177.3 jit_solution(18280033397262280653)
XLA Ops:
  13.0 3.9 %collective-permute-start.5 = (s32[3]{0:T(128)S(1)}, s32[3]{0:T(128)S(1)}, u32[]{:S(2)}, u32[]{:S(2)}) collective-permute-start(s32[3]{0:T(128)S(1)} %bitcast.44), channel_id=1, source_target_pairs={{0,1},{1,2},{2,3},{3,4},{4,5},{5,6},{6,7},{8,9},{9,10},{10,11},{11... | collective-permute-start | bytes 44 | tf_op jit(solution)/shard_map/ppermute | solution.py:488
  21.4 2.9 %collective-permute-start.9 = (bf16[14,32,128]{2,1,0:T(8,128)(2,1)S(1)}, bf16[14,32,128]{2,1,0:T(8,128)(2,1)S(1)}, u32[]{:S(2)}, u32[]{:S(2)}) collective-permute-start(bf16[14,32,128]{2,1,0:T(8,128)(2,1)S(1)} %slice.64), channel_id=1, source_target_pairs={{0,24},{8,0},{16,8},{24,16},{32,56},{40,32},{48,40},{56,48},{64,88... | collective-permute-start | bytes 344072 | tf_op jit(solution)/shard_map/ppermute | solution.py:34
  24.6 3.0 %collective-permute-start.7 = (bf16[14,32,128]{2,1,0:T(8,128)(2,1)S(1)}, bf16[14,32,128]{2,1,0:T(8,128)(2,1)S(1)}, u32[]{:S(2)}, u32[]{:S(2)}) collective-permute-start(bf16[14,32,128]{2,1,0:T(8,128)(2,1)S(1)} %slice.62), channel_id=1, source_target_pairs={{0,96},{8,104},{16,112},{24,120},{32,0},{40,8},{48,16},{56,24},{64... | collective-permute-start | bytes 344072 | tf_op jit(solution)/shard_map/ppermute | solution.py:34
  31.6 3.2 %collective-permute-start.11 = (bf16[112,32,128]{2,1,0:T(8,128)(2,1)}, bf16[112,32,128]{2,1,0:T(8,128)(2,1)S(1)}, u32[]{:S(2)}, u32[]{:S(2)}) collective-permute-start(bf16[112,32,128]{2,1,0:T(8,128)(2,1)} %constant_dynamic-update-slice_fusion.refs_3_.refs_0_), channel_id=1, source_target_pairs={{0,24},{8,0},{16,8},{24,16},{32,56},{40,32},{48,40},{56,48},{64,88... | collective-permute-start | bytes 2752520 | tf_op jit(solution)/shard_map/ppermute | solution.py:34
  34.9 3.2 %collective-permute-start.13 = (bf16[112,32,128]{2,1,0:T(8,128)(2,1)}, bf16[112,32,128]{2,1,0:T(8,128)(2,1)}, u32[]{:S(2)}, u32[]{:S(2)}) collective-permute-start(bf16[112,32,128]{2,1,0:T(8,128)(2,1)} %constant_dynamic-update-slice_fusion.5.refs_8_.refs_0_), channel_id=1, source_target_pairs={{0,96},{8,104},{16,112},{24,120},{32,0},{40,8},{48,16},{56,24},{64... | collective-permute-start | bytes 2752520 | tf_op jit(solution)/shard_map/ppermute | solution.py:34
  39.7 4.0 %copy.67 = bf16[1,1,3,2,58,58,128]{6,5,4,3,2,1,0:T(8,128)(2,1)} copy(bf16[1,1,3,2,58,58,128]{6,3,5,4,2,1,0:T(2,128)(2,1)S(1)} %copy-done.7) | data formatting | bytes 10334208 | tf_op jit(solution)/shard_map/optimization_barrier | solution.py:491
  49.3 4.1 %collective-permute-done.10.refs_0_.refs_4_.refs_1_ = bf16[112,32,128]{2,1,0:T(8,128)(2,1)S(1)} collective-permute-done((bf16[112,32,128]{2,1,0:T(8,128)(2,1)}, bf16[112,32,128]{2,1,0:T(8,128)(2,1)S(1)}, u32[]{:S(2)}, u32[]{:S(2)}) %collective-permute-start.10) | collective-permute-done | bytes 917536 | tf_op jit(solution)/shard_map/ppermute | solution.py:34
  53.5 2.7 %collective-permute-done.12.refs_2_.refs_9_.refs_1_ = bf16[112,32,128]{2,1,0:T(8,128)(2,1)S(1)} collective-permute-done((bf16[112,32,128]{2,1,0:T(8,128)(2,1)}, bf16[112,32,128]{2,1,0:T(8,128)(2,1)S(1)}, u32[]{:S(2)}, u32[]{:S(2)}) %collective-permute-start.12) | collective-permute-done | bytes 917536 | tf_op jit(solution)/shard_map/ppermute | solution.py:34
  56.1 3.0 %halves.1 = (bf16[56,32,128]{2,1,0:T(8,128)(2,1)}, bf16[56,32,128]{2,1,0:T(8,128)(2,1)}, bf16[56,32,128]{2,1,0:T(8,128)(2,1)}, bf16[56,32,128]{2,1,0:T(8,128)(2,1)}) custom-call(bf16[112,32,128]{2,1,0:T(8,128)(2,1)S(1)} %collective-permute-done.10.refs_0_.refs_4_.refs_1_, bf16[112,32,128]{2,1,0:T(8,128)(2,1)S(1)} %collective-permute-done.11.refs_1_.refs_5_.refs_2_, ...), custom_call_target="tpu_custom_call" | custom-call | tf_op jit(solution)/shard_map/halves/pallas_call | solution.py:69
  59.2 3.2 %collective-permute-start.15 = (bf16[56,32,128]{2,1,0:T(8,128)(2,1)}, bf16[56,32,128]{2,1,0:T(8,128)(2,1)}, u32[]{:S(2)}, u32[]{:S(2)}) collective-permute-start(bf16[56,32,128]{2,1,0:T(8,128)(2,1)} %get-tuple-element.60), channel_id=1, source_target_pairs={{0,24},{8,0},{16,8},{24,16},{32,56},{40,32},{48,40},{56,48},{64,88... | collective-permute-start | bytes 1376264 | tf_op jit(solution)/shard_map/ppermute | solution.py:34
  63.1 2.6 %collective-permute-start.17 = (bf16[56,32,128]{2,1,0:T(8,128)(2,1)}, bf16[56,32,128]{2,1,0:T(8,128)(2,1)}, u32[]{:S(2)}, u32[]{:S(2)}) collective-permute-start(bf16[56,32,128]{2,1,0:T(8,128)(2,1)} %get-tuple-element.65), channel_id=1, source_target_pairs={{0,96},{8,104},{16,112},{24,120},{32,0},{40,8},{48,16},{56,24},{64... | collective-permute-start | bytes 1376264 | tf_op jit(solution)/shard_map/ppermute | solution.py:34
  65.7 4.0 %collective-permute-done.14.refs_6_.refs_3_ = bf16[56,32,128]{2,1,0:T(8,128)(2,1)S(1)} collective-permute-done((bf16[56,32,128]{2,1,0:T(8,128)(2,1)}, bf16[56,32,128]{2,1,0:T(8,128)(2,1)S(1)}, u32[]{:S(2)}, u32[]{:S(2)}) %collective-permute-start.14) | collective-permute-done | bytes 458784 | tf_op jit(solution)/shard_map/ppermute | solution.py:34
  69.7 2.8 %collective-permute-done.16.refs_11_.refs_3_ = bf16[56,32,128]{2,1,0:T(8,128)(2,1)} collective-permute-done((bf16[56,32,128]{2,1,0:T(8,128)(2,1)}, bf16[56,32,128]{2,1,0:T(8,128)(2,1)}, u32[]{:S(2)}, u32[]{:S(2)}) %collective-permute-start.16) | collective-permute-done | bytes 458784 | tf_op jit(solution)/shard_map/ppermute | solution.py:34
  72.5 3.7 %margins.1 = (bf16[3,58,16,128]{3,2,1,0:T(8,128)(2,1)}, bf16[3,58,16,128]{3,2,1,0:T(8,128)(2,1)}, bf16[3,58,16,128]{3,2,1,0:T(8,128)(2,1)}, bf16[3,58,16,128]{3,2,1,0:T(8,128)(2,1)}) custom-call(s32[1]{0:T(128)} %bitcast.16.refs_0_.me, s32[3]{0:T(128)S(1)} %collective-permute-done.4.refs_1_, s32[3]{0:T(128)S(1)} %collective-permute-done.5.refs_2_, ...), custom_call_target="tpu_custom_call" | custom-call | tf_op jit(solution)/shard_map/margins/pallas_call | solution.py:176
  78.1 3.6 %collective-permute-start.21 = (bf16[3,58,16,128]{3,2,1,0:T(8,128)(2,1)}, bf16[3,58,16,128]{3,2,1,0:T(8,128)(2,1)S(1)}, u32[]{:S(2)}, u32[]{:S(2)}) collective-permute-start(bf16[3,58,16,128]{3,2,1,0:T(8,128)(2,1)} %get-tuple-element.76), channel_id=1, source_target_pairs={{1,0},{2,1},{3,2},{4,3},{5,4},{6,5},{7,6},{9,8},{10,9},{11,10},{12... | collective-permute-start | bytes 2138120 | tf_op jit(solution)/shard_map/ppermute | solution.py:506
  83.8 3.6 %collective-permute-start.19 = (bf16[3,58,16,128]{3,2,1,0:T(8,128)(2,1)}, bf16[3,58,16,128]{3,2,1,0:T(8,128)(2,1)}, u32[]{:S(2)}, u32[]{:S(2)}) collective-permute-start(bf16[3,58,16,128]{3,2,1,0:T(8,128)(2,1)} %get-tuple-element.67), channel_id=1, source_target_pairs={{1,0},{2,1},{3,2},{4,3},{5,4},{6,5},{7,6},{9,8},{10,9},{11,10},{12... | collective-permute-start | bytes 2138120 | tf_op jit(solution)/shard_map/ppermute | solution.py:506
  91.7 19.3 %jobs.3 = s16[16,3,56,128]{3,2,1,0:T(8,128)(2,1)} custom-call(s32[1]{0:T(128)} %bitcast.16.refs_0_.me, s32[3]{0:T(128)S(1)} %bitcast.46, s32[3]{0:T(128)S(1)} %bitcast.41, f32[6]{0:T(128)S(1)} %copy-done.4, f32[6]{0:T(128)S(1)} %multiply_add_fusion.logs, bf16[112,32,128]{2,1,0:T(8,128)(2,1)} %constant_dynamic-update-slice_fusion.5.refs_8_.refs_0_, ...), custom_call_target="tpu_custom_call" | custom-call | flops 23624417280 | bytes 7077888 | tf_op jit(solution)/shard_map/jobs/pallas_call | solution.py:345
  110.9 4.7 %all-to-all-start.1 = ((s16[16,3,56,128]{3,2,1,0:T(8,128)(2,1)}), s16[16,3,56,128]{3,2,1,0:T(8,128)(2,1)S(1)}, u32[]{:S(2)}, u32[]{:S(2)}) async-start(s16[16,3,56,128]{3,2,1,0:T(8,128)(2,1)} %jobs.3), calls=%async_computation.1 | async-start | bytes 1376256 | tf_op jit(solution)/shard_map/all_to_all | solution.py:520
  116.5 19.3 %jobs.2 = s16[16,3,56,128]{3,2,1,0:T(8,128)(2,1)} custom-call(s32[1]{0:T(128)} %bitcast.16.refs_0_.me, s32[3]{0:T(128)S(1)} %bitcast.47, s32[3]{0:T(128)S(1)} %bitcast.42, f32[6]{0:T(128)S(1)} %copy-done.4, f32[6]{0:T(128)S(1)} %multiply_add_fusion.logs, bf16[112,32,128]{2,1,0:T(8,128)(2,1)} %constant_dynamic-update-slice_fusion.refs_3_.refs_0_, ...), custom_call_target="tpu_custom_call" | custom-call | flops 23624417280 | bytes 7077888 | tf_op jit(solution)/shard_map/jobs/pallas_call | solution.py:345
  135.9 7.3 %all-to-all-start = ((s16[16,3,56,128]{3,2,1,0:T(8,128)(2,1)}), s16[16,3,56,128]{3,2,1,0:T(8,128)(2,1)S(1)}, u32[]{:S(2)}, u32[]{:S(2)}) async-start(s16[16,3,56,128]{3,2,1,0:T(8,128)(2,1)} %jobs.2), calls=%async_computation | async-start | bytes 1376256 | tf_op jit(solution)/shard_map/all_to_all | solution.py:520
  147.9 10.0 %all-to-all-done.refs_0_ = s16[16,3,56,128]{3,2,1,0:T(8,128)(2,1)S(1)} async-done(((s16[16,3,56,128]{3,2,1,0:T(8,128)(2,1)}), s16[16,3,56,128]{3,2,1,0:T(8,128)(2,1)S(1)}, u32[]{:S(2)}, u32[]{:S(2)}) %all-to-all-start) | async-done | bytes 688160 | tf_op jit(solution)/shard_map/all_to_all | solution.py:520
  157.9 2.3 %add_up.1 = s16[16,2,56,128]{3,2,1,0:T(8,128)(2,1)} custom-call(s32[48]{0:T(128)S(1)} %reshape.391.owners, s32[48]{0:T(128)S(1)} %reshape.392.views, f32[6]{0:T(128)S(1)} %multiply_add_fusion.logs, s16[16,3,56,128]{3,2,1,0:T(8,128)(2,1)S(1)} %all-to-all-done.refs_0_, s16[16,3,56,128]{3,2,1,0:T(8,128)(2,1)S(1)} %all-to-all-done.1.refs_1_), custom_call_target="tpu_custom_call" | custom-call | tf_op jit(solution)/shard_map/add_up/pallas_call | solution.py:436
  160.1 3.6 %all-to-all-start.2 = ((s16[16,2,56,128]{3,2,1,0:T(8,128)(2,1)}), s16[16,2,56,128]{3,2,1,0:T(8,128)(2,1)S(1)}, u32[]{:S(2)}, u32[]{:S(2)}) async-start(s16[16,2,56,128]{3,2,1,0:T(8,128)(2,1)} %add_up.1), calls=%async_computation.2 | async-start | bytes 917504 | tf_op jit(solution)/shard_map/all_to_all | solution.py:521
  163.8 11.2 %all-to-all-done.2.total = s16[16,2,56,128]{3,2,1,0:T(8,128)(2,1)S(1)} async-done(((s16[16,2,56,128]{3,2,1,0:T(8,128)(2,1)}), s16[16,2,56,128]{3,2,1,0:T(8,128)(2,1)S(1)}, u32[]{:S(2)}, u32[]{:S(2)}) %all-to-all-start.2) | async-done | bytes 458784 | tf_op jit(solution)/shard_map/all_to_all | solution.py:521
  (147 shorter events, 45.6 us)
Async XLA Ops:
  3.2 14.9 %collective-permute-start = (bf16[28,32,128]{2,1,0:T(8,128)(2,1)S(1)}, bf16[28,32,128]{2,1,0:T(8,128)(2,1)S(1)}, u32[]{:S(2)}, u32[]{:S(2)}) collective-permute-start(bf16[28,32,128]{2,1,0:T(8,128)(2,1)S(1)} %get-tuple-element.41), channel_id=1, source_target_pairs={{0,32},{8,40},{16,48},{24,56},{32,64},{40,72},{48,80},{56,88},{64,... | collective-permute-start | bytes 688136 | tf_op jit(solution)/shard_map/ppermute | solution.py:34
  4.8 13.3 %collective-permute-start.1 = (bf16[28,32,128]{2,1,0:T(8,128)(2,1)S(1)}, bf16[28,32,128]{2,1,0:T(8,128)(2,1)S(1)}, u32[]{:S(2)}, u32[]{:S(2)}) collective-permute-start(bf16[28,32,128]{2,1,0:T(8,128)(2,1)S(1)} %get-tuple-element.41), channel_id=1, source_target_pairs={{0,96},{8,104},{16,112},{24,120},{32,0},{40,8},{48,16},{56,24},{64... | collective-permute-start | bytes 688136 | tf_op jit(solution)/shard_map/ppermute | solution.py:34
  6.5 11.6 %collective-permute-start.2 = (bf16[28,32,128]{2,1,0:T(8,128)(2,1)S(1)}, bf16[28,32,128]{2,1,0:T(8,128)(2,1)S(1)}, u32[]{:S(2)}, u32[]{:S(2)}) collective-permute-start(bf16[28,32,128]{2,1,0:T(8,128)(2,1)S(1)} %get-tuple-element.44), channel_id=1, source_target_pairs={{0,8},{8,16},{16,24},{24,0},{32,40},{40,48},{48,56},{56,32},{64,72... | collective-permute-start | bytes 688136 | tf_op jit(solution)/shard_map/ppermute | solution.py:34
  8.1 10.0 %collective-permute-start.3 = (bf16[28,32,128]{2,1,0:T(8,128)(2,1)S(1)}, bf16[28,32,128]{2,1,0:T(8,128)(2,1)S(1)}, u32[]{:S(2)}, u32[]{:S(2)}) collective-permute-start(bf16[28,32,128]{2,1,0:T(8,128)(2,1)S(1)} %get-tuple-element.44), channel_id=1, source_target_pairs={{0,24},{8,0},{16,8},{24,16},{32,56},{40,32},{48,40},{56,48},{64,88... | collective-permute-start | bytes 688136 | tf_op jit(solution)/shard_map/ppermute | solution.py:34
  13.0 5.1 %collective-permute-start.5 = (s32[3]{0:T(128)S(1)}, s32[3]{0:T(128)S(1)}, u32[]{:S(2)}, u32[]{:S(2)}) collective-permute-start(s32[3]{0:T(128)S(1)} %bitcast.44), channel_id=1, source_target_pairs={{0,1},{1,2},{2,3},{3,4},{4,5},{5,6},{6,7},{8,9},{9,10},{10,11},{11... | collective-permute-start | bytes 44 | tf_op jit(solution)/shard_map/ppermute | solution.py:488
  21.0 7.4 %collective-permute-start.8 = (bf16[14,32,128]{2,1,0:T(8,128)(2,1)S(1)}, bf16[14,32,128]{2,1,0:T(8,128)(2,1)S(1)}, u32[]{:S(2)}, u32[]{:S(2)}) collective-permute-start(bf16[14,32,128]{2,1,0:T(8,128)(2,1)S(1)} %slice.63), channel_id=1, source_target_pairs={{0,8},{8,16},{16,24},{24,0},{32,40},{40,48},{48,56},{56,32},{64,72... | collective-permute-start | bytes 344072 | tf_op jit(solution)/shard_map/ppermute | solution.py:34
  21.4 7.7 %collective-permute-start.9 = (bf16[14,32,128]{2,1,0:T(8,128)(2,1)S(1)}, bf16[14,32,128]{2,1,0:T(8,128)(2,1)S(1)}, u32[]{:S(2)}, u32[]{:S(2)}) collective-permute-start(bf16[14,32,128]{2,1,0:T(8,128)(2,1)S(1)} %slice.64), channel_id=1, source_target_pairs={{0,24},{8,0},{16,8},{24,16},{32,56},{40,32},{48,40},{56,48},{64,88... | collective-permute-start | bytes 344072 | tf_op jit(solution)/shard_map/ppermute | solution.py:34
  24.3 6.0 %collective-permute-start.6 = (bf16[14,32,128]{2,1,0:T(8,128)(2,1)S(1)}, bf16[14,32,128]{2,1,0:T(8,128)(2,1)S(1)}, u32[]{:S(2)}, u32[]{:S(2)}) collective-permute-start(bf16[14,32,128]{2,1,0:T(8,128)(2,1)S(1)} %slice.61), channel_id=1, source_target_pairs={{0,32},{8,40},{16,48},{24,56},{32,64},{40,72},{48,80},{56,88},{64,... | collective-permute-start | bytes 344072 | tf_op jit(solution)/shard_map/ppermute | solution.py:34
  24.6 6.4 %collective-permute-start.7 = (bf16[14,32,128]{2,1,0:T(8,128)(2,1)S(1)}, bf16[14,32,128]{2,1,0:T(8,128)(2,1)S(1)}, u32[]{:S(2)}, u32[]{:S(2)}) collective-permute-start(bf16[14,32,128]{2,1,0:T(8,128)(2,1)S(1)} %slice.62), channel_id=1, source_target_pairs={{0,96},{8,104},{16,112},{24,120},{32,0},{40,8},{48,16},{56,24},{64... | collective-permute-start | bytes 344072 | tf_op jit(solution)/shard_map/ppermute | solution.py:34
  31.6 21.8 %collective-permute-start.10 = (bf16[112,32,128]{2,1,0:T(8,128)(2,1)}, bf16[112,32,128]{2,1,0:T(8,128)(2,1)S(1)}, u32[]{:S(2)}, u32[]{:S(2)}) collective-permute-start(bf16[112,32,128]{2,1,0:T(8,128)(2,1)} %constant_dynamic-update-slice_fusion.refs_3_.refs_0_), channel_id=1, source_target_pairs={{0,8},{8,16},{16,24},{24,0},{32,40},{40,48},{48,56},{56,32},{64,72... | collective-permute-start | bytes 2752520 | tf_op jit(solution)/shard_map/ppermute | solution.py:34
  31.6 21.8 %collective-permute-start.11 = (bf16[112,32,128]{2,1,0:T(8,128)(2,1)}, bf16[112,32,128]{2,1,0:T(8,128)(2,1)S(1)}, u32[]{:S(2)}, u32[]{:S(2)}) collective-permute-start(bf16[112,32,128]{2,1,0:T(8,128)(2,1)} %constant_dynamic-update-slice_fusion.refs_3_.refs_0_), channel_id=1, source_target_pairs={{0,24},{8,0},{16,8},{24,16},{32,56},{40,32},{48,40},{56,48},{64,88... | collective-permute-start | bytes 2752520 | tf_op jit(solution)/shard_map/ppermute | solution.py:34
  34.9 21.3 %collective-permute-start.12 = (bf16[112,32,128]{2,1,0:T(8,128)(2,1)}, bf16[112,32,128]{2,1,0:T(8,128)(2,1)S(1)}, u32[]{:S(2)}, u32[]{:S(2)}) collective-permute-start(bf16[112,32,128]{2,1,0:T(8,128)(2,1)} %constant_dynamic-update-slice_fusion.5.refs_8_.refs_0_), channel_id=1, source_target_pairs={{0,32},{8,40},{16,48},{24,56},{32,64},{40,72},{48,80},{56,88},{64,... | collective-permute-start | bytes 2752520 | tf_op jit(solution)/shard_map/ppermute | solution.py:34
  34.9 21.3 %collective-permute-start.13 = (bf16[112,32,128]{2,1,0:T(8,128)(2,1)}, bf16[112,32,128]{2,1,0:T(8,128)(2,1)}, u32[]{:S(2)}, u32[]{:S(2)}) collective-permute-start(bf16[112,32,128]{2,1,0:T(8,128)(2,1)} %constant_dynamic-update-slice_fusion.5.refs_8_.refs_0_), channel_id=1, source_target_pairs={{0,96},{8,104},{16,112},{24,120},{32,0},{40,8},{48,16},{56,24},{64... | collective-permute-start | bytes 2752520 | tf_op jit(solution)/shard_map/ppermute | solution.py:34
  59.1 10.6 %collective-permute-start.14 = (bf16[56,32,128]{2,1,0:T(8,128)(2,1)}, bf16[56,32,128]{2,1,0:T(8,128)(2,1)S(1)}, u32[]{:S(2)}, u32[]{:S(2)}) collective-permute-start(bf16[56,32,128]{2,1,0:T(8,128)(2,1)} %get-tuple-element.59), channel_id=1, source_target_pairs={{0,8},{8,16},{16,24},{24,0},{32,40},{40,48},{48,56},{56,32},{64,72... | collective-permute-start | bytes 1376264 | tf_op jit(solution)/shard_map/ppermute | solution.py:34
  59.2 10.5 %collective-permute-start.15 = (bf16[56,32,128]{2,1,0:T(8,128)(2,1)}, bf16[56,32,128]{2,1,0:T(8,128)(2,1)}, u32[]{:S(2)}, u32[]{:S(2)}) collective-permute-start(bf16[56,32,128]{2,1,0:T(8,128)(2,1)} %get-tuple-element.60), channel_id=1, source_target_pairs={{0,24},{8,0},{16,8},{24,16},{32,56},{40,32},{48,40},{56,48},{64,88... | collective-permute-start | bytes 1376264 | tf_op jit(solution)/shard_map/ppermute | solution.py:34
  62.5 10.1 %collective-permute-start.16 = (bf16[56,32,128]{2,1,0:T(8,128)(2,1)}, bf16[56,32,128]{2,1,0:T(8,128)(2,1)}, u32[]{:S(2)}, u32[]{:S(2)}) collective-permute-start(bf16[56,32,128]{2,1,0:T(8,128)(2,1)} %get-tuple-element.64), channel_id=1, source_target_pairs={{0,32},{8,40},{16,48},{24,56},{32,64},{40,72},{48,80},{56,88},{64,... | collective-permute-start | bytes 1376264 | tf_op jit(solution)/shard_map/ppermute | solution.py:34
  63.1 9.4 %collective-permute-start.17 = (bf16[56,32,128]{2,1,0:T(8,128)(2,1)}, bf16[56,32,128]{2,1,0:T(8,128)(2,1)}, u32[]{:S(2)}, u32[]{:S(2)}) collective-permute-start(bf16[56,32,128]{2,1,0:T(8,128)(2,1)} %get-tuple-element.65), channel_id=1, source_target_pairs={{0,96},{8,104},{16,112},{24,120},{32,0},{40,8},{48,16},{56,24},{64... | collective-permute-start | bytes 1376264 | tf_op jit(solution)/shard_map/ppermute | solution.py:34
  76.2 12.7 %collective-permute-start.20 = (bf16[3,58,16,128]{3,2,1,0:T(8,128)(2,1)}, bf16[3,58,16,128]{3,2,1,0:T(8,128)(2,1)S(1)}, u32[]{:S(2)}, u32[]{:S(2)}) collective-permute-start(bf16[3,58,16,128]{3,2,1,0:T(8,128)(2,1)} %get-tuple-element.75), channel_id=1, source_target_pairs={{0,1},{1,2},{2,3},{3,4},{4,5},{5,6},{6,7},{8,9},{9,10},{10,11},{11... | collective-permute-start | bytes 2138120 | tf_op jit(solution)/shard_map/ppermute | solution.py:506
  78.1 12.7 %collective-permute-start.21 = (bf16[3,58,16,128]{3,2,1,0:T(8,128)(2,1)}, bf16[3,58,16,128]{3,2,1,0:T(8,128)(2,1)S(1)}, u32[]{:S(2)}, u32[]{:S(2)}) collective-permute-start(bf16[3,58,16,128]{3,2,1,0:T(8,128)(2,1)} %get-tuple-element.76), channel_id=1, source_target_pairs={{1,0},{2,1},{3,2},{4,3},{5,4},{6,5},{7,6},{9,8},{10,9},{11,10},{12... | collective-permute-start | bytes 2138120 | tf_op jit(solution)/shard_map/ppermute | solution.py:506
  81.8 33.8 %collective-permute-start.18 = (bf16[3,58,16,128]{3,2,1,0:T(8,128)(2,1)}, bf16[3,58,16,128]{3,2,1,0:T(8,128)(2,1)S(1)}, u32[]{:S(2)}, u32[]{:S(2)}) collective-permute-start(bf16[3,58,16,128]{3,2,1,0:T(8,128)(2,1)} %get-tuple-element.66), channel_id=1, source_target_pairs={{0,1},{1,2},{2,3},{3,4},{4,5},{5,6},{6,7},{8,9},{9,10},{10,11},{11... | collective-permute-start | bytes 2138120 | tf_op jit(solution)/shard_map/ppermute | solution.py:506
  83.8 31.9 %collective-permute-start.19 = (bf16[3,58,16,128]{3,2,1,0:T(8,128)(2,1)}, bf16[3,58,16,128]{3,2,1,0:T(8,128)(2,1)}, u32[]{:S(2)}, u32[]{:S(2)}) collective-permute-start(bf16[3,58,16,128]{3,2,1,0:T(8,128)(2,1)} %get-tuple-element.67), channel_id=1, source_target_pairs={{1,0},{2,1},{3,2},{4,3},{5,4},{6,5},{7,6},{9,8},{10,9},{11,10},{12... | collective-permute-start | bytes 2138120 | tf_op jit(solution)/shard_map/ppermute | solution.py:506
  110.9 24.9 %all-to-all-start.1 = ((s16[16,3,56,128]{3,2,1,0:T(8,128)(2,1)}), s16[16,3,56,128]{3,2,1,0:T(8,128)(2,1)S(1)}, u32[]{:S(2)}, u32[]{:S(2)}) async-start(s16[16,3,56,128]{3,2,1,0:T(8,128)(2,1)} %jobs.3), calls=%async_computation.1 | async-start | bytes 1376256 | tf_op jit(solution)/shard_map/all_to_all | solution.py:520
  135.9 22.0 %all-to-all-start = ((s16[16,3,56,128]{3,2,1,0:T(8,128)(2,1)}), s16[16,3,56,128]{3,2,1,0:T(8,128)(2,1)S(1)}, u32[]{:S(2)}, u32[]{:S(2)}) async-start(s16[16,3,56,128]{3,2,1,0:T(8,128)(2,1)} %jobs.2), calls=%async_computation | async-start | bytes 1376256 | tf_op jit(solution)/shard_map/all_to_all | solution.py:520
  160.1 14.9 %all-to-all-start.2 = ((s16[16,2,56,128]{3,2,1,0:T(8,128)(2,1)}), s16[16,2,56,128]{3,2,1,0:T(8,128)(2,1)S(1)}, u32[]{:S(2)}, u32[]{:S(2)}) async-start(s16[16,2,56,128]{3,2,1,0:T(8,128)(2,1)} %add_up.1), calls=%async_computation.2 | async-start | bytes 917504 | tf_op jit(solution)/shard_map/all_to_all | solution.py:521
  (15 other events, 243.6 us)

commit v7 on v6

--- a/solution.py
+++ b/solution.py
@@ -22,7 +22,7 @@
 
 
 def gathered_memory(parts):
-    return [parts[0]] + far_memory(*parts[1:])
+    return far_memory(*parts)
 
 
 def torus_step(array, dx, dy):
@@ -43,6 +43,49 @@
         [a, torus_step(a, *along(ax, 1)), torus_step(a, *along(ax, -1))]
         for a, ax in zip(arrays, axes)
     ]
+
+
+def ring_whole(arrays, axes):
+    return [
+        [a] + [torus_step(a, *along(ax, d)) for d in (1, -1, 2)] for a, ax in zip(arrays, axes)
+    ]
+
+
+def join_kernel(*refs):
+    stage, sems, refs = refs[-2], refs[-1], refs[:-2]
+    outs, refs = refs[-2:], refs[:-2]
+    each = len(refs) // len(outs)
+    rows = refs[0].shape[0]
+    ins = []
+    for i, ref in enumerate(refs):
+        target = stage.at[i // each, pl.ds(i % each * rows, rows)]
+        ins.append(pltpu.make_async_copy(ref, target, sems.at[i]))
+        ins[i].start()
+    sends = []
+    for i, out in enumerate(outs):
+        for copy in ins[i * each : (i + 1) * each]:
+            copy.wait()
+        sends.append(pltpu.make_async_copy(stage.at[i], out, sems.at[len(refs) + i]))
+        sends[i].start()
+    for send in sends:
+        send.wait()
+
+
+def join(rings):
+    arrays = [a for ring in rings for a in ring]
+    whole = (len(rings[0]) * arrays[0].shape[0],) + arrays[0].shape[1:]
+    return pl.pallas_call(
+        join_kernel,
+        in_specs=[pl.BlockSpec(memory_space=pl.ANY)] * len(arrays),
+        out_specs=[pl.BlockSpec(memory_space=pltpu.HBM)] * len(rings),
+        out_shape=[pltpu.HBM(whole, BF16)] * len(rings),
+        scratch_shapes=[
+            pltpu.VMEM((len(rings),) + whole, BF16),
+            pltpu.SemaphoreType.DMA((len(arrays) + len(rings),)),
+        ],
+        compiler_params=pltpu.CompilerParams(vmem_limit_bytes=4 << 20),
+        name="join",
+    )(*arrays)
 
 
 def halves_kernel(*refs):
@@ -86,15 +129,6 @@
         [*n, torus_step(low, *along(ax, 1)), torus_step(high, *along(ax, -1))]
         for n, (low, high), ax in zip(near, take_halves(near), axes)
     ]
-
-
-def ring_far(near, axes):
-    result = []
-    for (own, lower, upper), ax in zip(near, axes):
-        half = lower.shape[0] // 2
-        far = [torus_step(lower[:half], *along(ax, 1)), torus_step(upper[half:], *along(ax, -1))]
-        result.append([own, lower, upper, *far])
-    return result
 
 
 def rank(delta):
@@ -365,7 +399,7 @@
             bytes_accessed=slots * (2 * WIN * PADW * 128 * 2 + 16 * 2 * SIDE * 128 * 4),
         ),
         name="jobs",
-    )(*scalars, *gathered_memory(parts), *far_memory(top, bottom, view_data, *mats))
+    )(*scalars, *gathered_memory(parts), top, bottom, *far_memory(view_data, *mats))
 
 
 def bands(taps, positions_out, positions_in):
@@ -479,15 +513,11 @@
     slots = bricks.shape[0]
 
     wire = estimate.astype(BF16).transpose(0, 2, 1, 3)
-    jobs = jnp.concatenate([bricks, views])
+    jobs = lax.optimization_barrier(jnp.concatenate([bricks, views]))
     note = jnp.pad(jobs.astype(BF16)[None, None], ((0, 0), (0, SIDE - 1), (0, 128 - 2 * slots)))
     note = jnp.broadcast_to(note, (wire.shape[0],) + note.shape[1:])
     wire = jnp.concatenate([wire[:, :, :RIM], note[:, :, None], wire[:, :, SIDE - RIM + 1 :]], axis=2)
-    near = ring_near([wire[0], wire[1]], (0, 1))
-    above = lax.ppermute(bricks, "view", downward)
-    below = lax.ppermute(bricks, "view", upward)
-    near, above, below = lax.optimization_barrier((near, above, below))
-    rings = [jnp.concatenate(parts, axis=0) for parts in ring_far(near, (0, 1))]
+    rings = join(ring_whole([wire[0], wire[1]], (0, 1)))
     rings, view_data, psf, views, bricks = lax.optimization_barrier(
         (rings, view_data, psf, views, bricks)
     )
@@ -498,7 +528,12 @@
     mats = job_matrices(taps, bricks)
     data = view_data[0, 0]
     logs = jnp.log2(jnp.maximum(4.0 / background * jnp.prod(jnp.sum(psf, axis=2), axis=1), 1e-30)) - 15.9
-    near, mats, data, logs = lax.optimization_barrier((near, mats, data, logs))
+    mats, bricks = lax.optimization_barrier((mats, bricks))
+    above = lax.ppermute(bricks, "view", downward)
+    below = lax.ppermute(bricks, "view", upward)
+    near, mats, data, above, below, logs = lax.optimization_barrier(
+        (near, mats, data, above, below, logs)
+    )
     gathered = ring_pass_on(near, (1, 0))
 
     rims = margins(gathered, me, above, below)

time: 178 us -> 175 us (0.983)
  local copies, waits for them, and re-layouts: 18.5 us -> 13 us
  starting transfers between devices: 58.6 us -> 55.1 us
  Pallas kernels: 48.3 us -> 51.7 us
  waiting for transfers between devices: 40.4 us -> 43.7 us
    unnamed x39 -> x23, local copies, waits for them, and re-layouts: 6.86 us -> 0.18 us
    pallas_call x0 -> x1, Pallas kernels: none -> 3.75 us  [join(): pl.pallas_call(join_kernel, in_specs=[pl.BlockSpec(memory_space=pl.ANY)]...]
    ppermute x16 -> x14, waiting for transfers between devices: 14.2 us -> 16.9 us  [torus_step(): return lax.ppermute(array, 'tile', pairs)]
    optimization_barrier x2, local copies, waits for them, and re-layouts: 4.01 us -> 6.47 us  [on_device(): lax.optimization_barrier((rings, view_data, psf, views, bricks))]
    ppermute x16 -> x14, starting transfers between devices: 26.2 us -> 24.3 us  [torus_step(): return lax.ppermute(array, 'tile', pairs)]
  transfers between devices with their start and end apart: 25 -> 23, of which waited for: 11 -> 10; matrix products, arithmetic and copies ran while one was open for 11% -> 11% of each run, Pallas kernels for 22% -> 22%
where the time goes in v7:
time: 175 us; the launch traced here: 174 us
  starting transfers between devices  55.1 us (31%)
  Pallas kernels  51.7 us (30%)
  waiting for transfers between devices  43.7 us (25%)
  local copies, waits for them, and re-layouts  13 us (7%)
  other arithmetic  10.3 us (6%)
    pallas_call x2, Pallas kernels, run_jobs(): pl.pallas_call(functools.partial(job_kernel, channel), grid=(slots,), in_...  38.2 us
    ppermute x14, starting transfers between devices, torus_step(): return lax.ppermute(array, 'tile', pairs)  24.3 us
    ppermute x14, waiting for transfers between devices, torus_step(): return lax.ppermute(array, 'tile', pairs)  16.9 us
    all_to_all x2, starting transfers between devices, on_device(): parts.append(lax.all_to_all(factors, 'tile', 0, 0, tiled=True))  11.7 us
    all_to_all x1, waiting for transfers between devices, on_device(): lax.all_to_all(add_up(owners, seen_by, logs, parts), 'tile', 0, 0, tiled=...  11.2 us
    all_to_all x2, waiting for transfers between devices, on_device(): parts.append(lax.all_to_all(factors, 'tile', 0, 0, tiled=True))  9.98 us
    ppermute x2, starting transfers between devices, on_device(): lax.ppermute(rims[2 * c + 1], 'view', downward)  7.46 us
    optimization_barrier x2, local copies, waits for them, and re-layouts, on_device(): lax.optimization_barrier((rings, view_data, psf, views, bricks))  6.47 us
  transfers between devices with their start and end apart: 23, of which 10 were waited for; matrix products, arithmetic and copies ran while one was open for 11% of the time, Pallas kernels for 22%

profile of v7, /device:TPU:32, one launch (start us, length us, event | category | flops | bytes accessed | tf_op | source)
XLA Modules:
  0.0 174.4 jit_solution(5945575462832866396)
XLA Ops:
  11.8 2.8 %collective-permute-start.5 = (bf16[28,32,128]{2,1,0:T(8,128)(2,1)S(1)}, bf16[28,32,128]{2,1,0:T(8,128)(2,1)S(1)}, u32[]{:S(2)}, u32[]{:S(2)}) collective-permute-start(bf16[28,32,128]{2,1,0:T(8,128)(2,1)S(1)} %get-tuple-element.85.refs_4_), channel_id=1, source_target_pairs={{0,16},{8,24},{16,0},{24,8},{32,48},{40,56},{48,32},{56,40},{64,80... | collective-permute-start | bytes 688136 | tf_op jit(solution)/shard_map/ppermute | solution.py:34
  17.2 4.5 %collective-permute-done.5.refs_7_ = bf16[28,32,128]{2,1,0:T(8,128)(2,1)S(1)} collective-permute-done((bf16[28,32,128]{2,1,0:T(8,128)(2,1)S(1)}, bf16[28,32,128]{2,1,0:T(8,128)(2,1)S(1)}, u32[]{:S(2)}, u32[]{:S(2)}) %collective-permute-start.5) | collective-permute-done | bytes 229408 | tf_op jit(solution)/shard_map/ppermute | solution.py:34
  21.6 3.8 %join.1 = (bf16[112,32,128]{2,1,0:T(8,128)(2,1)}, bf16[112,32,128]{2,1,0:T(8,128)(2,1)}) custom-call(bf16[28,32,128]{2,1,0:T(8,128)(2,1)S(1)} %get-tuple-element.86.refs_0_, bf16[28,32,128]{2,1,0:T(8,128)(2,1)S(1)} %collective-permute-done.refs_1_, bf16[28,32,128]{2,1,0:T(8,128)(2,1)S(1)} %collective-permute-done.1.refs_2_, ...), custom_call_target="tpu_custom_call" | custom-call | tf_op jit(solution)/shard_map/join/pallas_call | solution.py:77
  26.6 2.1 %collective-permute-start.7 = (bf16[112,32,128]{2,1,0:T(8,128)(2,1)}, bf16[112,32,128]{2,1,0:T(8,128)(2,1)S(1)}, u32[]{:S(2)}, u32[]{:S(2)}) collective-permute-start(bf16[112,32,128]{2,1,0:T(8,128)(2,1)} %get-tuple-element.60.refs_3_.refs_0_), channel_id=1, source_target_pairs={{0,24},{8,0},{16,8},{24,16},{32,56},{40,32},{48,40},{56,48},{64,88... | collective-permute-start | bytes 2752520 | tf_op jit(solution)/shard_map/ppermute | solution.py:34
  29.3 2.6 %collective-permute-start.9 = (bf16[112,32,128]{2,1,0:T(8,128)(2,1)}, bf16[112,32,128]{2,1,0:T(8,128)(2,1)}, u32[]{:S(2)}, u32[]{:S(2)}) collective-permute-start(bf16[112,32,128]{2,1,0:T(8,128)(2,1)} %get-tuple-element.69.refs_8_.refs_0_), channel_id=1, source_target_pairs={{0,96},{8,104},{16,112},{24,120},{32,0},{40,8},{48,16},{56,24},{64... | collective-permute-start | bytes 2752520 | tf_op jit(solution)/shard_map/ppermute | solution.py:34
  40.9 6.5 %copy.67 = bf16[1,1,3,2,58,58,128]{6,5,4,3,2,1,0:T(8,128)(2,1)} copy(bf16[1,1,3,2,58,58,128]{6,3,5,4,2,1,0:T(2,128)(2,1)} %param.8) | data formatting | bytes 10334208 | tf_op jit(solution)/shard_map/optimization_barrier | solution.py:521
  47.6 2.4 %collective-permute-start.11 = (s32[3]{0:T(128)S(1)}, s32[3]{0:T(128)S(1)}, u32[]{:S(2)}, u32[]{:S(2)}) collective-permute-start(s32[3]{0:T(128)S(1)} %bitcast.47), channel_id=1, source_target_pairs={{0,1},{1,2},{2,3},{3,4},{4,5},{5,6},{6,7},{8,9},{9,10},{10,11},{11... | collective-permute-start | bytes 44 | tf_op jit(solution)/shard_map/ppermute | solution.py:533
  50.0 2.4 %collective-permute-done.11.refs_2_ = s32[3]{0:T(128)S(1)} collective-permute-done((s32[3]{0:T(128)S(1)}, s32[3]{0:T(128)S(1)}, u32[]{:S(2)}, u32[]{:S(2)}) %collective-permute-start.11) | collective-permute-done | bytes 44 | tf_op jit(solution)/shard_map/ppermute | solution.py:533
  52.5 3.0 %halves.1 = (bf16[56,32,128]{2,1,0:T(8,128)(2,1)}, bf16[56,32,128]{2,1,0:T(8,128)(2,1)}, bf16[56,32,128]{2,1,0:T(8,128)(2,1)}, bf16[56,32,128]{2,1,0:T(8,128)(2,1)}) custom-call(bf16[112,32,128]{2,1,0:T(8,128)(2,1)S(1)} %collective-permute-done.6.refs_0_.refs_4_.refs_1_, bf16[112,32,128]{2,1,0:T(8,128)(2,1)S(1)} %collective-permute-done.7.refs_1_.refs_5_.refs_2_, ...), custom_call_target="tpu_custom_call" | custom-call | tf_op jit(solution)/shard_map/halves/pallas_call | solution.py:112
  55.6 3.2 %collective-permute-start.13 = (bf16[56,32,128]{2,1,0:T(8,128)(2,1)}, bf16[56,32,128]{2,1,0:T(8,128)(2,1)}, u32[]{:S(2)}, u32[]{:S(2)}) collective-permute-start(bf16[56,32,128]{2,1,0:T(8,128)(2,1)} %get-tuple-element.66), channel_id=1, source_target_pairs={{0,24},{8,0},{16,8},{24,16},{32,56},{40,32},{48,40},{56,48},{64,88... | collective-permute-start | bytes 1376264 | tf_op jit(solution)/shard_map/ppermute | solution.py:34
  58.8 3.2 %collective-permute-start.15 = (bf16[56,32,128]{2,1,0:T(8,128)(2,1)}, bf16[56,32,128]{2,1,0:T(8,128)(2,1)}, u32[]{:S(2)}, u32[]{:S(2)}) collective-permute-start(bf16[56,32,128]{2,1,0:T(8,128)(2,1)} %get-tuple-element.71), channel_id=1, source_target_pairs={{0,96},{8,104},{16,112},{24,120},{32,0},{40,8},{48,16},{56,24},{64... | collective-permute-start | bytes 1376264 | tf_op jit(solution)/shard_map/ppermute | solution.py:34
  62.1 7.2 %collective-permute-done.12.refs_6_.refs_3_ = bf16[56,32,128]{2,1,0:T(8,128)(2,1)S(1)} collective-permute-done((bf16[56,32,128]{2,1,0:T(8,128)(2,1)}, bf16[56,32,128]{2,1,0:T(8,128)(2,1)S(1)}, u32[]{:S(2)}, u32[]{:S(2)}) %collective-permute-start.12) | collective-permute-done | bytes 458784 | tf_op jit(solution)/shard_map/ppermute | solution.py:34
  69.2 2.8 %collective-permute-done.14.refs_11_.refs_3_ = bf16[56,32,128]{2,1,0:T(8,128)(2,1)} collective-permute-done((bf16[56,32,128]{2,1,0:T(8,128)(2,1)}, bf16[56,32,128]{2,1,0:T(8,128)(2,1)}, u32[]{:S(2)}, u32[]{:S(2)}) %collective-permute-start.14) | collective-permute-done | bytes 458784 | tf_op jit(solution)/shard_map/ppermute | solution.py:34
  72.0 3.7 %margins.1 = (bf16[3,58,16,128]{3,2,1,0:T(8,128)(2,1)}, bf16[3,58,16,128]{3,2,1,0:T(8,128)(2,1)}, bf16[3,58,16,128]{3,2,1,0:T(8,128)(2,1)}, bf16[3,58,16,128]{3,2,1,0:T(8,128)(2,1)}) custom-call(s32[1]{0:T(128)} %bitcast.17.refs_0_.me, s32[3]{0:T(128)S(1)} %collective-permute-done.10.refs_1_, s32[3]{0:T(128)S(1)} %collective-permute-done.11.refs_2_, ...), custom_call_target="tpu_custom_call" | custom-call | tf_op jit(solution)/shard_map/margins/pallas_call | solution.py:210
  77.6 3.6 %collective-permute-start.19 = (bf16[3,58,16,128]{3,2,1,0:T(8,128)(2,1)}, bf16[3,58,16,128]{3,2,1,0:T(8,128)(2,1)S(1)}, u32[]{:S(2)}, u32[]{:S(2)}) collective-permute-start(bf16[3,58,16,128]{3,2,1,0:T(8,128)(2,1)} %get-tuple-element.82), channel_id=1, source_target_pairs={{1,0},{2,1},{3,2},{4,3},{5,4},{6,5},{7,6},{9,8},{10,9},{11,10},{12... | collective-permute-start | bytes 2138120 | tf_op jit(solution)/shard_map/ppermute | solution.py:541
  83.2 3.8 %collective-permute-start.17 = (bf16[3,58,16,128]{3,2,1,0:T(8,128)(2,1)}, bf16[3,58,16,128]{3,2,1,0:T(8,128)(2,1)S(1)}, u32[]{:S(2)}, u32[]{:S(2)}) collective-permute-start(bf16[3,58,16,128]{3,2,1,0:T(8,128)(2,1)} %get-tuple-element.73), channel_id=1, source_target_pairs={{1,0},{2,1},{3,2},{4,3},{5,4},{6,5},{7,6},{9,8},{10,9},{11,10},{12... | collective-permute-start | bytes 2138120 | tf_op jit(solution)/shard_map/ppermute | solution.py:541
  90.3 19.1 %jobs.3 = s16[16,3,56,128]{3,2,1,0:T(8,128)(2,1)} custom-call(s32[1]{0:T(128)} %bitcast.17.refs_0_.me, s32[3]{0:T(128)S(1)} %bitcast.48, s32[3]{0:T(128)S(1)} %bitcast.42, f32[6]{0:T(128)S(1)} %copy-done.4, f32[6]{0:T(128)S(1)} %multiply_add_fusion.logs, bf16[112,32,128]{2,1,0:T(8,128)(2,1)} %get-tuple-element.69.refs_8_.refs_0_, ...), custom_call_target="tpu_custom_call" | custom-call | flops 23624417280 | bytes 7077888 | tf_op jit(solution)/shard_map/jobs/pallas_call | solution.py:379
  109.4 4.3 %all-to-all-start.1 = ((s16[16,3,56,128]{3,2,1,0:T(8,128)(2,1)}), s16[16,3,56,128]{3,2,1,0:T(8,128)(2,1)S(1)}, u32[]{:S(2)}, u32[]{:S(2)}) async-start(s16[16,3,56,128]{3,2,1,0:T(8,128)(2,1)} %jobs.3), calls=%async_computation.1 | async-start | bytes 1376256 | tf_op jit(solution)/shard_map/all_to_all | solution.py:555
  113.8 19.1 %jobs.2 = s16[16,3,56,128]{3,2,1,0:T(8,128)(2,1)} custom-call(s32[1]{0:T(128)} %bitcast.17.refs_0_.me, s32[3]{0:T(128)S(1)} %bitcast.49, s32[3]{0:T(128)S(1)} %bitcast.43, f32[6]{0:T(128)S(1)} %copy-done.4, f32[6]{0:T(128)S(1)} %multiply_add_fusion.logs, bf16[112,32,128]{2,1,0:T(8,128)(2,1)} %get-tuple-element.60.refs_3_.refs_0_, ...), custom_call_target="tpu_custom_call" | custom-call | flops 23624417280 | bytes 7077888 | tf_op jit(solution)/shard_map/jobs/pallas_call | solution.py:379
  132.9 7.4 %all-to-all-start = ((s16[16,3,56,128]{3,2,1,0:T(8,128)(2,1)}), s16[16,3,56,128]{3,2,1,0:T(8,128)(2,1)S(1)}, u32[]{:S(2)}, u32[]{:S(2)}) async-start(s16[16,3,56,128]{3,2,1,0:T(8,128)(2,1)} %jobs.2), calls=%async_computation | async-start | bytes 1376256 | tf_op jit(solution)/shard_map/all_to_all | solution.py:555
  145.0 10.0 %all-to-all-done.refs_0_ = s16[16,3,56,128]{3,2,1,0:T(8,128)(2,1)S(1)} async-done(((s16[16,3,56,128]{3,2,1,0:T(8,128)(2,1)}), s16[16,3,56,128]{3,2,1,0:T(8,128)(2,1)S(1)}, u32[]{:S(2)}, u32[]{:S(2)}) %all-to-all-start) | async-done | bytes 688160 | tf_op jit(solution)/shard_map/all_to_all | solution.py:555
  154.9 2.3 %add_up.1 = s16[16,2,56,128]{3,2,1,0:T(8,128)(2,1)} custom-call(s32[48]{0:T(128)S(1)} %reshape.366.owners, s32[48]{0:T(128)S(1)} %reshape.367.views, f32[6]{0:T(128)S(1)} %multiply_add_fusion.logs, s16[16,3,56,128]{3,2,1,0:T(8,128)(2,1)S(1)} %all-to-all-done.refs_0_, s16[16,3,56,128]{3,2,1,0:T(8,128)(2,1)S(1)} %all-to-all-done.1.refs_1_), custom_call_target="tpu_custom_call" | custom-call | tf_op jit(solution)/shard_map/add_up/pallas_call | solution.py:470
  157.2 3.6 %all-to-all-start.2 = ((s16[16,2,56,128]{3,2,1,0:T(8,128)(2,1)}), s16[16,2,56,128]{3,2,1,0:T(8,128)(2,1)S(1)}, u32[]{:S(2)}, u32[]{:S(2)}) async-start(s16[16,2,56,128]{3,2,1,0:T(8,128)(2,1)} %add_up.1), calls=%async_computation.2 | async-start | bytes 917504 | tf_op jit(solution)/shard_map/all_to_all | solution.py:556
  160.9 11.2 %all-to-all-done.2.total = s16[16,2,56,128]{3,2,1,0:T(8,128)(2,1)S(1)} async-done(((s16[16,2,56,128]{3,2,1,0:T(8,128)(2,1)}), s16[16,2,56,128]{3,2,1,0:T(8,128)(2,1)S(1)}, u32[]{:S(2)}, u32[]{:S(2)}) %all-to-all-start.2) | async-done | bytes 458784 | tf_op jit(solution)/shard_map/all_to_all | solution.py:556
  (122 shorter events, 39.3 us)
Async XLA Ops:
  2.6 9.1 %collective-permute-start = (bf16[28,32,128]{2,1,0:T(8,128)(2,1)S(1)}, bf16[28,32,128]{2,1,0:T(8,128)(2,1)S(1)}, u32[]{:S(2)}, u32[]{:S(2)}) collective-permute-start(bf16[28,32,128]{2,1,0:T(8,128)(2,1)S(1)} %get-tuple-element.86.refs_0_), channel_id=1, source_target_pairs={{0,32},{8,40},{16,48},{24,56},{32,64},{40,72},{48,80},{56,88},{64,... | collective-permute-start | bytes 688136 | tf_op jit(solution)/shard_map/ppermute | solution.py:34
  4.2 11.3 %collective-permute-start.1 = (bf16[28,32,128]{2,1,0:T(8,128)(2,1)S(1)}, bf16[28,32,128]{2,1,0:T(8,128)(2,1)S(1)}, u32[]{:S(2)}, u32[]{:S(2)}) collective-permute-start(bf16[28,32,128]{2,1,0:T(8,128)(2,1)S(1)} %get-tuple-element.86.refs_0_), channel_id=1, source_target_pairs={{0,96},{8,104},{16,112},{24,120},{32,0},{40,8},{48,16},{56,24},{64... | collective-permute-start | bytes 688136 | tf_op jit(solution)/shard_map/ppermute | solution.py:34
  6.0 11.2 %collective-permute-start.2 = (bf16[28,32,128]{2,1,0:T(8,128)(2,1)S(1)}, bf16[28,32,128]{2,1,0:T(8,128)(2,1)S(1)}, u32[]{:S(2)}, u32[]{:S(2)}) collective-permute-start(bf16[28,32,128]{2,1,0:T(8,128)(2,1)S(1)} %get-tuple-element.86.refs_0_), channel_id=1, source_target_pairs={{0,64},{8,72},{16,80},{24,88},{32,96},{40,104},{48,112},{56,120},{... | collective-permute-start | bytes 688136 | tf_op jit(solution)/shard_map/ppermute | solution.py:34
  7.8 9.4 %collective-permute-start.3 = (bf16[28,32,128]{2,1,0:T(8,128)(2,1)S(1)}, bf16[28,32,128]{2,1,0:T(8,128)(2,1)S(1)}, u32[]{:S(2)}, u32[]{:S(2)}) collective-permute-start(bf16[28,32,128]{2,1,0:T(8,128)(2,1)S(1)} %get-tuple-element.85.refs_4_), channel_id=1, source_target_pairs={{0,8},{8,16},{16,24},{24,0},{32,40},{40,48},{48,56},{56,32},{64,72... | collective-permute-start | bytes 688136 | tf_op jit(solution)/shard_map/ppermute | solution.py:34
  9.3 7.8 %collective-permute-start.4 = (bf16[28,32,128]{2,1,0:T(8,128)(2,1)S(1)}, bf16[28,32,128]{2,1,0:T(8,128)(2,1)S(1)}, u32[]{:S(2)}, u32[]{:S(2)}) collective-permute-start(bf16[28,32,128]{2,1,0:T(8,128)(2,1)S(1)} %get-tuple-element.85.refs_4_), channel_id=1, source_target_pairs={{0,24},{8,0},{16,8},{24,16},{32,56},{40,32},{48,40},{56,48},{64,88... | collective-permute-start | bytes 688136 | tf_op jit(solution)/shard_map/ppermute | solution.py:34
  11.8 9.8 %collective-permute-start.5 = (bf16[28,32,128]{2,1,0:T(8,128)(2,1)S(1)}, bf16[28,32,128]{2,1,0:T(8,128)(2,1)S(1)}, u32[]{:S(2)}, u32[]{:S(2)}) collective-permute-start(bf16[28,32,128]{2,1,0:T(8,128)(2,1)S(1)} %get-tuple-element.85.refs_4_), channel_id=1, source_target_pairs={{0,16},{8,24},{16,0},{24,8},{32,48},{40,56},{48,32},{56,40},{64,80... | collective-permute-start | bytes 688136 | tf_op jit(solution)/shard_map/ppermute | solution.py:34
  25.4 27.0 %collective-permute-start.6 = (bf16[112,32,128]{2,1,0:T(8,128)(2,1)}, bf16[112,32,128]{2,1,0:T(8,128)(2,1)S(1)}, u32[]{:S(2)}, u32[]{:S(2)}) collective-permute-start(bf16[112,32,128]{2,1,0:T(8,128)(2,1)} %get-tuple-element.60.refs_3_.refs_0_), channel_id=1, source_target_pairs={{0,8},{8,16},{16,24},{24,0},{32,40},{40,48},{48,56},{56,32},{64,72... | collective-permute-start | bytes 2752520 | tf_op jit(solution)/shard_map/ppermute | solution.py:34
  26.6 25.8 %collective-permute-start.7 = (bf16[112,32,128]{2,1,0:T(8,128)(2,1)}, bf16[112,32,128]{2,1,0:T(8,128)(2,1)S(1)}, u32[]{:S(2)}, u32[]{:S(2)}) collective-permute-start(bf16[112,32,128]{2,1,0:T(8,128)(2,1)} %get-tuple-element.60.refs_3_.refs_0_), channel_id=1, source_target_pairs={{0,24},{8,0},{16,8},{24,16},{32,56},{40,32},{48,40},{56,48},{64,88... | collective-permute-start | bytes 2752520 | tf_op jit(solution)/shard_map/ppermute | solution.py:34
  28.7 23.7 %collective-permute-start.8 = (bf16[112,32,128]{2,1,0:T(8,128)(2,1)}, bf16[112,32,128]{2,1,0:T(8,128)(2,1)S(1)}, u32[]{:S(2)}, u32[]{:S(2)}) collective-permute-start(bf16[112,32,128]{2,1,0:T(8,128)(2,1)} %get-tuple-element.69.refs_8_.refs_0_), channel_id=1, source_target_pairs={{0,32},{8,40},{16,48},{24,56},{32,64},{40,72},{48,80},{56,88},{64,... | collective-permute-start | bytes 2752520 | tf_op jit(solution)/shard_map/ppermute | solution.py:34
  29.3 23.2 %collective-permute-start.9 = (bf16[112,32,128]{2,1,0:T(8,128)(2,1)}, bf16[112,32,128]{2,1,0:T(8,128)(2,1)}, u32[]{:S(2)}, u32[]{:S(2)}) collective-permute-start(bf16[112,32,128]{2,1,0:T(8,128)(2,1)} %get-tuple-element.69.refs_8_.refs_0_), channel_id=1, source_target_pairs={{0,96},{8,104},{16,112},{24,120},{32,0},{40,8},{48,16},{56,24},{64... | collective-permute-start | bytes 2752520 | tf_op jit(solution)/shard_map/ppermute | solution.py:34
  38.9 8.6 %collective-permute-start.10 = (s32[3]{0:T(128)S(1)}, s32[3]{0:T(128)S(1)}, u32[]{:S(2)}, u32[]{:S(2)}) collective-permute-start(s32[3]{0:T(128)S(1)} %bitcast.46), channel_id=1, source_target_pairs={{1,0},{2,1},{3,2},{4,3},{5,4},{6,5},{7,6},{9,8},{10,9},{11,10},{12... | collective-permute-start | bytes 44 | tf_op jit(solution)/shard_map/ppermute | solution.py:532
  47.6 4.9 %collective-permute-start.11 = (s32[3]{0:T(128)S(1)}, s32[3]{0:T(128)S(1)}, u32[]{:S(2)}, u32[]{:S(2)}) collective-permute-start(s32[3]{0:T(128)S(1)} %bitcast.47), channel_id=1, source_target_pairs={{0,1},{1,2},{2,3},{3,4},{4,5},{5,6},{6,7},{8,9},{9,10},{10,11},{11... | collective-permute-start | bytes 44 | tf_op jit(solution)/shard_map/ppermute | solution.py:533
  55.5 13.7 %collective-permute-start.12 = (bf16[56,32,128]{2,1,0:T(8,128)(2,1)}, bf16[56,32,128]{2,1,0:T(8,128)(2,1)S(1)}, u32[]{:S(2)}, u32[]{:S(2)}) collective-permute-start(bf16[56,32,128]{2,1,0:T(8,128)(2,1)} %get-tuple-element.65), channel_id=1, source_target_pairs={{0,8},{8,16},{16,24},{24,0},{32,40},{40,48},{48,56},{56,32},{64,72... | collective-permute-start | bytes 1376264 | tf_op jit(solution)/shard_map/ppermute | solution.py:34
  55.6 13.6 %collective-permute-start.13 = (bf16[56,32,128]{2,1,0:T(8,128)(2,1)}, bf16[56,32,128]{2,1,0:T(8,128)(2,1)}, u32[]{:S(2)}, u32[]{:S(2)}) collective-permute-start(bf16[56,32,128]{2,1,0:T(8,128)(2,1)} %get-tuple-element.66), channel_id=1, source_target_pairs={{0,24},{8,0},{16,8},{24,16},{32,56},{40,32},{48,40},{56,48},{64,88... | collective-permute-start | bytes 1376264 | tf_op jit(solution)/shard_map/ppermute | solution.py:34
  58.8 13.2 %collective-permute-start.14 = (bf16[56,32,128]{2,1,0:T(8,128)(2,1)}, bf16[56,32,128]{2,1,0:T(8,128)(2,1)}, u32[]{:S(2)}, u32[]{:S(2)}) collective-permute-start(bf16[56,32,128]{2,1,0:T(8,128)(2,1)} %get-tuple-element.70), channel_id=1, source_target_pairs={{0,32},{8,40},{16,48},{24,56},{32,64},{40,72},{48,80},{56,88},{64,... | collective-permute-start | bytes 1376264 | tf_op jit(solution)/shard_map/ppermute | solution.py:34
  58.8 13.2 %collective-permute-start.15 = (bf16[56,32,128]{2,1,0:T(8,128)(2,1)}, bf16[56,32,128]{2,1,0:T(8,128)(2,1)}, u32[]{:S(2)}, u32[]{:S(2)}) collective-permute-start(bf16[56,32,128]{2,1,0:T(8,128)(2,1)} %get-tuple-element.71), channel_id=1, source_target_pairs={{0,96},{8,104},{16,112},{24,120},{32,0},{40,8},{48,16},{56,24},{64... | collective-permute-start | bytes 1376264 | tf_op jit(solution)/shard_map/ppermute | solution.py:34
  75.7 12.7 %collective-permute-start.18 = (bf16[3,58,16,128]{3,2,1,0:T(8,128)(2,1)}, bf16[3,58,16,128]{3,2,1,0:T(8,128)(2,1)S(1)}, u32[]{:S(2)}, u32[]{:S(2)}) collective-permute-start(bf16[3,58,16,128]{3,2,1,0:T(8,128)(2,1)} %get-tuple-element.81), channel_id=1, source_target_pairs={{0,1},{1,2},{2,3},{3,4},{4,5},{5,6},{6,7},{8,9},{9,10},{10,11},{11... | collective-permute-start | bytes 2138120 | tf_op jit(solution)/shard_map/ppermute | solution.py:541
  77.6 12.7 %collective-permute-start.19 = (bf16[3,58,16,128]{3,2,1,0:T(8,128)(2,1)}, bf16[3,58,16,128]{3,2,1,0:T(8,128)(2,1)S(1)}, u32[]{:S(2)}, u32[]{:S(2)}) collective-permute-start(bf16[3,58,16,128]{3,2,1,0:T(8,128)(2,1)} %get-tuple-element.82), channel_id=1, source_target_pairs={{1,0},{2,1},{3,2},{4,3},{5,4},{6,5},{7,6},{9,8},{10,9},{11,10},{12... | collective-permute-start | bytes 2138120 | tf_op jit(solution)/shard_map/ppermute | solution.py:541
  81.3 32.5 %collective-permute-start.16 = (bf16[3,58,16,128]{3,2,1,0:T(8,128)(2,1)}, bf16[3,58,16,128]{3,2,1,0:T(8,128)(2,1)S(1)}, u32[]{:S(2)}, u32[]{:S(2)}) collective-permute-start(bf16[3,58,16,128]{3,2,1,0:T(8,128)(2,1)} %get-tuple-element.72), channel_id=1, source_target_pairs={{0,1},{1,2},{2,3},{3,4},{4,5},{5,6},{6,7},{8,9},{9,10},{10,11},{11... | collective-permute-start | bytes 2138120 | tf_op jit(solution)/shard_map/ppermute | solution.py:541
  83.2 30.6 %collective-permute-start.17 = (bf16[3,58,16,128]{3,2,1,0:T(8,128)(2,1)}, bf16[3,58,16,128]{3,2,1,0:T(8,128)(2,1)S(1)}, u32[]{:S(2)}, u32[]{:S(2)}) collective-permute-start(bf16[3,58,16,128]{3,2,1,0:T(8,128)(2,1)} %get-tuple-element.73), channel_id=1, source_target_pairs={{1,0},{2,1},{3,2},{4,3},{5,4},{6,5},{7,6},{9,8},{10,9},{11,10},{12... | collective-permute-start | bytes 2138120 | tf_op jit(solution)/shard_map/ppermute | solution.py:541
  109.4 23.5 %all-to-all-start.1 = ((s16[16,3,56,128]{3,2,1,0:T(8,128)(2,1)}), s16[16,3,56,128]{3,2,1,0:T(8,128)(2,1)S(1)}, u32[]{:S(2)}, u32[]{:S(2)}) async-start(s16[16,3,56,128]{3,2,1,0:T(8,128)(2,1)} %jobs.3), calls=%async_computation.1 | async-start | bytes 1376256 | tf_op jit(solution)/shard_map/all_to_all | solution.py:555
  132.9 39.2 %copy-start.3 = (s32[1,1,6]{2,1,0:T(1,128)S(1)}, s32[1,1,6]{2,1,0:T(1,128)}, u32[]{:S(2)}) copy-start(s32[1,1,6]{2,1,0:T(1,128)} %param.13) | copy-start | bytes 76
  132.9 22.0 %all-to-all-start = ((s16[16,3,56,128]{3,2,1,0:T(8,128)(2,1)}), s16[16,3,56,128]{3,2,1,0:T(8,128)(2,1)S(1)}, u32[]{:S(2)}, u32[]{:S(2)}) async-start(s16[16,3,56,128]{3,2,1,0:T(8,128)(2,1)} %jobs.2), calls=%async_computation | async-start | bytes 1376256 | tf_op jit(solution)/shard_map/all_to_all | solution.py:555
  157.2 14.9 %all-to-all-start.2 = ((s16[16,2,56,128]{3,2,1,0:T(8,128)(2,1)}), s16[16,2,56,128]{3,2,1,0:T(8,128)(2,1)S(1)}, u32[]{:S(2)}, u32[]{:S(2)}) async-start(s16[16,2,56,128]{3,2,1,0:T(8,128)(2,1)} %add_up.1), calls=%async_computation.2 | async-start | bytes 917504 | tf_op jit(solution)/shard_map/all_to_all | solution.py:556
  (9 other events, 188.4 us)

commit v8 on v7

--- a/solution.py
+++ b/solution.py
@@ -308,7 +308,7 @@
         z_low[pl.ds(start, CHUNK)] = low.reshape(CHUNK, PADW, 128)
         return carry
 
-    lax.fori_loop(0, -(-WIN // CHUNK), along_z, 0, unroll=UZ)
+    lax.fori_loop(0, WIN // CHUNK, along_z, 0, unroll=WIN // CHUNK)
 
     def along_x_first(i, carry):
         y = 2 * i
@@ -320,7 +320,7 @@
         blurred_x[pl.ds(start + PW, PADW), :] = in_x[:, 128:]
         return carry
 
-    lax.fori_loop(0, WIN // 2, along_x_first, 0, unroll=UNROLL)
+    lax.fori_loop(0, WIN // 2, along_x_first, 0, unroll=WIN // 2)
 
     past = jnp.zeros((PADW - WIN, 256), F32)
 
@@ -336,7 +336,7 @@
         back_y[pl.ds(start + PS, PADS), :] = in_y[:, 128:]
         return carry
 
-    lax.fori_loop(0, WIN // 2, along_y, 0, unroll=UNROLL)
+    lax.fori_loop(0, WIN // 2, along_y, 0, unroll=WIN // 2)
 
     def along_x(i, carry):
         y = 2 * i
@@ -347,7 +347,7 @@
         back_x[pl.ds(start + PS, PADS), :] = in_x[:, 128:]
         return carry
 
-    lax.fori_loop(0, SIDE // 2, along_x, 0, unroll=UNROLL)
+    lax.fori_loop(0, SIDE // 2, along_x, 0, unroll=SIDE // 2)
 
     group = 4
     for i in range(SIDE // group):
@@ -361,13 +361,11 @@
         out_ref[k, 0] = jnp.zeros_like(out_ref[k, 0])
 
 
-UNROLL = 29
 CHUNK = 29
 PEXTRA = 8
 SEXTRA = 8
 PW = PADW + PEXTRA
 PS = PADS + SEXTRA
-UZ = 1
 
 
 def run_jobs(channel, parts, scalars, top, bottom, view_data, mats):

time: 175 us -> 163 us (0.931)
  Pallas kernels: 51.7 us -> 39.5 us
    pallas_call x2, Pallas kernels: 38.2 us -> 26.1 us  [run_jobs(): pl.pallas_call(functools.partial(job_kernel, channel), grid=(slots,), in_...]
  transfers between devices with their start and end apart: 23 -> 23, of which waited for: 10 -> 10; matrix products, arithmetic and copies ran while one was open for 11% -> 12% of each run, Pallas kernels for 22% -> 16%
where the time goes in v8:
time: 163 us; the launch traced here: 162 us
  starting transfers between devices  55.1 us (34%)
  waiting for transfers between devices  43.8 us (27%)
  Pallas kernels  39.5 us (24%)
  local copies, waits for them, and re-layouts  13 us (8%)
  other arithmetic  10.3 us (6%)
    pallas_call x2, Pallas kernels, run_jobs(): pl.pallas_call(functools.partial(job_kernel, channel), grid=(slots,), in_...  26.1 us
    ppermute x14, starting transfers between devices, torus_step(): return lax.ppermute(array, 'tile', pairs)  24.3 us
    ppermute x14, waiting for transfers between devices, torus_step(): return lax.ppermute(array, 'tile', pairs)  16.9 us
    all_to_all x2, starting transfers between devices, on_device(): parts.append(lax.all_to_all(factors, 'tile', 0, 0, tiled=True))  11.7 us
    all_to_all x1, waiting for transfers between devices, on_device(): lax.all_to_all(add_up(owners, seen_by, logs, parts), 'tile', 0, 0, tiled=...  11.1 us
    all_to_all x2, waiting for transfers between devices, on_device(): parts.append(lax.all_to_all(factors, 'tile', 0, 0, tiled=True))  10 us
    ppermute x2, starting transfers between devices, on_device(): lax.ppermute(rims[2 * c + 1], 'view', downward)  7.46 us
    optimization_barrier x2, local copies, waits for them, and re-layouts, on_device(): lax.optimization_barrier((rings, view_data, psf, views, bricks))  6.47 us
  transfers between devices with their start and end apart: 23, of which 10 were waited for; matrix products, arithmetic and copies ran while one was open for 12% of the time, Pallas kernels for 16%

profile of v8, /device:TPU:32, one launch (start us, length us, event | category | flops | bytes accessed | tf_op | source)
XLA Modules:
  0.0 162.2 jit_solution(5050655013169760401)
XLA Ops:
  11.8 2.8 %collective-permute-start.5 = (bf16[28,32,128]{2,1,0:T(8,128)(2,1)S(1)}, bf16[28,32,128]{2,1,0:T(8,128)(2,1)S(1)}, u32[]{:S(2)}, u32[]{:S(2)}) collective-permute-start(bf16[28,32,128]{2,1,0:T(8,128)(2,1)S(1)} %get-tuple-element.85.refs_4_), channel_id=1, source_target_pairs={{0,16},{8,24},{16,0},{24,8},{32,48},{40,56},{48,32},{56,40},{64,80... | collective-permute-start | bytes 688136 | tf_op jit(solution)/shard_map/ppermute | solution.py:34
  17.2 4.5 %collective-permute-done.5.refs_7_ = bf16[28,32,128]{2,1,0:T(8,128)(2,1)S(1)} collective-permute-done((bf16[28,32,128]{2,1,0:T(8,128)(2,1)S(1)}, bf16[28,32,128]{2,1,0:T(8,128)(2,1)S(1)}, u32[]{:S(2)}, u32[]{:S(2)}) %collective-permute-start.5) | collective-permute-done | bytes 229408 | tf_op jit(solution)/shard_map/ppermute | solution.py:34
  21.6 3.8 %join.1 = (bf16[112,32,128]{2,1,0:T(8,128)(2,1)}, bf16[112,32,128]{2,1,0:T(8,128)(2,1)}) custom-call(bf16[28,32,128]{2,1,0:T(8,128)(2,1)S(1)} %get-tuple-element.86.refs_0_, bf16[28,32,128]{2,1,0:T(8,128)(2,1)S(1)} %collective-permute-done.refs_1_, bf16[28,32,128]{2,1,0:T(8,128)(2,1)S(1)} %collective-permute-done.1.refs_2_, ...), custom_call_target="tpu_custom_call" | custom-call | tf_op jit(solution)/shard_map/join/pallas_call | solution.py:77
  26.6 2.1 %collective-permute-start.7 = (bf16[112,32,128]{2,1,0:T(8,128)(2,1)}, bf16[112,32,128]{2,1,0:T(8,128)(2,1)S(1)}, u32[]{:S(2)}, u32[]{:S(2)}) collective-permute-start(bf16[112,32,128]{2,1,0:T(8,128)(2,1)} %get-tuple-element.60.refs_3_.refs_0_), channel_id=1, source_target_pairs={{0,24},{8,0},{16,8},{24,16},{32,56},{40,32},{48,40},{56,48},{64,88... | collective-permute-start | bytes 2752520 | tf_op jit(solution)/shard_map/ppermute | solution.py:34
  29.3 2.6 %collective-permute-start.9 = (bf16[112,32,128]{2,1,0:T(8,128)(2,1)}, bf16[112,32,128]{2,1,0:T(8,128)(2,1)}, u32[]{:S(2)}, u32[]{:S(2)}) collective-permute-start(bf16[112,32,128]{2,1,0:T(8,128)(2,1)} %get-tuple-element.69.refs_8_.refs_0_), channel_id=1, source_target_pairs={{0,96},{8,104},{16,112},{24,120},{32,0},{40,8},{48,16},{56,24},{64... | collective-permute-start | bytes 2752520 | tf_op jit(solution)/shard_map/ppermute | solution.py:34
  40.9 6.5 %copy.67 = bf16[1,1,3,2,58,58,128]{6,5,4,3,2,1,0:T(8,128)(2,1)} copy(bf16[1,1,3,2,58,58,128]{6,3,5,4,2,1,0:T(2,128)(2,1)} %param.8) | data formatting | bytes 10334208 | tf_op jit(solution)/shard_map/optimization_barrier | solution.py:519
  47.6 2.4 %collective-permute-start.11 = (s32[3]{0:T(128)S(1)}, s32[3]{0:T(128)S(1)}, u32[]{:S(2)}, u32[]{:S(2)}) collective-permute-start(s32[3]{0:T(128)S(1)} %bitcast.47), channel_id=1, source_target_pairs={{0,1},{1,2},{2,3},{3,4},{4,5},{5,6},{6,7},{8,9},{9,10},{10,11},{11... | collective-permute-start | bytes 44 | tf_op jit(solution)/shard_map/ppermute | solution.py:531
  50.0 2.4 %collective-permute-done.11.refs_2_ = s32[3]{0:T(128)S(1)} collective-permute-done((s32[3]{0:T(128)S(1)}, s32[3]{0:T(128)S(1)}, u32[]{:S(2)}, u32[]{:S(2)}) %collective-permute-start.11) | collective-permute-done | bytes 44 | tf_op jit(solution)/shard_map/ppermute | solution.py:531
  52.5 3.0 %halves.1 = (bf16[56,32,128]{2,1,0:T(8,128)(2,1)}, bf16[56,32,128]{2,1,0:T(8,128)(2,1)}, bf16[56,32,128]{2,1,0:T(8,128)(2,1)}, bf16[56,32,128]{2,1,0:T(8,128)(2,1)}) custom-call(bf16[112,32,128]{2,1,0:T(8,128)(2,1)S(1)} %collective-permute-done.6.refs_0_.refs_4_.refs_1_, bf16[112,32,128]{2,1,0:T(8,128)(2,1)S(1)} %collective-permute-done.7.refs_1_.refs_5_.refs_2_, ...), custom_call_target="tpu_custom_call" | custom-call | tf_op jit(solution)/shard_map/halves/pallas_call | solution.py:112
  55.6 3.2 %collective-permute-start.13 = (bf16[56,32,128]{2,1,0:T(8,128)(2,1)}, bf16[56,32,128]{2,1,0:T(8,128)(2,1)}, u32[]{:S(2)}, u32[]{:S(2)}) collective-permute-start(bf16[56,32,128]{2,1,0:T(8,128)(2,1)} %get-tuple-element.66), channel_id=1, source_target_pairs={{0,24},{8,0},{16,8},{24,16},{32,56},{40,32},{48,40},{56,48},{64,88... | collective-permute-start | bytes 1376264 | tf_op jit(solution)/shard_map/ppermute | solution.py:34
  58.8 3.2 %collective-permute-start.15 = (bf16[56,32,128]{2,1,0:T(8,128)(2,1)}, bf16[56,32,128]{2,1,0:T(8,128)(2,1)}, u32[]{:S(2)}, u32[]{:S(2)}) collective-permute-start(bf16[56,32,128]{2,1,0:T(8,128)(2,1)} %get-tuple-element.71), channel_id=1, source_target_pairs={{0,96},{8,104},{16,112},{24,120},{32,0},{40,8},{48,16},{56,24},{64... | collective-permute-start | bytes 1376264 | tf_op jit(solution)/shard_map/ppermute | solution.py:34
  62.1 7.2 %collective-permute-done.12.refs_6_.refs_3_ = bf16[56,32,128]{2,1,0:T(8,128)(2,1)S(1)} collective-permute-done((bf16[56,32,128]{2,1,0:T(8,128)(2,1)}, bf16[56,32,128]{2,1,0:T(8,128)(2,1)S(1)}, u32[]{:S(2)}, u32[]{:S(2)}) %collective-permute-start.12) | collective-permute-done | bytes 458784 | tf_op jit(solution)/shard_map/ppermute | solution.py:34
  69.2 2.8 %collective-permute-done.14.refs_11_.refs_3_ = bf16[56,32,128]{2,1,0:T(8,128)(2,1)} collective-permute-done((bf16[56,32,128]{2,1,0:T(8,128)(2,1)}, bf16[56,32,128]{2,1,0:T(8,128)(2,1)}, u32[]{:S(2)}, u32[]{:S(2)}) %collective-permute-start.14) | collective-permute-done | bytes 458784 | tf_op jit(solution)/shard_map/ppermute | solution.py:34
  72.0 3.7 %margins.1 = (bf16[3,58,16,128]{3,2,1,0:T(8,128)(2,1)}, bf16[3,58,16,128]{3,2,1,0:T(8,128)(2,1)}, bf16[3,58,16,128]{3,2,1,0:T(8,128)(2,1)}, bf16[3,58,16,128]{3,2,1,0:T(8,128)(2,1)}) custom-call(s32[1]{0:T(128)} %bitcast.17.refs_0_.me, s32[3]{0:T(128)S(1)} %collective-permute-done.10.refs_1_, s32[3]{0:T(128)S(1)} %collective-permute-done.11.refs_2_, ...), custom_call_target="tpu_custom_call" | custom-call | tf_op jit(solution)/shard_map/margins/pallas_call | solution.py:210
  77.6 3.6 %collective-permute-start.19 = (bf16[3,58,16,128]{3,2,1,0:T(8,128)(2,1)}, bf16[3,58,16,128]{3,2,1,0:T(8,128)(2,1)S(1)}, u32[]{:S(2)}, u32[]{:S(2)}) collective-permute-start(bf16[3,58,16,128]{3,2,1,0:T(8,128)(2,1)} %get-tuple-element.82), channel_id=1, source_target_pairs={{1,0},{2,1},{3,2},{4,3},{5,4},{6,5},{7,6},{9,8},{10,9},{11,10},{12... | collective-permute-start | bytes 2138120 | tf_op jit(solution)/shard_map/ppermute | solution.py:539
  83.2 3.8 %collective-permute-start.17 = (bf16[3,58,16,128]{3,2,1,0:T(8,128)(2,1)}, bf16[3,58,16,128]{3,2,1,0:T(8,128)(2,1)S(1)}, u32[]{:S(2)}, u32[]{:S(2)}) collective-permute-start(bf16[3,58,16,128]{3,2,1,0:T(8,128)(2,1)} %get-tuple-element.73), channel_id=1, source_target_pairs={{1,0},{2,1},{3,2},{4,3},{5,4},{6,5},{7,6},{9,8},{10,9},{11,10},{12... | collective-permute-start | bytes 2138120 | tf_op jit(solution)/shard_map/ppermute | solution.py:539
  90.3 13.0 %jobs.3 = s16[16,3,56,128]{3,2,1,0:T(8,128)(2,1)} custom-call(s32[1]{0:T(128)} %bitcast.17.refs_0_.me, s32[3]{0:T(128)S(1)} %bitcast.48, s32[3]{0:T(128)S(1)} %bitcast.42, f32[6]{0:T(128)S(1)} %copy-done.4, f32[6]{0:T(128)S(1)} %multiply_add_fusion.logs, bf16[112,32,128]{2,1,0:T(8,128)(2,1)} %get-tuple-element.69.refs_8_.refs_0_, ...), custom_call_target="tpu_custom_call" | custom-call | flops 23624417280 | bytes 7077888 | tf_op jit(solution)/shard_map/jobs/pallas_call | solution.py:377
  103.3 4.3 %all-to-all-start.1 = ((s16[16,3,56,128]{3,2,1,0:T(8,128)(2,1)}), s16[16,3,56,128]{3,2,1,0:T(8,128)(2,1)S(1)}, u32[]{:S(2)}, u32[]{:S(2)}) async-start(s16[16,3,56,128]{3,2,1,0:T(8,128)(2,1)} %jobs.3), calls=%async_computation.1 | async-start | bytes 1376256 | tf_op jit(solution)/shard_map/all_to_all | solution.py:553
  107.7 13.0 %jobs.2 = s16[16,3,56,128]{3,2,1,0:T(8,128)(2,1)} custom-call(s32[1]{0:T(128)} %bitcast.17.refs_0_.me, s32[3]{0:T(128)S(1)} %bitcast.49, s32[3]{0:T(128)S(1)} %bitcast.43, f32[6]{0:T(128)S(1)} %copy-done.4, f32[6]{0:T(128)S(1)} %multiply_add_fusion.logs, bf16[112,32,128]{2,1,0:T(8,128)(2,1)} %get-tuple-element.60.refs_3_.refs_0_, ...), custom_call_target="tpu_custom_call" | custom-call | flops 23624417280 | bytes 7077888 | tf_op jit(solution)/shard_map/jobs/pallas_call | solution.py:377
  120.8 7.4 %all-to-all-start = ((s16[16,3,56,128]{3,2,1,0:T(8,128)(2,1)}), s16[16,3,56,128]{3,2,1,0:T(8,128)(2,1)S(1)}, u32[]{:S(2)}, u32[]{:S(2)}) async-start(s16[16,3,56,128]{3,2,1,0:T(8,128)(2,1)} %jobs.2), calls=%async_computation | async-start | bytes 1376256 | tf_op jit(solution)/shard_map/all_to_all | solution.py:553
  132.8 10.0 %all-to-all-done.refs_0_ = s16[16,3,56,128]{3,2,1,0:T(8,128)(2,1)S(1)} async-done(((s16[16,3,56,128]{3,2,1,0:T(8,128)(2,1)}), s16[16,3,56,128]{3,2,1,0:T(8,128)(2,1)S(1)}, u32[]{:S(2)}, u32[]{:S(2)}) %all-to-all-start) | async-done | bytes 688160 | tf_op jit(solution)/shard_map/all_to_all | solution.py:553
  142.8 2.3 %add_up.1 = s16[16,2,56,128]{3,2,1,0:T(8,128)(2,1)} custom-call(s32[48]{0:T(128)S(1)} %reshape.366.owners, s32[48]{0:T(128)S(1)} %reshape.367.views, f32[6]{0:T(128)S(1)} %multiply_add_fusion.logs, s16[16,3,56,128]{3,2,1,0:T(8,128)(2,1)S(1)} %all-to-all-done.refs_0_, s16[16,3,56,128]{3,2,1,0:T(8,128)(2,1)S(1)} %all-to-all-done.1.refs_1_), custom_call_target="tpu_custom_call" | custom-call | tf_op jit(solution)/shard_map/add_up/pallas_call | solution.py:468
  145.1 3.6 %all-to-all-start.2 = ((s16[16,2,56,128]{3,2,1,0:T(8,128)(2,1)}), s16[16,2,56,128]{3,2,1,0:T(8,128)(2,1)S(1)}, u32[]{:S(2)}, u32[]{:S(2)}) async-start(s16[16,2,56,128]{3,2,1,0:T(8,128)(2,1)} %add_up.1), calls=%async_computation.2 | async-start | bytes 917504 | tf_op jit(solution)/shard_map/all_to_all | solution.py:554
  148.8 11.1 %all-to-all-done.2.total = s16[16,2,56,128]{3,2,1,0:T(8,128)(2,1)S(1)} async-done(((s16[16,2,56,128]{3,2,1,0:T(8,128)(2,1)}), s16[16,2,56,128]{3,2,1,0:T(8,128)(2,1)S(1)}, u32[]{:S(2)}, u32[]{:S(2)}) %all-to-all-start.2) | async-done | bytes 458784 | tf_op jit(solution)/shard_map/all_to_all | solution.py:554
  (122 shorter events, 39.3 us)
Async XLA Ops:
  2.6 9.1 %collective-permute-start = (bf16[28,32,128]{2,1,0:T(8,128)(2,1)S(1)}, bf16[28,32,128]{2,1,0:T(8,128)(2,1)S(1)}, u32[]{:S(2)}, u32[]{:S(2)}) collective-permute-start(bf16[28,32,128]{2,1,0:T(8,128)(2,1)S(1)} %get-tuple-element.86.refs_0_), channel_id=1, source_target_pairs={{0,32},{8,40},{16,48},{24,56},{32,64},{40,72},{48,80},{56,88},{64,... | collective-permute-start | bytes 688136 | tf_op jit(solution)/shard_map/ppermute | solution.py:34
  4.2 11.3 %collective-permute-start.1 = (bf16[28,32,128]{2,1,0:T(8,128)(2,1)S(1)}, bf16[28,32,128]{2,1,0:T(8,128)(2,1)S(1)}, u32[]{:S(2)}, u32[]{:S(2)}) collective-permute-start(bf16[28,32,128]{2,1,0:T(8,128)(2,1)S(1)} %get-tuple-element.86.refs_0_), channel_id=1, source_target_pairs={{0,96},{8,104},{16,112},{24,120},{32,0},{40,8},{48,16},{56,24},{64... | collective-permute-start | bytes 688136 | tf_op jit(solution)/shard_map/ppermute | solution.py:34
  6.0 11.2 %collective-permute-start.2 = (bf16[28,32,128]{2,1,0:T(8,128)(2,1)S(1)}, bf16[28,32,128]{2,1,0:T(8,128)(2,1)S(1)}, u32[]{:S(2)}, u32[]{:S(2)}) collective-permute-start(bf16[28,32,128]{2,1,0:T(8,128)(2,1)S(1)} %get-tuple-element.86.refs_0_), channel_id=1, source_target_pairs={{0,64},{8,72},{16,80},{24,88},{32,96},{40,104},{48,112},{56,120},{... | collective-permute-start | bytes 688136 | tf_op jit(solution)/shard_map/ppermute | solution.py:34
  7.8 9.4 %collective-permute-start.3 = (bf16[28,32,128]{2,1,0:T(8,128)(2,1)S(1)}, bf16[28,32,128]{2,1,0:T(8,128)(2,1)S(1)}, u32[]{:S(2)}, u32[]{:S(2)}) collective-permute-start(bf16[28,32,128]{2,1,0:T(8,128)(2,1)S(1)} %get-tuple-element.85.refs_4_), channel_id=1, source_target_pairs={{0,8},{8,16},{16,24},{24,0},{32,40},{40,48},{48,56},{56,32},{64,72... | collective-permute-start | bytes 688136 | tf_op jit(solution)/shard_map/ppermute | solution.py:34
  9.3 7.8 %collective-permute-start.4 = (bf16[28,32,128]{2,1,0:T(8,128)(2,1)S(1)}, bf16[28,32,128]{2,1,0:T(8,128)(2,1)S(1)}, u32[]{:S(2)}, u32[]{:S(2)}) collective-permute-start(bf16[28,32,128]{2,1,0:T(8,128)(2,1)S(1)} %get-tuple-element.85.refs_4_), channel_id=1, source_target_pairs={{0,24},{8,0},{16,8},{24,16},{32,56},{40,32},{48,40},{56,48},{64,88... | collective-permute-start | bytes 688136 | tf_op jit(solution)/shard_map/ppermute | solution.py:34
  11.8 9.8 %collective-permute-start.5 = (bf16[28,32,128]{2,1,0:T(8,128)(2,1)S(1)}, bf16[28,32,128]{2,1,0:T(8,128)(2,1)S(1)}, u32[]{:S(2)}, u32[]{:S(2)}) collective-permute-start(bf16[28,32,128]{2,1,0:T(8,128)(2,1)S(1)} %get-tuple-element.85.refs_4_), channel_id=1, source_target_pairs={{0,16},{8,24},{16,0},{24,8},{32,48},{40,56},{48,32},{56,40},{64,80... | collective-permute-start | bytes 688136 | tf_op jit(solution)/shard_map/ppermute | solution.py:34
  25.4 27.0 %collective-permute-start.6 = (bf16[112,32,128]{2,1,0:T(8,128)(2,1)}, bf16[112,32,128]{2,1,0:T(8,128)(2,1)S(1)}, u32[]{:S(2)}, u32[]{:S(2)}) collective-permute-start(bf16[112,32,128]{2,1,0:T(8,128)(2,1)} %get-tuple-element.60.refs_3_.refs_0_), channel_id=1, source_target_pairs={{0,8},{8,16},{16,24},{24,0},{32,40},{40,48},{48,56},{56,32},{64,72... | collective-permute-start | bytes 2752520 | tf_op jit(solution)/shard_map/ppermute | solution.py:34
  26.6 25.8 %collective-permute-start.7 = (bf16[112,32,128]{2,1,0:T(8,128)(2,1)}, bf16[112,32,128]{2,1,0:T(8,128)(2,1)S(1)}, u32[]{:S(2)}, u32[]{:S(2)}) collective-permute-start(bf16[112,32,128]{2,1,0:T(8,128)(2,1)} %get-tuple-element.60.refs_3_.refs_0_), channel_id=1, source_target_pairs={{0,24},{8,0},{16,8},{24,16},{32,56},{40,32},{48,40},{56,48},{64,88... | collective-permute-start | bytes 2752520 | tf_op jit(solution)/shard_map/ppermute | solution.py:34
  28.7 23.7 %collective-permute-start.8 = (bf16[112,32,128]{2,1,0:T(8,128)(2,1)}, bf16[112,32,128]{2,1,0:T(8,128)(2,1)S(1)}, u32[]{:S(2)}, u32[]{:S(2)}) collective-permute-start(bf16[112,32,128]{2,1,0:T(8,128)(2,1)} %get-tuple-element.69.refs_8_.refs_0_), channel_id=1, source_target_pairs={{0,32},{8,40},{16,48},{24,56},{32,64},{40,72},{48,80},{56,88},{64,... | collective-permute-start | bytes 2752520 | tf_op jit(solution)/shard_map/ppermute | solution.py:34
  29.3 23.2 %collective-permute-start.9 = (bf16[112,32,128]{2,1,0:T(8,128)(2,1)}, bf16[112,32,128]{2,1,0:T(8,128)(2,1)}, u32[]{:S(2)}, u32[]{:S(2)}) collective-permute-start(bf16[112,32,128]{2,1,0:T(8,128)(2,1)} %get-tuple-element.69.refs_8_.refs_0_), channel_id=1, source_target_pairs={{0,96},{8,104},{16,112},{24,120},{32,0},{40,8},{48,16},{56,24},{64... | collective-permute-start | bytes 2752520 | tf_op jit(solution)/shard_map/ppermute | solution.py:34
  38.9 8.6 %collective-permute-start.10 = (s32[3]{0:T(128)S(1)}, s32[3]{0:T(128)S(1)}, u32[]{:S(2)}, u32[]{:S(2)}) collective-permute-start(s32[3]{0:T(128)S(1)} %bitcast.46), channel_id=1, source_target_pairs={{1,0},{2,1},{3,2},{4,3},{5,4},{6,5},{7,6},{9,8},{10,9},{11,10},{12... | collective-permute-start | bytes 44 | tf_op jit(solution)/shard_map/ppermute | solution.py:530
  47.6 4.9 %collective-permute-start.11 = (s32[3]{0:T(128)S(1)}, s32[3]{0:T(128)S(1)}, u32[]{:S(2)}, u32[]{:S(2)}) collective-permute-start(s32[3]{0:T(128)S(1)} %bitcast.47), channel_id=1, source_target_pairs={{0,1},{1,2},{2,3},{3,4},{4,5},{5,6},{6,7},{8,9},{9,10},{10,11},{11... | collective-permute-start | bytes 44 | tf_op jit(solution)/shard_map/ppermute | solution.py:531
  55.5 13.7 %collective-permute-start.12 = (bf16[56,32,128]{2,1,0:T(8,128)(2,1)}, bf16[56,32,128]{2,1,0:T(8,128)(2,1)S(1)}, u32[]{:S(2)}, u32[]{:S(2)}) collective-permute-start(bf16[56,32,128]{2,1,0:T(8,128)(2,1)} %get-tuple-element.65), channel_id=1, source_target_pairs={{0,8},{8,16},{16,24},{24,0},{32,40},{40,48},{48,56},{56,32},{64,72... | collective-permute-start | bytes 1376264 | tf_op jit(solution)/shard_map/ppermute | solution.py:34
  55.6 13.6 %collective-permute-start.13 = (bf16[56,32,128]{2,1,0:T(8,128)(2,1)}, bf16[56,32,128]{2,1,0:T(8,128)(2,1)}, u32[]{:S(2)}, u32[]{:S(2)}) collective-permute-start(bf16[56,32,128]{2,1,0:T(8,128)(2,1)} %get-tuple-element.66), channel_id=1, source_target_pairs={{0,24},{8,0},{16,8},{24,16},{32,56},{40,32},{48,40},{56,48},{64,88... | collective-permute-start | bytes 1376264 | tf_op jit(solution)/shard_map/ppermute | solution.py:34
  58.8 13.2 %collective-permute-start.14 = (bf16[56,32,128]{2,1,0:T(8,128)(2,1)}, bf16[56,32,128]{2,1,0:T(8,128)(2,1)}, u32[]{:S(2)}, u32[]{:S(2)}) collective-permute-start(bf16[56,32,128]{2,1,0:T(8,128)(2,1)} %get-tuple-element.70), channel_id=1, source_target_pairs={{0,32},{8,40},{16,48},{24,56},{32,64},{40,72},{48,80},{56,88},{64,... | collective-permute-start | bytes 1376264 | tf_op jit(solution)/shard_map/ppermute | solution.py:34
  58.8 13.2 %collective-permute-start.15 = (bf16[56,32,128]{2,1,0:T(8,128)(2,1)}, bf16[56,32,128]{2,1,0:T(8,128)(2,1)}, u32[]{:S(2)}, u32[]{:S(2)}) collective-permute-start(bf16[56,32,128]{2,1,0:T(8,128)(2,1)} %get-tuple-element.71), channel_id=1, source_target_pairs={{0,96},{8,104},{16,112},{24,120},{32,0},{40,8},{48,16},{56,24},{64... | collective-permute-start | bytes 1376264 | tf_op jit(solution)/shard_map/ppermute | solution.py:34
  75.7 12.7 %collective-permute-start.18 = (bf16[3,58,16,128]{3,2,1,0:T(8,128)(2,1)}, bf16[3,58,16,128]{3,2,1,0:T(8,128)(2,1)S(1)}, u32[]{:S(2)}, u32[]{:S(2)}) collective-permute-start(bf16[3,58,16,128]{3,2,1,0:T(8,128)(2,1)} %get-tuple-element.81), channel_id=1, source_target_pairs={{0,1},{1,2},{2,3},{3,4},{4,5},{5,6},{6,7},{8,9},{9,10},{10,11},{11... | collective-permute-start | bytes 2138120 | tf_op jit(solution)/shard_map/ppermute | solution.py:539
  77.6 12.7 %collective-permute-start.19 = (bf16[3,58,16,128]{3,2,1,0:T(8,128)(2,1)}, bf16[3,58,16,128]{3,2,1,0:T(8,128)(2,1)S(1)}, u32[]{:S(2)}, u32[]{:S(2)}) collective-permute-start(bf16[3,58,16,128]{3,2,1,0:T(8,128)(2,1)} %get-tuple-element.82), channel_id=1, source_target_pairs={{1,0},{2,1},{3,2},{4,3},{5,4},{6,5},{7,6},{9,8},{10,9},{11,10},{12... | collective-permute-start | bytes 2138120 | tf_op jit(solution)/shard_map/ppermute | solution.py:539
  81.3 26.4 %collective-permute-start.16 = (bf16[3,58,16,128]{3,2,1,0:T(8,128)(2,1)}, bf16[3,58,16,128]{3,2,1,0:T(8,128)(2,1)S(1)}, u32[]{:S(2)}, u32[]{:S(2)}) collective-permute-start(bf16[3,58,16,128]{3,2,1,0:T(8,128)(2,1)} %get-tuple-element.72), channel_id=1, source_target_pairs={{0,1},{1,2},{2,3},{3,4},{4,5},{5,6},{6,7},{8,9},{9,10},{10,11},{11... | collective-permute-start | bytes 2138120 | tf_op jit(solution)/shard_map/ppermute | solution.py:539
  83.2 24.5 %collective-permute-start.17 = (bf16[3,58,16,128]{3,2,1,0:T(8,128)(2,1)}, bf16[3,58,16,128]{3,2,1,0:T(8,128)(2,1)S(1)}, u32[]{:S(2)}, u32[]{:S(2)}) collective-permute-start(bf16[3,58,16,128]{3,2,1,0:T(8,128)(2,1)} %get-tuple-element.73), channel_id=1, source_target_pairs={{1,0},{2,1},{3,2},{4,3},{5,4},{6,5},{7,6},{9,8},{10,9},{11,10},{12... | collective-permute-start | bytes 2138120 | tf_op jit(solution)/shard_map/ppermute | solution.py:539
  103.3 17.4 %all-to-all-start.1 = ((s16[16,3,56,128]{3,2,1,0:T(8,128)(2,1)}), s16[16,3,56,128]{3,2,1,0:T(8,128)(2,1)S(1)}, u32[]{:S(2)}, u32[]{:S(2)}) async-start(s16[16,3,56,128]{3,2,1,0:T(8,128)(2,1)} %jobs.3), calls=%async_computation.1 | async-start | bytes 1376256 | tf_op jit(solution)/shard_map/all_to_all | solution.py:553
  120.7 39.2 %copy-start.3 = (s32[1,1,6]{2,1,0:T(1,128)S(1)}, s32[1,1,6]{2,1,0:T(1,128)}, u32[]{:S(2)}) copy-start(s32[1,1,6]{2,1,0:T(1,128)} %param.13) | copy-start | bytes 76
  120.8 22.1 %all-to-all-start = ((s16[16,3,56,128]{3,2,1,0:T(8,128)(2,1)}), s16[16,3,56,128]{3,2,1,0:T(8,128)(2,1)S(1)}, u32[]{:S(2)}, u32[]{:S(2)}) async-start(s16[16,3,56,128]{3,2,1,0:T(8,128)(2,1)} %jobs.2), calls=%async_computation | async-start | bytes 1376256 | tf_op jit(solution)/shard_map/all_to_all | solution.py:553
  145.1 14.9 %all-to-all-start.2 = ((s16[16,2,56,128]{3,2,1,0:T(8,128)(2,1)}), s16[16,2,56,128]{3,2,1,0:T(8,128)(2,1)S(1)}, u32[]{:S(2)}, u32[]{:S(2)}) async-start(s16[16,2,56,128]{3,2,1,0:T(8,128)(2,1)} %add_up.1), calls=%async_computation.2 | async-start | bytes 917504 | tf_op jit(solution)/shard_map/all_to_all | solution.py:554
  (9 other events, 188.4 us)

commit v9 on v8

--- a/solution.py
+++ b/solution.py
@@ -515,23 +515,19 @@
     note = jnp.pad(jobs.astype(BF16)[None, None], ((0, 0), (0, SIDE - 1), (0, 128 - 2 * slots)))
     note = jnp.broadcast_to(note, (wire.shape[0],) + note.shape[1:])
     wire = jnp.concatenate([wire[:, :, :RIM], note[:, :, None], wire[:, :, SIDE - RIM + 1 :]], axis=2)
-    rings = join(ring_whole([wire[0], wire[1]], (0, 1)))
-    rings, view_data, psf, views, bricks = lax.optimization_barrier(
-        (rings, view_data, psf, views, bricks)
-    )
-    near = ring_near(rings, (1, 0))
-
+    rings = ring_whole([wire[0], wire[1]], (0, 1))
+    rings[0][1], psf, views = lax.optimization_barrier((rings[0][1], psf, views))
     chosen = views[:, None] == jnp.arange(psf.shape[0])[None, :]
     taps = jnp.sum(jnp.where(chosen[:, :, None, None], psf[None], 0.0), axis=1)
     mats = job_matrices(taps, bricks)
-    data = view_data[0, 0]
     logs = jnp.log2(jnp.maximum(4.0 / background * jnp.prod(jnp.sum(psf, axis=2), axis=1), 1e-30)) - 15.9
-    mats, bricks = lax.optimization_barrier((mats, bricks))
+    rings, mats, logs = lax.optimization_barrier((rings, mats, logs))
+    rings, view_data, bricks = lax.optimization_barrier((join(rings), view_data, bricks))
+    near = ring_near(rings, (1, 0))
     above = lax.ppermute(bricks, "view", downward)
     below = lax.ppermute(bricks, "view", upward)
-    near, mats, data, above, below, logs = lax.optimization_barrier(
-        (near, mats, data, above, below, logs)
-    )
+    data = view_data[0, 0]
+    near, data, above, below = lax.optimization_barrier((near, data, above, below))
     gathered = ring_pass_on(near, (1, 0))
 
     rims = margins(gathered, me, above, below)

time: 163 us -> 159 us (0.975)
  waiting for transfers between devices: 43.8 us -> 36.9 us
  starting transfers between devices: 55.1 us -> 57.1 us
    ppermute x14, waiting for transfers between devices: 16.9 us -> 10.9 us  [torus_step(): return lax.ppermute(array, 'tile', pairs)]
    ppermute x1, starting transfers between devices: 2.41 us -> 4.15 us  [on_device(): below = lax.ppermute(bricks, 'view', upward)]
  transfers between devices with their start and end apart: 23 -> 23, of which waited for: 10 -> 10; matrix products, arithmetic and copies ran while one was open for 12% -> 12% of each run, Pallas kernels for 16% -> 17%
where the time goes in v9:
time: 159 us; the launch traced here: 158 us
  starting transfers between devices  57.1 us (36%)
  Pallas kernels  38.9 us (24%)
  waiting for transfers between devices  36.9 us (23%)
  local copies, waits for them, and re-layouts  13.9 us (9%)
  other arithmetic  10.3 us (6%)
    pallas_call x2, Pallas kernels, run_jobs(): pl.pallas_call(functools.partial(job_kernel, channel), grid=(slots,), in_...  26 us
    ppermute x14, starting transfers between devices, torus_step(): return lax.ppermute(array, 'tile', pairs)  24 us
    all_to_all x2, starting transfers between devices, on_device(): parts.append(lax.all_to_all(factors, 'tile', 0, 0, tiled=True))  11.7 us
    all_to_all x1, waiting for transfers between devices, on_device(): lax.all_to_all(add_up(owners, seen_by, logs, parts), 'tile', 0, 0, tiled=...  11.3 us
    ppermute x14, waiting for transfers between devices, torus_step(): return lax.ppermute(array, 'tile', pairs)  10.9 us
    all_to_all x2, waiting for transfers between devices, on_device(): parts.append(lax.all_to_all(factors, 'tile', 0, 0, tiled=True))  9.24 us
    ppermute x2, starting transfers between devices, on_device(): lax.ppermute(rims[2 * c + 1], 'view', downward)  7.18 us
    optimization_barrier x1, local copies, waits for them, and re-layouts, on_device(): lax.optimization_barrier((join(rings), view_data, bricks))  6.45 us
  transfers between devices with their start and end apart: 23, of which 10 were waited for; matrix products, arithmetic and copies ran while one was open for 12% of the time, Pallas kernels for 17%

profile of v9, /device:TPU:32, one launch (start us, length us, event | category | flops | bytes accessed | tf_op | source)
XLA Modules:
  0.0 157.6 jit_solution(18077450110130858593)
XLA Ops:
  11.9 2.6 %collective-permute-start.5 = (bf16[28,32,128]{2,1,0:T(8,128)(2,1)S(1)}, bf16[28,32,128]{2,1,0:T(8,128)(2,1)S(1)}, u32[]{:S(2)}, u32[]{:S(2)}) collective-permute-start(bf16[28,32,128]{2,1,0:T(8,128)(2,1)S(1)} %get-tuple-element.54.refs_4_), channel_id=1, source_target_pairs={{0,16},{8,24},{16,0},{24,8},{32,48},{40,56},{48,32},{56,40},{64,80... | collective-permute-start | bytes 688136 | tf_op jit(solution)/shard_map/ppermute | solution.py:34
  21.8 3.8 %join.1 = (bf16[112,32,128]{2,1,0:T(8,128)(2,1)}, bf16[112,32,128]{2,1,0:T(8,128)(2,1)}) custom-call(bf16[28,32,128]{2,1,0:T(8,128)(2,1)S(1)} %get-tuple-element.50.refs_0_, bf16[28,32,128]{2,1,0:T(8,128)(2,1)S(1)} %collective-permute-done.refs_1_, bf16[28,32,128]{2,1,0:T(8,128)(2,1)S(1)} %collective-permute-done.1.refs_2_, ...), custom_call_target="tpu_custom_call" | custom-call | tf_op jit(solution)/shard_map/join/pallas_call | solution.py:77
  26.6 2.3 %collective-permute-start.7 = (bf16[112,32,128]{2,1,0:T(8,128)(2,1)}, bf16[112,32,128]{2,1,0:T(8,128)(2,1)S(1)}, u32[]{:S(2)}, u32[]{:S(2)}) collective-permute-start(bf16[112,32,128]{2,1,0:T(8,128)(2,1)} %get-tuple-element.64.refs_3_.refs_0_), channel_id=1, source_target_pairs={{0,24},{8,0},{16,8},{24,16},{32,56},{40,32},{48,40},{56,48},{64,88... | collective-permute-start | bytes 2752520 | tf_op jit(solution)/shard_map/ppermute | solution.py:34
  30.2 2.0 %collective-permute-start.9 = (bf16[112,32,128]{2,1,0:T(8,128)(2,1)}, bf16[112,32,128]{2,1,0:T(8,128)(2,1)S(1)}, u32[]{:S(2)}, u32[]{:S(2)}) collective-permute-start(bf16[112,32,128]{2,1,0:T(8,128)(2,1)} %get-tuple-element.73.refs_8_.refs_0_), channel_id=1, source_target_pairs={{0,96},{8,104},{16,112},{24,120},{32,0},{40,8},{48,16},{56,24},{64... | collective-permute-start | bytes 2752520 | tf_op jit(solution)/shard_map/ppermute | solution.py:34
  32.1 6.5 %copy.67 = bf16[1,1,3,2,58,58,128]{6,5,4,3,2,1,0:T(8,128)(2,1)} copy(bf16[1,1,3,2,58,58,128]{6,3,5,4,2,1,0:T(2,128)(2,1)} %param.8) | data formatting | bytes 10334208 | tf_op jit(solution)/shard_map/optimization_barrier | solution.py:525
  41.8 4.1 %collective-permute-start.11 = (s32[3]{0:T(128)S(1)}, s32[3]{0:T(128)S(1)}, u32[]{:S(2)}, u32[]{:S(2)}) collective-permute-start(s32[3]{0:T(128)S(1)} %bitcast.48), channel_id=1, source_target_pairs={{0,1},{1,2},{2,3},{3,4},{4,5},{5,6},{6,7},{8,9},{9,10},{10,11},{11... | collective-permute-start | bytes 44 | tf_op jit(solution)/shard_map/ppermute | solution.py:528
  47.9 2.7 %collective-permute-done.8.refs_2_.refs_9_.refs_1_ = bf16[112,32,128]{2,1,0:T(8,128)(2,1)S(1)} collective-permute-done((bf16[112,32,128]{2,1,0:T(8,128)(2,1)}, bf16[112,32,128]{2,1,0:T(8,128)(2,1)S(1)}, u32[]{:S(2)}, u32[]{:S(2)}) %collective-permute-start.8) | collective-permute-done | bytes 917536 | tf_op jit(solution)/shard_map/ppermute | solution.py:34
  50.5 2.4 %halves.1 = (bf16[56,32,128]{2,1,0:T(8,128)(2,1)}, bf16[56,32,128]{2,1,0:T(8,128)(2,1)}, bf16[56,32,128]{2,1,0:T(8,128)(2,1)}, bf16[56,32,128]{2,1,0:T(8,128)(2,1)}) custom-call(bf16[112,32,128]{2,1,0:T(8,128)(2,1)S(1)} %collective-permute-done.6.refs_0_.refs_4_.refs_1_, bf16[112,32,128]{2,1,0:T(8,128)(2,1)S(1)} %collective-permute-done.7.refs_1_.refs_5_.refs_2_, ...), custom_call_target="tpu_custom_call" | custom-call | tf_op jit(solution)/shard_map/halves/pallas_call | solution.py:112
  53.9 3.2 %collective-permute-start.13 = (bf16[56,32,128]{2,1,0:T(8,128)(2,1)}, bf16[56,32,128]{2,1,0:T(8,128)(2,1)}, u32[]{:S(2)}, u32[]{:S(2)}) collective-permute-start(bf16[56,32,128]{2,1,0:T(8,128)(2,1)} %get-tuple-element.70), channel_id=1, source_target_pairs={{0,24},{8,0},{16,8},{24,16},{32,56},{40,32},{48,40},{56,48},{64,88... | collective-permute-start | bytes 1376264 | tf_op jit(solution)/shard_map/ppermute | solution.py:34
  57.4 2.9 %collective-permute-start.15 = (bf16[56,32,128]{2,1,0:T(8,128)(2,1)}, bf16[56,32,128]{2,1,0:T(8,128)(2,1)}, u32[]{:S(2)}, u32[]{:S(2)}) collective-permute-start(bf16[56,32,128]{2,1,0:T(8,128)(2,1)} %get-tuple-element.75), channel_id=1, source_target_pairs={{0,96},{8,104},{16,112},{24,120},{32,0},{40,8},{48,16},{56,24},{64... | collective-permute-start | bytes 1376264 | tf_op jit(solution)/shard_map/ppermute | solution.py:34
  60.4 4.4 %collective-permute-done.12.refs_6_.refs_3_ = bf16[56,32,128]{2,1,0:T(8,128)(2,1)S(1)} collective-permute-done((bf16[56,32,128]{2,1,0:T(8,128)(2,1)}, bf16[56,32,128]{2,1,0:T(8,128)(2,1)S(1)}, u32[]{:S(2)}, u32[]{:S(2)}) %collective-permute-start.12) | collective-permute-done | bytes 458784 | tf_op jit(solution)/shard_map/ppermute | solution.py:34
  64.8 2.8 %collective-permute-done.14.refs_11_.refs_3_ = bf16[56,32,128]{2,1,0:T(8,128)(2,1)} collective-permute-done((bf16[56,32,128]{2,1,0:T(8,128)(2,1)}, bf16[56,32,128]{2,1,0:T(8,128)(2,1)}, u32[]{:S(2)}, u32[]{:S(2)}) %collective-permute-start.14) | collective-permute-done | bytes 458784 | tf_op jit(solution)/shard_map/ppermute | solution.py:34
  67.6 3.7 %margins.1 = (bf16[3,58,16,128]{3,2,1,0:T(8,128)(2,1)}, bf16[3,58,16,128]{3,2,1,0:T(8,128)(2,1)}, bf16[3,58,16,128]{3,2,1,0:T(8,128)(2,1)}, bf16[3,58,16,128]{3,2,1,0:T(8,128)(2,1)}) custom-call(s32[1]{0:T(128)} %bitcast.17.refs_0_.me, s32[3]{0:T(128)S(1)} %collective-permute-done.10.refs_1_, s32[3]{0:T(128)S(1)} %collective-permute-done.11.refs_2_, ...), custom_call_target="tpu_custom_call" | custom-call | tf_op jit(solution)/shard_map/margins/pallas_call | solution.py:210
  73.2 3.6 %collective-permute-start.19 = (bf16[3,58,16,128]{3,2,1,0:T(8,128)(2,1)}, bf16[3,58,16,128]{3,2,1,0:T(8,128)(2,1)S(1)}, u32[]{:S(2)}, u32[]{:S(2)}) collective-permute-start(bf16[3,58,16,128]{3,2,1,0:T(8,128)(2,1)} %get-tuple-element.86), channel_id=1, source_target_pairs={{1,0},{2,1},{3,2},{4,3},{5,4},{6,5},{7,6},{9,8},{10,9},{11,10},{12... | collective-permute-start | bytes 2138120 | tf_op jit(solution)/shard_map/ppermute | solution.py:535
  76.8 2.2 %collective-permute-start.16 = (bf16[3,58,16,128]{3,2,1,0:T(8,128)(2,1)}, bf16[3,58,16,128]{3,2,1,0:T(8,128)(2,1)S(1)}, u32[]{:S(2)}, u32[]{:S(2)}) collective-permute-start(bf16[3,58,16,128]{3,2,1,0:T(8,128)(2,1)} %get-tuple-element.76), channel_id=1, source_target_pairs={{0,1},{1,2},{2,3},{3,4},{4,5},{5,6},{6,7},{8,9},{9,10},{10,11},{11... | collective-permute-start | bytes 2138120 | tf_op jit(solution)/shard_map/ppermute | solution.py:535
  79.0 3.5 %collective-permute-start.17 = (bf16[3,58,16,128]{3,2,1,0:T(8,128)(2,1)}, bf16[3,58,16,128]{3,2,1,0:T(8,128)(2,1)S(1)}, u32[]{:S(2)}, u32[]{:S(2)}) collective-permute-start(bf16[3,58,16,128]{3,2,1,0:T(8,128)(2,1)} %get-tuple-element.77), channel_id=1, source_target_pairs={{1,0},{2,1},{3,2},{4,3},{5,4},{6,5},{7,6},{9,8},{10,9},{11,10},{12... | collective-permute-start | bytes 2138120 | tf_op jit(solution)/shard_map/ppermute | solution.py:535
  85.8 13.0 %jobs.3 = s16[16,3,56,128]{3,2,1,0:T(8,128)(2,1)} custom-call(s32[1]{0:T(128)} %bitcast.17.refs_0_.me, s32[3]{0:T(128)S(1)} %bitcast.49, s32[3]{0:T(128)S(1)} %bitcast.44, f32[6]{0:T(128)S(1)} %copy-done.5, f32[6]{0:T(128)S(1)} %multiply_add_fusion.logs, bf16[112,32,128]{2,1,0:T(8,128)(2,1)} %get-tuple-element.73.refs_8_.refs_0_, ...), custom_call_target="tpu_custom_call" | custom-call | flops 23624417280 | bytes 7077888 | tf_op jit(solution)/shard_map/jobs/pallas_call | solution.py:377
  98.9 4.3 %all-to-all-start.1 = ((s16[16,3,56,128]{3,2,1,0:T(8,128)(2,1)}), s16[16,3,56,128]{3,2,1,0:T(8,128)(2,1)S(1)}, u32[]{:S(2)}, u32[]{:S(2)}) async-start(s16[16,3,56,128]{3,2,1,0:T(8,128)(2,1)} %jobs.3), calls=%async_computation.1 | async-start | bytes 1376256 | tf_op jit(solution)/shard_map/all_to_all | solution.py:549
  103.2 13.0 %jobs.2 = s16[16,3,56,128]{3,2,1,0:T(8,128)(2,1)} custom-call(s32[1]{0:T(128)} %bitcast.17.refs_0_.me, s32[3]{0:T(128)S(1)} %bitcast.50, s32[3]{0:T(128)S(1)} %bitcast.45, f32[6]{0:T(128)S(1)} %copy-done.5, f32[6]{0:T(128)S(1)} %multiply_add_fusion.logs, bf16[112,32,128]{2,1,0:T(8,128)(2,1)} %get-tuple-element.64.refs_3_.refs_0_, ...), custom_call_target="tpu_custom_call" | custom-call | flops 23624417280 | bytes 7077888 | tf_op jit(solution)/shard_map/jobs/pallas_call | solution.py:377
  116.3 7.4 %all-to-all-start = ((s16[16,3,56,128]{3,2,1,0:T(8,128)(2,1)}), s16[16,3,56,128]{3,2,1,0:T(8,128)(2,1)S(1)}, u32[]{:S(2)}, u32[]{:S(2)}) async-start(s16[16,3,56,128]{3,2,1,0:T(8,128)(2,1)} %jobs.2), calls=%async_computation | async-start | bytes 1376256 | tf_op jit(solution)/shard_map/all_to_all | solution.py:549
  128.3 9.2 %all-to-all-done.refs_0_ = s16[16,3,56,128]{3,2,1,0:T(8,128)(2,1)S(1)} async-done(((s16[16,3,56,128]{3,2,1,0:T(8,128)(2,1)}), s16[16,3,56,128]{3,2,1,0:T(8,128)(2,1)S(1)}, u32[]{:S(2)}, u32[]{:S(2)}) %all-to-all-start) | async-done | bytes 688160 | tf_op jit(solution)/shard_map/all_to_all | solution.py:549
  137.5 2.3 %add_up.1 = s16[16,2,56,128]{3,2,1,0:T(8,128)(2,1)} custom-call(s32[48]{0:T(128)S(1)} %reshape.376.owners, s32[48]{0:T(128)S(1)} %reshape.377.views, f32[6]{0:T(128)S(1)} %multiply_add_fusion.logs, s16[16,3,56,128]{3,2,1,0:T(8,128)(2,1)S(1)} %all-to-all-done.refs_0_, s16[16,3,56,128]{3,2,1,0:T(8,128)(2,1)S(1)} %all-to-all-done.1.refs_1_), custom_call_target="tpu_custom_call" | custom-call | tf_op jit(solution)/shard_map/add_up/pallas_call | solution.py:468
  139.8 4.1 %all-to-all-start.2 = ((s16[16,2,56,128]{3,2,1,0:T(8,128)(2,1)}), s16[16,2,56,128]{3,2,1,0:T(8,128)(2,1)S(1)}, u32[]{:S(2)}, u32[]{:S(2)}) async-start(s16[16,2,56,128]{3,2,1,0:T(8,128)(2,1)} %add_up.1), calls=%async_computation.2 | async-start | bytes 917504 | tf_op jit(solution)/shard_map/all_to_all | solution.py:550
  144.0 11.3 %all-to-all-done.2.total = s16[16,2,56,128]{3,2,1,0:T(8,128)(2,1)S(1)} async-done(((s16[16,2,56,128]{3,2,1,0:T(8,128)(2,1)}), s16[16,2,56,128]{3,2,1,0:T(8,128)(2,1)S(1)}, u32[]{:S(2)}, u32[]{:S(2)}) %all-to-all-start.2) | async-done | bytes 458784 | tf_op jit(solution)/shard_map/all_to_all | solution.py:550
  (124 shorter events, 39.7 us)
Async XLA Ops:
  2.6 9.3 %collective-permute-start = (bf16[28,32,128]{2,1,0:T(8,128)(2,1)S(1)}, bf16[28,32,128]{2,1,0:T(8,128)(2,1)S(1)}, u32[]{:S(2)}, u32[]{:S(2)}) collective-permute-start(bf16[28,32,128]{2,1,0:T(8,128)(2,1)S(1)} %get-tuple-element.50.refs_0_), channel_id=1, source_target_pairs={{0,32},{8,40},{16,48},{24,56},{32,64},{40,72},{48,80},{56,88},{64,... | collective-permute-start | bytes 688136 | tf_op jit(solution)/shard_map/ppermute | solution.py:34
  4.2 17.6 %collective-permute-start.1 = (bf16[28,32,128]{2,1,0:T(8,128)(2,1)S(1)}, bf16[28,32,128]{2,1,0:T(8,128)(2,1)S(1)}, u32[]{:S(2)}, u32[]{:S(2)}) collective-permute-start(bf16[28,32,128]{2,1,0:T(8,128)(2,1)S(1)} %get-tuple-element.50.refs_0_), channel_id=1, source_target_pairs={{0,96},{8,104},{16,112},{24,120},{32,0},{40,8},{48,16},{56,24},{64... | collective-permute-start | bytes 688136 | tf_op jit(solution)/shard_map/ppermute | solution.py:34
  5.9 15.8 %collective-permute-start.2 = (bf16[28,32,128]{2,1,0:T(8,128)(2,1)S(1)}, bf16[28,32,128]{2,1,0:T(8,128)(2,1)S(1)}, u32[]{:S(2)}, u32[]{:S(2)}) collective-permute-start(bf16[28,32,128]{2,1,0:T(8,128)(2,1)S(1)} %get-tuple-element.50.refs_0_), channel_id=1, source_target_pairs={{0,64},{8,72},{16,80},{24,88},{32,96},{40,104},{48,112},{56,120},{... | collective-permute-start | bytes 688136 | tf_op jit(solution)/shard_map/ppermute | solution.py:34
  7.7 14.0 %collective-permute-start.3 = (bf16[28,32,128]{2,1,0:T(8,128)(2,1)S(1)}, bf16[28,32,128]{2,1,0:T(8,128)(2,1)S(1)}, u32[]{:S(2)}, u32[]{:S(2)}) collective-permute-start(bf16[28,32,128]{2,1,0:T(8,128)(2,1)S(1)} %get-tuple-element.54.refs_4_), channel_id=1, source_target_pairs={{0,8},{8,16},{16,24},{24,0},{32,40},{40,48},{48,56},{56,32},{64,72... | collective-permute-start | bytes 688136 | tf_op jit(solution)/shard_map/ppermute | solution.py:34
  9.3 12.5 %collective-permute-start.4 = (bf16[28,32,128]{2,1,0:T(8,128)(2,1)S(1)}, bf16[28,32,128]{2,1,0:T(8,128)(2,1)S(1)}, u32[]{:S(2)}, u32[]{:S(2)}) collective-permute-start(bf16[28,32,128]{2,1,0:T(8,128)(2,1)S(1)} %get-tuple-element.54.refs_4_), channel_id=1, source_target_pairs={{0,24},{8,0},{16,8},{24,16},{32,56},{40,32},{48,40},{56,48},{64,88... | collective-permute-start | bytes 688136 | tf_op jit(solution)/shard_map/ppermute | solution.py:34
  11.9 9.8 %collective-permute-start.5 = (bf16[28,32,128]{2,1,0:T(8,128)(2,1)S(1)}, bf16[28,32,128]{2,1,0:T(8,128)(2,1)S(1)}, u32[]{:S(2)}, u32[]{:S(2)}) collective-permute-start(bf16[28,32,128]{2,1,0:T(8,128)(2,1)S(1)} %get-tuple-element.54.refs_4_), channel_id=1, source_target_pairs={{0,16},{8,24},{16,0},{24,8},{32,48},{40,56},{48,32},{56,40},{64,80... | collective-permute-start | bytes 688136 | tf_op jit(solution)/shard_map/ppermute | solution.py:34
  25.6 22.3 %collective-permute-start.6 = (bf16[112,32,128]{2,1,0:T(8,128)(2,1)}, bf16[112,32,128]{2,1,0:T(8,128)(2,1)S(1)}, u32[]{:S(2)}, u32[]{:S(2)}) collective-permute-start(bf16[112,32,128]{2,1,0:T(8,128)(2,1)} %get-tuple-element.64.refs_3_.refs_0_), channel_id=1, source_target_pairs={{0,8},{8,16},{16,24},{24,0},{32,40},{40,48},{48,56},{56,32},{64,72... | collective-permute-start | bytes 2752520 | tf_op jit(solution)/shard_map/ppermute | solution.py:34
  26.6 21.3 %collective-permute-start.7 = (bf16[112,32,128]{2,1,0:T(8,128)(2,1)}, bf16[112,32,128]{2,1,0:T(8,128)(2,1)S(1)}, u32[]{:S(2)}, u32[]{:S(2)}) collective-permute-start(bf16[112,32,128]{2,1,0:T(8,128)(2,1)} %get-tuple-element.64.refs_3_.refs_0_), channel_id=1, source_target_pairs={{0,24},{8,0},{16,8},{24,16},{32,56},{40,32},{48,40},{56,48},{64,88... | collective-permute-start | bytes 2752520 | tf_op jit(solution)/shard_map/ppermute | solution.py:34
  28.9 21.6 %collective-permute-start.8 = (bf16[112,32,128]{2,1,0:T(8,128)(2,1)}, bf16[112,32,128]{2,1,0:T(8,128)(2,1)S(1)}, u32[]{:S(2)}, u32[]{:S(2)}) collective-permute-start(bf16[112,32,128]{2,1,0:T(8,128)(2,1)} %get-tuple-element.73.refs_8_.refs_0_), channel_id=1, source_target_pairs={{0,32},{8,40},{16,48},{24,56},{32,64},{40,72},{48,80},{56,88},{64,... | collective-permute-start | bytes 2752520 | tf_op jit(solution)/shard_map/ppermute | solution.py:34
  30.2 20.4 %collective-permute-start.9 = (bf16[112,32,128]{2,1,0:T(8,128)(2,1)}, bf16[112,32,128]{2,1,0:T(8,128)(2,1)S(1)}, u32[]{:S(2)}, u32[]{:S(2)}) collective-permute-start(bf16[112,32,128]{2,1,0:T(8,128)(2,1)} %get-tuple-element.73.refs_8_.refs_0_), channel_id=1, source_target_pairs={{0,96},{8,104},{16,112},{24,120},{32,0},{40,8},{48,16},{56,24},{64... | collective-permute-start | bytes 2752520 | tf_op jit(solution)/shard_map/ppermute | solution.py:34
  38.6 3.2 %collective-permute-start.10 = (s32[3]{0:T(128)S(1)}, s32[3]{0:T(128)S(1)}, u32[]{:S(2)}, u32[]{:S(2)}) collective-permute-start(s32[3]{0:T(128)S(1)} %bitcast.47), channel_id=1, source_target_pairs={{1,0},{2,1},{3,2},{4,3},{5,4},{6,5},{7,6},{9,8},{10,9},{11,10},{12... | collective-permute-start | bytes 44 | tf_op jit(solution)/shard_map/ppermute | solution.py:527
  41.8 5.1 %collective-permute-start.11 = (s32[3]{0:T(128)S(1)}, s32[3]{0:T(128)S(1)}, u32[]{:S(2)}, u32[]{:S(2)}) collective-permute-start(s32[3]{0:T(128)S(1)} %bitcast.48), channel_id=1, source_target_pairs={{0,1},{1,2},{2,3},{3,4},{4,5},{5,6},{6,7},{8,9},{9,10},{10,11},{11... | collective-permute-start | bytes 44 | tf_op jit(solution)/shard_map/ppermute | solution.py:528
  53.9 10.9 %collective-permute-start.12 = (bf16[56,32,128]{2,1,0:T(8,128)(2,1)}, bf16[56,32,128]{2,1,0:T(8,128)(2,1)S(1)}, u32[]{:S(2)}, u32[]{:S(2)}) collective-permute-start(bf16[56,32,128]{2,1,0:T(8,128)(2,1)} %get-tuple-element.69), channel_id=1, source_target_pairs={{0,8},{8,16},{16,24},{24,0},{32,40},{40,48},{48,56},{56,32},{64,72... | collective-permute-start | bytes 1376264 | tf_op jit(solution)/shard_map/ppermute | solution.py:34
  53.9 10.9 %collective-permute-start.13 = (bf16[56,32,128]{2,1,0:T(8,128)(2,1)}, bf16[56,32,128]{2,1,0:T(8,128)(2,1)}, u32[]{:S(2)}, u32[]{:S(2)}) collective-permute-start(bf16[56,32,128]{2,1,0:T(8,128)(2,1)} %get-tuple-element.70), channel_id=1, source_target_pairs={{0,24},{8,0},{16,8},{24,16},{32,56},{40,32},{48,40},{56,48},{64,88... | collective-permute-start | bytes 1376264 | tf_op jit(solution)/shard_map/ppermute | solution.py:34
  57.1 10.4 %collective-permute-start.14 = (bf16[56,32,128]{2,1,0:T(8,128)(2,1)}, bf16[56,32,128]{2,1,0:T(8,128)(2,1)}, u32[]{:S(2)}, u32[]{:S(2)}) collective-permute-start(bf16[56,32,128]{2,1,0:T(8,128)(2,1)} %get-tuple-element.74), channel_id=1, source_target_pairs={{0,32},{8,40},{16,48},{24,56},{32,64},{40,72},{48,80},{56,88},{64,... | collective-permute-start | bytes 1376264 | tf_op jit(solution)/shard_map/ppermute | solution.py:34
  57.4 10.1 %collective-permute-start.15 = (bf16[56,32,128]{2,1,0:T(8,128)(2,1)}, bf16[56,32,128]{2,1,0:T(8,128)(2,1)}, u32[]{:S(2)}, u32[]{:S(2)}) collective-permute-start(bf16[56,32,128]{2,1,0:T(8,128)(2,1)} %get-tuple-element.75), channel_id=1, source_target_pairs={{0,96},{8,104},{16,112},{24,120},{32,0},{40,8},{48,16},{56,24},{64... | collective-permute-start | bytes 1376264 | tf_op jit(solution)/shard_map/ppermute | solution.py:34
  71.3 12.7 %collective-permute-start.18 = (bf16[3,58,16,128]{3,2,1,0:T(8,128)(2,1)}, bf16[3,58,16,128]{3,2,1,0:T(8,128)(2,1)S(1)}, u32[]{:S(2)}, u32[]{:S(2)}) collective-permute-start(bf16[3,58,16,128]{3,2,1,0:T(8,128)(2,1)} %get-tuple-element.85), channel_id=1, source_target_pairs={{0,1},{1,2},{2,3},{3,4},{4,5},{5,6},{6,7},{8,9},{9,10},{10,11},{11... | collective-permute-start | bytes 2138120 | tf_op jit(solution)/shard_map/ppermute | solution.py:535
  73.2 12.7 %collective-permute-start.19 = (bf16[3,58,16,128]{3,2,1,0:T(8,128)(2,1)}, bf16[3,58,16,128]{3,2,1,0:T(8,128)(2,1)S(1)}, u32[]{:S(2)}, u32[]{:S(2)}) collective-permute-start(bf16[3,58,16,128]{3,2,1,0:T(8,128)(2,1)} %get-tuple-element.86), channel_id=1, source_target_pairs={{1,0},{2,1},{3,2},{4,3},{5,4},{6,5},{7,6},{9,8},{10,9},{11,10},{12... | collective-permute-start | bytes 2138120 | tf_op jit(solution)/shard_map/ppermute | solution.py:535
  76.8 26.4 %collective-permute-start.16 = (bf16[3,58,16,128]{3,2,1,0:T(8,128)(2,1)}, bf16[3,58,16,128]{3,2,1,0:T(8,128)(2,1)S(1)}, u32[]{:S(2)}, u32[]{:S(2)}) collective-permute-start(bf16[3,58,16,128]{3,2,1,0:T(8,128)(2,1)} %get-tuple-element.76), channel_id=1, source_target_pairs={{0,1},{1,2},{2,3},{3,4},{4,5},{5,6},{6,7},{8,9},{9,10},{10,11},{11... | collective-permute-start | bytes 2138120 | tf_op jit(solution)/shard_map/ppermute | solution.py:535
  79.0 24.2 %collective-permute-start.17 = (bf16[3,58,16,128]{3,2,1,0:T(8,128)(2,1)}, bf16[3,58,16,128]{3,2,1,0:T(8,128)(2,1)S(1)}, u32[]{:S(2)}, u32[]{:S(2)}) collective-permute-start(bf16[3,58,16,128]{3,2,1,0:T(8,128)(2,1)} %get-tuple-element.77), channel_id=1, source_target_pairs={{1,0},{2,1},{3,2},{4,3},{5,4},{6,5},{7,6},{9,8},{10,9},{11,10},{12... | collective-permute-start | bytes 2138120 | tf_op jit(solution)/shard_map/ppermute | solution.py:535
  98.9 17.4 %all-to-all-start.1 = ((s16[16,3,56,128]{3,2,1,0:T(8,128)(2,1)}), s16[16,3,56,128]{3,2,1,0:T(8,128)(2,1)S(1)}, u32[]{:S(2)}, u32[]{:S(2)}) async-start(s16[16,3,56,128]{3,2,1,0:T(8,128)(2,1)} %jobs.3), calls=%async_computation.1 | async-start | bytes 1376256 | tf_op jit(solution)/shard_map/all_to_all | solution.py:549
  116.3 39.1 %copy-start.4 = (s32[1,1,6]{2,1,0:T(1,128)S(1)}, s32[1,1,6]{2,1,0:T(1,128)}, u32[]{:S(2)}) copy-start(s32[1,1,6]{2,1,0:T(1,128)} %param.13) | copy-start | bytes 76
  116.3 21.3 %all-to-all-start = ((s16[16,3,56,128]{3,2,1,0:T(8,128)(2,1)}), s16[16,3,56,128]{3,2,1,0:T(8,128)(2,1)S(1)}, u32[]{:S(2)}, u32[]{:S(2)}) async-start(s16[16,3,56,128]{3,2,1,0:T(8,128)(2,1)} %jobs.2), calls=%async_computation | async-start | bytes 1376256 | tf_op jit(solution)/shard_map/all_to_all | solution.py:549
  139.8 15.5 %all-to-all-start.2 = ((s16[16,2,56,128]{3,2,1,0:T(8,128)(2,1)}), s16[16,2,56,128]{3,2,1,0:T(8,128)(2,1)S(1)}, u32[]{:S(2)}, u32[]{:S(2)}) async-start(s16[16,2,56,128]{3,2,1,0:T(8,128)(2,1)} %add_up.1), calls=%async_computation.2 | async-start | bytes 917504 | tf_op jit(solution)/shard_map/all_to_all | solution.py:550
  (10 other events, 138.4 us)

commit v10 on v9

--- a/solution.py
+++ b/solution.py
@@ -253,6 +253,8 @@
 
 
 def job_kernel(channel, me, bricks, views, backdrops, logs, *refs):
+    if channel:
+        refs = refs[1:]
     parts, refs = refs[:PARTS], refs[PARTS:]
     top_ref, bottom_ref, data_ref, mz_ref, mx_ref, my_ref, myt_ref, mxt_ref, mzt_ref, out_ref = refs[:10]
     blocks, seen_data, z_high, z_low, blurred_x, back_y, back_x, sems = refs[10:]
@@ -356,9 +358,9 @@
         factor = encode(dot(jnp.concatenate([high, low, high], axis=1), mzt), level)
         for j in range(0, group, 2):
             rows = [factor[k * PADS : k * PADS + SIDE] for k in (j, j + 1)]
-            out_ref[(group * i + j) // 2, 0] = jnp.concatenate(rows, axis=0).astype(I16)
+            out_ref[(group * i + j) // 2, 0, 0] = jnp.concatenate(rows, axis=0).astype(I16)
     for k in range(SIDE // 2, 16):
-        out_ref[k, 0] = jnp.zeros_like(out_ref[k, 0])
+        out_ref[k, 0, 0] = jnp.zeros_like(out_ref[k, 0, 0])
 
 
 CHUNK = 29
@@ -368,17 +370,20 @@
 PS = PADS + SEXTRA
 
 
-def run_jobs(channel, parts, scalars, top, bottom, view_data, mats):
+def run_jobs(channel, before, parts, scalars, top, bottom, view_data, mats):
     slots = mats[0].shape[0]
     hbm = pl.BlockSpec(memory_space=pltpu.HBM)
     smem = pl.BlockSpec(memory_space=pltpu.SMEM)
-    specs = [smem] * len(scalars) + [hbm] * (len(parts) + 3)
+    specs = [smem] * len(scalars) + [hbm] * (len(before) + len(parts) + 3)
     specs += [pl.BlockSpec((1,) + m.shape[1:], lambda slot: (slot, 0, 0)) for m in mats]
     return pl.pallas_call(
         functools.partial(job_kernel, channel),
         grid=(slots,),
         in_specs=specs,
-        out_specs=pl.BlockSpec((16, 1, 2 * SIDE, 128), lambda slot: (0, slot, 0, 0)),
+        out_specs=pl.BlockSpec(
+            (16, 1, 1, 2 * SIDE, 128), lambda slot: (0, channel, slot, 0, 0)
+        ),
+        input_output_aliases={len(scalars): 0} if before else {},
         scratch_shapes=[
             pltpu.VMEM((2, WIN, PADW, 128), BF16),
             pltpu.VMEM((2, WIN, WIN, 128), BF16),
@@ -389,7 +394,7 @@
             pltpu.VMEM((PADS * PS, 128), F32),
             pltpu.SemaphoreType.DMA((2, 6)),
         ],
-        out_shape=pltpu.HBM((16, slots, 2 * SIDE, 128), I16),
+        out_shape=pltpu.HBM((16, 2, slots, 2 * SIDE, 128), I16),
         compiler_params=pltpu.CompilerParams(vmem_limit_bytes=18 << 20),
         cost_estimate=pl.CostEstimate(
             flops=slots * 20 * 128 * (WIN * PADW * (256 + 192 + 192 + 96) + 2 * SIDE * PADS * 192),
@@ -397,7 +402,7 @@
             bytes_accessed=slots * (2 * WIN * PADW * 128 * 2 + 16 * 2 * SIDE * 128 * 4),
         ),
         name="jobs",
-    )(*scalars, *gathered_memory(parts), top, bottom, *far_memory(view_data, *mats))
+    )(*scalars, *before, *gathered_memory(parts), top, bottom, *far_memory(view_data, *mats))
 
 
 def bands(taps, positions_out, positions_in):
@@ -448,32 +453,34 @@
 def add_kernel(owners, views, logs, *refs):
     total, level = refs[-2:]
     out_ref = refs[-3]
-    workers, slots = refs[0].shape[:2]
+    parts_ref = refs[0]
+    workers, channels, slots = parts_ref.shape[:3]
     jobs = range(workers * slots)
     for b in range(workers):
         level[b] = -200.0
     for i in jobs:
         level[owners[i]] = jnp.maximum(level[owners[i]], logs[views[i]] + MORE)
-    for channel, parts_ref in enumerate(refs[:-3]):
+    for channel in range(channels):
         total[...] = jnp.zeros_like(total)
         for i in jobs:
-            total[owners[i]] += decode(parts_ref[i // slots, i % slots], logs[views[i]])
+            total[owners[i]] += decode(parts_ref[i // slots, channel, i % slots], logs[views[i]])
         for b in range(workers):
             out_ref[b, channel] = encode(total[b], level[b]).astype(I16)
 
 
 def add_up(owners, views, logs, parts):
     vmem, smem = pl.BlockSpec(memory_space=pltpu.VMEM), pl.BlockSpec(memory_space=pltpu.SMEM)
-    workers, rows = parts[0].shape[0], parts[0].shape[2:]
+    workers, channels, _, *rows = parts.shape
+    rows = tuple(rows)
     return pl.pallas_call(
         add_kernel,
-        in_specs=[smem] * 3 + [vmem] * len(parts),
+        in_specs=[smem] * 3 + [vmem],
         out_specs=vmem,
-        out_shape=pltpu.HBM((workers, len(parts)) + rows, I16),
+        out_shape=pltpu.HBM((workers, channels) + rows, I16),
         scratch_shapes=[pltpu.VMEM((workers,) + rows, F32), pltpu.SMEM((workers,), F32)],
         compiler_params=pltpu.CompilerParams(vmem_limit_bytes=8 << 20),
         name="add_up",
-    )(owners, views, logs, *parts)
+    )(owners, views, logs, parts)
 
 
 def update_kernel(met, logs, est_ref, total, out_ref):
@@ -542,11 +549,15 @@
     notes = notes.astype(I32)
     owners, seen_by = notes[:, :slots].reshape(-1), notes[:, slots:].reshape(-1)
 
-    parts = []
+    factors = []
     scalars = (me, bricks, views, background, logs)
     for channel in range(2):
-        factors = run_jobs(channel, gathered[channel], scalars, *edges[channel], data, mats)
-        parts.append(lax.all_to_all(factors, "tile", 0, 0, tiled=True))
+        factors = [
+            run_jobs(
+                channel, factors, gathered[channel], scalars, *edges[channel], data, mats
+            )
+        ]
+    parts = lax.all_to_all(factors[0], "tile", 0, 0, tiled=True)
     total = lax.all_to_all(add_up(owners, seen_by, logs, parts), "tile", 0, 0, tiled=True)
     return update(intersection[0, 0], logs, estimate, total)
 

time: 159 us -> 160 us (level)
  waiting for transfers between devices: 36.9 us -> 43.9 us
  starting transfers between devices: 57.1 us -> 51 us
    all_to_all x2 -> x1, starting transfers between devices: 11.7 us -> 4.49 us  [on_device(): parts = lax.all_to_all(factors[0], 'tile', 0, 0, tiled=True)]
    all_to_all x2 -> x1, waiting for transfers between devices: 9.24 us -> 15.6 us  [on_device(): parts = lax.all_to_all(factors[0], 'tile', 0, 0, tiled=True)]
  transfers between devices with their start and end apart: 23 -> 22, of which waited for: 10 -> 10; matrix products, arithmetic and copies ran while one was open for 12% -> 12% of each run, Pallas kernels for 17% -> 8%
where the time goes in v10:
time: 160 us; the launch traced here: 158 us
  starting transfers between devices  51 us (32%)
  waiting for transfers between devices  43.9 us (27%)
  Pallas kernels  38.8 us (24%)
  local copies, waits for them, and re-layouts  13.9 us (9%)
  other arithmetic  10.3 us (6%)
    pallas_call x2, Pallas kernels, run_jobs(): pl.pallas_call(functools.partial(job_kernel, channel), grid=(slots,), in_...  26 us
    ppermute x14, starting transfers between devices, torus_step(): return lax.ppermute(array, 'tile', pairs)  24 us
    all_to_all x1, waiting for transfers between devices, on_device(): parts = lax.all_to_all(factors[0], 'tile', 0, 0, tiled=True)  15.6 us
    all_to_all x1, waiting for transfers between devices, on_device(): lax.all_to_all(add_up(owners, seen_by, logs, parts), 'tile', 0, 0, tiled=...  12 us
    ppermute x14, waiting for transfers between devices, torus_step(): return lax.ppermute(array, 'tile', pairs)  10.9 us
    ppermute x2, starting transfers between devices, on_device(): lax.ppermute(rims[2 * c + 1], 'view', downward)  7.17 us
    optimization_barrier x1, local copies, waits for them, and re-layouts, on_device(): lax.optimization_barrier((join(rings), view_data, bricks))  6.46 us
    all_to_all x1, starting transfers between devices, on_device(): lax.all_to_all(add_up(owners, seen_by, logs, parts), 'tile', 0, 0, tiled=...  5.15 us
  transfers between devices with their start and end apart: 22, of which 10 were waited for; matrix products, arithmetic and copies ran while one was open for 12% of the time, Pallas kernels for 8%

profile of v10, /device:TPU:32, one launch (start us, length us, event | category | flops | bytes accessed | tf_op | source)
XLA Modules:
  0.0 158.4 jit_solution(10496560688825195628)
XLA Ops:
  11.9 2.6 %collective-permute-start.5 = (bf16[28,32,128]{2,1,0:T(8,128)(2,1)S(1)}, bf16[28,32,128]{2,1,0:T(8,128)(2,1)S(1)}, u32[]{:S(2)}, u32[]{:S(2)}) collective-permute-start(bf16[28,32,128]{2,1,0:T(8,128)(2,1)S(1)} %get-tuple-element.54.refs_4_), channel_id=1, source_target_pairs={{0,16},{8,24},{16,0},{24,8},{32,48},{40,56},{48,32},{56,40},{64,80... | collective-permute-start | bytes 688136 | tf_op jit(solution)/shard_map/ppermute | solution.py:34
  21.8 3.7 %join.1 = (bf16[112,32,128]{2,1,0:T(8,128)(2,1)}, bf16[112,32,128]{2,1,0:T(8,128)(2,1)}) custom-call(bf16[28,32,128]{2,1,0:T(8,128)(2,1)S(1)} %get-tuple-element.50.refs_0_, bf16[28,32,128]{2,1,0:T(8,128)(2,1)S(1)} %collective-permute-done.refs_1_, bf16[28,32,128]{2,1,0:T(8,128)(2,1)S(1)} %collective-permute-done.1.refs_2_, ...), custom_call_target="tpu_custom_call" | custom-call | tf_op jit(solution)/shard_map/join/pallas_call | solution.py:77
  26.5 2.3 %collective-permute-start.7 = (bf16[112,32,128]{2,1,0:T(8,128)(2,1)}, bf16[112,32,128]{2,1,0:T(8,128)(2,1)S(1)}, u32[]{:S(2)}, u32[]{:S(2)}) collective-permute-start(bf16[112,32,128]{2,1,0:T(8,128)(2,1)} %get-tuple-element.64.refs_3_.refs_0_), channel_id=1, source_target_pairs={{0,24},{8,0},{16,8},{24,16},{32,56},{40,32},{48,40},{56,48},{64,88... | collective-permute-start | bytes 2752520 | tf_op jit(solution)/shard_map/ppermute | solution.py:34
  30.1 2.0 %collective-permute-start.9 = (bf16[112,32,128]{2,1,0:T(8,128)(2,1)}, bf16[112,32,128]{2,1,0:T(8,128)(2,1)S(1)}, u32[]{:S(2)}, u32[]{:S(2)}) collective-permute-start(bf16[112,32,128]{2,1,0:T(8,128)(2,1)} %get-tuple-element.73.refs_8_.refs_1_), channel_id=1, source_target_pairs={{0,96},{8,104},{16,112},{24,120},{32,0},{40,8},{48,16},{56,24},{64... | collective-permute-start | bytes 2752520 | tf_op jit(solution)/shard_map/ppermute | solution.py:34
  32.0 6.5 %copy.68 = bf16[1,1,3,2,58,58,128]{6,5,4,3,2,1,0:T(8,128)(2,1)} copy(bf16[1,1,3,2,58,58,128]{6,3,5,4,2,1,0:T(2,128)(2,1)} %param.8) | data formatting | bytes 10334208 | tf_op jit(solution)/shard_map/optimization_barrier | solution.py:532
  41.7 4.1 %collective-permute-start.11 = (s32[3]{0:T(128)S(1)}, s32[3]{0:T(128)S(1)}, u32[]{:S(2)}, u32[]{:S(2)}) collective-permute-start(s32[3]{0:T(128)S(1)} %bitcast.48), channel_id=1, source_target_pairs={{0,1},{1,2},{2,3},{3,4},{4,5},{5,6},{6,7},{8,9},{9,10},{10,11},{11... | collective-permute-start | bytes 44 | tf_op jit(solution)/shard_map/ppermute | solution.py:535
  47.8 2.7 %collective-permute-done.8.refs_2_.refs_9_ = bf16[112,32,128]{2,1,0:T(8,128)(2,1)S(1)} collective-permute-done((bf16[112,32,128]{2,1,0:T(8,128)(2,1)}, bf16[112,32,128]{2,1,0:T(8,128)(2,1)S(1)}, u32[]{:S(2)}, u32[]{:S(2)}) %collective-permute-start.8) | collective-permute-done | bytes 917536 | tf_op jit(solution)/shard_map/ppermute | solution.py:34
  50.4 2.4 %halves.1 = (bf16[56,32,128]{2,1,0:T(8,128)(2,1)}, bf16[56,32,128]{2,1,0:T(8,128)(2,1)}, bf16[56,32,128]{2,1,0:T(8,128)(2,1)}, bf16[56,32,128]{2,1,0:T(8,128)(2,1)}) custom-call(bf16[112,32,128]{2,1,0:T(8,128)(2,1)S(1)} %collective-permute-done.6.refs_0_.refs_4_.refs_1_, bf16[112,32,128]{2,1,0:T(8,128)(2,1)S(1)} %collective-permute-done.7.refs_1_.refs_5_.refs_2_, ...), custom_call_target="tpu_custom_call" | custom-call | tf_op jit(solution)/shard_map/halves/pallas_call | solution.py:112
  53.8 3.2 %collective-permute-start.13 = (bf16[56,32,128]{2,1,0:T(8,128)(2,1)}, bf16[56,32,128]{2,1,0:T(8,128)(2,1)}, u32[]{:S(2)}, u32[]{:S(2)}) collective-permute-start(bf16[56,32,128]{2,1,0:T(8,128)(2,1)} %get-tuple-element.70), channel_id=1, source_target_pairs={{0,24},{8,0},{16,8},{24,16},{32,56},{40,32},{48,40},{56,48},{64,88... | collective-permute-start | bytes 1376264 | tf_op jit(solution)/shard_map/ppermute | solution.py:34
  57.3 2.9 %collective-permute-start.15 = (bf16[56,32,128]{2,1,0:T(8,128)(2,1)}, bf16[56,32,128]{2,1,0:T(8,128)(2,1)}, u32[]{:S(2)}, u32[]{:S(2)}) collective-permute-start(bf16[56,32,128]{2,1,0:T(8,128)(2,1)} %get-tuple-element.75), channel_id=1, source_target_pairs={{0,96},{8,104},{16,112},{24,120},{32,0},{40,8},{48,16},{56,24},{64... | collective-permute-start | bytes 1376264 | tf_op jit(solution)/shard_map/ppermute | solution.py:34
  60.2 4.4 %collective-permute-done.12.refs_6_.refs_3_ = bf16[56,32,128]{2,1,0:T(8,128)(2,1)S(1)} collective-permute-done((bf16[56,32,128]{2,1,0:T(8,128)(2,1)}, bf16[56,32,128]{2,1,0:T(8,128)(2,1)S(1)}, u32[]{:S(2)}, u32[]{:S(2)}) %collective-permute-start.12) | collective-permute-done | bytes 458784 | tf_op jit(solution)/shard_map/ppermute | solution.py:34
  64.7 2.8 %collective-permute-done.14.refs_11_.refs_4_ = bf16[56,32,128]{2,1,0:T(8,128)(2,1)} collective-permute-done((bf16[56,32,128]{2,1,0:T(8,128)(2,1)}, bf16[56,32,128]{2,1,0:T(8,128)(2,1)}, u32[]{:S(2)}, u32[]{:S(2)}) %collective-permute-start.14) | collective-permute-done | bytes 458784 | tf_op jit(solution)/shard_map/ppermute | solution.py:34
  67.5 3.7 %margins.1 = (bf16[3,58,16,128]{3,2,1,0:T(8,128)(2,1)}, bf16[3,58,16,128]{3,2,1,0:T(8,128)(2,1)}, bf16[3,58,16,128]{3,2,1,0:T(8,128)(2,1)}, bf16[3,58,16,128]{3,2,1,0:T(8,128)(2,1)}) custom-call(s32[1]{0:T(128)} %bitcast.17.refs_0_.me, s32[3]{0:T(128)S(1)} %collective-permute-done.10.refs_1_, s32[3]{0:T(128)S(1)} %collective-permute-done.11.refs_2_, ...), custom_call_target="tpu_custom_call" | custom-call | tf_op jit(solution)/shard_map/margins/pallas_call | solution.py:210
  71.1 1.9 %collective-permute-start.16 = (bf16[3,58,16,128]{3,2,1,0:T(8,128)(2,1)}, bf16[3,58,16,128]{3,2,1,0:T(8,128)(2,1)S(1)}, u32[]{:S(2)}, u32[]{:S(2)}) collective-permute-start(bf16[3,58,16,128]{3,2,1,0:T(8,128)(2,1)} %get-tuple-element.76), channel_id=1, source_target_pairs={{0,1},{1,2},{2,3},{3,4},{4,5},{5,6},{6,7},{8,9},{9,10},{10,11},{11... | collective-permute-start | bytes 2138120 | tf_op jit(solution)/shard_map/ppermute | solution.py:542
  73.1 3.6 %collective-permute-start.17 = (bf16[3,58,16,128]{3,2,1,0:T(8,128)(2,1)}, bf16[3,58,16,128]{3,2,1,0:T(8,128)(2,1)S(1)}, u32[]{:S(2)}, u32[]{:S(2)}) collective-permute-start(bf16[3,58,16,128]{3,2,1,0:T(8,128)(2,1)} %get-tuple-element.77), channel_id=1, source_target_pairs={{1,0},{2,1},{3,2},{4,3},{5,4},{6,5},{7,6},{9,8},{10,9},{11,10},{12... | collective-permute-start | bytes 2138120 | tf_op jit(solution)/shard_map/ppermute | solution.py:542
  76.7 2.2 %collective-permute-start.18 = (bf16[3,58,16,128]{3,2,1,0:T(8,128)(2,1)}, bf16[3,58,16,128]{3,2,1,0:T(8,128)(2,1)S(1)}, u32[]{:S(2)}, u32[]{:S(2)}) collective-permute-start(bf16[3,58,16,128]{3,2,1,0:T(8,128)(2,1)} %get-tuple-element.85), channel_id=1, source_target_pairs={{0,1},{1,2},{2,3},{3,4},{4,5},{5,6},{6,7},{8,9},{9,10},{10,11},{11... | collective-permute-start | bytes 2138120 | tf_op jit(solution)/shard_map/ppermute | solution.py:542
  78.9 3.5 %collective-permute-start.19 = (bf16[3,58,16,128]{3,2,1,0:T(8,128)(2,1)}, bf16[3,58,16,128]{3,2,1,0:T(8,128)(2,1)S(1)}, u32[]{:S(2)}, u32[]{:S(2)}) collective-permute-start(bf16[3,58,16,128]{3,2,1,0:T(8,128)(2,1)} %get-tuple-element.86), channel_id=1, source_target_pairs={{1,0},{2,1},{3,2},{4,3},{5,4},{6,5},{7,6},{9,8},{10,9},{11,10},{12... | collective-permute-start | bytes 2138120 | tf_op jit(solution)/shard_map/ppermute | solution.py:542
  85.7 13.0 %jobs.2.refs_0_ = s16[16,2,3,56,128]{4,3,2,1,0:T(8,128)(2,1)} custom-call(s32[1]{0:T(128)} %bitcast.17.refs_0_.me, s32[3]{0:T(128)S(1)} %bitcast.49, s32[3]{0:T(128)S(1)} %bitcast.44, f32[6]{0:T(128)S(1)} %copy-done.5, f32[6]{0:T(128)S(1)} %multiply_add_fusion.logs, bf16[112,32,128]{2,1,0:T(8,128)(2,1)} %get-tuple-element.64.refs_3_.refs_0_, ...), custom_call_target="tpu_custom_call" | custom-call | flops 23624417280 | bytes 7077888 | tf_op jit(solution)/shard_map/jobs/pallas_call | solution.py:379
  98.7 13.0 %jobs.3 = s16[16,2,3,56,128]{4,3,2,1,0:T(8,128)(2,1)} custom-call(s32[1]{0:T(128)} %bitcast.17.refs_0_.me, s32[3]{0:T(128)S(1)} %bitcast.50, s32[3]{0:T(128)S(1)} %bitcast.45, f32[6]{0:T(128)S(1)} %copy-done.5, f32[6]{0:T(128)S(1)} %multiply_add_fusion.logs, s16[16,2,3,56,128]{4,3,2,1,0:T(8,128)(2,1)} %jobs.2.refs_0_, ...), custom_call_target="tpu_custom_call", output_to_operand_aliasing={{}: (5, {})} | custom-call | flops 23624417280 | bytes 7077888 | tf_op jit(solution)/shard_map/jobs/pallas_call | solution.py:379
  111.8 4.5 %all-to-all-start = ((s16[16,2,3,56,128]{4,3,2,1,0:T(8,128)(2,1)}), s16[16,2,3,56,128]{4,3,2,1,0:T(8,128)(2,1)S(1)}, u32[]{:S(2)}, u32[]{:S(2)}) async-start(s16[16,2,3,56,128]{4,3,2,1,0:T(8,128)(2,1)} %jobs.3), calls=%async_computation | async-start | bytes 2752512 | tf_op jit(solution)/shard_map/all_to_all | solution.py:560
  121.0 15.6 %all-to-all-done.refs_0_ = s16[16,2,3,56,128]{4,3,2,1,0:T(8,128)(2,1)S(1)} async-done(((s16[16,2,3,56,128]{4,3,2,1,0:T(8,128)(2,1)}), s16[16,2,3,56,128]{4,3,2,1,0:T(8,128)(2,1)S(1)}, u32[]{:S(2)}, u32[]{:S(2)}) %all-to-all-start) | async-done | bytes 1376288 | tf_op jit(solution)/shard_map/all_to_all | solution.py:560
  136.5 2.3 %add_up.1 = s16[16,2,56,128]{3,2,1,0:T(8,128)(2,1)} custom-call(s32[48]{0:T(128)S(1)} %reshape.376.owners, s32[48]{0:T(128)S(1)} %reshape.377.views, f32[6]{0:T(128)S(1)} %multiply_add_fusion.logs, s16[16,2,3,56,128]{4,3,2,1,0:T(8,128)(2,1)S(1)} %all-to-all-done.refs_0_), custom_call_target="tpu_custom_call" | custom-call | tf_op jit(solution)/shard_map/add_up/pallas_call | solution.py:475
  138.8 5.2 %all-to-all-start.1 = ((s16[16,2,56,128]{3,2,1,0:T(8,128)(2,1)}), s16[16,2,56,128]{3,2,1,0:T(8,128)(2,1)S(1)}, u32[]{:S(2)}, u32[]{:S(2)}) async-start(s16[16,2,56,128]{3,2,1,0:T(8,128)(2,1)} %add_up.1), calls=%async_computation.1 | async-start | bytes 917504 | tf_op jit(solution)/shard_map/all_to_all | solution.py:561
  144.1 12.0 %all-to-all-done.1.total = s16[16,2,56,128]{3,2,1,0:T(8,128)(2,1)S(1)} async-done(((s16[16,2,56,128]{3,2,1,0:T(8,128)(2,1)}), s16[16,2,56,128]{3,2,1,0:T(8,128)(2,1)S(1)}, u32[]{:S(2)}, u32[]{:S(2)}) %all-to-all-start.1) | async-done | bytes 458784 | tf_op jit(solution)/shard_map/all_to_all | solution.py:561
  (122 shorter events, 37.8 us)
Async XLA Ops:
  2.6 9.3 %collective-permute-start = (bf16[28,32,128]{2,1,0:T(8,128)(2,1)S(1)}, bf16[28,32,128]{2,1,0:T(8,128)(2,1)S(1)}, u32[]{:S(2)}, u32[]{:S(2)}) collective-permute-start(bf16[28,32,128]{2,1,0:T(8,128)(2,1)S(1)} %get-tuple-element.50.refs_0_), channel_id=1, source_target_pairs={{0,32},{8,40},{16,48},{24,56},{32,64},{40,72},{48,80},{56,88},{64,... | collective-permute-start | bytes 688136 | tf_op jit(solution)/shard_map/ppermute | solution.py:34
  4.2 17.5 %collective-permute-start.1 = (bf16[28,32,128]{2,1,0:T(8,128)(2,1)S(1)}, bf16[28,32,128]{2,1,0:T(8,128)(2,1)S(1)}, u32[]{:S(2)}, u32[]{:S(2)}) collective-permute-start(bf16[28,32,128]{2,1,0:T(8,128)(2,1)S(1)} %get-tuple-element.50.refs_0_), channel_id=1, source_target_pairs={{0,96},{8,104},{16,112},{24,120},{32,0},{40,8},{48,16},{56,24},{64... | collective-permute-start | bytes 688136 | tf_op jit(solution)/shard_map/ppermute | solution.py:34
  5.9 15.8 %collective-permute-start.2 = (bf16[28,32,128]{2,1,0:T(8,128)(2,1)S(1)}, bf16[28,32,128]{2,1,0:T(8,128)(2,1)S(1)}, u32[]{:S(2)}, u32[]{:S(2)}) collective-permute-start(bf16[28,32,128]{2,1,0:T(8,128)(2,1)S(1)} %get-tuple-element.50.refs_0_), channel_id=1, source_target_pairs={{0,64},{8,72},{16,80},{24,88},{32,96},{40,104},{48,112},{56,120},{... | collective-permute-start | bytes 688136 | tf_op jit(solution)/shard_map/ppermute | solution.py:34
  7.7 14.0 %collective-permute-start.3 = (bf16[28,32,128]{2,1,0:T(8,128)(2,1)S(1)}, bf16[28,32,128]{2,1,0:T(8,128)(2,1)S(1)}, u32[]{:S(2)}, u32[]{:S(2)}) collective-permute-start(bf16[28,32,128]{2,1,0:T(8,128)(2,1)S(1)} %get-tuple-element.54.refs_4_), channel_id=1, source_target_pairs={{0,8},{8,16},{16,24},{24,0},{32,40},{40,48},{48,56},{56,32},{64,72... | collective-permute-start | bytes 688136 | tf_op jit(solution)/shard_map/ppermute | solution.py:34
  9.3 12.4 %collective-permute-start.4 = (bf16[28,32,128]{2,1,0:T(8,128)(2,1)S(1)}, bf16[28,32,128]{2,1,0:T(8,128)(2,1)S(1)}, u32[]{:S(2)}, u32[]{:S(2)}) collective-permute-start(bf16[28,32,128]{2,1,0:T(8,128)(2,1)S(1)} %get-tuple-element.54.refs_4_), channel_id=1, source_target_pairs={{0,24},{8,0},{16,8},{24,16},{32,56},{40,32},{48,40},{56,48},{64,88... | collective-permute-start | bytes 688136 | tf_op jit(solution)/shard_map/ppermute | solution.py:34
  11.9 9.8 %collective-permute-start.5 = (bf16[28,32,128]{2,1,0:T(8,128)(2,1)S(1)}, bf16[28,32,128]{2,1,0:T(8,128)(2,1)S(1)}, u32[]{:S(2)}, u32[]{:S(2)}) collective-permute-start(bf16[28,32,128]{2,1,0:T(8,128)(2,1)S(1)} %get-tuple-element.54.refs_4_), channel_id=1, source_target_pairs={{0,16},{8,24},{16,0},{24,8},{32,48},{40,56},{48,32},{56,40},{64,80... | collective-permute-start | bytes 688136 | tf_op jit(solution)/shard_map/ppermute | solution.py:34
  25.5 22.3 %collective-permute-start.6 = (bf16[112,32,128]{2,1,0:T(8,128)(2,1)}, bf16[112,32,128]{2,1,0:T(8,128)(2,1)S(1)}, u32[]{:S(2)}, u32[]{:S(2)}) collective-permute-start(bf16[112,32,128]{2,1,0:T(8,128)(2,1)} %get-tuple-element.64.refs_3_.refs_0_), channel_id=1, source_target_pairs={{0,8},{8,16},{16,24},{24,0},{32,40},{40,48},{48,56},{56,32},{64,72... | collective-permute-start | bytes 2752520 | tf_op jit(solution)/shard_map/ppermute | solution.py:34
  26.5 21.3 %collective-permute-start.7 = (bf16[112,32,128]{2,1,0:T(8,128)(2,1)}, bf16[112,32,128]{2,1,0:T(8,128)(2,1)S(1)}, u32[]{:S(2)}, u32[]{:S(2)}) collective-permute-start(bf16[112,32,128]{2,1,0:T(8,128)(2,1)} %get-tuple-element.64.refs_3_.refs_0_), channel_id=1, source_target_pairs={{0,24},{8,0},{16,8},{24,16},{32,56},{40,32},{48,40},{56,48},{64,88... | collective-permute-start | bytes 2752520 | tf_op jit(solution)/shard_map/ppermute | solution.py:34
  28.8 21.6 %collective-permute-start.8 = (bf16[112,32,128]{2,1,0:T(8,128)(2,1)}, bf16[112,32,128]{2,1,0:T(8,128)(2,1)S(1)}, u32[]{:S(2)}, u32[]{:S(2)}) collective-permute-start(bf16[112,32,128]{2,1,0:T(8,128)(2,1)} %get-tuple-element.73.refs_8_.refs_1_), channel_id=1, source_target_pairs={{0,32},{8,40},{16,48},{24,56},{32,64},{40,72},{48,80},{56,88},{64,... | collective-permute-start | bytes 2752520 | tf_op jit(solution)/shard_map/ppermute | solution.py:34
  30.1 20.4 %collective-permute-start.9 = (bf16[112,32,128]{2,1,0:T(8,128)(2,1)}, bf16[112,32,128]{2,1,0:T(8,128)(2,1)S(1)}, u32[]{:S(2)}, u32[]{:S(2)}) collective-permute-start(bf16[112,32,128]{2,1,0:T(8,128)(2,1)} %get-tuple-element.73.refs_8_.refs_1_), channel_id=1, source_target_pairs={{0,96},{8,104},{16,112},{24,120},{32,0},{40,8},{48,16},{56,24},{64... | collective-permute-start | bytes 2752520 | tf_op jit(solution)/shard_map/ppermute | solution.py:34
  38.5 3.2 %collective-permute-start.10 = (s32[3]{0:T(128)S(1)}, s32[3]{0:T(128)S(1)}, u32[]{:S(2)}, u32[]{:S(2)}) collective-permute-start(s32[3]{0:T(128)S(1)} %bitcast.47), channel_id=1, source_target_pairs={{1,0},{2,1},{3,2},{4,3},{5,4},{6,5},{7,6},{9,8},{10,9},{11,10},{12... | collective-permute-start | bytes 44 | tf_op jit(solution)/shard_map/ppermute | solution.py:534
  41.7 5.1 %collective-permute-start.11 = (s32[3]{0:T(128)S(1)}, s32[3]{0:T(128)S(1)}, u32[]{:S(2)}, u32[]{:S(2)}) collective-permute-start(s32[3]{0:T(128)S(1)} %bitcast.48), channel_id=1, source_target_pairs={{0,1},{1,2},{2,3},{3,4},{4,5},{5,6},{6,7},{8,9},{9,10},{10,11},{11... | collective-permute-start | bytes 44 | tf_op jit(solution)/shard_map/ppermute | solution.py:535
  53.8 10.9 %collective-permute-start.12 = (bf16[56,32,128]{2,1,0:T(8,128)(2,1)}, bf16[56,32,128]{2,1,0:T(8,128)(2,1)S(1)}, u32[]{:S(2)}, u32[]{:S(2)}) collective-permute-start(bf16[56,32,128]{2,1,0:T(8,128)(2,1)} %get-tuple-element.69), channel_id=1, source_target_pairs={{0,8},{8,16},{16,24},{24,0},{32,40},{40,48},{48,56},{56,32},{64,72... | collective-permute-start | bytes 1376264 | tf_op jit(solution)/shard_map/ppermute | solution.py:34
  53.8 10.9 %collective-permute-start.13 = (bf16[56,32,128]{2,1,0:T(8,128)(2,1)}, bf16[56,32,128]{2,1,0:T(8,128)(2,1)}, u32[]{:S(2)}, u32[]{:S(2)}) collective-permute-start(bf16[56,32,128]{2,1,0:T(8,128)(2,1)} %get-tuple-element.70), channel_id=1, source_target_pairs={{0,24},{8,0},{16,8},{24,16},{32,56},{40,32},{48,40},{56,48},{64,88... | collective-permute-start | bytes 1376264 | tf_op jit(solution)/shard_map/ppermute | solution.py:34
  57.0 10.4 %collective-permute-start.14 = (bf16[56,32,128]{2,1,0:T(8,128)(2,1)}, bf16[56,32,128]{2,1,0:T(8,128)(2,1)}, u32[]{:S(2)}, u32[]{:S(2)}) collective-permute-start(bf16[56,32,128]{2,1,0:T(8,128)(2,1)} %get-tuple-element.74), channel_id=1, source_target_pairs={{0,32},{8,40},{16,48},{24,56},{32,64},{40,72},{48,80},{56,88},{64,... | collective-permute-start | bytes 1376264 | tf_op jit(solution)/shard_map/ppermute | solution.py:34
  57.3 10.1 %collective-permute-start.15 = (bf16[56,32,128]{2,1,0:T(8,128)(2,1)}, bf16[56,32,128]{2,1,0:T(8,128)(2,1)}, u32[]{:S(2)}, u32[]{:S(2)}) collective-permute-start(bf16[56,32,128]{2,1,0:T(8,128)(2,1)} %get-tuple-element.75), channel_id=1, source_target_pairs={{0,96},{8,104},{16,112},{24,120},{32,0},{40,8},{48,16},{56,24},{64... | collective-permute-start | bytes 1376264 | tf_op jit(solution)/shard_map/ppermute | solution.py:34
  71.1 12.7 %collective-permute-start.16 = (bf16[3,58,16,128]{3,2,1,0:T(8,128)(2,1)}, bf16[3,58,16,128]{3,2,1,0:T(8,128)(2,1)S(1)}, u32[]{:S(2)}, u32[]{:S(2)}) collective-permute-start(bf16[3,58,16,128]{3,2,1,0:T(8,128)(2,1)} %get-tuple-element.76), channel_id=1, source_target_pairs={{0,1},{1,2},{2,3},{3,4},{4,5},{5,6},{6,7},{8,9},{9,10},{10,11},{11... | collective-permute-start | bytes 2138120 | tf_op jit(solution)/shard_map/ppermute | solution.py:542
  73.1 12.7 %collective-permute-start.17 = (bf16[3,58,16,128]{3,2,1,0:T(8,128)(2,1)}, bf16[3,58,16,128]{3,2,1,0:T(8,128)(2,1)S(1)}, u32[]{:S(2)}, u32[]{:S(2)}) collective-permute-start(bf16[3,58,16,128]{3,2,1,0:T(8,128)(2,1)} %get-tuple-element.77), channel_id=1, source_target_pairs={{1,0},{2,1},{3,2},{4,3},{5,4},{6,5},{7,6},{9,8},{10,9},{11,10},{12... | collective-permute-start | bytes 2138120 | tf_op jit(solution)/shard_map/ppermute | solution.py:542
  76.7 22.0 %collective-permute-start.18 = (bf16[3,58,16,128]{3,2,1,0:T(8,128)(2,1)}, bf16[3,58,16,128]{3,2,1,0:T(8,128)(2,1)S(1)}, u32[]{:S(2)}, u32[]{:S(2)}) collective-permute-start(bf16[3,58,16,128]{3,2,1,0:T(8,128)(2,1)} %get-tuple-element.85), channel_id=1, source_target_pairs={{0,1},{1,2},{2,3},{3,4},{4,5},{5,6},{6,7},{8,9},{9,10},{10,11},{11... | collective-permute-start | bytes 2138120 | tf_op jit(solution)/shard_map/ppermute | solution.py:542
  78.9 19.8 %collective-permute-start.19 = (bf16[3,58,16,128]{3,2,1,0:T(8,128)(2,1)}, bf16[3,58,16,128]{3,2,1,0:T(8,128)(2,1)S(1)}, u32[]{:S(2)}, u32[]{:S(2)}) collective-permute-start(bf16[3,58,16,128]{3,2,1,0:T(8,128)(2,1)} %get-tuple-element.86), channel_id=1, source_target_pairs={{1,0},{2,1},{3,2},{4,3},{5,4},{6,5},{7,6},{9,8},{10,9},{11,10},{12... | collective-permute-start | bytes 2138120 | tf_op jit(solution)/shard_map/ppermute | solution.py:542
  111.8 32.2 %copy-start.8 = (f32[2,28,28,128]{3,0,2,1:T(2,128)S(1)}, f32[2,28,28,128]{3,0,2,1:T(2,128)}, u32[]{:S(2)}) copy-start(f32[2,28,28,128]{3,0,2,1:T(2,128)} %param.7) | copy-start | bytes 2408452
  111.8 44.3 %copy-start.4 = (s32[1,1,6]{2,1,0:T(1,128)S(1)}, s32[1,1,6]{2,1,0:T(1,128)}, u32[]{:S(2)}) copy-start(s32[1,1,6]{2,1,0:T(1,128)} %param.13) | copy-start | bytes 76
  111.8 24.7 %all-to-all-start = ((s16[16,2,3,56,128]{4,3,2,1,0:T(8,128)(2,1)}), s16[16,2,3,56,128]{4,3,2,1,0:T(8,128)(2,1)S(1)}, u32[]{:S(2)}, u32[]{:S(2)}) async-start(s16[16,2,3,56,128]{4,3,2,1,0:T(8,128)(2,1)} %jobs.3), calls=%async_computation | async-start | bytes 2752512 | tf_op jit(solution)/shard_map/all_to_all | solution.py:560
  138.8 17.3 %all-to-all-start.1 = ((s16[16,2,56,128]{3,2,1,0:T(8,128)(2,1)}), s16[16,2,56,128]{3,2,1,0:T(8,128)(2,1)S(1)}, u32[]{:S(2)}, u32[]{:S(2)}) async-start(s16[16,2,56,128]{3,2,1,0:T(8,128)(2,1)} %add_up.1), calls=%async_computation.1 | async-start | bytes 917504 | tf_op jit(solution)/shard_map/all_to_all | solution.py:561
  (9 other events, 110.7 us)

commit v11 on v9

--- a/solution.py
+++ b/solution.py
@@ -52,23 +52,17 @@
 
 
 def join_kernel(*refs):
-    stage, sems, refs = refs[-2], refs[-1], refs[:-2]
+    sems, refs = refs[-1], refs[:-1]
     outs, refs = refs[-2:], refs[:-2]
     each = len(refs) // len(outs)
     rows = refs[0].shape[0]
-    ins = []
+    copies = []
     for i, ref in enumerate(refs):
-        target = stage.at[i // each, pl.ds(i % each * rows, rows)]
-        ins.append(pltpu.make_async_copy(ref, target, sems.at[i]))
-        ins[i].start()
-    sends = []
-    for i, out in enumerate(outs):
-        for copy in ins[i * each : (i + 1) * each]:
-            copy.wait()
-        sends.append(pltpu.make_async_copy(stage.at[i], out, sems.at[len(refs) + i]))
-        sends[i].start()
-    for send in sends:
-        send.wait()
+        target = outs[i // each].at[pl.ds(i % each * rows, rows)]
+        copies.append(pltpu.make_async_copy(ref, target, sems.at[i]))
+        copies[i].start()
+    for copy in copies:
+        copy.wait()
 
 
 def join(rings):
@@ -79,30 +73,23 @@
         in_specs=[pl.BlockSpec(memory_space=pl.ANY)] * len(arrays),
         out_specs=[pl.BlockSpec(memory_space=pltpu.HBM)] * len(rings),
         out_shape=[pltpu.HBM(whole, BF16)] * len(rings),
-        scratch_shapes=[
-            pltpu.VMEM((len(rings),) + whole, BF16),
-            pltpu.SemaphoreType.DMA((len(arrays) + len(rings),)),
-        ],
-        compiler_params=pltpu.CompilerParams(vmem_limit_bytes=4 << 20),
+        scratch_shapes=[pltpu.SemaphoreType.DMA((len(arrays),))],
+        compiler_params=pltpu.CompilerParams(vmem_limit_bytes=1 << 20),
         name="join",
     )(*arrays)
 
 
 def halves_kernel(*refs):
-    stage, sems, refs = refs[-2], refs[-1], refs[:-2]
+    sems, refs = refs[-1], refs[:-1]
     count = len(refs) // 2
-    ins, outs = [], []
+    copies = []
     for i in range(count):
         half = refs[i].shape[0] // 2
         source = refs[i].at[pl.ds(0 if i % 2 == 0 else half, half)]
-        ins.append(pltpu.make_async_copy(source, stage.at[i], sems.at[i, 0]))
-        outs.append(pltpu.make_async_copy(stage.at[i], refs[count + i], sems.at[i, 1]))
-        ins[i].start()
-    for i in range(count):
-        ins[i].wait()
-        outs[i].start()
-    for i in range(count):
-        outs[i].wait()
+        copies.append(pltpu.make_async_copy(source, refs[count + i], sems.at[i]))
+        copies[i].start()
+    for copy in copies:
+        copy.wait()
 
 
 def take_halves(near):
@@ -114,11 +101,8 @@
         in_specs=[anywhere] * len(arrays),
         out_specs=[anywhere] * len(arrays),
         out_shape=[pltpu.HBM((shape[0] // 2,) + shape[1:], BF16)] * len(arrays),
-        scratch_shapes=[
-            pltpu.VMEM((len(arrays), shape[0] // 2) + shape[1:], BF16),
-            pltpu.SemaphoreType.DMA((len(arrays), 2)),
-        ],
-        compiler_params=pltpu.CompilerParams(vmem_limit_bytes=4 << 20),
+        scratch_shapes=[pltpu.SemaphoreType.DMA((len(arrays),))],
+        compiler_params=pltpu.CompilerParams(vmem_limit_bytes=1 << 20),
         name="halves",
     )(*arrays)
     return [(taken[2 * i], taken[2 * i + 1]) for i in range(len(near))]

time: 159 us -> 155 us (0.975)
  Pallas kernels: 38.9 us -> 35.5 us
    pallas_call x1, Pallas kernels: 3.8 us -> 1.42 us  [join(): pl.pallas_call(join_kernel, in_specs=[pl.BlockSpec(memory_space=pl.ANY)]...]
where the time goes in v11:
time: 155 us; the launch traced here: 154 us
  starting transfers between devices  57 us (37%)
  waiting for transfers between devices  37.1 us (24%)
  Pallas kernels  35.5 us (23%)
  local copies, waits for them, and re-layouts  13.9 us (9%)
  other arithmetic  10.3 us (7%)
    pallas_call x2, Pallas kernels, run_jobs(): pl.pallas_call(functools.partial(job_kernel, channel), grid=(slots,), in_...  26 us
    ppermute x14, starting transfers between devices, torus_step(): return lax.ppermute(array, 'tile', pairs)  24 us
    all_to_all x2, starting transfers between devices, on_device(): parts.append(lax.all_to_all(factors, 'tile', 0, 0, tiled=True))  11.7 us
    all_to_all x1, waiting for transfers between devices, on_device(): lax.all_to_all(add_up(owners, seen_by, logs, parts), 'tile', 0, 0, tiled=...  11.3 us
    ppermute x14, waiting for transfers between devices, torus_step(): return lax.ppermute(array, 'tile', pairs)  10.9 us
    all_to_all x2, waiting for transfers between devices, on_device(): parts.append(lax.all_to_all(factors, 'tile', 0, 0, tiled=True))  9.37 us
    ppermute x2, starting transfers between devices, on_device(): lax.ppermute(rims[2 * c + 1], 'view', downward)  7.18 us
    optimization_barrier x1, local copies, waits for them, and re-layouts, on_device(): lax.optimization_barrier((join(rings), view_data, bricks))  6.45 us
  transfers between devices with their start and end apart: 23, of which 10 were waited for; matrix products, arithmetic and copies ran while one was open for 12% of the time, Pallas kernels for 17%

profile of v11, /device:TPU:32, one launch (start us, length us, event | category | flops | bytes accessed | tf_op | source)
XLA Modules:
  0.0 154.3 jit_solution(1903692556633629318)
XLA Ops:
  11.9 2.6 %collective-permute-start.5 = (bf16[28,32,128]{2,1,0:T(8,128)(2,1)S(1)}, bf16[28,32,128]{2,1,0:T(8,128)(2,1)S(1)}, u32[]{:S(2)}, u32[]{:S(2)}) collective-permute-start(bf16[28,32,128]{2,1,0:T(8,128)(2,1)S(1)} %get-tuple-element.54.refs_4_), channel_id=1, source_target_pairs={{0,16},{8,24},{16,0},{24,8},{32,48},{40,56},{48,32},{56,40},{64,80... | collective-permute-start | bytes 688136 | tf_op jit(solution)/shard_map/ppermute | solution.py:34
  24.2 2.3 %collective-permute-start.7 = (bf16[112,32,128]{2,1,0:T(8,128)(2,1)}, bf16[112,32,128]{2,1,0:T(8,128)(2,1)S(1)}, u32[]{:S(2)}, u32[]{:S(2)}) collective-permute-start(bf16[112,32,128]{2,1,0:T(8,128)(2,1)} %get-tuple-element.64.refs_3_.refs_0_), channel_id=1, source_target_pairs={{0,24},{8,0},{16,8},{24,16},{32,56},{40,32},{48,40},{56,48},{64,88... | collective-permute-start | bytes 2752520 | tf_op jit(solution)/shard_map/ppermute | solution.py:34
  27.8 2.0 %collective-permute-start.9 = (bf16[112,32,128]{2,1,0:T(8,128)(2,1)}, bf16[112,32,128]{2,1,0:T(8,128)(2,1)S(1)}, u32[]{:S(2)}, u32[]{:S(2)}) collective-permute-start(bf16[112,32,128]{2,1,0:T(8,128)(2,1)} %get-tuple-element.73.refs_8_.refs_0_), channel_id=1, source_target_pairs={{0,96},{8,104},{16,112},{24,120},{32,0},{40,8},{48,16},{56,24},{64... | collective-permute-start | bytes 2752520 | tf_op jit(solution)/shard_map/ppermute | solution.py:34
  29.8 6.5 %copy.67 = bf16[1,1,3,2,58,58,128]{6,5,4,3,2,1,0:T(8,128)(2,1)} copy(bf16[1,1,3,2,58,58,128]{6,3,5,4,2,1,0:T(2,128)(2,1)} %param.8) | data formatting | bytes 10334208 | tf_op jit(solution)/shard_map/optimization_barrier | solution.py:509
  36.2 1.9 %collective-permute-start.10 = (s32[3]{0:T(128)S(1)}, s32[3]{0:T(128)S(1)}, u32[]{:S(2)}, u32[]{:S(2)}) collective-permute-start(s32[3]{0:T(128)S(1)} %bitcast.47), channel_id=1, source_target_pairs={{1,0},{2,1},{3,2},{4,3},{5,4},{6,5},{7,6},{9,8},{10,9},{11,10},{12... | collective-permute-start | bytes 44 | tf_op jit(solution)/shard_map/ppermute | solution.py:511
  39.4 4.1 %collective-permute-start.11 = (s32[3]{0:T(128)S(1)}, s32[3]{0:T(128)S(1)}, u32[]{:S(2)}, u32[]{:S(2)}) collective-permute-start(s32[3]{0:T(128)S(1)} %bitcast.48), channel_id=1, source_target_pairs={{0,1},{1,2},{2,3},{3,4},{4,5},{5,6},{6,7},{8,9},{9,10},{10,11},{11... | collective-permute-start | bytes 44 | tf_op jit(solution)/shard_map/ppermute | solution.py:512
  45.5 2.7 %collective-permute-done.8.refs_2_.refs_9_.refs_1_ = bf16[112,32,128]{2,1,0:T(8,128)(2,1)S(1)} collective-permute-done((bf16[112,32,128]{2,1,0:T(8,128)(2,1)}, bf16[112,32,128]{2,1,0:T(8,128)(2,1)S(1)}, u32[]{:S(2)}, u32[]{:S(2)}) %collective-permute-start.8) | collective-permute-done | bytes 917536 | tf_op jit(solution)/shard_map/ppermute | solution.py:34
  50.5 3.2 %collective-permute-start.13 = (bf16[56,32,128]{2,1,0:T(8,128)(2,1)}, bf16[56,32,128]{2,1,0:T(8,128)(2,1)}, u32[]{:S(2)}, u32[]{:S(2)}) collective-permute-start(bf16[56,32,128]{2,1,0:T(8,128)(2,1)} %get-tuple-element.70), channel_id=1, source_target_pairs={{0,24},{8,0},{16,8},{24,16},{32,56},{40,32},{48,40},{56,48},{64,88... | collective-permute-start | bytes 1376264 | tf_op jit(solution)/shard_map/ppermute | solution.py:34
  53.9 3.0 %collective-permute-start.15 = (bf16[56,32,128]{2,1,0:T(8,128)(2,1)}, bf16[56,32,128]{2,1,0:T(8,128)(2,1)}, u32[]{:S(2)}, u32[]{:S(2)}) collective-permute-start(bf16[56,32,128]{2,1,0:T(8,128)(2,1)} %get-tuple-element.75), channel_id=1, source_target_pairs={{0,96},{8,104},{16,112},{24,120},{32,0},{40,8},{48,16},{56,24},{64... | collective-permute-start | bytes 1376264 | tf_op jit(solution)/shard_map/ppermute | solution.py:34
  56.9 4.4 %collective-permute-done.12.refs_6_.refs_3_ = bf16[56,32,128]{2,1,0:T(8,128)(2,1)S(1)} collective-permute-done((bf16[56,32,128]{2,1,0:T(8,128)(2,1)}, bf16[56,32,128]{2,1,0:T(8,128)(2,1)S(1)}, u32[]{:S(2)}, u32[]{:S(2)}) %collective-permute-start.12) | collective-permute-done | bytes 458784 | tf_op jit(solution)/shard_map/ppermute | solution.py:34
  61.4 2.8 %collective-permute-done.14.refs_11_.refs_3_ = bf16[56,32,128]{2,1,0:T(8,128)(2,1)} collective-permute-done((bf16[56,32,128]{2,1,0:T(8,128)(2,1)}, bf16[56,32,128]{2,1,0:T(8,128)(2,1)}, u32[]{:S(2)}, u32[]{:S(2)}) %collective-permute-start.14) | collective-permute-done | bytes 458784 | tf_op jit(solution)/shard_map/ppermute | solution.py:34
  64.2 3.7 %margins.1 = (bf16[3,58,16,128]{3,2,1,0:T(8,128)(2,1)}, bf16[3,58,16,128]{3,2,1,0:T(8,128)(2,1)}, bf16[3,58,16,128]{3,2,1,0:T(8,128)(2,1)}, bf16[3,58,16,128]{3,2,1,0:T(8,128)(2,1)}) custom-call(s32[1]{0:T(128)} %bitcast.17.refs_0_.me, s32[3]{0:T(128)S(1)} %collective-permute-done.10.refs_1_, s32[3]{0:T(128)S(1)} %collective-permute-done.11.refs_2_, ...), custom_call_target="tpu_custom_call" | custom-call | tf_op jit(solution)/shard_map/margins/pallas_call | solution.py:194
  67.8 1.9 %collective-permute-start.18 = (bf16[3,58,16,128]{3,2,1,0:T(8,128)(2,1)}, bf16[3,58,16,128]{3,2,1,0:T(8,128)(2,1)S(1)}, u32[]{:S(2)}, u32[]{:S(2)}) collective-permute-start(bf16[3,58,16,128]{3,2,1,0:T(8,128)(2,1)} %get-tuple-element.85), channel_id=1, source_target_pairs={{0,1},{1,2},{2,3},{3,4},{4,5},{5,6},{6,7},{8,9},{9,10},{10,11},{11... | collective-permute-start | bytes 2138120 | tf_op jit(solution)/shard_map/ppermute | solution.py:519
  69.8 3.6 %collective-permute-start.19 = (bf16[3,58,16,128]{3,2,1,0:T(8,128)(2,1)}, bf16[3,58,16,128]{3,2,1,0:T(8,128)(2,1)S(1)}, u32[]{:S(2)}, u32[]{:S(2)}) collective-permute-start(bf16[3,58,16,128]{3,2,1,0:T(8,128)(2,1)} %get-tuple-element.86), channel_id=1, source_target_pairs={{1,0},{2,1},{3,2},{4,3},{5,4},{6,5},{7,6},{9,8},{10,9},{11,10},{12... | collective-permute-start | bytes 2138120 | tf_op jit(solution)/shard_map/ppermute | solution.py:519
  73.4 2.2 %collective-permute-start.16 = (bf16[3,58,16,128]{3,2,1,0:T(8,128)(2,1)}, bf16[3,58,16,128]{3,2,1,0:T(8,128)(2,1)S(1)}, u32[]{:S(2)}, u32[]{:S(2)}) collective-permute-start(bf16[3,58,16,128]{3,2,1,0:T(8,128)(2,1)} %get-tuple-element.76), channel_id=1, source_target_pairs={{0,1},{1,2},{2,3},{3,4},{4,5},{5,6},{6,7},{8,9},{9,10},{10,11},{11... | collective-permute-start | bytes 2138120 | tf_op jit(solution)/shard_map/ppermute | solution.py:519
  75.6 3.5 %collective-permute-start.17 = (bf16[3,58,16,128]{3,2,1,0:T(8,128)(2,1)}, bf16[3,58,16,128]{3,2,1,0:T(8,128)(2,1)S(1)}, u32[]{:S(2)}, u32[]{:S(2)}) collective-permute-start(bf16[3,58,16,128]{3,2,1,0:T(8,128)(2,1)} %get-tuple-element.77), channel_id=1, source_target_pairs={{1,0},{2,1},{3,2},{4,3},{5,4},{6,5},{7,6},{9,8},{10,9},{11,10},{12... | collective-permute-start | bytes 2138120 | tf_op jit(solution)/shard_map/ppermute | solution.py:519
  82.4 13.0 %jobs.3 = s16[16,3,56,128]{3,2,1,0:T(8,128)(2,1)} custom-call(s32[1]{0:T(128)} %bitcast.17.refs_0_.me, s32[3]{0:T(128)S(1)} %bitcast.49, s32[3]{0:T(128)S(1)} %bitcast.44, f32[6]{0:T(128)S(1)} %copy-done.5, f32[6]{0:T(128)S(1)} %multiply_add_fusion.logs, bf16[112,32,128]{2,1,0:T(8,128)(2,1)} %get-tuple-element.73.refs_8_.refs_0_, ...), custom_call_target="tpu_custom_call" | custom-call | flops 23624417280 | bytes 7077888 | tf_op jit(solution)/shard_map/jobs/pallas_call | solution.py:361
  95.5 4.4 %all-to-all-start.1 = ((s16[16,3,56,128]{3,2,1,0:T(8,128)(2,1)}), s16[16,3,56,128]{3,2,1,0:T(8,128)(2,1)S(1)}, u32[]{:S(2)}, u32[]{:S(2)}) async-start(s16[16,3,56,128]{3,2,1,0:T(8,128)(2,1)} %jobs.3), calls=%async_computation.1 | async-start | bytes 1376256 | tf_op jit(solution)/shard_map/all_to_all | solution.py:533
  99.8 13.0 %jobs.2 = s16[16,3,56,128]{3,2,1,0:T(8,128)(2,1)} custom-call(s32[1]{0:T(128)} %bitcast.17.refs_0_.me, s32[3]{0:T(128)S(1)} %bitcast.50, s32[3]{0:T(128)S(1)} %bitcast.45, f32[6]{0:T(128)S(1)} %copy-done.5, f32[6]{0:T(128)S(1)} %multiply_add_fusion.logs, bf16[112,32,128]{2,1,0:T(8,128)(2,1)} %get-tuple-element.64.refs_3_.refs_0_, ...), custom_call_target="tpu_custom_call" | custom-call | flops 23624417280 | bytes 7077888 | tf_op jit(solution)/shard_map/jobs/pallas_call | solution.py:361
  112.9 7.4 %all-to-all-start = ((s16[16,3,56,128]{3,2,1,0:T(8,128)(2,1)}), s16[16,3,56,128]{3,2,1,0:T(8,128)(2,1)S(1)}, u32[]{:S(2)}, u32[]{:S(2)}) async-start(s16[16,3,56,128]{3,2,1,0:T(8,128)(2,1)} %jobs.2), calls=%async_computation | async-start | bytes 1376256 | tf_op jit(solution)/shard_map/all_to_all | solution.py:533
  124.9 9.4 %all-to-all-done.refs_0_ = s16[16,3,56,128]{3,2,1,0:T(8,128)(2,1)S(1)} async-done(((s16[16,3,56,128]{3,2,1,0:T(8,128)(2,1)}), s16[16,3,56,128]{3,2,1,0:T(8,128)(2,1)S(1)}, u32[]{:S(2)}, u32[]{:S(2)}) %all-to-all-start) | async-done | bytes 688160 | tf_op jit(solution)/shard_map/all_to_all | solution.py:533
  134.3 2.3 %add_up.1 = s16[16,2,56,128]{3,2,1,0:T(8,128)(2,1)} custom-call(s32[48]{0:T(128)S(1)} %reshape.376.owners, s32[48]{0:T(128)S(1)} %reshape.377.views, f32[6]{0:T(128)S(1)} %multiply_add_fusion.logs, s16[16,3,56,128]{3,2,1,0:T(8,128)(2,1)S(1)} %all-to-all-done.refs_0_, s16[16,3,56,128]{3,2,1,0:T(8,128)(2,1)S(1)} %all-to-all-done.1.refs_1_), custom_call_target="tpu_custom_call" | custom-call | tf_op jit(solution)/shard_map/add_up/pallas_call | solution.py:452
  136.6 3.9 %all-to-all-start.2 = ((s16[16,2,56,128]{3,2,1,0:T(8,128)(2,1)}), s16[16,2,56,128]{3,2,1,0:T(8,128)(2,1)S(1)}, u32[]{:S(2)}, u32[]{:S(2)}) async-start(s16[16,2,56,128]{3,2,1,0:T(8,128)(2,1)} %add_up.1), calls=%async_computation.2 | async-start | bytes 917504 | tf_op jit(solution)/shard_map/all_to_all | solution.py:534
  140.6 11.3 %all-to-all-done.2.total = s16[16,2,56,128]{3,2,1,0:T(8,128)(2,1)S(1)} async-done(((s16[16,2,56,128]{3,2,1,0:T(8,128)(2,1)}), s16[16,2,56,128]{3,2,1,0:T(8,128)(2,1)S(1)}, u32[]{:S(2)}, u32[]{:S(2)}) %all-to-all-start.2) | async-done | bytes 458784 | tf_op jit(solution)/shard_map/all_to_all | solution.py:534
  (124 shorter events, 38.6 us)
Async XLA Ops:
  2.6 9.3 %collective-permute-start = (bf16[28,32,128]{2,1,0:T(8,128)(2,1)S(1)}, bf16[28,32,128]{2,1,0:T(8,128)(2,1)S(1)}, u32[]{:S(2)}, u32[]{:S(2)}) collective-permute-start(bf16[28,32,128]{2,1,0:T(8,128)(2,1)S(1)} %get-tuple-element.50.refs_0_), channel_id=1, source_target_pairs={{0,32},{8,40},{16,48},{24,56},{32,64},{40,72},{48,80},{56,88},{64,... | collective-permute-start | bytes 688136 | tf_op jit(solution)/shard_map/ppermute | solution.py:34
  4.2 17.6 %collective-permute-start.1 = (bf16[28,32,128]{2,1,0:T(8,128)(2,1)S(1)}, bf16[28,32,128]{2,1,0:T(8,128)(2,1)S(1)}, u32[]{:S(2)}, u32[]{:S(2)}) collective-permute-start(bf16[28,32,128]{2,1,0:T(8,128)(2,1)S(1)} %get-tuple-element.50.refs_0_), channel_id=1, source_target_pairs={{0,96},{8,104},{16,112},{24,120},{32,0},{40,8},{48,16},{56,24},{64... | collective-permute-start | bytes 688136 | tf_op jit(solution)/shard_map/ppermute | solution.py:34
  5.9 15.8 %collective-permute-start.2 = (bf16[28,32,128]{2,1,0:T(8,128)(2,1)S(1)}, bf16[28,32,128]{2,1,0:T(8,128)(2,1)S(1)}, u32[]{:S(2)}, u32[]{:S(2)}) collective-permute-start(bf16[28,32,128]{2,1,0:T(8,128)(2,1)S(1)} %get-tuple-element.50.refs_0_), channel_id=1, source_target_pairs={{0,64},{8,72},{16,80},{24,88},{32,96},{40,104},{48,112},{56,120},{... | collective-permute-start | bytes 688136 | tf_op jit(solution)/shard_map/ppermute | solution.py:34
  7.7 14.0 %collective-permute-start.3 = (bf16[28,32,128]{2,1,0:T(8,128)(2,1)S(1)}, bf16[28,32,128]{2,1,0:T(8,128)(2,1)S(1)}, u32[]{:S(2)}, u32[]{:S(2)}) collective-permute-start(bf16[28,32,128]{2,1,0:T(8,128)(2,1)S(1)} %get-tuple-element.54.refs_4_), channel_id=1, source_target_pairs={{0,8},{8,16},{16,24},{24,0},{32,40},{40,48},{48,56},{56,32},{64,72... | collective-permute-start | bytes 688136 | tf_op jit(solution)/shard_map/ppermute | solution.py:34
  9.3 12.5 %collective-permute-start.4 = (bf16[28,32,128]{2,1,0:T(8,128)(2,1)S(1)}, bf16[28,32,128]{2,1,0:T(8,128)(2,1)S(1)}, u32[]{:S(2)}, u32[]{:S(2)}) collective-permute-start(bf16[28,32,128]{2,1,0:T(8,128)(2,1)S(1)} %get-tuple-element.54.refs_4_), channel_id=1, source_target_pairs={{0,24},{8,0},{16,8},{24,16},{32,56},{40,32},{48,40},{56,48},{64,88... | collective-permute-start | bytes 688136 | tf_op jit(solution)/shard_map/ppermute | solution.py:34
  11.9 9.8 %collective-permute-start.5 = (bf16[28,32,128]{2,1,0:T(8,128)(2,1)S(1)}, bf16[28,32,128]{2,1,0:T(8,128)(2,1)S(1)}, u32[]{:S(2)}, u32[]{:S(2)}) collective-permute-start(bf16[28,32,128]{2,1,0:T(8,128)(2,1)S(1)} %get-tuple-element.54.refs_4_), channel_id=1, source_target_pairs={{0,16},{8,24},{16,0},{24,8},{32,48},{40,56},{48,32},{56,40},{64,80... | collective-permute-start | bytes 688136 | tf_op jit(solution)/shard_map/ppermute | solution.py:34
  23.2 22.3 %collective-permute-start.6 = (bf16[112,32,128]{2,1,0:T(8,128)(2,1)}, bf16[112,32,128]{2,1,0:T(8,128)(2,1)S(1)}, u32[]{:S(2)}, u32[]{:S(2)}) collective-permute-start(bf16[112,32,128]{2,1,0:T(8,128)(2,1)} %get-tuple-element.64.refs_3_.refs_0_), channel_id=1, source_target_pairs={{0,8},{8,16},{16,24},{24,0},{32,40},{40,48},{48,56},{56,32},{64,72... | collective-permute-start | bytes 2752520 | tf_op jit(solution)/shard_map/ppermute | solution.py:34
  24.2 21.3 %collective-permute-start.7 = (bf16[112,32,128]{2,1,0:T(8,128)(2,1)}, bf16[112,32,128]{2,1,0:T(8,128)(2,1)S(1)}, u32[]{:S(2)}, u32[]{:S(2)}) collective-permute-start(bf16[112,32,128]{2,1,0:T(8,128)(2,1)} %get-tuple-element.64.refs_3_.refs_0_), channel_id=1, source_target_pairs={{0,24},{8,0},{16,8},{24,16},{32,56},{40,32},{48,40},{56,48},{64,88... | collective-permute-start | bytes 2752520 | tf_op jit(solution)/shard_map/ppermute | solution.py:34
  26.5 21.6 %collective-permute-start.8 = (bf16[112,32,128]{2,1,0:T(8,128)(2,1)}, bf16[112,32,128]{2,1,0:T(8,128)(2,1)S(1)}, u32[]{:S(2)}, u32[]{:S(2)}) collective-permute-start(bf16[112,32,128]{2,1,0:T(8,128)(2,1)} %get-tuple-element.73.refs_8_.refs_0_), channel_id=1, source_target_pairs={{0,32},{8,40},{16,48},{24,56},{32,64},{40,72},{48,80},{56,88},{64,... | collective-permute-start | bytes 2752520 | tf_op jit(solution)/shard_map/ppermute | solution.py:34
  27.8 20.4 %collective-permute-start.9 = (bf16[112,32,128]{2,1,0:T(8,128)(2,1)}, bf16[112,32,128]{2,1,0:T(8,128)(2,1)S(1)}, u32[]{:S(2)}, u32[]{:S(2)}) collective-permute-start(bf16[112,32,128]{2,1,0:T(8,128)(2,1)} %get-tuple-element.73.refs_8_.refs_0_), channel_id=1, source_target_pairs={{0,96},{8,104},{16,112},{24,120},{32,0},{40,8},{48,16},{56,24},{64... | collective-permute-start | bytes 2752520 | tf_op jit(solution)/shard_map/ppermute | solution.py:34
  36.2 3.2 %collective-permute-start.10 = (s32[3]{0:T(128)S(1)}, s32[3]{0:T(128)S(1)}, u32[]{:S(2)}, u32[]{:S(2)}) collective-permute-start(s32[3]{0:T(128)S(1)} %bitcast.47), channel_id=1, source_target_pairs={{1,0},{2,1},{3,2},{4,3},{5,4},{6,5},{7,6},{9,8},{10,9},{11,10},{12... | collective-permute-start | bytes 44 | tf_op jit(solution)/shard_map/ppermute | solution.py:511
  39.4 5.1 %collective-permute-start.11 = (s32[3]{0:T(128)S(1)}, s32[3]{0:T(128)S(1)}, u32[]{:S(2)}, u32[]{:S(2)}) collective-permute-start(s32[3]{0:T(128)S(1)} %bitcast.48), channel_id=1, source_target_pairs={{0,1},{1,2},{2,3},{3,4},{4,5},{5,6},{6,7},{8,9},{9,10},{10,11},{11... | collective-permute-start | bytes 44 | tf_op jit(solution)/shard_map/ppermute | solution.py:512
  50.5 10.9 %collective-permute-start.12 = (bf16[56,32,128]{2,1,0:T(8,128)(2,1)}, bf16[56,32,128]{2,1,0:T(8,128)(2,1)S(1)}, u32[]{:S(2)}, u32[]{:S(2)}) collective-permute-start(bf16[56,32,128]{2,1,0:T(8,128)(2,1)} %get-tuple-element.69), channel_id=1, source_target_pairs={{0,8},{8,16},{16,24},{24,0},{32,40},{40,48},{48,56},{56,32},{64,72... | collective-permute-start | bytes 1376264 | tf_op jit(solution)/shard_map/ppermute | solution.py:34
  50.5 10.9 %collective-permute-start.13 = (bf16[56,32,128]{2,1,0:T(8,128)(2,1)}, bf16[56,32,128]{2,1,0:T(8,128)(2,1)}, u32[]{:S(2)}, u32[]{:S(2)}) collective-permute-start(bf16[56,32,128]{2,1,0:T(8,128)(2,1)} %get-tuple-element.70), channel_id=1, source_target_pairs={{0,24},{8,0},{16,8},{24,16},{32,56},{40,32},{48,40},{56,48},{64,88... | collective-permute-start | bytes 1376264 | tf_op jit(solution)/shard_map/ppermute | solution.py:34
  53.7 10.4 %collective-permute-start.14 = (bf16[56,32,128]{2,1,0:T(8,128)(2,1)}, bf16[56,32,128]{2,1,0:T(8,128)(2,1)}, u32[]{:S(2)}, u32[]{:S(2)}) collective-permute-start(bf16[56,32,128]{2,1,0:T(8,128)(2,1)} %get-tuple-element.74), channel_id=1, source_target_pairs={{0,32},{8,40},{16,48},{24,56},{32,64},{40,72},{48,80},{56,88},{64,... | collective-permute-start | bytes 1376264 | tf_op jit(solution)/shard_map/ppermute | solution.py:34
  53.9 10.2 %collective-permute-start.15 = (bf16[56,32,128]{2,1,0:T(8,128)(2,1)}, bf16[56,32,128]{2,1,0:T(8,128)(2,1)}, u32[]{:S(2)}, u32[]{:S(2)}) collective-permute-start(bf16[56,32,128]{2,1,0:T(8,128)(2,1)} %get-tuple-element.75), channel_id=1, source_target_pairs={{0,96},{8,104},{16,112},{24,120},{32,0},{40,8},{48,16},{56,24},{64... | collective-permute-start | bytes 1376264 | tf_op jit(solution)/shard_map/ppermute | solution.py:34
  67.8 12.7 %collective-permute-start.18 = (bf16[3,58,16,128]{3,2,1,0:T(8,128)(2,1)}, bf16[3,58,16,128]{3,2,1,0:T(8,128)(2,1)S(1)}, u32[]{:S(2)}, u32[]{:S(2)}) collective-permute-start(bf16[3,58,16,128]{3,2,1,0:T(8,128)(2,1)} %get-tuple-element.85), channel_id=1, source_target_pairs={{0,1},{1,2},{2,3},{3,4},{4,5},{5,6},{6,7},{8,9},{9,10},{10,11},{11... | collective-permute-start | bytes 2138120 | tf_op jit(solution)/shard_map/ppermute | solution.py:519
  69.8 12.7 %collective-permute-start.19 = (bf16[3,58,16,128]{3,2,1,0:T(8,128)(2,1)}, bf16[3,58,16,128]{3,2,1,0:T(8,128)(2,1)S(1)}, u32[]{:S(2)}, u32[]{:S(2)}) collective-permute-start(bf16[3,58,16,128]{3,2,1,0:T(8,128)(2,1)} %get-tuple-element.86), channel_id=1, source_target_pairs={{1,0},{2,1},{3,2},{4,3},{5,4},{6,5},{7,6},{9,8},{10,9},{11,10},{12... | collective-permute-start | bytes 2138120 | tf_op jit(solution)/shard_map/ppermute | solution.py:519
  73.4 26.4 %collective-permute-start.16 = (bf16[3,58,16,128]{3,2,1,0:T(8,128)(2,1)}, bf16[3,58,16,128]{3,2,1,0:T(8,128)(2,1)S(1)}, u32[]{:S(2)}, u32[]{:S(2)}) collective-permute-start(bf16[3,58,16,128]{3,2,1,0:T(8,128)(2,1)} %get-tuple-element.76), channel_id=1, source_target_pairs={{0,1},{1,2},{2,3},{3,4},{4,5},{5,6},{6,7},{8,9},{9,10},{10,11},{11... | collective-permute-start | bytes 2138120 | tf_op jit(solution)/shard_map/ppermute | solution.py:519
  75.6 24.2 %collective-permute-start.17 = (bf16[3,58,16,128]{3,2,1,0:T(8,128)(2,1)}, bf16[3,58,16,128]{3,2,1,0:T(8,128)(2,1)S(1)}, u32[]{:S(2)}, u32[]{:S(2)}) collective-permute-start(bf16[3,58,16,128]{3,2,1,0:T(8,128)(2,1)} %get-tuple-element.77), channel_id=1, source_target_pairs={{1,0},{2,1},{3,2},{4,3},{5,4},{6,5},{7,6},{9,8},{10,9},{11,10},{12... | collective-permute-start | bytes 2138120 | tf_op jit(solution)/shard_map/ppermute | solution.py:519
  95.5 17.4 %all-to-all-start.1 = ((s16[16,3,56,128]{3,2,1,0:T(8,128)(2,1)}), s16[16,3,56,128]{3,2,1,0:T(8,128)(2,1)S(1)}, u32[]{:S(2)}, u32[]{:S(2)}) async-start(s16[16,3,56,128]{3,2,1,0:T(8,128)(2,1)} %jobs.3), calls=%async_computation.1 | async-start | bytes 1376256 | tf_op jit(solution)/shard_map/all_to_all | solution.py:533
  112.9 39.1 %copy-start.4 = (s32[1,1,6]{2,1,0:T(1,128)S(1)}, s32[1,1,6]{2,1,0:T(1,128)}, u32[]{:S(2)}) copy-start(s32[1,1,6]{2,1,0:T(1,128)} %param.13) | copy-start | bytes 76
  112.9 21.4 %all-to-all-start = ((s16[16,3,56,128]{3,2,1,0:T(8,128)(2,1)}), s16[16,3,56,128]{3,2,1,0:T(8,128)(2,1)S(1)}, u32[]{:S(2)}, u32[]{:S(2)}) async-start(s16[16,3,56,128]{3,2,1,0:T(8,128)(2,1)} %jobs.2), calls=%async_computation | async-start | bytes 1376256 | tf_op jit(solution)/shard_map/all_to_all | solution.py:533
  136.6 15.4 %all-to-all-start.2 = ((s16[16,2,56,128]{3,2,1,0:T(8,128)(2,1)}), s16[16,2,56,128]{3,2,1,0:T(8,128)(2,1)S(1)}, u32[]{:S(2)}, u32[]{:S(2)}) async-start(s16[16,2,56,128]{3,2,1,0:T(8,128)(2,1)} %add_up.1), calls=%async_computation.2 | async-start | bytes 917504 | tf_op jit(solution)/shard_map/all_to_all | solution.py:534
  (10 other events, 135.3 us)
